TPU v7x, 32 devices: a whole 2x2x4 slice. The times are simulated.
32 devices in a mesh: nodes: 8 (over y, x, core), shard: 4 (over z).
Axes of the slice: x: 2, y: 2, z: 4, core: 2. Of those that a mesh axis runs over, the one named last changes fastest.
Arguments:
- node_feats: bfloat16 [65536, 512], P(('nodes', 'shard')), may hold values from -6 to 6
- cotangent: bfloat16 [65536, 512], P(('nodes', 'shard')), may hold values from -6 to 6
- batch_ids: int32 [65536], P(('nodes', 'shard')), may hold values from 0 to 3, as said below
- valid_counts: int32 [32], P(('nodes', 'shard')), may hold values from 1024 to 2048, as said below
- proj_master: float32 [512, 2048], P('shard'), may hold values from -0.25 to 0.25
- proj_moment: float32 [512, 2048], P('shard'), may hold values from -0.25 to 0.25
- proj_square: float32 [512, 2048], P('shard'), may hold values from 0.0001 to 0.002
- out_master: float32 [512, 512], P('shard'), may hold values from -0.25 to 0.25
- out_moment: float32 [512, 512], P('shard'), may hold values from -0.25 to 0.25
- out_square: float32 [512, 512], P('shard'), may hold values from 0.0001 to 0.002
- norm_master: float32 [2, 512], P(None, 'shard')
- norm_moment: float32 [2, 512], P(None, 'shard'), may hold values from -0.5 to 0.5
- norm_square: float32 [2, 512], P(None, 'shard'), may hold values from 0.0002 to 0.01
Outputs:
- block_out: float32 [65536, 512], P(('nodes', 'shard'))
- input_grad: float32 [65536, 512], P(('nodes', 'shard'))
- global_norm: float32 [1], replicated
- moment_proj: float32 [512, 2048], P('shard')
- square_proj: float32 [512, 2048], P('shard')
- updated_proj: float32 [512, 2048], P('shard')
- copy_proj: bfloat16 [512, 2048], P('shard')
- moment_out: float32 [512, 512], P('shard')
- square_out: float32 [512, 512], P('shard')
- updated_out: float32 [512, 512], P('shard')
- copy_out: bfloat16 [512, 512], P('shard')
- clipped_norm: float32 [2, 512], P(None, 'shard')
- moment_norm: float32 [2, 512], P(None, 'shard')
- square_norm: float32 [2, 512], P(None, 'shard')
- updated_norm: float32 [2, 512], P(None, 'shard')
Inputs may be any that keep to these rules, and one draw needn't show every extreme that they name: `batch_ids`: slots 0 to 3 of every device hold mini-batches 0 to 3 in order. `valid_counts`: entry i counts the valid leading slots of device i in nodes+shard order; some device has all 2048 slots valid.
All inputs are finite; a program needn't handle non-finite values.
Results may differ from a plain program's by a relative error of at most 0.0073.
Values may be sent and summed in bfloat16 or wider, within the bound.
No kernel may reach another device: no remote copies, remote signals or barrier semaphores. Data moves between devices by JAX's collectives and lax.ppermute only.
A program may use at most 128 MiB of HBM per device.

v0:
```python
import math

import jax
import jax.numpy as jnp
from jax import lax
from jax.sharding import PartitionSpec as P

HEADS = 8
CLUSTERS = 4
STEP = 10


norm_eps = 1e-05
beta_one = 0.9
beta_two = 0.999
learn_rate = 0.05
norm_rate = 0.5
decay_rate = 0.01
adam_eps = 1e-08
highest = lax.Precision.HIGHEST
bf_type = jnp.bfloat16
fl_type = jnp.float32


def adam_update(master_w, moment_old, square_old, grad_in, clip_scale, decay_coef, step_rate):
    clipped = grad_in * clip_scale
    moment_new = beta_one * moment_old + (1.0 - beta_one) * clipped
    square_new = beta_two * square_old + (1.0 - beta_two) * clipped * clipped
    moment_hat = moment_new / (1.0 - beta_one**STEP)
    square_hat = square_new / (1.0 - beta_two**STEP)
    master_new = master_w * (1.0 - step_rate * decay_coef) - step_rate * moment_hat / (
        jnp.sqrt(square_hat) + adam_eps
    )
    return (clipped, moment_new, square_new, master_new)


def squares_of(first_arr, second_arr, third_arr):
    return (
        jnp.sum(first_arr * first_arr)
        + jnp.sum(second_arr * second_arr)
        + jnp.sum(third_arr * third_arr)
    )


def local(
    node_feats,
    cotangent,
    batch_ids,
    valid_counts,
    proj_master,
    proj_moment,
    proj_square,
    out_master,
    out_moment,
    out_square,
    norm_master,
    norm_moment,
    norm_square,
):
    row_count = node_feats.shape[0]
    feat_width = node_feats.shape[1]
    head_size = feat_width // HEADS
    valid_mask = (jnp.arange(row_count, dtype=jnp.int32) < valid_counts[0]).astype(fl_type)
    member_table = (batch_ids[:, None] == jnp.arange(CLUSTERS, dtype=jnp.int32)[None, :]).astype(
        fl_type
    )
    member_low = member_table.astype(bf_type)
    w_proj, w_out, w_norm = (
        lax.all_gather(proj_master.astype(bf_type), "shard", axis=0, tiled=True),
        lax.all_gather(out_master.astype(bf_type), "shard", axis=0, tiled=True),
        lax.all_gather(norm_master.astype(bf_type), "shard", axis=1, tiled=True),
    )
    norm_gain = w_norm[0].astype(fl_type)
    norm_shift = w_norm[1].astype(fl_type)
    projected = jnp.dot(node_feats, w_proj, preferred_element_type=fl_type)
    query_pre = projected[:, :feat_width]
    key_pre = projected[:, feat_width : 2 * feat_width]
    value_pre = projected[:, 2 * feat_width : 3 * feat_width]
    gate_pre = projected[:, 3 * feat_width :]
    sig_query = jax.nn.sigmoid(query_pre)
    sig_key = jax.nn.sigmoid(key_pre)
    query_low = sig_query.astype(bf_type)
    key_low = (sig_key * valid_mask[:, None]).astype(bf_type)
    value_low = value_pre.astype(bf_type)
    key_groups = (key_low[:, None, :] * member_low[:, :, None]).reshape(
        row_count, CLUSTERS, HEADS, head_size
    )
    query_groups = (query_low[:, None, :] * member_low[:, :, None]).reshape(
        row_count, CLUSTERS, HEADS, head_size
    )
    value_heads = value_low.reshape(row_count, HEADS, head_size)
    local_kv = jnp.einsum("nchk,nhv->chkv", key_groups, value_heads, preferred_element_type=fl_type)
    local_ks = jnp.dot(member_low.T, key_low, preferred_element_type=fl_type)
    summary, key_sum = lax.psum((local_kv, local_ks), ("nodes", "shard"))
    summary_low = summary.astype(bf_type)
    numer = jnp.einsum("nchk,chkv->nhv", query_groups, summary_low, preferred_element_type=fl_type)
    key_pick = jnp.dot(member_table, key_sum, precision=highest).reshape(
        row_count, HEADS, head_size
    )
    query_full = query_low.astype(fl_type).reshape(row_count, HEADS, head_size)
    denom = jnp.sum(query_full * key_pick, axis=-1)
    attended = numer / denom[:, :, None]
    att_flat = attended.reshape(row_count, feat_width)
    centered = att_flat - jnp.mean(att_flat, axis=-1, keepdims=True)
    inv_scale = lax.rsqrt(jnp.mean(centered * centered, axis=-1, keepdims=True) + norm_eps)
    normed = centered * inv_scale
    mixed = normed * norm_gain + norm_shift
    product = (mixed * gate_pre).astype(bf_type)
    block_out = node_feats.astype(fl_type) + valid_mask[:, None] * jnp.dot(
        product, w_out, preferred_element_type=fl_type
    )
    grad_y = cotangent * valid_mask[:, None].astype(bf_type)
    grad_wout = jnp.dot(product.T, grad_y, preferred_element_type=fl_type)
    grad_prod = jnp.dot(grad_y, w_out.T, preferred_element_type=fl_type)
    grad_mixed = grad_prod * gate_pre
    grad_gate = grad_prod * mixed
    grad_gain = jnp.sum(grad_mixed * normed, axis=0)
    grad_shift = jnp.sum(grad_mixed, axis=0)
    grad_normed = grad_mixed * norm_gain
    grad_att = inv_scale * (
        grad_normed
        - jnp.mean(grad_normed, axis=-1, keepdims=True)
        - normed * jnp.mean(grad_normed * normed, axis=-1, keepdims=True)
    )
    grad_att = grad_att.reshape(row_count, HEADS, head_size)
    grad_num_low = (grad_att / denom[:, :, None]).astype(bf_type)
    grad_den = -jnp.sum(grad_att * attended, axis=-1) / denom
    grad_num_groups = grad_num_low[:, None, :, :] * member_low[:, :, None, None]
    grad_query = (
        jnp.einsum("nchv,chkv->nhk", grad_num_groups, summary_low, preferred_element_type=fl_type)
        + grad_den[:, :, None] * key_pick
    )
    local_dkv = jnp.einsum(
        "nchk,nhv->chkv", query_groups, grad_num_low, preferred_element_type=fl_type
    )
    local_dks = jnp.dot(
        member_table.T,
        (grad_den[:, :, None] * query_full).reshape(row_count, feat_width),
        precision=highest,
    )
    grad_summary, grad_keysum = lax.psum((local_dkv, local_dks), ("nodes", "shard"))
    grad_sum_low = grad_summary.astype(bf_type)
    value_groups = (value_low[:, None, :] * member_low[:, :, None]).reshape(
        row_count, CLUSTERS, HEADS, head_size
    )
    grad_key = jnp.einsum(
        "nchv,chkv->nhk", value_groups, grad_sum_low, preferred_element_type=fl_type
    ).reshape(row_count, feat_width)
    grad_key = grad_key + jnp.dot(member_table, grad_keysum, precision=highest)
    grad_value = jnp.einsum(
        "nchk,chkv->nhv", key_groups, grad_sum_low, preferred_element_type=fl_type
    ).reshape(row_count, feat_width)
    grad_qpre = grad_query.reshape(row_count, feat_width) * sig_query * (1.0 - sig_query)
    grad_kpre = grad_key * valid_mask[:, None] * sig_key * (1.0 - sig_key)
    grad_pre = jnp.concatenate([grad_qpre, grad_kpre, grad_value, grad_gate], axis=1).astype(
        bf_type
    )
    grad_wproj = jnp.dot(node_feats.T, grad_pre, preferred_element_type=fl_type)
    input_grad = jnp.dot(grad_pre, w_proj.T, preferred_element_type=fl_type) + cotangent.astype(
        fl_type
    )
    grad_wnorm = jnp.stack([grad_gain, grad_shift])
    full_proj, full_out, full_norm = lax.psum(
        (grad_wproj, grad_wout, grad_wnorm), ("nodes", "shard")
    )
    square_sum = squares_of(full_proj, full_out, full_norm)
    owner_place = lax.axis_index("shard")
    proj_rows = proj_master.shape[0]
    norm_cols = norm_master.shape[1]
    mine_proj = lax.dynamic_slice_in_dim(full_proj, owner_place * proj_rows, proj_rows, 0)
    mine_out = lax.dynamic_slice_in_dim(full_out, owner_place * proj_rows, proj_rows, 0)
    mine_norm = lax.dynamic_slice_in_dim(full_norm, owner_place * norm_cols, norm_cols, 1)
    grad_size = jnp.sqrt(square_sum)
    clip_level = 0.5 * math.sqrt(5 * feat_width * feat_width + 2 * feat_width)
    clip_scale = jnp.minimum(1.0, clip_level / grad_size)
    unused_one, proj_mnew, proj_snew, proj_wnew = adam_update(
        proj_master, proj_moment, proj_square, mine_proj, clip_scale, decay_rate, learn_rate
    )
    unused_two, out_mnew, out_snew, out_wnew = adam_update(
        out_master, out_moment, out_square, mine_out, clip_scale, decay_rate, learn_rate
    )
    norm_clip, norm_mnew, norm_snew, norm_wnew = adam_update(
        norm_master, norm_moment, norm_square, mine_norm, clip_scale, 0.0, norm_rate
    )
    return (
        block_out,
        input_grad,
        grad_size.reshape(1),
        proj_mnew,
        proj_snew,
        proj_wnew,
        proj_wnew.astype(bf_type),
        out_mnew,
        out_snew,
        out_wnew,
        out_wnew.astype(bf_type),
        norm_clip,
        norm_mnew,
        norm_snew,
        norm_wnew,
    )


def solution(mesh):
    return jax.shard_map(
        local,
        mesh=mesh,
        in_specs=(
            P(("nodes", "shard"), None),
            P(("nodes", "shard"), None),
            P(("nodes", "shard")),
            P(("nodes", "shard")),
            P("shard", None),
            P("shard", None),
            P("shard", None),
            P("shard", None),
            P("shard", None),
            P("shard", None),
            P(None, "shard"),
            P(None, "shard"),
            P(None, "shard"),
        ),
        out_specs=(
            P(("nodes", "shard"), None),
            P(("nodes", "shard"), None),
            P(),
            P("shard", None),
            P("shard", None),
            P("shard", None),
            P("shard", None),
            P("shard", None),
            P("shard", None),
            P("shard", None),
            P("shard", None),
            P(None, "shard"),
            P(None, "shard"),
            P(None, "shard"),
            P(None, "shard"),
        ),
        check_vma=False,
    )
```

profile of v0, /device:TPU:0, one launch (start us, length us, event | category | flops | bytes accessed | tf_op | source)
XLA Modules:
  0.0 421.5 jit_solution(16435085940373340518)
XLA Ops:
  7.2 0.0 all-gather.2.cloned.1.call-start
  7.2 2.1 convert_element_type.94
  9.3 0.0 all-gather.2.cloned.1.call-update
  9.3 0.0 all-reduce.7.cloned.1.call-start
  10.0 0.7 convert_element_type.101
  10.7 1.0 convert_element_type.103
  11.7 12.6 %all_gather.10 = bf16[2,512]{1,0:T(2,128)(2,1)S(1)} all-gather(bf16[2,128]{1,0:T(2,128)(2,1)S(1)} %convert_element_type.101), channel_id=1, replica_groups=mesh['nodes'=8,'shard'=4] {'shard'}, dimensions={1}, use_global_device_ids=true | all-gather | bytes 2560 | tf_op jit(solution)/shard_map/all_gather | solution.py:71
  24.2 21.2 %all_gather.11 = bf16[512,512]{1,0:T(8,128)(2,1)S(1)} all-gather(bf16[128,512]{1,0:T(8,128)(2,1)S(1)} %convert_element_type.103), channel_id=1, replica_groups=mesh['nodes'=8,'shard'=4] {'shard'}, dimensions={0}, use_global_device_ids=true | all-gather | bytes 655360 | tf_op jit(solution)/shard_map/all_gather | solution.py:70
  45.5 0.7 convert_convert_fusion
  46.2 20.3 %all-gather.2.cloned.1.call-done = bf16[512,2048]{1,0:T(8,128)(2,1)} async-done(((bf16[128,2048]{1,0:T(8,128)(2,1)}), bf16[512,2048]{1,0:T(8,128)(2,1)}) %all-gather.2.cloned.1.call-update) | async-done | bytes 2097168 | tf_op jit(solution)/shard_map/all_gather | solution.py:69
  66.5 6.8 %fusion.83 = f32[2048,2048]{0,1:T(8,128)S(1)} fusion(bf16[2048,512]{1,0:T(8,128)(2,1)} %param.13, bf16[512,2048]{1,0:T(8,128)(2,1)} %all-gather.2.cloned.1.call-done), kind=kOutput, calls=%fused_computation.120 | convolution fusion | flops 4294967296 | bytes 20971520 | tf_op jit(solution)/shard_map/dot_general | solution.py:75
  73.3 0.3 slice.58
  73.6 0.0 copy-start.11
  73.7 0.0 copy-start.18
  73.7 5.4 %copy-done = f32[2048,2048]{0,1:T(8,128)} copy-done((f32[2048,2048]{0,1:T(8,128)}, f32[2048,2048]{0,1:T(8,128)S(1)}, u32[]{:S(2)}) %copy-start) | copy-done | bytes 16777240
  79.0 1.1 multiply_convert_fusion.2
  80.1 0.6 fusion.75
  80.8 5.1 %fusion.48 = f32[4,8,64,64]{2,3,0,1:T(8,128)} fusion(bf16[2048,8,64,1]{0,2,3,1:T(8,128)(2,1)S(1)} %bitcast.110, bf16[2048,4]{0,1:T(4,128)(2,1)S(1)} %convert_convert_fusion, bf16[2048,8,64]{0,2,1:T(8,128)(2,1)S(1)} %bitcast.106), kind=kOutput, calls=%fused_computation.71 | convolution fusion | flops 553648128 | bytes 4734976 | tf_op jit(solution)/shard_map/nchk,nhv->chkv/dot_general | solution.py:92
  85.9 51.8 %all-reduce.8 = (f32[4,512]{1,0:T(4,128)S(1)}, bf16[4,8,64,64]{2,3,0,1:T(8,128)(2,1)S(1)}) all-reduce(f32[4,512]{1,0:T(4,128)S(1)} %fusion.75, f32[4,8,64,64]{2,3,0,1:T(8,128)} %fusion.48), channel_id=1, replica_groups=mesh['nodes'=8,'shard'=4] {'nodes','shard'}, use_global_device_ids=true, to_apply=%region_1.0 | all-reduce | flops 133120 | bytes 802816 | tf_op jit(solution)/shard_map/psum | solution.py:94
  137.7 4.9 %multiply_reduce_fusion.5 = (f32[2048,8]{0,1:T(8,128)S(1)}, bf16[2048,512]{0,1:T(8,128)(2,1)S(1)}, f32[2048,512]{0,1:T(8,128)S(1)}) fusion(f32[2048,2048]{0,1:T(8,128)} %copy-done, f32[4,512]{1,0:T(4,128)S(1)} %get-tuple-element.37, s32[2048]{0:T(1024)S(1)} %copy-done.18), kind=kOutput, calls=%fused_computation.50 | convolution fusion | flops 57663488 | bytes 10567680 | tf_op jit(solution)/shard_map/dot_general | solution.py:97
  142.6 1.9 fusion.82
  144.6 0.5 multiply_reduce_fusion.4
  145.1 1.0 copy-done.22
  146.2 6.7 %multiply_reduce_fusion = (f32[512]{0:T(512)S(1)}, f32[2048]{0:T(1024)S(1)}, f32[2048]{0:T(1024)S(1)}, f32[512]{0:T(512)S(1)}, f32[2048,512]{0,1:T(8,128)S(1)}, ...) fusion(f32[2048,8,64]{0,2,1:T(8,128)S(1)} %get-tuple-element.64, f32[2048]{0:T(1024)S(1)} %add_rsqrt_fusion, ...), kind=kOutput, calls=%fused_computation.36 | convolution fusion | flops 1091562496 | bytes 19443712 | tf_op jit(solution)/shard_map/dot_general | solution.py:114
  152.8 1.8 multiply_reduce_fusion.2
  154.7 0.5 divide_convert_fusion
  155.2 0.6 bitcast_multiply_fusion
  155.8 5.1 %fusion.51 = f32[4,8,64,64]{2,3,0,1:T(8,128)} fusion(bf16[2048,8,64]{0,2,1:T(8,128)(2,1)S(1)} %bitcast.109, bf16[2048,4]{0,1:T(4,128)(2,1)S(1)} %convert_convert_fusion, bf16[2048,8,64]{0,2,1:T(8,128)(2,1)S(1)} %divide_convert_fusion), kind=kOutput, calls=%fused_computation.72 | convolution fusion | flops 553648128 | bytes 4734976 | tf_op jit(solution)/shard_map/nchk,nhv->chkv/dot_general | solution.py:133
  160.9 1.7 bitcast_add_fusion.1
  162.5 5.1 %fusion.23 = bf16[2048,512]{0,1:T(8,128)(2,1)} fusion(f32[2048,8,64]{0,2,1:T(8,128)S(1)} %bitcast_add_fusion.1, f32[2048,2048]{0,1:T(8,128)} %copy-done), kind=kLoop, calls=%fused_computation.33 | loop fusion | flops 7340032 | bytes 10485760 | tf_op jit(solution)/shard_map/convert.2
  167.7 2.0 fusion.65
  169.7 49.3 %all-reduce.9 = (bf16[4,8,64,64]{2,3,0,1:T(8,128)(2,1)}, f32[4,512]{1,0:T(4,128)S(1)}, f32[2,512]{1,0:T(2,128)S(1)}) all-reduce(f32[4,8,64,64]{2,3,0,1:T(8,128)S(1)} %copy-done.15, f32[4,512]{1,0:T(4,128)S(1)} %fusion.65, f32[2,512]{1,0:T(2,128)S(1)} %pad_maximum_fusion.3), channel_id=1, replica_groups=mesh['nodes'=8,'shard'=4] {'nodes','shard'}, use_global_device_ids=true, to_apply=%region_8.0 | all-reduce | flops 134144 | bytes 811008 | tf_op jit(solution)/shard_map/psum | solution.py:141
  219.0 2.8 bitcast_convert_fusion
  221.9 0.0 copy-start.5
  221.9 0.0 copy-start.23
  221.9 1.6 fusion.8
  223.5 0.7 copy-done.5
  224.2 0.6 copy-done.23
  224.8 2.3 fusion.42
  227.1 5.0 %fusion.21 = bf16[2048,512]{0,1:T(8,128)(2,1)S(1)} fusion(f32[8,64,2048,1]{2,1,3,0:T(8,128)S(1)} %fusion.8, f32[4,512]{1,0:T(4,128)S(1)} %get-tuple-element.35, f32[2048]{0:T(1024)S(1)} %get-tuple-element.65, f32[2048,2048]{0,1:T(8,128)} %copy-done, s32[2048]{0:T(1024)S(1)} %copy-done.18), kind=kOutput, calls=%fused_computation.26 | convolution fusion | flops 59777024 | bytes 10510336 | tf_op jit(solution)/shard_map/dot_general | solution.py:149
  232.2 1.3 copy-done.27
  233.5 11.7 %convolution_bitcast_fusion = f32[512,2048]{0,1:T(8,128)} fusion(bf16[2048,512]{1,0:T(8,128)(2,1)S(1)} %copy-done.10, bf16[2048,512]{0,1:T(8,128)(2,1)S(1)} %copy-done.26, bf16[2048,512]{0,1:T(8,128)(2,1)S(1)} %bitcast.117, bf16[2048,512]{0,1:T(8,128)(2,1)S(1)} %fusion.21, bf16[2048,512]{0,1:T(8,128)(2,1)S(1)} %copy-done.6), kind=kOutput, calls=%fused_computation.64 | convolution fusion | flops 4328521728 | bytes 14680064 | tf_op jit(solution)/shard_map/dot_general | solution.py:158
  245.2 0.0 all-reduce.7.cloned.1.call-update
  245.2 1.2 copy-done.4
  246.4 0.3 copy.34
  246.8 3.1 copy.28
  249.9 2.8 copy.32
  252.8 2.5 copy.33
  255.3 5.1 %multiply_add_fusion = f32[2048,512]{0,1:T(8,128)} fusion(bf16[2048,512]{0,1:T(8,128)(2,1)S(1)} %copy.28, bf16[2048,512]{0,1:T(8,128)(2,1)} %get-tuple-element.58, bf16[512,512]{1,0:T(8,128)(2,1)} %copy-done.8, f32[2048]{0:T(1024)S(1)} %get-tuple-element.65), kind=kOutput, calls=%fused_computation.46 | convolution fusion | flops 1076887552 | bytes 8921088 | tf_op jit(solution)/shard_map/dot_general | solution.py:109
  260.4 5.5 %copy.35 = f32[2048,512]{1,0:T(8,128)} copy(f32[2048,512]{0,1:T(8,128)} %multiply_add_fusion) | data formatting | bytes 8388608
  265.9 0.6 multiply_reduce_fusion.8
  266.5 9.0 %convert_add_fusion = f32[2048,512]{1,0:T(8,128)} fusion(bf16[2048,512]{1,0:T(8,128)(2,1)} %param.14, bf16[512,2048]{1,0:T(8,128)(2,1)} %all-gather.2.cloned.1.call-done, bf16[2048,512]{0,1:T(8,128)(2,1)} %get-tuple-element.59, bf16[2048,512]{0,1:T(8,128)(2,1)} %bitcast.118, bf16[2048,512]{0,1:T(8,128)(2,1)} %copy-done.27, bf16[2048,512]{0,1:T(8,128)(2,1)S(1)} %copy-done.7), kind=kOutput, calls=%fused_computation.38 | convolution fusion | flops 4330618880 | bytes 16777216 | tf_op jit(solution)/shard_map/dot_general | solution.py:159
  275.5 117.1 %all-reduce.7.cloned.1.call-done = (f32[512,2048]{0,1:T(8,128)}, f32[512,512]{1,0:T(8,128)}) async-done(((f32[512,2048]{0,1:T(8,128)}, f32[512,512]{1,0:T(8,128)}), (f32[512,2048]{0,1:T(8,128)}, f32[512,512]{1,0:T(8,128)})) %all-reduce.7.cloned.1.call-update) | async-done | bytes 5242896 | tf_op jit(solution)/shard_map/psum | solution.py:163
  392.7 4.0 multiply_reduce_fusion.1
  396.6 0.9 multiply_reduce_fusion.7
  399.5 3.5 fusion.79
  403.1 0.0 copy-start.16
  403.1 0.0 copy-start.17
  403.1 2.7 copy.36
  405.8 2.5 copy.37
  408.4 1.3 copy.38
  409.7 1.0 copy.39
  410.7 0.6 divide_subtract_fusion.2
  411.3 2.0 fusion.77
  (52 shorter events, 0.2 us)
Async XLA Ops:
  7.2 59.4 %all-gather.2.cloned.1.call-start = ((), (), s32[]{:S(2)}) async-start(), calls=%async_computation | async-start | bytes 2621440 | tf_op jit(solution)/shard_map/all_gather | solution.py:69
  9.3 383.3 %all-reduce.7.cloned.1.call-start = ((), (), s32[]{:S(2)}) async-start(), calls=%async_computation.1 | async-start | bytes 10485760 | tf_op jit(solution)/shard_map/psum | solution.py:163
  45.5 99.6 %copy-start.8 = (bf16[512,512]{1,0:T(8,128)(2,1)}, bf16[512,512]{1,0:T(8,128)(2,1)S(1)}, u32[]{:S(2)}) copy-start(bf16[512,512]{1,0:T(8,128)(2,1)S(1)} %all_gather.11) | copy-start | bytes 1572868
  73.3 5.7 %copy-start = (f32[2048,2048]{0,1:T(8,128)}, f32[2048,2048]{0,1:T(8,128)S(1)}, u32[]{:S(2)}) copy-start(f32[2048,2048]{0,1:T(8,128)S(1)} %fusion.83) | copy-start | bytes 50331652
  73.6 7.1 %copy-start.11 = (bf16[2048,512]{0,1:T(8,128)(2,1)}, bf16[2048,512]{0,1:T(8,128)(2,1)S(1)}, u32[]{:S(2)}) copy-start(bf16[2048,512]{0,1:T(8,128)(2,1)S(1)} %slice.58) | copy-start | bytes 6291460
  73.7 6.5 %copy-start.18 = (s32[2048]{0:T(1024)S(1)}, s32[2048]{0:T(1024)}, u32[]{:S(2)}) copy-start(s32[2048]{0:T(1024)} %param.15) | copy-start | bytes 24580
  144.6 1.6 copy-start.22
  167.6 2.0 copy-start.15
  219.0 2.8 copy-start.12
  219.0 2.8 copy-start.24
  221.8 10.3 %copy-start.25 = (bf16[8,64,2048]{2,1,0:T(8,128)(2,1)}, bf16[8,64,2048]{2,1,0:T(8,128)(2,1)S(1)}, u32[]{:S(2)}) copy-start(bf16[8,64,2048]{2,1,0:T(8,128)(2,1)S(1)} %bitcast_convert_fusion) | copy-start | bytes 6291460
  221.9 2.3 copy-start.5
  221.9 3.0 copy-start.23
  227.1 6.4 %copy-start.6 = (bf16[2048,512]{0,1:T(8,128)(2,1)S(1)}, bf16[2048,512]{0,1:T(8,128)(2,1)}, u32[]{:S(2)}) copy-start(bf16[2048,512]{0,1:T(8,128)(2,1)} %fusion.23) | copy-start | bytes 6291460
  227.1 6.4 %copy-start.10 = (bf16[2048,512]{1,0:T(8,128)(2,1)S(1)}, bf16[2048,512]{1,0:T(8,128)(2,1)}, u32[]{:S(2)}) copy-start(bf16[2048,512]{1,0:T(8,128)(2,1)} %param.13) | copy-start | bytes 6291460
  227.1 6.4 %copy-start.26 = (bf16[2048,512]{0,1:T(8,128)(2,1)S(1)}, bf16[2048,512]{0,1:T(8,128)(2,1)}, u32[]{:S(2)}) copy-start(bf16[2048,512]{0,1:T(8,128)(2,1)} %get-tuple-element.59) | copy-start | bytes 6291460
  232.1 1.4 copy-start.27
  245.2 1.2 copy-start.4
  260.4 6.1 %copy-start.7 = (bf16[2048,512]{0,1:T(8,128)(2,1)S(1)}, bf16[2048,512]{0,1:T(8,128)(2,1)}, u32[]{:S(2)}) copy-start(bf16[2048,512]{0,1:T(8,128)(2,1)} %fusion.23) | copy-start | bytes 6291460
  275.5 124.0 %copy-start.1 = (f32[128,2048]{0,1:T(8,128)S(1)}, f32[128,2048]{0,1:T(8,128)}, u32[]{:S(2)}) copy-start(f32[128,2048]{0,1:T(8,128)} %copy.32) | copy-start | bytes 3145732
  275.5 124.0 %copy-start.2 = (f32[128,2048]{0,1:T(8,128)S(1)}, f32[128,2048]{0,1:T(8,128)}, u32[]{:S(2)}) copy-start(f32[128,2048]{0,1:T(8,128)} %copy.33) | copy-start | bytes 3145732
  392.7 4.0 copy-start.13
  403.1 5.3 %copy-start.3 = (f32[128,2048]{0,1:T(8,128)S(1)}, f32[128,2048]{0,1:T(8,128)}, u32[]{:S(2)}) copy-start(f32[128,2048]{0,1:T(8,128)} %get-tuple-element.50) | copy-start | bytes 3145732
  403.1 6.6 %copy-start.9 = (bf16[128,2048]{0,1:T(8,128)(2,1)S(1)}, bf16[128,2048]{0,1:T(8,128)(2,1)}, u32[]{:S(2)}) copy-start(bf16[128,2048]{0,1:T(8,128)(2,1)} %get-tuple-element.49) | copy-start | bytes 1572868
  403.1 7.6 %copy-start.19 = (f32[2,128]{1,0:T(2,128)S(1)}, f32[2,128]{1,0:T(2,128)}, u32[]{:S(2)}) copy-start(f32[2,128]{1,0:T(2,128)} %param.23) | copy-start | bytes 3076
  403.1 7.6 %copy-start.20 = (f32[2,128]{1,0:T(2,128)S(1)}, f32[2,128]{1,0:T(2,128)}, u32[]{:S(2)}) copy-start(f32[2,128]{1,0:T(2,128)} %param.25) | copy-start | bytes 3076
  403.1 7.6 %copy-start.21 = (f32[2,128]{1,0:T(2,128)S(1)}, f32[2,128]{1,0:T(2,128)}, u32[]{:S(2)}) copy-start(f32[2,128]{1,0:T(2,128)} %param.24) | copy-start | bytes 3076
  403.1 8.2 %copy-start.14 = (f32[128,512]{1,0:T(8,128)S(1)}, f32[128,512]{1,0:T(8,128)}, u32[]{:S(2)}) copy-start(f32[128,512]{1,0:T(8,128)} %param.20) | copy-start | bytes 786436
  403.1 8.2 %copy-start.16 = (f32[128,512]{1,0:T(8,128)S(1)}, f32[128,512]{1,0:T(8,128)}, u32[]{:S(2)}) copy-start(f32[128,512]{1,0:T(8,128)} %param.22) | copy-start | bytes 786436
  403.1 8.2 %copy-start.17 = (f32[128,512]{1,0:T(8,128)S(1)}, f32[128,512]{1,0:T(8,128)}, u32[]{:S(2)}) copy-start(f32[128,512]{1,0:T(8,128)} %param.21) | copy-start | bytes 786436
Sparse Core Ops, SparseCore 0:
  10.2 56.3 all-gather.1
  245.4 147.2 all-reduce.6
where the time goes:
time: 429 us; the launch traced here: 421 us
  waiting for transfers between devices  137 us (32%)
  blocking collectives  135 us (31%)
  matrix products  72.3 us (17%)
  local copies, waits for them, and re-layouts  32.6 us (8%)
  other arithmetic  25.7 us (6%)
  between operations  18.5 us (4%)
    psum x1, waiting for transfers between devices, local(): lax.psum((grad_wproj, grad_wout, grad_wnorm), ('nodes', 'shard'))  117 us
    psum x1, blocking collectives, local(): summary, key_sum = lax.psum((local_kv, local_ks), ('nodes', 'shard'))  51.8 us
    psum x1, blocking collectives, local(): lax.psum((local_dkv, local_dks), ('nodes', 'shard'))  49.3 us
    unnamed x65, local copies, waits for them, and re-layouts  32.2 us
    all_gather x1, blocking collectives, local(): lax.all_gather(out_master.astype(bf_type), 'shard', axis=0, tiled=True)  21.2 us
    all_gather x1, waiting for transfers between devices, local(): lax.all_gather(proj_master.astype(bf_type), 'shard', axis=0, tiled=True)  20.3 us
    all_gather x1, blocking collectives, local(): lax.all_gather(norm_master.astype(bf_type), 'shard', axis=1, tiled=True)  12.6 us
    dot_general x1, matrix products, local(): grad_wproj = jnp.dot(node_feats.T, grad_pre, preferred_element_type=fl_type)  11.7 us
  transfers between devices with their start and end apart: 2, of which 2 were waited for; matrix products, arithmetic and copies ran while one was open for 7% of the time, Pallas kernels for 0%

commit v1 on v0

v1 whole, which is shorter than its diff:
```python
import functools
import math

import jax
import jax.numpy as jnp
from jax import lax
from jax.experimental import pallas as pl
from jax.experimental.pallas import tpu as pltpu
from jax.sharding import PartitionSpec as P

HEADS = 8
CLUSTERS = 4
STEP = 10
AXES = ("nodes", "shard")

norm_eps = 1e-05
beta_one = 0.9
beta_two = 0.999
learn_rate = 0.05
norm_rate = 0.5
decay_rate = 0.01
adam_eps = 1e-08
bf_type = jnp.bfloat16
fl_type = jnp.float32

GROUPS = 2
CHUNKS = GROUPS * CLUSTERS
PAD = 16


def dot_nn(a, b):
    return lax.dot_general(a, b, (((1,), (0,)), ((), ())), preferred_element_type=fl_type)


def dot_nt(a, b):
    return lax.dot_general(a, b, (((1,), (1,)), ((), ())), preferred_element_type=fl_type)


def dot_tn(a, b):
    return lax.dot_general(a, b, (((0,), (0,)), ((), ())), preferred_element_type=fl_type)


def whole(shape):
    return pl.BlockSpec(shape, lambda *_: (0,) * len(shape))


def smem():
    return pl.BlockSpec(memory_space=pltpu.SMEM)


def call(kernel, grid, ins, in_specs, outs, out_specs, scratch, flops, name):
    moved = sum(math.prod(a.shape) * a.dtype.itemsize for a in (*ins, *outs))
    return pl.pallas_call(
        kernel,
        grid=grid,
        in_specs=in_specs,
        out_specs=out_specs,
        out_shape=outs,
        scratch_shapes=scratch,
        cost_estimate=pl.CostEstimate(flops=int(flops), transcendentals=0, bytes_accessed=int(moved)),
        compiler_params=pltpu.CompilerParams(
            dimension_semantics=("arbitrary",) * len(grid), vmem_limit_bytes=60 * 1024 * 1024
        ),
        name=name,
    )(*ins)


def out(shape, dtype):
    return jax.ShapeDtypeStruct(shape, dtype)


def prep_kernel(place, wp, wo, wn, kv_mine, kv_other, qo_mine, qo_other, kv_all, qo_all):
    core = place[0]
    width = wo.shape[1]
    shard = wo.shape[0]

    def turned(block):
        return block.T.astype(bf_type)

    qo_all[0:width] = turned(wp[:, 0:width])
    kv_all[0:width] = turned(wp[:, width : 2 * width])
    kv_all[width : 2 * width] = turned(wp[:, 2 * width : 3 * width])
    qo_all[width : 2 * width] = turned(wp[:, 3 * width : 4 * width])
    qo_all[2 * width : 3 * width] = turned(wo[...])
    rows = jnp.concatenate([wn[...], jnp.zeros((30, shard), fl_type)], axis=0)
    qo_all[3 * width : 3 * width + 32] = rows.astype(bf_type)
    for whole_ref, mine, other in ((kv_all, kv_mine, kv_other), (qo_all, qo_mine, qo_other)):
        half = mine.shape[0]
        mine[...] = whole_ref[pl.ds(pl.multiple_of(core * half, 16), half)]
        other[...] = whole_ref[pl.ds(pl.multiple_of((1 - core) * half, 16), half)]


def members(ids_ref):
    rows = ids_ref.shape[1]
    classes = lax.broadcasted_iota(jnp.int32, (PAD, rows), 0)
    return (classes == ids_ref[...]).astype(fl_type).astype(bf_type)


def valid_row(count, start, rows):
    slots = lax.broadcasted_iota(jnp.int32, (1, rows), 1) + start
    return slots < count


def put_chunks(acc, keep, send, node, extra):
    width = acc.shape[2]
    head = width // 4
    for g in range(GROUPS):
        for c in range(CLUSTERS):
            chunk = g * CLUSTERS + c
            distance = lax.bitwise_xor(node, chunk)
            slot = lax.shift_right_logical(distance, 1)
            lane_head = lax.broadcasted_iota(jnp.int32, (head, width), 1) // head
            body = jnp.zeros((head, width), fl_type)
            for h in range(4):
                rows = acc[g, c * width + h * head : c * width + (h + 1) * head, :]
                body = jnp.where(lane_head == h, rows, body)
            block = jnp.concatenate([body, extra(g, c)], axis=0)

            @pl.when(lax.bitwise_and(distance, 1) == 0)
            def _():
                keep[slot] = block

            @pl.when(lax.bitwise_and(distance, 1) == 1)
            def _():
                send[slot] = block.astype(bf_type)


def key_kernel(pieces, place, x, ids, *refs):
    mine, other = refs[:pieces], refs[pieces : 2 * pieces]
    sig_key, value_out, keep, send, weights, masked, keys, acc = refs[2 * pieces :]
    step = pl.program_id(0)
    core, node, count = place[0], place[1], place[3]
    width = x.shape[1]
    rows = x.shape[0]
    half = width // GROUPS

    @pl.when(step == 0)
    def _():
        span = mine[0].shape[1]
        height = mine[0].shape[0]
        for d in range(pieces):
            weights[pl.ds(pl.multiple_of(core * height, 16), height), d * span : (d + 1) * span] = mine[d][...]
            weights[pl.ds(pl.multiple_of((1 - core) * height, 16), height), d * span : (d + 1) * span] = other[d][...]
        acc[...] = jnp.zeros_like(acc)

    table = members(ids)
    valid = valid_row(count, step * rows, rows)
    for g in range(GROUPS):
        sig = jax.nn.sigmoid(dot_nt(weights[g * half : (g + 1) * half, :], x[...]))
        sig_key[g * half : (g + 1) * half, :] = sig
        keys[...] = jnp.where(valid, sig, 0.0).astype(bf_type)
        value = dot_nt(weights[width + g * half : width + (g + 1) * half, :], x[...]).astype(bf_type)
        value_out[g * half : (g + 1) * half, :] = value
        for c in range(CLUSTERS):
            masked[c * half : (c + 1) * half, :] = value * table[c : c + 1, :]
        masked[CLUSTERS * half :, :] = table
        acc[g] += dot_nt(masked[...], keys[...])

    @pl.when(step == pl.num_programs(0) - 1)
    def _():
        def extra(g, c):
            row = acc[g, CLUSTERS * half + c : CLUSTERS * half + c + 1, :]
            return jnp.concatenate([row, jnp.zeros((PAD - 1, half), fl_type)], axis=0)

        put_chunks(acc, keep, send, node, extra)


def weights_kernel(pieces, place, *refs):
    q_mine, q_other = refs[:pieces], refs[pieces : 2 * pieces]
    k_mine, k_other = refs[2 * pieces : 3 * pieces], refs[3 * pieces : 4 * pieces]
    query_gate, out_weight, gain, shift, full, stage_q, stage_k = refs[4 * pieces :]
    core, shard = place[0], place[2]
    width = out_weight.shape[0]
    span = q_mine[0].shape[1]
    for mine, other, stage in ((q_mine, q_other, stage_q), (k_mine, k_other, stage_k)):
        half = mine[0].shape[0]
        for d in range(pieces):
            stage[d, pl.ds(pl.multiple_of(core * half, 16), half), :] = mine[d][...]
            stage[d, pl.ds(pl.multiple_of((1 - core) * half, 16), half), :] = other[d][...]
    norm_rows = []
    for z in range(pieces):
        where = lax.bitwise_xor(shard, z)
        cols = slice(z * span, (z + 1) * span)
        query_gate[:, cols] = stage_q[z, 0 : 2 * width, :]
        full[0:width, cols] = stage_q[where, 0:width, :]
        full[width : 3 * width, cols] = stage_k[where]
        full[3 * width :, cols] = stage_q[where, width : 2 * width, :]
        out_weight[cols, :] = stage_q[where, 2 * width : 3 * width, :].T
        norm_rows.append(stage_q[where, 3 * width : 3 * width + 16, :])
    turned = jnp.concatenate(norm_rows, axis=1).astype(fl_type).T
    gain[...] = jnp.broadcast_to(turned[:, 0:1], gain.shape)
    shift[...] = jnp.broadcast_to(turned[:, 1:2], shift.shape)


def query_kernel(place, x, g, query_gate, out_weight, sig_query, query, gate, grad_prod):
    step = pl.program_id(0)
    count = place[3]
    rows, width = x.shape
    half = width // GROUPS
    valid = valid_row(count, step * rows, rows)
    for p in range(GROUPS):
        span = slice(p * half, (p + 1) * half)
        sig = jax.nn.sigmoid(dot_nt(query_gate[span, :], x[...]))
        sig_query[span, :] = sig
        query[span, :] = sig.astype(bf_type)
        gate[span, :] = dot_nt(query_gate[width + p * half : width + (p + 1) * half, :], x[...])
        grad_prod[span, :] = jnp.where(valid, dot_nt(out_weight[span, :], g[...]), 0.0)


def place_chunks(chunk_refs, place, stage):
    node = place[1]
    for d in range(CHUNKS):
        stage[lax.bitwise_xor(node, d)] = chunk_refs[d][...]


def head_rows(width, h, value):
    lane_head = lax.broadcasted_iota(jnp.int32, (1, width), 1) // (width // 4)
    return jnp.where(lane_head == h, value, jnp.zeros_like(value))


def middle_kernel(place, ids, query, gate, grad_prod, gain, shift, *refs):
    chunk_refs = refs[:CHUNKS]
    prod_out, dgate_out, dnum_out, dden_out, keep, send = refs[CHUNKS : CHUNKS + 6]
    stage, left, stack, num, normed, dnormed, den, dden, acc, dgain, dshift = refs[CHUNKS + 6 :]
    step = pl.program_id(0)
    node, count = place[1], place[3]
    width, rows = query.shape
    half = width // GROUPS
    head = half // 4
    lanes = 256

    @pl.when(step == 0)
    def _():
        place_chunks(chunk_refs, place, stage)
        for g in range(GROUPS):
            for c in range(CLUSTERS):
                chunk = stage[g * CLUSTERS + c].astype(fl_type)
                cols = slice(c * half, (c + 1) * half)
                for h in range(4):
                    left[g, h * head : (h + 1) * head, cols] = head_rows(half, h, chunk[:head]).astype(bf_type)
                sums = [head_rows(half, h, chunk[head : head + 1]) for h in range(4)]
                sums.append(jnp.zeros((PAD - 4, half), fl_type))
                left[g, half : half + PAD, cols] = jnp.concatenate(sums, axis=0).astype(bf_type)
        acc[...] = jnp.zeros_like(acc)
        dgain[...] = jnp.zeros_like(dgain)
        dshift[...] = jnp.zeros_like(dshift)

    table = members(ids)
    for g in range(GROUPS):
        part = query[g * half : (g + 1) * half, :]
        for c in range(CLUSTERS):
            stack[c * half : (c + 1) * half, :] = part * table[c : c + 1, :]
        both = dot_nn(left[g], stack[0 : CLUSTERS * half, :])
        num[g * half : (g + 1) * half, :] = both[:half]
        den[g * 8 : g * 8 + 8, :] = 1.0 / both[half : half + 8]

    for lane in range(rows // lanes):
        cols = slice(lane * lanes, (lane + 1) * lanes)
        valid = valid_row(count, step * rows + lane * lanes, lanes)
        total = jnp.zeros((1, lanes), fl_type)
        for h in range(HEADS):
            span = slice(h * head, (h + 1) * head)
            row = (h // 4) * 8 + h % 4
            att = num[span, cols] * den[row : row + 1, cols]
            num[span, cols] = att
            total = total + jnp.sum(att, axis=0, keepdims=True)
        mean = total * (1.0 / width)
        total = jnp.zeros((1, lanes), fl_type)
        for h in range(HEADS):
            centered = num[h * head : (h + 1) * head, cols] - mean
            total = total + jnp.sum(centered * centered, axis=0, keepdims=True)
        scale = lax.rsqrt(total * (1.0 / width) + norm_eps)
        first = jnp.zeros((1, lanes), fl_type)
        second = jnp.zeros((1, lanes), fl_type)
        for h in range(HEADS):
            span = slice(h * head, (h + 1) * head)
            ah = (num[span, cols] - mean) * scale
            gamma = jnp.concatenate([gain[span, :]] * (lanes // 128), axis=1)
            beta = jnp.concatenate([shift[span, :]] * (lanes // 128), axis=1)
            u = ah * gamma + beta
            zg = gate[span, cols]
            dp = grad_prod[span, cols]
            prod_out[span, cols] = jnp.where(valid, u * zg, 0.0).astype(bf_type)
            du = dp * zg
            dgate_out[span, cols] = (dp * u).astype(bf_type)
            du_ah = du * ah
            for part in range(lanes // 128):
                sub = slice(part * 128, (part + 1) * 128)
                dgain[span, :] += du_ah[:, sub]
                dshift[span, :] += du[:, sub]
            dah = gamma * du
            first = first + jnp.sum(dah, axis=0, keepdims=True)
            second = second + jnp.sum(dah * ah, axis=0, keepdims=True)
            normed[span, cols] = ah
            dnormed[span, cols] = dah
        first = first * (1.0 / width)
        second = second * (1.0 / width)
        for h in range(HEADS):
            span = slice(h * head, (h + 1) * head)
            row = (h // 4) * 8 + h % 4
            da = scale * (dnormed[span, cols] - first - normed[span, cols] * second)
            inverse = den[row : row + 1, cols]
            dnum_out[span, cols] = (da * inverse).astype(bf_type)
            dden[row : row + 1, cols] = -jnp.sum(da * num[span, cols], axis=0, keepdims=True) * inverse

    dden_out[...] = dden[...]
    for g in range(GROUPS):
        part = dnum_out[g * half : (g + 1) * half, :]
        for c in range(CLUSTERS):
            stack[c * half : (c + 1) * half, :] = part * table[c : c + 1, :]
        den_rows = dden[g * 8 : g * 8 + 4, :]
        high = den_rows.astype(bf_type)
        low = (den_rows - high.astype(fl_type)).astype(bf_type)
        four_high = jnp.concatenate([high * table[c : c + 1, :] for c in range(CLUSTERS)], axis=0)
        four_low = jnp.concatenate([low * table[c : c + 1, :] for c in range(CLUSTERS)], axis=0)
        stack[CLUSTERS * half :, :] = jnp.concatenate([four_high, four_low], axis=0)
        acc[g] += dot_nt(stack[...], query[g * half : (g + 1) * half, :])

    @pl.when(step == pl.num_programs(0) - 1)
    def _():
        gain_row = jnp.sum(dgain[...].T, axis=0, keepdims=True)
        shift_row = jnp.sum(dshift[...].T, axis=0, keepdims=True)

        def extra(g, c):
            base = CLUSTERS * half
            row = jnp.zeros((1, half), fl_type)
            for h in range(4):
                at = base + c * 4 + h
                row = row + head_rows(half, h, acc[g, at : at + 1, :] + acc[g, at + 16 : at + 17, :])
            cols = slice(g * half, (g + 1) * half)
            tail = [row]
            if c == 0:
                tail += [gain_row[:, cols], shift_row[:, cols]]
            tail.append(jnp.zeros((PAD - len(tail), half), fl_type))
            return jnp.concatenate(tail, axis=0)

        put_chunks(acc, keep, send, node, extra)


def write_pieces(pieces, node, shard, span, keep, send, blocks):
    for chunk in range(8):
        distance = lax.bitwise_xor(node, chunk)
        slot = lax.shift_right_logical(distance, 1)
        even = lax.bitwise_and(distance, 1) == 0
        for z in range(pieces):
            block = blocks(z, chunk)

            @pl.when(even)
            def _():
                keep[slot, z] = block

            @pl.when(jnp.logical_not(even))
            def _():
                send[slot, z] = block.astype(bf_type)


def query_back_kernel(pieces, place, ids, dnum, dden, dgate, sig_query, prod, x, g, *refs):
    chunk_refs = refs[:CHUNKS]
    dquery_out, keep, send = refs[CHUNKS : CHUNKS + 3]
    stage, left, sums, stack, acc, acc_out = refs[CHUNKS + 3 :]
    step = pl.program_id(0)
    node, shard = place[1], place[2]
    width, rows = dnum.shape
    half = width // GROUPS
    head = half // 4
    span = width // pieces

    @pl.when(step == 0)
    def _():
        place_chunks(chunk_refs, place, stage)
        for gr in range(GROUPS):
            for c in range(CLUSTERS):
                chunk = stage[gr * CLUSTERS + c].astype(fl_type)
                block = jnp.concatenate([head_rows(half, h, chunk[:head]) for h in range(4)], axis=0)
                left[gr, :, c * half : (c + 1) * half] = block.T.astype(bf_type)
                column = jnp.broadcast_to(chunk[head : head + 8], (8, half)).T
                sums[c, gr * half : (gr + 1) * half, :] = jnp.broadcast_to(column[:, 0:1], (half, 128))
        acc[...] = jnp.zeros_like(acc)
        acc_out[...] = jnp.zeros_like(acc_out)

    table = members(ids)
    for gr in range(GROUPS):
        part = dnum[gr * half : (gr + 1) * half, :]
        for c in range(CLUSTERS):
            stack[c * half : (c + 1) * half, :] = part * table[c : c + 1, :]
        dq = dot_nn(left[gr], stack[...])
        for h in range(4):
            at = slice(gr * half + h * head, gr * half + (h + 1) * head)
            pick = pick_rows(sums, at, ids, rows)
            row = gr * 8 + h
            full = dq[h * head : (h + 1) * head] + dden[row : row + 1, :] * pick
            sig = sig_query[at, :]
            dquery_out[at, :] = (full * (sig * (1.0 - sig))).astype(bf_type)
    acc[0:width] += dot_nn(dquery_out[...], x[...])
    acc[width : 2 * width] += dot_nn(dgate[...], x[...])
    acc_out[...] += dot_nn(prod[...], g[...])

    @pl.when(step == pl.num_programs(0) - 1)
    def _():
        tall = 2 * width // 8

        def blocks(z, chunk):
            top = acc[chunk * tall : (chunk + 1) * tall, z * span : (z + 1) * span]
            start = lax.bitwise_xor(shard, z) * span
            rows_out = span // 2
            start = pl.multiple_of(start + (chunk % 2) * rows_out, 8)
            lanes = width // 4
            bottom = acc_out[pl.ds(start, rows_out), (chunk // 2) * lanes : (chunk // 2 + 1) * lanes]
            bottom = bottom.reshape(-1, span) if lanes == span else fold(bottom, span)
            return jnp.concatenate([top, bottom], axis=0)

        write_pieces(pieces, node, shard, span, keep, send, blocks)


def fold(block, span):
    return jnp.concatenate(
        [block[:, i * span : (i + 1) * span] for i in range(block.shape[1] // span)], axis=0
    )


def pick_rows(sums, at, ids, rows):
    reps = rows // 128
    wide = [jnp.concatenate([sums[c, at, :]] * reps, axis=1) for c in range(CLUSTERS)]
    pick = wide[CLUSTERS - 1]
    for c in range(CLUSTERS - 1):
        pick = jnp.where(ids[...] == c, wide[c], pick)
    return pick


def output_kernel(place, x, prod, out_weight, result):
    result[...] = x[...].astype(fl_type) + dot_tn(prod[...], out_weight[...])


def key_back_kernel(pieces, place, ids, sig_key, value, x, *refs):
    chunk_refs = refs[:CHUNKS]
    dkey_out, dvalue_out, norm_out, keep, send = refs[CHUNKS : CHUNKS + 5]
    stage, left_key, left_value, sums, stack, acc = refs[CHUNKS + 5 :]
    step = pl.program_id(0)
    node, shard, count = place[1], place[2], place[3]
    width, rows = value.shape
    half = width // GROUPS
    head = half // 4
    span = width // pieces

    @pl.when(step == 0)
    def _():
        place_chunks(chunk_refs, place, stage)
        for gr in range(GROUPS):
            for c in range(CLUSTERS):
                chunk = stage[gr * CLUSTERS + c].astype(fl_type)
                block = jnp.concatenate([head_rows(half, h, chunk[:head]) for h in range(4)], axis=0)
                left_value[gr, :, c * half : (c + 1) * half] = block.astype(bf_type)
                left_key[gr, :, c * half : (c + 1) * half] = block.T.astype(bf_type)
                column = chunk[head : head + 8].T
                sums[c, gr * half : (gr + 1) * half, :] = jnp.broadcast_to(column[:, 0:1], (half, 128))
                if c == 0:
                    norm_out[:, gr * half : (gr + 1) * half] = chunk[head : head + 8]
        acc[...] = jnp.zeros_like(acc)

    table = members(ids)
    valid = valid_row(count, step * rows, rows)
    for gr in range(GROUPS):
        at = slice(gr * half, (gr + 1) * half)
        part = value[at, :]
        for c in range(CLUSTERS):
            stack[c * half : (c + 1) * half, :] = part * table[c : c + 1, :]
        dk = dot_nn(left_key[gr], stack[...])
        for h in range(4):
            sub = slice(gr * half + h * head, gr * half + (h + 1) * head)
            full = dk[h * head : (h + 1) * head] + pick_rows(sums, sub, ids, rows)
            sig = sig_key[sub, :]
            dkey_out[sub, :] = jnp.where(valid, full * (sig * (1.0 - sig)), 0.0).astype(bf_type)
        key = jnp.where(valid, sig_key[at, :], 0.0).astype(bf_type)
        for c in range(CLUSTERS):
            stack[c * half : (c + 1) * half, :] = key * table[c : c + 1, :]
        dvalue_out[at, :] = dot_nn(left_value[gr], stack[...]).astype(bf_type)
    acc[0:width] += dot_nn(dkey_out[...], x[...])
    acc[width : 2 * width] += dot_nn(dvalue_out[...], x[...])

    @pl.when(step == pl.num_programs(0) - 1)
    def _():
        tall = 2 * width // 8

        def blocks(z, chunk):
            return acc[chunk * tall : (chunk + 1) * tall, z * span : (z + 1) * span]

        write_pieces(pieces, node, shard, span, keep, send, blocks)


def input_kernel(dquery, dkey, dvalue, dgate, full, g, result):
    width = g.shape[1]
    total = g[...].astype(fl_type)
    for i, part in enumerate((dquery, dkey, dvalue, dgate)):
        total = total + dot_tn(part[...], full[i * width : (i + 1) * width, :])
    result[...] = total


def gather_kernel(place, *refs):
    parts = refs[:CHUNKS]
    grad_proj, grad_out, squares = refs[CHUNKS : CHUNKS + 3]
    stage_kv, stage_qg = refs[CHUNKS + 3 :]
    node = place[1]
    span, width = grad_out.shape
    tall = 2 * width // 8
    total = jnp.zeros((8, span), fl_type)
    for d in range(CHUNKS):
        chunk = lax.bitwise_xor(node, d)
        part = parts[d][...].astype(fl_type)
        stage_kv[chunk] = part[:tall]
        stage_qg[chunk] = part[tall : 2 * tall]
        square = part * part
        for r in range(part.shape[0] // 8):
            total = total + square[r * 8 : (r + 1) * 8]
        bottom = part[2 * tall :]
        lanes = width // 4
        folds = lanes // span
        rows = span // 2
        row_start = pl.multiple_of(lax.bitwise_and(chunk, 1) * rows, 8)
        quarter = lax.shift_right_logical(chunk, 1)
        for q in range(4):

            @pl.when(quarter == q)
            def _():
                for i in range(folds):
                    at = slice(q * lanes + i * span, q * lanes + (i + 1) * span)
                    grad_out[pl.ds(row_start, rows), at] = bottom[i * rows : (i + 1) * rows]

    for chunk in range(8):
        half = chunk % 4
        key_or_value = width if chunk < 4 else 2 * width
        grad_proj[:, key_or_value + half * tall : key_or_value + (half + 1) * tall] = stage_kv[chunk].T
        query_or_gate = 0 if chunk < 4 else 3 * width
        grad_proj[:, query_or_gate + half * tall : query_or_gate + (half + 1) * tall] = stage_qg[chunk].T
    squares[...] = total


def adam(master_w, moment_old, square_old, clipped, decay_coef, step_rate):
    moment_new = beta_one * moment_old + (1.0 - beta_one) * clipped
    square_new = beta_two * square_old + (1.0 - beta_two) * clipped * clipped
    moment_hat = moment_new * (1.0 / (1.0 - beta_one**STEP))
    square_hat = square_new * (1.0 / (1.0 - beta_two**STEP))
    master_new = master_w * (1.0 - step_rate * decay_coef) - step_rate * moment_hat / (
        jnp.sqrt(square_hat) + adam_eps
    )
    return moment_new, square_new, master_new


def update_kernel(scale, gp, go, gn, pw, pm, ps, ow, om, osq, nw, nm, ns, *outs):
    p_m, p_s, p_w, p_c, o_m, o_s, o_w, o_c, n_g, n_m, n_s, n_w = outs
    factor = scale[0]
    p_m[...], p_s[...], new = adam(pw[...], pm[...], ps[...], gp[...] * factor, decay_rate, learn_rate)
    p_w[...] = new
    p_c[...] = new.astype(bf_type)
    o_m[...], o_s[...], new = adam(ow[...], om[...], osq[...], go[...] * factor, decay_rate, learn_rate)
    o_w[...] = new
    o_c[...] = new.astype(bf_type)
    clipped = gn[...] * factor
    n_g[...] = clipped
    n_m[...], n_s[...], n_w[...] = adam(nw[...], nm[...], ns[...], clipped, 0.0, norm_rate)


def make_exchange(nodes, shards):
    count = nodes * shards

    def exchange(value, node_bits, shard_bits):
        pairs = [
            (i, ((i // shards) ^ node_bits) * shards + ((i % shards) ^ shard_bits)) for i in range(count)
        ]
        return lax.ppermute(value, AXES, pairs)

    return exchange


def tree_sum(parts):
    parts = list(parts)
    while len(parts) > 1:
        parts = [parts[i] + parts[i + 1] for i in range(0, len(parts), 2)]
    return parts[0]


def to_float(parts):
    return [p.astype(fl_type) for p in parts]


def local(nodes, shards, *args):
    (x, g, ids, counts, pw, pm, ps, ow, om, osq, nw, nm, ns) = args
    exchange = make_exchange(nodes, shards)
    outer = nodes // 8
    rows, width = x.shape
    half = width // GROUPS
    head = width // HEADS
    span = pw.shape[0]
    block = min(512, rows)
    steps = rows // block
    tall = 2 * width // 8

    node = lax.axis_index("nodes").astype(jnp.int32)
    shard = lax.axis_index("shard").astype(jnp.int32)
    chunk_node = lax.bitwise_and(node, 7)
    place = jnp.stack([lax.bitwise_and(node, 1), chunk_node, shard, counts[0]])
    ids = ids.reshape(1, rows)

    half_kv, half_qo = width, (3 * width + 32) // 2
    kv_mine, kv_other, qo_mine, qo_other = call(
        prep_kernel,
        (),
        (place, pw, ow, nw),
        [smem(), whole(pw.shape), whole(ow.shape), whole(nw.shape)],
        [out((half_kv, span), bf_type)] * 2 + [out((half_qo, span), bf_type)] * 2,
        [whole((half_kv, span))] * 2 + [whole((half_qo, span))] * 2,
        [pltpu.VMEM((2 * half_kv, span), bf_type), pltpu.VMEM((2 * half_qo, span), bf_type)],
        1e6,
        "prep",
    )
    kv_mine, kv_other, qo_mine, qo_other = [kv_mine], [kv_other], [qo_mine], [qo_other]
    for z in range(1, shards):
        kv_mine.append(exchange(kv_mine[0], 0, z))
    for z in range(1, shards):
        qo_mine.append(exchange(qo_mine[0], 0, z))
    for z in range(1, shards):
        kv_other.append(exchange(kv_mine[z], 1, 0))
    for z in range(1, shards):
        qo_other.append(exchange(qo_mine[z], 1, 0))
    x_turned = jnp.concatenate(
        [
            lax.dynamic_slice(x, (0, lax.bitwise_xor(shard, z) * span), (rows, span))
            for z in range(shards)
        ],
        axis=1,
    )

    by_row = pl.BlockSpec((block, width), lambda i: (i, 0))
    by_lane = pl.BlockSpec((width, block), lambda i: (0, i))
    id_lane = pl.BlockSpec((1, block), lambda i: (0, i))
    chunk_shape = (4, head + PAD, half)
    piece_shape = (4, shards, tall, span)
    chunk_specs = [whole((head + PAD, half))] * CHUNKS

    sig_key, value, keep, send = call(
        functools.partial(key_kernel, shards),
        (steps,),
        (place, x_turned, ids, *kv_mine, *kv_other),
        [smem(), by_row, id_lane] + [whole((half_kv, span))] * (2 * shards),
        [
            out((width, rows), fl_type),
            out((width, rows), bf_type),
            out(chunk_shape, fl_type),
            out(chunk_shape, bf_type),
        ],
        [by_lane, by_lane, whole(chunk_shape), whole(chunk_shape)],
        [
            pltpu.VMEM((2 * width, width), bf_type),
            pltpu.VMEM((CLUSTERS * half + PAD, block), bf_type),
            pltpu.VMEM((half, block), bf_type),
            pltpu.VMEM((GROUPS, CLUSTERS * half + PAD, half), fl_type),
        ],
        8 * rows * width * width,
        "keys",
    )

    def reduce_chunks(keep, send):
        mine = keep + exchange(send, 1, 0).astype(fl_type)
        got = [exchange(mine[e].astype(bf_type), 2 * e, 0) for e in range(1, 4)]
        mine = tree_sum([mine[0], *to_float(got)])
        own = mine.astype(bf_type)
        got = [own] + [exchange(own, 0, z) for z in range(1, shards)]
        own = tree_sum(to_float(got)).astype(bf_type)
        if outer > 1:
            got = [own] + [exchange(own, 8 * o, 0) for o in range(1, outer)]
            own = tree_sum(to_float(got)).astype(bf_type)
        return spread(own)

    def spread(own):
        chunks = [None] * 8
        chunks[0] = own
        for e in range(1, 4):
            chunks[2 * e] = exchange(own, 2 * e, 0)
        for e in range(4):
            chunks[2 * e + 1] = exchange(chunks[2 * e], 1, 0)
        return chunks

    chunks = reduce_chunks(keep, send)

    query_gate, out_weight, gain, shift, full = call(
        functools.partial(weights_kernel, shards),
        (),
        (place, *qo_mine, *qo_other, *kv_mine, *kv_other),
        [smem()] + [whole((half_qo, span))] * (2 * shards) + [whole((half_kv, span))] * (2 * shards),
        [
            out((2 * width, width), bf_type),
            out((width, width), bf_type),
            out((width, 128), fl_type),
            out((width, 128), fl_type),
            out((4 * width, width), bf_type),
        ],
        [
            whole((2 * width, width)),
            whole((width, width)),
            whole((width, 128)),
            whole((width, 128)),
            whole((4 * width, width)),
        ],
        [
            pltpu.VMEM((shards, 2 * half_qo, span), bf_type),
            pltpu.VMEM((shards, 2 * half_kv, span), bf_type),
        ],
        1e6,
        "weights",
    )

    sig_query, query, gate, grad_prod = call(
        query_kernel,
        (steps,),
        (place, x_turned, g, query_gate, out_weight),
        [smem(), by_row, by_row, whole((2 * width, width)), whole((width, width))],
        [
            out((width, rows), fl_type),
            out((width, rows), bf_type),
            out((width, rows), fl_type),
            out((width, rows), fl_type),
        ],
        [by_lane] * 4,
        [],
        6 * rows * width * width,
        "queries",
    )

    lane16 = pl.BlockSpec((16, block), lambda i: (0, i))
    prod, dgate, dnum, dden, keep, send = call(
        middle_kernel,
        (steps,),
        (place, ids, query, gate, grad_prod, gain, shift, *chunks),
        [smem(), id_lane, by_lane, by_lane, by_lane, whole((width, 128)), whole((width, 128))] + chunk_specs,
        [
            out((width, rows), bf_type),
            out((width, rows), bf_type),
            out((width, rows), bf_type),
            out((16, rows), fl_type),
            out(chunk_shape, fl_type),
            out(chunk_shape, bf_type),
        ],
        [by_lane, by_lane, by_lane, lane16, whole(chunk_shape), whole(chunk_shape)],
        [
            pltpu.VMEM((CHUNKS, head + PAD, half), bf_type),
            pltpu.VMEM((GROUPS, half + PAD, CLUSTERS * half), bf_type),
            pltpu.VMEM((CLUSTERS * half + 32, block), bf_type),
            pltpu.VMEM((width, block), fl_type),
            pltpu.VMEM((width, block), fl_type),
            pltpu.VMEM((width, block), fl_type),
            pltpu.VMEM((16, block), fl_type),
            pltpu.VMEM((16, block), fl_type),
            pltpu.VMEM((GROUPS, CLUSTERS * half + 32, half), fl_type),
            pltpu.VMEM((width, 128), fl_type),
            pltpu.VMEM((width, 128), fl_type),
        ],
        12 * rows * width * width,
        "middle",
    )

    back_chunks = reduce_chunks(keep, send)

    early = tall + tall // 2
    early_shape = (4, shards, early * 1, span)
    if width // 4 != span:
        early_shape = (4, shards, tall + (span // 2) * (width // 4 // span), span)
    early = early_shape[2]
    dquery, early_keep, early_send = call(
        functools.partial(query_back_kernel, shards),
        (steps,),
        (place, ids, dnum, dden, dgate, sig_query, prod, x_turned, g, *chunks),
        [smem(), id_lane, by_lane, lane16, by_lane, by_lane, by_lane, by_row, by_row] + chunk_specs,
        [out((width, rows), bf_type), out(early_shape, fl_type), out(early_shape, bf_type)],
        [by_lane, whole(early_shape), whole(early_shape)],
        [
            pltpu.VMEM((CHUNKS, head + PAD, half), bf_type),
            pltpu.VMEM((GROUPS, half, CLUSTERS * half), bf_type),
            pltpu.VMEM((CLUSTERS, width, 128), fl_type),
            pltpu.VMEM((CLUSTERS * half, block), bf_type),
            pltpu.VMEM((2 * width, width), fl_type),
            pltpu.VMEM((width, width), fl_type),
        ],
        10 * rows * width * width,
        "query_back",
    )
    block_out = call(
        output_kernel,
        (steps,),
        (place, x, prod, out_weight),
        [smem(), by_row, by_lane, whole((width, width))],
        [out((rows, width), fl_type)],
        [by_row],
        [],
        2 * rows * width * width,
        "output",
    )[0]

    dkey, dvalue, norm_grad, late_keep, late_send = call(
        functools.partial(key_back_kernel, shards),
        (steps,),
        (place, ids, sig_key, value, x_turned, *back_chunks),
        [smem(), id_lane, by_lane, by_lane, by_row] + chunk_specs,
        [
            out((width, rows), bf_type),
            out((width, rows), bf_type),
            out((8, width), fl_type),
            out(piece_shape, fl_type),
            out(piece_shape, bf_type),
        ],
        [by_lane, by_lane, whole((8, width)), whole(piece_shape), whole(piece_shape)],
        [
            pltpu.VMEM((CHUNKS, head + PAD, half), bf_type),
            pltpu.VMEM((GROUPS, half, CLUSTERS * half), bf_type),
            pltpu.VMEM((GROUPS, half, CLUSTERS * half), bf_type),
            pltpu.VMEM((CLUSTERS, width, 128), fl_type),
            pltpu.VMEM((CLUSTERS * half, block), bf_type),
            pltpu.VMEM((2 * width, width), fl_type),
        ],
        12 * rows * width * width,
        "key_back",
    )

    def reduce_pieces(keep, send):
        mine = keep + exchange(send, 1, 0).astype(fl_type)
        got = [exchange(mine[e].astype(bf_type), 2 * e, 0) for e in range(1, 4)]
        mine = tree_sum([mine[0], *to_float(got)])
        got = [exchange(mine[z].astype(bf_type), 0, z) for z in range(1, shards)]
        mine = tree_sum([mine[0], *to_float(got)])
        if outer > 1:
            own = mine.astype(bf_type)
            got = [own] + [exchange(own, 8 * o, 0) for o in range(1, outer)]
            mine = tree_sum(to_float(got))
        return mine.astype(bf_type)

    early_sum = reduce_pieces(early_keep, early_send)
    late_sum = reduce_pieces(late_keep, late_send)

    input_grad = call(
        input_kernel,
        (steps,),
        (dquery, dkey, dvalue, dgate, full, g),
        [by_lane] * 4 + [whole((4 * width, width)), by_row],
        [out((rows, width), fl_type)],
        [by_row],
        [],
        8 * rows * width * width,
        "inputs",
    )[0]

    parts = spread(jnp.concatenate([late_sum, early_sum], axis=0))
    grad_proj, grad_out, squares = call(
        gather_kernel,
        (),
        (place, *parts),
        [smem()] + [whole((tall + early, span))] * 8,
        [out((span, 4 * width), fl_type), out((span, width), fl_type), out((8, span), fl_type)],
        [whole((span, 4 * width)), whole((span, width)), whole((8, span))],
        [pltpu.VMEM((8, tall, span), fl_type), pltpu.VMEM((8, tall, span), fl_type)],
        1e6,
        "gather",
    )
    gain_grad = norm_grad[1:3]
    squares = jnp.broadcast_to(jnp.sum(squares), (8, 128))
    square_sum = tree_sum([squares] + [exchange(squares, 0, z) for z in range(1, shards)])[0, 0]
    grad_size = jnp.sqrt(square_sum + jnp.sum(gain_grad * gain_grad))
    clip_level = 0.5 * math.sqrt(5 * width * width + 2 * width)
    factor = jnp.minimum(1.0, clip_level / grad_size).reshape(1)
    mine_norm = lax.dynamic_slice_in_dim(gain_grad, shard * span, span, 1)
    states = (grad_proj, grad_out, mine_norm, pw, pm, ps, ow, om, osq, nw, nm, ns)
    like = [pw, pw, pw, pw, ow, ow, ow, ow, nw, nw, nw, nw]
    kinds = [fl_type] * 3 + [bf_type] + [fl_type] * 3 + [bf_type] + [fl_type] * 4
    new = call(
        update_kernel,
        (),
        (factor, *states),
        [smem()] + [whole(s.shape) for s in states],
        [out(s.shape, k) for s, k in zip(like, kinds)],
        [whole(s.shape) for s in like],
        [],
        1e6,
        "update",
    )
    return (block_out, input_grad, grad_size.reshape(1), *new)


def solution(mesh):
    nodes, shards = mesh.shape["nodes"], mesh.shape["shard"]
    by_node = P(AXES, None)
    rows = P("shard", None)
    cols = P(None, "shard")
    return jax.shard_map(
        functools.partial(local, nodes, shards),
        mesh=mesh,
        in_specs=(by_node, by_node, P(AXES), P(AXES)) + (rows,) * 6 + (cols,) * 3,
        out_specs=(by_node, by_node, P()) + (rows,) * 8 + (cols,) * 4,
        check_vma=False,
    )
```

time: 429 us -> 218 us (0.51); the launches traced: 421 us -> 217 us
  blocking collectives: 135 us -> 0 us
  waiting for transfers between devices: 137 us -> 43.6 us
  Pallas kernels: 0 us -> 89 us
  matrix products: 72.3 us -> 0 us
  starting transfers between devices: 0.08 us -> 63.4 us
  local copies, waits for them, and re-layouts: 32.6 us -> 8.42 us
  other arithmetic: 25.7 us -> 8.2 us
  between operations: 18.5 us -> 4.46 us
    psum x1 -> x0, waiting for transfers between devices: 117 us -> none  [local(): lax.psum((grad_wproj, grad_wout, grad_wnorm), ('nodes', 'shard'))]
    psum x2 -> x0, blocking collectives: 101 us -> none  [the longest x1 51.8 us: local(): summary, key_sum = lax.psum((local_kv, local_ks), ('nodes', 'shard'))]
    pallas_call x0 -> x11, Pallas kernels: none -> 89 us  [call(): pl.pallas_call(kernel, grid=grid, in_specs=in_specs, out_specs=out_specs,...]
    dot_general x16 -> x0, matrix products: 72.3 us -> none  [the longest x1 11.7 us: local(): grad_wproj = jnp.dot(node_feats.T, grad_pre, preferred_element_type=fl_type)]
    ppermute x0 -> x64, starting transfers between devices: none -> 63.4 us  [exchange(): return lax.ppermute(value, AXES, pairs)]
    ppermute x0 -> x64, waiting for transfers between devices: none -> 43.6 us  [exchange(): return lax.ppermute(value, AXES, pairs)]
    all_gather x2 -> x0, blocking collectives: 33.8 us -> none  [the longest x1 21.2 us: local(): lax.all_gather(out_master.astype(bf_type), 'shard', axis=0, tiled=True)]
    unnamed x65 -> x78, local copies, waits for them, and re-layouts: 32.2 us -> 4.92 us
  transfers between devices with their start and end apart: 2 -> 64, of which waited for: 2 -> 25; matrix products, arithmetic and copies ran while one was open for 7% -> 3% of each run, Pallas kernels for 0% -> 25%
where the time goes in v1:
time: 218 us; the launch traced here: 217 us
  Pallas kernels  89 us (41%)
  starting transfers between devices  63.4 us (29%)
  waiting for transfers between devices  43.6 us (20%)
  local copies, waits for them, and re-layouts  8.42 us (4%)
  other arithmetic  8.2 us (4%)
  between operations  4.46 us (2%)
    pallas_call x11, Pallas kernels, call(): pl.pallas_call(kernel, grid=grid, in_specs=in_specs, out_specs=out_specs,...  89 us
    ppermute x64, starting transfers between devices, exchange(): return lax.ppermute(value, AXES, pairs)  63.4 us
    ppermute x64, waiting for transfers between devices, exchange(): return lax.ppermute(value, AXES, pairs)  43.6 us
    unnamed x78, local copies, waits for them, and re-layouts  4.92 us
  transfers between devices with their start and end apart: 64, of which 25 were waited for; matrix products, arithmetic and copies ran while one was open for 3% of the time, Pallas kernels for 25%

profile of v1, /device:TPU:0, one launch (start us, length us, event | category | flops | bytes accessed | tf_op | source)
XLA Modules:
  0.0 217.1 jit_solution(8276093248442153902)
XLA Ops:
  1.9 2.3 %prep.1 = (bf16[512,128]{1,0:T(8,128)(2,1)}, bf16[512,128]{1,0:T(8,128)(2,1)}, bf16[784,128]{1,0:T(8,128)(2,1)}, bf16[784,128]{1,0:T(8,128)(2,1)}) custom-call(s32[4]{0:T(128)} %pad_add_fusion.place, f32[128,2048]{1,0:T(8,128)} %pw.1, f32[128,512]{1,0:T(8,128)} %ow.1, f32[2,128]{1,0:T(2,128)} %nw.1), custom_call_target="tpu_custom_call" | custom-call | flops 1000000 | bytes 1975312 | tf_op jit(solution)/shard_map/prep/pallas_call | solution.py:53
  4.2 5.0 %collective-permute-start.8 = (bf16[512,128]{1,0:T(8,128)(2,1)}, bf16[512,128]{1,0:T(8,128)(2,1)S(1)}, u32[]{:S(2)}, u32[]{:S(2)}) collective-permute-start(bf16[512,128]{1,0:T(8,128)(2,1)} %get-tuple-element.63.refs_8_.refs_0_), channel_id=1, source_target_pairs={{0,3},{1,2},{2,1},{3,0},{4,7},{5,6},{6,5},{7,4},{8,11},{9,10},{10,... | collective-permute-start | bytes 393224 | tf_op jit(solution)/shard_map/ppermute | solution.py:569
  9.8 1.7 constant_dynamic-slice_fusion.4
  11.5 2.4 %collective-permute-done.8.refs_11_.refs_3_ = bf16[512,128]{1,0:T(8,128)(2,1)S(1)} collective-permute-done((bf16[512,128]{1,0:T(8,128)(2,1)}, bf16[512,128]{1,0:T(8,128)(2,1)S(1)}, u32[]{:S(2)}, u32[]{:S(2)}) %collective-permute-start.8) | collective-permute-done | bytes 131104 | tf_op jit(solution)/shard_map/ppermute | solution.py:569
  13.9 6.6 %collective-permute-done.7.refs_10_.refs_2_ = bf16[512,128]{1,0:T(8,128)(2,1)S(1)} collective-permute-done((bf16[512,128]{1,0:T(8,128)(2,1)}, bf16[512,128]{1,0:T(8,128)(2,1)S(1)}, u32[]{:S(2)}, u32[]{:S(2)}) %collective-permute-start.7) | collective-permute-done | bytes 131104 | tf_op jit(solution)/shard_map/ppermute | solution.py:569
  21.1 1.5 pad_maximum_fusion.x
  23.4 8.8 %keys.1 = (f32[512,2048]{1,0:T(8,128)}, bf16[512,2048]{1,0:T(8,128)(2,1)}, f32[4,80,256]{2,1,0:T(8,128)}, bf16[4,80,256]{2,1,0:T(8,128)(2,1)}) custom-call(s32[4]{0:T(128)} %pad_add_fusion.place, bf16[2048,512]{1,0:T(8,128)(2,1)} %pad_maximum_fusion.x, s32[1,2048]{1,0:T(1,128)} %bitcast.89, bf16[512,128]{1,0:T(8,128)(2,1)} %get-tuple-element.63.refs_8_.refs_0_, ...), custom_call_target="tpu_custom_call" | custom-call | flops 4294967296 | bytes 9936912 | tf_op jit(solution)/shard_map/keys/pallas_call | solution.py:53
  32.3 1.5 collective-permute-done.12
  33.8 1.0 fusion.23
  34.9 1.6 collective-permute-start.13
  36.4 1.5 collective-permute-start.15
  38.4 2.5 %collective-permute-start.2 = (bf16[784,128]{1,0:T(8,128)(2,1)S(1)}, bf16[784,128]{1,0:T(8,128)(2,1)S(1)}, u32[]{:S(2)}, u32[]{:S(2)}) collective-permute-start(bf16[784,128]{1,0:T(8,128)(2,1)S(1)} %copy-done.3), channel_id=1, source_target_pairs={{0,3},{1,2},{2,1},{3,0},{4,7},{5,6},{6,5},{7,4},{8,11},{9,10},{10,... | collective-permute-start | bytes 602120 | tf_op jit(solution)/shard_map/ppermute | solution.py:569
  40.9 1.9 collective-permute-start
  42.9 2.5 %collective-permute-start.18 = (bf16[80,256]{1,0:T(8,128)(2,1)S(1)}, bf16[80,256]{1,0:T(8,128)(2,1)S(1)}, u32[]{:S(2)}, u32[]{:S(2)}) collective-permute-start(bf16[80,256]{1,0:T(8,128)(2,1)S(1)} %fusion.12), channel_id=1, source_target_pairs={{0,3},{1,2},{2,1},{3,0},{4,7},{5,6},{6,5},{7,4},{8,11},{9,10},{10,... | collective-permute-start | bytes 122888 | tf_op jit(solution)/shard_map/ppermute | solution.py:569
  45.4 2.9 %collective-permute-done.2.refs_3_ = bf16[784,128]{1,0:T(8,128)(2,1)S(1)} collective-permute-done((bf16[784,128]{1,0:T(8,128)(2,1)S(1)}, bf16[784,128]{1,0:T(8,128)(2,1)S(1)}, u32[]{:S(2)}, u32[]{:S(2)}) %collective-permute-start.2) | collective-permute-done | bytes 200736 | tf_op jit(solution)/shard_map/ppermute | solution.py:569
  48.3 6.8 %collective-permute-start.16 = (bf16[80,256]{1,0:T(8,128)(2,1)S(1)}, bf16[80,256]{1,0:T(8,128)(2,1)S(1)}, u32[]{:S(2)}, u32[]{:S(2)}) collective-permute-start(bf16[80,256]{1,0:T(8,128)(2,1)S(1)} %fusion.12), channel_id=1, source_target_pairs={{0,1},{1,0},{2,3},{3,2},{4,5},{5,4},{6,7},{7,6},{8,9},{9,8},{10,11... | collective-permute-start | bytes 122888 | tf_op jit(solution)/shard_map/ppermute | solution.py:569
  55.1 4.3 %collective-permute-done.1.refs_2_ = bf16[784,128]{1,0:T(8,128)(2,1)S(1)} collective-permute-done((bf16[784,128]{1,0:T(8,128)(2,1)S(1)}, bf16[784,128]{1,0:T(8,128)(2,1)S(1)}, u32[]{:S(2)}, u32[]{:S(2)}) %collective-permute-start.1) | collective-permute-done | bytes 200736 | tf_op jit(solution)/shard_map/ppermute | solution.py:569
  60.3 2.5 %collective-permute-start.24 = (bf16[80,256]{1,0:T(8,128)(2,1)S(1)}, bf16[80,256]{1,0:T(8,128)(2,1)S(1)}, u32[]{:S(2)}, u32[]{:S(2)}) collective-permute-start(bf16[80,256]{1,0:T(8,128)(2,1)S(1)} %add_convert_fusion.1.refs_0_), channel_id=1, source_target_pairs={{0,24},{1,25},{2,26},{3,27},{4,28},{5,29},{6,30},{7,31},{8,16},{9,... | collective-permute-start | bytes 122888 | tf_op jit(solution)/shard_map/ppermute | solution.py:569
  64.6 4.2 %weights.1 = (bf16[1024,512]{1,0:T(8,128)(2,1)}, bf16[512,512]{1,0:T(8,128)(2,1)}, f32[512,128]{1,0:T(8,128)}, f32[512,128]{1,0:T(8,128)}, bf16[2048,512]{1,0:T(8,128)(2,1)}) custom-call(s32[4]{0:T(128)} %pad_add_fusion.place, bf16[784,128]{1,0:T(8,128)(2,1)} %get-tuple-element.61.refs_0_, bf16[784,128]{1,0:T(8,128)(2,1)} %copy-done.6, ...), custom_call_target="tpu_custom_call" | custom-call | flops 1000000 | bytes 6848528 | tf_op jit(solution)/shard_map/weights/pallas_call | solution.py:53
  69.8 8.9 %queries.1 = (f32[512,2048]{1,0:T(8,128)}, bf16[512,2048]{1,0:T(8,128)(2,1)}, f32[512,2048]{1,0:T(8,128)}, f32[512,2048]{1,0:T(8,128)}) custom-call(s32[4]{0:T(128)} %pad_add_fusion.place, bf16[2048,512]{1,0:T(8,128)(2,1)} %pad_maximum_fusion.x, bf16[2048,512]{1,0:T(8,128)(2,1)} %g.5, bf16[1024,512]{1,0:T(8,128)(2,1)} %get-tuple-element.65.query_gate, ...), custom_call_target="tpu_custom_call" | custom-call | flops 3221225472 | bytes 20447248 | tf_op jit(solution)/shard_map/queries/pallas_call | solution.py:53
  79.5 15.0 %middle.1 = (bf16[512,2048]{1,0:T(8,128)(2,1)}, bf16[512,2048]{1,0:T(8,128)(2,1)}, bf16[512,2048]{1,0:T(8,128)(2,1)}, f32[16,2048]{1,0:T(8,128)}, f32[4,80,256]{2,1,0:T(8,128)}, /*index=5*/bf16[4,80,256]{2,1,0:T(8,128)(2,1)}) custom-call(s32[4]{0:T(128)} %pad_add_fusion.place, s32[1,2048]{1,0:T(1,128)} %bitcast.90, ...), custom_call_target="tpu_custom_call" | custom-call | flops 6442450944 | bytes 18259984 | tf_op jit(solution)/shard_map/middle/pallas_call | solution.py:53
  94.7 1.5 collective-permute-done.26
  96.2 1.0 fusion.22
  97.2 1.6 collective-permute-start.27
  98.8 1.5 collective-permute-start.29
  101.3 2.4 %collective-permute-done.29 = bf16[80,256]{1,0:T(8,128)(2,1)S(1)} collective-permute-done((bf16[80,256]{1,0:T(8,128)(2,1)S(1)}, bf16[80,256]{1,0:T(8,128)(2,1)S(1)}, u32[]{:S(2)}, u32[]{:S(2)}) %collective-permute-start.29) | collective-permute-done | bytes 40992 | tf_op jit(solution)/shard_map/ppermute | solution.py:569
  104.3 2.1 collective-permute-start.32
  106.4 2.4 %collective-permute-start.30 = (bf16[80,256]{1,0:T(8,128)(2,1)S(1)}, bf16[80,256]{1,0:T(8,128)(2,1)S(1)}, u32[]{:S(2)}, u32[]{:S(2)}) collective-permute-start(bf16[80,256]{1,0:T(8,128)(2,1)S(1)} %fusion.9), channel_id=1, source_target_pairs={{0,1},{1,0},{2,3},{3,2},{4,5},{5,4},{6,7},{7,6},{8,9},{9,8},{10,11... | collective-permute-start | bytes 122888 | tf_op jit(solution)/shard_map/ppermute | solution.py:569
  108.8 1.5 collective-permute-done.32
  110.3 1.0 collective-permute-done.31
  111.3 1.5 collective-permute-start.38
  112.8 1.5 collective-permute-start.36
  114.9 1.4 collective-permute-done.38.refs_6_
  116.8 1.5 collective-permute-done.34.refs_2_
  118.3 13.0 %query_back.1 = (bf16[512,2048]{1,0:T(8,128)(2,1)}, f32[4,4,192,128]{3,2,1,0:T(8,128)}, bf16[4,4,192,128]{3,2,1,0:T(8,128)(2,1)}) custom-call(s32[4]{0:T(128)} %pad_add_fusion.place, s32[1,2048]{1,0:T(1,128)} %bitcast.91, bf16[512,2048]{1,0:T(8,128)(2,1)} %get-tuple-element.75.dnum, f32[16,2048]{1,0:T(8,128)} %get-tuple-element.76.dden, ...), custom_call_target="tpu_custom_call" | custom-call | flops 5368709120 | bytes 19603472 | tf_op jit(solution)/shard_map/query_back/pallas_call | solution.py:53
  132.6 12.5 %key_back.1 = (bf16[512,2048]{1,0:T(8,128)(2,1)}, bf16[512,2048]{1,0:T(8,128)(2,1)}, f32[8,512]{1,0:T(8,128)}, f32[4,4,128,128]{3,2,1,0:T(8,128)}, bf16[4,4,128,128]{3,2,1,0:T(8,128)(2,1)}) custom-call(s32[4]{0:T(128)} %pad_add_fusion.place, s32[1,2048]{1,0:T(1,128)} %bitcast.92, f32[512,2048]{1,0:T(8,128)} %get-tuple-element.80.sig_key, ...), custom_call_target="tpu_custom_call" | custom-call | flops 6442450944 | bytes 14508048 | tf_op jit(solution)/shard_map/key_back/pallas_call | solution.py:53
  145.2 6.0 %output.1 = f32[2048,512]{1,0:T(8,128)} custom-call(s32[4]{0:T(128)} %pad_add_fusion.place, bf16[2048,512]{1,0:T(8,128)(2,1)} %x.1, bf16[512,2048]{1,0:T(8,128)(2,1)} %get-tuple-element.74.prod, bf16[512,512]{1,0:T(8,128)(2,1)} %get-tuple-element.66.out_weight), custom_call_target="tpu_custom_call" | custom-call | flops 1073741824 | bytes 8912912 | tf_op jit(solution)/shard_map/output/pallas_call | solution.py:53
  151.5 0.9 copy-done.1
  153.3 1.4 collective-permute-start.43
  154.7 1.5 collective-permute-start.42
  156.9 1.4 collective-permute-start.50
  159.1 0.8 collective-permute-start.49
  159.9 2.0 collective-permute-done.43
  161.9 1.9 collective-permute-done.42
  163.8 1.6 collective-permute-start.44
  165.4 2.0 collective-permute-start.46
  167.4 0.8 collective-permute-start.45
  168.2 1.7 collective-permute-done.50
  169.9 1.3 collective-permute-done.49
  171.3 1.6 collective-permute-start.51
  172.9 2.0 collective-permute-start.53
  175.5 3.3 %collective-permute-done.53 = bf16[192,128]{1,0:T(8,128)(2,1)S(1)} collective-permute-done((bf16[192,128]{1,0:T(8,128)(2,1)S(1)}, bf16[192,128]{1,0:T(8,128)(2,1)S(1)}, u32[]{:S(2)}, u32[]{:S(2)}) %collective-permute-start.53) | collective-permute-done | bytes 49184 | tf_op jit(solution)/shard_map/ppermute | solution.py:569
  178.8 1.1 collective-permute-done.52
  179.9 1.6 collective-permute-start.59
  181.5 1.0 collective-permute-start.57
  182.4 1.0 collective-permute-start.55
  183.5 10.0 %inputs.1 = f32[2048,512]{1,0:T(8,128)} custom-call(bf16[512,2048]{1,0:T(8,128)(2,1)} %get-tuple-element.79.dquery, bf16[512,2048]{1,0:T(8,128)(2,1)} %get-tuple-element.84.dkey, bf16[512,2048]{1,0:T(8,128)(2,1)} %get-tuple-element.85.dvalue, bf16[512,2048]{1,0:T(8,128)(2,1)} %get-tuple-element.77.dgate, bf16[2048,512]{1,0:T(8,128)(2,1)} %get-tuple-element.86.full, ...), custom_call_target="tpu_custom_call" | custom-call | flops 4294967296 | bytes 16777216 | tf_op jit(solution)/shard_map/inputs/pallas_call | solution.py:53
  194.5 1.3 fusion.24
  197.2 2.9 %gather.1 = (f32[128,2048]{1,0:T(8,128)}, f32[128,512]{1,0:T(8,128)}, f32[8,128]{1,0:T(8,128)}) custom-call(s32[4]{0:T(128)} %pad_add_fusion.place, bf16[320,128]{1,0:T(8,128)(2,1)} %copy-done.2, bf16[320,128]{1,0:T(8,128)(2,1)} %copy-done.19, bf16[320,128]{1,0:T(8,128)(2,1)} %copy-done.18, bf16[320,128]{1,0:T(8,128)(2,1)} %copy-done.22, ...), custom_call_target="tpu_custom_call" | custom-call | flops 1000000 | bytes 1970192 | tf_op jit(solution)/shard_map/gather/pallas_call | solution.py:53
  200.1 1.3 reduce_sum.18
  202.6 1.8 collective-permute-start.63
  204.4 1.1 collective-permute-start.61
  206.5 1.4 collective-permute-done.63
  210.6 5.4 %update.1 = (f32[128,2048]{1,0:T(8,128)}, f32[128,2048]{1,0:T(8,128)}, f32[128,2048]{1,0:T(8,128)}, bf16[128,2048]{1,0:T(8,128)(2,1)}, f32[128,512]{1,0:T(8,128)...) custom-call(f32[1]{0:T(128)} %bitcast.30.scale, ...), custom_call_target="tpu_custom_call" | custom-call | flops 1000000 | bytes 9838596 | tf_op jit(solution)/shard_map/update/pallas_call | solution.py:53
  (181 shorter events, 20.7 us)
Async XLA Ops:
  4.2 9.7 %collective-permute-start.8 = (bf16[512,128]{1,0:T(8,128)(2,1)}, bf16[512,128]{1,0:T(8,128)(2,1)S(1)}, u32[]{:S(2)}, u32[]{:S(2)}) collective-permute-start(bf16[512,128]{1,0:T(8,128)(2,1)} %get-tuple-element.63.refs_8_.refs_0_), channel_id=1, source_target_pairs={{0,3},{1,2},{2,1},{3,0},{4,7},{5,6},{6,5},{7,4},{8,11},{9,10},{10,... | collective-permute-start | bytes 393224 | tf_op jit(solution)/shard_map/ppermute | solution.py:569
  9.3 11.3 %collective-permute-start.7 = (bf16[512,128]{1,0:T(8,128)(2,1)}, bf16[512,128]{1,0:T(8,128)(2,1)S(1)}, u32[]{:S(2)}, u32[]{:S(2)}) collective-permute-start(bf16[512,128]{1,0:T(8,128)(2,1)} %get-tuple-element.63.refs_8_.refs_0_), channel_id=1, source_target_pairs={{0,2},{1,3},{2,0},{3,1},{4,6},{5,7},{6,4},{7,5},{8,10},{9,11},{10,... | collective-permute-start | bytes 393224 | tf_op jit(solution)/shard_map/ppermute | solution.py:569
  9.3 11.3 %collective-permute-start.6 = (bf16[512,128]{1,0:T(8,128)(2,1)}, bf16[512,128]{1,0:T(8,128)(2,1)S(1)}, u32[]{:S(2)}, u32[]{:S(2)}) collective-permute-start(bf16[512,128]{1,0:T(8,128)(2,1)} %get-tuple-element.63.refs_8_.refs_0_), channel_id=1, source_target_pairs={{0,1},{1,0},{2,3},{3,2},{4,5},{5,4},{6,7},{7,6},{8,9},{9,8},{10,11... | collective-permute-start | bytes 393224 | tf_op jit(solution)/shard_map/ppermute | solution.py:569
  13.9 8.7 %collective-permute-start.11 = (bf16[512,128]{1,0:T(8,128)(2,1)S(1)}, bf16[512,128]{1,0:T(8,128)(2,1)S(1)}, u32[]{:S(2)}, u32[]{:S(2)}) collective-permute-start(bf16[512,128]{1,0:T(8,128)(2,1)S(1)} %collective-permute-done.8.refs_11_.refs_3_), channel_id=1, source_target_pairs={{0,4},{1,5},{2,6},{3,7},{4,0},{5,1},{6,2},{7,3},{8,12},{9,13},{10,... | collective-permute-start | bytes 393224 | tf_op jit(solution)/shard_map/ppermute | solution.py:569
  20.6 2.1 collective-permute-start.10
  20.6 2.1 collective-permute-start.9
  32.2 1.7 collective-permute-start.12
  34.9 6.0 %collective-permute-start.13 = (bf16[80,256]{1,0:T(8,128)(2,1)S(1)}, bf16[80,256]{1,0:T(8,128)(2,1)S(1)}, u32[]{:S(2)}, u32[]{:S(2)}) collective-permute-start(bf16[80,256]{1,0:T(8,128)(2,1)S(1)} %get-tuple-element.135), channel_id=1, source_target_pairs={{0,8},{1,9},{2,10},{3,11},{4,12},{5,13},{6,14},{7,15},{8,0},{9,1},... | collective-permute-start | bytes 122888 | tf_op jit(solution)/shard_map/ppermute | solution.py:569
  36.4 6.4 %collective-permute-start.15 = (bf16[80,256]{1,0:T(8,128)(2,1)S(1)}, bf16[80,256]{1,0:T(8,128)(2,1)S(1)}, u32[]{:S(2)}, u32[]{:S(2)}) collective-permute-start(bf16[80,256]{1,0:T(8,128)(2,1)S(1)} %get-tuple-element.136), channel_id=1, source_target_pairs={{0,24},{1,25},{2,26},{3,27},{4,28},{5,29},{6,30},{7,31},{8,16},{9,... | collective-permute-start | bytes 122888 | tf_op jit(solution)/shard_map/ppermute | solution.py:569
  37.9 4.9 %collective-permute-start.14 = (bf16[80,256]{1,0:T(8,128)(2,1)S(1)}, bf16[80,256]{1,0:T(8,128)(2,1)S(1)}, u32[]{:S(2)}, u32[]{:S(2)}) collective-permute-start(bf16[80,256]{1,0:T(8,128)(2,1)S(1)} %get-tuple-element.137), channel_id=1, source_target_pairs={{0,16},{1,17},{2,18},{3,19},{4,20},{5,21},{6,22},{7,23},{8,24},{9,... | collective-permute-start | bytes 122888 | tf_op jit(solution)/shard_map/ppermute | solution.py:569
  38.4 9.8 %collective-permute-start.2 = (bf16[784,128]{1,0:T(8,128)(2,1)S(1)}, bf16[784,128]{1,0:T(8,128)(2,1)S(1)}, u32[]{:S(2)}, u32[]{:S(2)}) collective-permute-start(bf16[784,128]{1,0:T(8,128)(2,1)S(1)} %copy-done.3), channel_id=1, source_target_pairs={{0,3},{1,2},{2,1},{3,0},{4,7},{5,6},{6,5},{7,4},{8,11},{9,10},{10,... | collective-permute-start | bytes 602120 | tf_op jit(solution)/shard_map/ppermute | solution.py:569
  40.9 18.5 %collective-permute-start.1 = (bf16[784,128]{1,0:T(8,128)(2,1)S(1)}, bf16[784,128]{1,0:T(8,128)(2,1)S(1)}, u32[]{:S(2)}, u32[]{:S(2)}) collective-permute-start(bf16[784,128]{1,0:T(8,128)(2,1)S(1)} %copy-done.3), channel_id=1, source_target_pairs={{0,2},{1,3},{2,0},{3,1},{4,6},{5,7},{6,4},{7,5},{8,10},{9,11},{10,... | collective-permute-start | bytes 602120 | tf_op jit(solution)/shard_map/ppermute | solution.py:569
  40.9 18.5 %collective-permute-start = (bf16[784,128]{1,0:T(8,128)(2,1)S(1)}, bf16[784,128]{1,0:T(8,128)(2,1)S(1)}, u32[]{:S(2)}, u32[]{:S(2)}) collective-permute-start(bf16[784,128]{1,0:T(8,128)(2,1)S(1)} %copy-done.3), channel_id=1, source_target_pairs={{0,1},{1,0},{2,3},{3,2},{4,5},{5,4},{6,7},{7,6},{8,9},{9,8},{10,11... | collective-permute-start | bytes 602120 | tf_op jit(solution)/shard_map/ppermute | solution.py:569
  42.9 17.0 %collective-permute-start.18 = (bf16[80,256]{1,0:T(8,128)(2,1)S(1)}, bf16[80,256]{1,0:T(8,128)(2,1)S(1)}, u32[]{:S(2)}, u32[]{:S(2)}) collective-permute-start(bf16[80,256]{1,0:T(8,128)(2,1)S(1)} %fusion.12), channel_id=1, source_target_pairs={{0,3},{1,2},{2,1},{3,0},{4,7},{5,6},{6,5},{7,4},{8,11},{9,10},{10,... | collective-permute-start | bytes 122888 | tf_op jit(solution)/shard_map/ppermute | solution.py:569
  45.4 14.8 %collective-permute-start.17 = (bf16[80,256]{1,0:T(8,128)(2,1)S(1)}, bf16[80,256]{1,0:T(8,128)(2,1)S(1)}, u32[]{:S(2)}, u32[]{:S(2)}) collective-permute-start(bf16[80,256]{1,0:T(8,128)(2,1)S(1)} %fusion.12), channel_id=1, source_target_pairs={{0,2},{1,3},{2,0},{3,1},{4,6},{5,7},{6,4},{7,5},{8,10},{9,11},{10,... | collective-permute-start | bytes 122888 | tf_op jit(solution)/shard_map/ppermute | solution.py:569
  48.3 12.0 %collective-permute-start.16 = (bf16[80,256]{1,0:T(8,128)(2,1)S(1)}, bf16[80,256]{1,0:T(8,128)(2,1)S(1)}, u32[]{:S(2)}, u32[]{:S(2)}) collective-permute-start(bf16[80,256]{1,0:T(8,128)(2,1)S(1)} %fusion.12), channel_id=1, source_target_pairs={{0,1},{1,0},{2,3},{3,2},{4,5},{5,4},{6,7},{7,6},{8,9},{9,8},{10,11... | collective-permute-start | bytes 122888 | tf_op jit(solution)/shard_map/ppermute | solution.py:569
  59.4 3.9 %collective-permute-start.5 = (bf16[784,128]{1,0:T(8,128)(2,1)S(1)}, bf16[784,128]{1,0:T(8,128)(2,1)S(1)}, u32[]{:S(2)}, u32[]{:S(2)}) collective-permute-start(bf16[784,128]{1,0:T(8,128)(2,1)S(1)} %collective-permute-done.2.refs_3_), channel_id=1, source_target_pairs={{0,4},{1,5},{2,6},{3,7},{4,0},{5,1},{6,2},{7,3},{8,12},{9,13},{10,... | collective-permute-start | bytes 602120 | tf_op jit(solution)/shard_map/ppermute | solution.py:569
  59.4 4.5 %collective-permute-start.4 = (bf16[784,128]{1,0:T(8,128)(2,1)S(1)}, bf16[784,128]{1,0:T(8,128)(2,1)S(1)}, u32[]{:S(2)}, u32[]{:S(2)}) collective-permute-start(bf16[784,128]{1,0:T(8,128)(2,1)S(1)} %collective-permute-done.1.refs_2_), channel_id=1, source_target_pairs={{0,4},{1,5},{2,6},{3,7},{4,0},{5,1},{6,2},{7,3},{8,12},{9,13},{10,... | collective-permute-start | bytes 602120 | tf_op jit(solution)/shard_map/ppermute | solution.py:569
  59.9 4.0 %collective-permute-start.3 = (bf16[784,128]{1,0:T(8,128)(2,1)S(1)}, bf16[784,128]{1,0:T(8,128)(2,1)S(1)}, u32[]{:S(2)}, u32[]{:S(2)}) collective-permute-start(bf16[784,128]{1,0:T(8,128)(2,1)S(1)} %collective-permute-done.refs_1_), channel_id=1, source_target_pairs={{0,4},{1,5},{2,6},{3,7},{4,0},{5,1},{6,2},{7,3},{8,12},{9,13},{10,... | collective-permute-start | bytes 602120 | tf_op jit(solution)/shard_map/ppermute | solution.py:569
  60.3 8.5 %collective-permute-start.24 = (bf16[80,256]{1,0:T(8,128)(2,1)S(1)}, bf16[80,256]{1,0:T(8,128)(2,1)S(1)}, u32[]{:S(2)}, u32[]{:S(2)}) collective-permute-start(bf16[80,256]{1,0:T(8,128)(2,1)S(1)} %add_convert_fusion.1.refs_0_), channel_id=1, source_target_pairs={{0,24},{1,25},{2,26},{3,27},{4,28},{5,29},{6,30},{7,31},{8,16},{9,... | collective-permute-start | bytes 122888 | tf_op jit(solution)/shard_map/ppermute | solution.py:569
  62.8 6.5 %collective-permute-start.22 = (bf16[80,256]{1,0:T(8,128)(2,1)S(1)}, bf16[80,256]{1,0:T(8,128)(2,1)S(1)}, u32[]{:S(2)}, u32[]{:S(2)}) collective-permute-start(bf16[80,256]{1,0:T(8,128)(2,1)S(1)} %add_convert_fusion.1.refs_0_), channel_id=1, source_target_pairs={{0,16},{1,17},{2,18},{3,19},{4,20},{5,21},{6,22},{7,23},{8,24},{9,... | collective-permute-start | bytes 122888 | tf_op jit(solution)/shard_map/ppermute | solution.py:569
  63.3 6.1 %collective-permute-start.20 = (bf16[80,256]{1,0:T(8,128)(2,1)S(1)}, bf16[80,256]{1,0:T(8,128)(2,1)S(1)}, u32[]{:S(2)}, u32[]{:S(2)}) collective-permute-start(bf16[80,256]{1,0:T(8,128)(2,1)S(1)} %add_convert_fusion.1.refs_0_), channel_id=1, source_target_pairs={{0,8},{1,9},{2,10},{3,11},{4,12},{5,13},{6,14},{7,15},{8,0},{9,1},... | collective-permute-start | bytes 122888 | tf_op jit(solution)/shard_map/ppermute | solution.py:569
  68.8 10.0 %collective-permute-start.19 = (bf16[80,256]{1,0:T(8,128)(2,1)S(1)}, bf16[80,256]{1,0:T(8,128)(2,1)S(1)}, u32[]{:S(2)}, u32[]{:S(2)}) collective-permute-start(bf16[80,256]{1,0:T(8,128)(2,1)S(1)} %add_convert_fusion.1.refs_0_), channel_id=1, source_target_pairs={{0,4},{1,5},{2,6},{3,7},{4,0},{5,1},{6,2},{7,3},{8,12},{9,13},{10,... | collective-permute-start | bytes 122888 | tf_op jit(solution)/shard_map/ppermute | solution.py:569
  68.8 10.0 %collective-permute-start.25 = (bf16[80,256]{1,0:T(8,128)(2,1)S(1)}, bf16[80,256]{1,0:T(8,128)(2,1)S(1)}, u32[]{:S(2)}, u32[]{:S(2)}) collective-permute-start(bf16[80,256]{1,0:T(8,128)(2,1)S(1)} %collective-permute-done.24.refs_6_), channel_id=1, source_target_pairs={{0,4},{1,5},{2,6},{3,7},{4,0},{5,1},{6,2},{7,3},{8,12},{9,13},{10,... | collective-permute-start | bytes 122888 | tf_op jit(solution)/shard_map/ppermute | solution.py:569
  69.3 9.5 %collective-permute-start.23 = (bf16[80,256]{1,0:T(8,128)(2,1)S(1)}, bf16[80,256]{1,0:T(8,128)(2,1)S(1)}, u32[]{:S(2)}, u32[]{:S(2)}) collective-permute-start(bf16[80,256]{1,0:T(8,128)(2,1)S(1)} %collective-permute-done.22.refs_4_), channel_id=1, source_target_pairs={{0,4},{1,5},{2,6},{3,7},{4,0},{5,1},{6,2},{7,3},{8,12},{9,13},{10,... | collective-permute-start | bytes 122888 | tf_op jit(solution)/shard_map/ppermute | solution.py:569
  69.4 9.5 %collective-permute-start.21 = (bf16[80,256]{1,0:T(8,128)(2,1)S(1)}, bf16[80,256]{1,0:T(8,128)(2,1)S(1)}, u32[]{:S(2)}, u32[]{:S(2)}) collective-permute-start(bf16[80,256]{1,0:T(8,128)(2,1)S(1)} %collective-permute-done.20.refs_2_), channel_id=1, source_target_pairs={{0,4},{1,5},{2,6},{3,7},{4,0},{5,1},{6,2},{7,3},{8,12},{9,13},{10,... | collective-permute-start | bytes 122888 | tf_op jit(solution)/shard_map/ppermute | solution.py:569
  94.5 1.7 collective-permute-start.26
  97.2 4.1 %collective-permute-start.27 = (bf16[80,256]{1,0:T(8,128)(2,1)S(1)}, bf16[80,256]{1,0:T(8,128)(2,1)S(1)}, u32[]{:S(2)}, u32[]{:S(2)}) collective-permute-start(bf16[80,256]{1,0:T(8,128)(2,1)S(1)} %get-tuple-element.132), channel_id=1, source_target_pairs={{0,8},{1,9},{2,10},{3,11},{4,12},{5,13},{6,14},{7,15},{8,0},{9,1},... | collective-permute-start | bytes 122888 | tf_op jit(solution)/shard_map/ppermute | solution.py:569
  98.8 4.9 %collective-permute-start.29 = (bf16[80,256]{1,0:T(8,128)(2,1)S(1)}, bf16[80,256]{1,0:T(8,128)(2,1)S(1)}, u32[]{:S(2)}, u32[]{:S(2)}) collective-permute-start(bf16[80,256]{1,0:T(8,128)(2,1)S(1)} %get-tuple-element.133), channel_id=1, source_target_pairs={{0,24},{1,25},{2,26},{3,27},{4,28},{5,29},{6,30},{7,31},{8,16},{9,... | collective-permute-start | bytes 122888 | tf_op jit(solution)/shard_map/ppermute | solution.py:569
  100.3 4.0 %collective-permute-start.28 = (bf16[80,256]{1,0:T(8,128)(2,1)S(1)}, bf16[80,256]{1,0:T(8,128)(2,1)S(1)}, u32[]{:S(2)}, u32[]{:S(2)}) collective-permute-start(bf16[80,256]{1,0:T(8,128)(2,1)S(1)} %get-tuple-element.134), channel_id=1, source_target_pairs={{0,16},{1,17},{2,18},{3,19},{4,20},{5,21},{6,22},{7,23},{8,24},{9,... | collective-permute-start | bytes 122888 | tf_op jit(solution)/shard_map/ppermute | solution.py:569
  104.3 6.0 %collective-permute-start.32 = (bf16[80,256]{1,0:T(8,128)(2,1)S(1)}, bf16[80,256]{1,0:T(8,128)(2,1)S(1)}, u32[]{:S(2)}, u32[]{:S(2)}) collective-permute-start(bf16[80,256]{1,0:T(8,128)(2,1)S(1)} %fusion.9), channel_id=1, source_target_pairs={{0,3},{1,2},{2,1},{3,0},{4,7},{5,6},{6,5},{7,4},{8,11},{9,10},{10,... | collective-permute-start | bytes 122888 | tf_op jit(solution)/shard_map/ppermute | solution.py:569
  106.4 4.9 %collective-permute-start.31 = (bf16[80,256]{1,0:T(8,128)(2,1)S(1)}, bf16[80,256]{1,0:T(8,128)(2,1)S(1)}, u32[]{:S(2)}, u32[]{:S(2)}) collective-permute-start(bf16[80,256]{1,0:T(8,128)(2,1)S(1)} %fusion.9), channel_id=1, source_target_pairs={{0,2},{1,3},{2,0},{3,1},{4,6},{5,7},{6,4},{7,5},{8,10},{9,11},{10,... | collective-permute-start | bytes 122888 | tf_op jit(solution)/shard_map/ppermute | solution.py:569
  106.4 4.9 %collective-permute-start.30 = (bf16[80,256]{1,0:T(8,128)(2,1)S(1)}, bf16[80,256]{1,0:T(8,128)(2,1)S(1)}, u32[]{:S(2)}, u32[]{:S(2)}) collective-permute-start(bf16[80,256]{1,0:T(8,128)(2,1)S(1)} %fusion.9), channel_id=1, source_target_pairs={{0,1},{1,0},{2,3},{3,2},{4,5},{5,4},{6,7},{7,6},{8,9},{9,8},{10,11... | collective-permute-start | bytes 122888 | tf_op jit(solution)/shard_map/ppermute | solution.py:569
  111.3 5.0 %collective-permute-start.38 = (bf16[80,256]{1,0:T(8,128)(2,1)S(1)}, bf16[80,256]{1,0:T(8,128)(2,1)S(1)}, u32[]{:S(2)}, u32[]{:S(2)}) collective-permute-start(bf16[80,256]{1,0:T(8,128)(2,1)S(1)} %add_convert_fusion.refs_0_), channel_id=1, source_target_pairs={{0,24},{1,25},{2,26},{3,27},{4,28},{5,29},{6,30},{7,31},{8,16},{9,... | collective-permute-start | bytes 122888 | tf_op jit(solution)/shard_map/ppermute | solution.py:569
  112.8 4.0 %collective-permute-start.36 = (bf16[80,256]{1,0:T(8,128)(2,1)S(1)}, bf16[80,256]{1,0:T(8,128)(2,1)S(1)}, u32[]{:S(2)}, u32[]{:S(2)}) collective-permute-start(bf16[80,256]{1,0:T(8,128)(2,1)S(1)} %add_convert_fusion.refs_0_), channel_id=1, source_target_pairs={{0,16},{1,17},{2,18},{3,19},{4,20},{5,21},{6,22},{7,23},{8,24},{9,... | collective-permute-start | bytes 122888 | tf_op jit(solution)/shard_map/ppermute | solution.py:569
  114.3 4.0 %collective-permute-start.34 = (bf16[80,256]{1,0:T(8,128)(2,1)S(1)}, bf16[80,256]{1,0:T(8,128)(2,1)S(1)}, u32[]{:S(2)}, u32[]{:S(2)}) collective-permute-start(bf16[80,256]{1,0:T(8,128)(2,1)S(1)} %add_convert_fusion.refs_0_), channel_id=1, source_target_pairs={{0,8},{1,9},{2,10},{3,11},{4,12},{5,13},{6,14},{7,15},{8,0},{9,1},... | collective-permute-start | bytes 122888 | tf_op jit(solution)/shard_map/ppermute | solution.py:569
  114.9 17.1 %collective-permute-start.33 = (bf16[80,256]{1,0:T(8,128)(2,1)S(1)}, bf16[80,256]{1,0:T(8,128)(2,1)S(1)}, u32[]{:S(2)}, u32[]{:S(2)}) collective-permute-start(bf16[80,256]{1,0:T(8,128)(2,1)S(1)} %add_convert_fusion.refs_0_), channel_id=1, source_target_pairs={{0,4},{1,5},{2,6},{3,7},{4,0},{5,1},{6,2},{7,3},{8,12},{9,13},{10,... | collective-permute-start | bytes 122888 | tf_op jit(solution)/shard_map/ppermute | solution.py:569
  116.3 15.7 %collective-permute-start.39 = (bf16[80,256]{1,0:T(8,128)(2,1)S(1)}, bf16[80,256]{1,0:T(8,128)(2,1)S(1)}, u32[]{:S(2)}, u32[]{:S(2)}) collective-permute-start(bf16[80,256]{1,0:T(8,128)(2,1)S(1)} %collective-permute-done.38.refs_6_), channel_id=1, source_target_pairs={{0,4},{1,5},{2,6},{3,7},{4,0},{5,1},{6,2},{7,3},{8,12},{9,13},{10,... | collective-permute-start | bytes 122888 | tf_op jit(solution)/shard_map/ppermute | solution.py:569
  116.8 15.2 %collective-permute-start.37 = (bf16[80,256]{1,0:T(8,128)(2,1)S(1)}, bf16[80,256]{1,0:T(8,128)(2,1)S(1)}, u32[]{:S(2)}, u32[]{:S(2)}) collective-permute-start(bf16[80,256]{1,0:T(8,128)(2,1)S(1)} %collective-permute-done.36.refs_4_), channel_id=1, source_target_pairs={{0,4},{1,5},{2,6},{3,7},{4,0},{5,1},{6,2},{7,3},{8,12},{9,13},{10,... | collective-permute-start | bytes 122888 | tf_op jit(solution)/shard_map/ppermute | solution.py:569
  118.3 13.7 %collective-permute-start.35 = (bf16[80,256]{1,0:T(8,128)(2,1)S(1)}, bf16[80,256]{1,0:T(8,128)(2,1)S(1)}, u32[]{:S(2)}, u32[]{:S(2)}) collective-permute-start(bf16[80,256]{1,0:T(8,128)(2,1)S(1)} %collective-permute-done.34.refs_2_), channel_id=1, source_target_pairs={{0,4},{1,5},{2,6},{3,7},{4,0},{5,1},{6,2},{7,3},{8,12},{9,13},{10,... | collective-permute-start | bytes 122888 | tf_op jit(solution)/shard_map/ppermute | solution.py:569
  131.4 19.8 %collective-permute-start.47 = (bf16[4,4,192,128]{3,2,1,0:T(8,128)(2,1)}, bf16[4,4,192,128]{3,2,1,0:T(8,128)(2,1)S(1)}, u32[]{:S(2)}, u32[]{:S(2)}) collective-permute-start(bf16[4,4,192,128]{3,2,1,0:T(8,128)(2,1)} %get-tuple-element.90), channel_id=1, source_target_pairs={{0,4},{1,5},{2,6},{3,7},{4,0},{5,1},{6,2},{7,3},{8,12},{9,13},{10,... | collective-permute-start | bytes 2359304 | tf_op jit(solution)/shard_map/ppermute | solution.py:569
  145.1 6.4 %collective-permute-start.40 = (bf16[4,4,128,128]{3,2,1,0:T(8,128)(2,1)}, bf16[4,4,128,128]{3,2,1,0:T(8,128)(2,1)S(1)}, u32[]{:S(2)}, u32[]{:S(2)}) collective-permute-start(bf16[4,4,128,128]{3,2,1,0:T(8,128)(2,1)} %get-tuple-element.88), channel_id=1, source_target_pairs={{0,4},{1,5},{2,6},{3,7},{4,0},{5,1},{6,2},{7,3},{8,12},{9,13},{10,... | collective-permute-start | bytes 1572872 | tf_op jit(solution)/shard_map/ppermute | solution.py:569
  152.7 6.4 %collective-permute-start.41 = (bf16[4,128,128]{2,1,0:T(8,128)(2,1)S(1)}, bf16[4,128,128]{2,1,0:T(8,128)(2,1)S(1)}, u32[]{:S(2)}, u32[]{:S(2)}) collective-permute-start(bf16[4,128,128]{2,1,0:T(8,128)(2,1)S(1)} %get-tuple-element.126), channel_id=1, source_target_pairs={{0,8},{1,9},{2,10},{3,11},{4,12},{5,13},{6,14},{7,15},{8,0},{9,1},... | collective-permute-start | bytes 393224 | tf_op jit(solution)/shard_map/ppermute | solution.py:569
  153.3 8.6 %collective-permute-start.43 = (bf16[4,128,128]{2,1,0:T(8,128)(2,1)S(1)}, bf16[4,128,128]{2,1,0:T(8,128)(2,1)S(1)}, u32[]{:S(2)}, u32[]{:S(2)}) collective-permute-start(bf16[4,128,128]{2,1,0:T(8,128)(2,1)S(1)} %get-tuple-element.127), channel_id=1, source_target_pairs={{0,24},{1,25},{2,26},{3,27},{4,28},{5,29},{6,30},{7,31},{8,16},{9,... | collective-permute-start | bytes 393224 | tf_op jit(solution)/shard_map/ppermute | solution.py:569
  154.7 9.0 %collective-permute-start.42 = (bf16[4,128,128]{2,1,0:T(8,128)(2,1)S(1)}, bf16[4,128,128]{2,1,0:T(8,128)(2,1)S(1)}, u32[]{:S(2)}, u32[]{:S(2)}) collective-permute-start(bf16[4,128,128]{2,1,0:T(8,128)(2,1)S(1)} %get-tuple-element.128), channel_id=1, source_target_pairs={{0,16},{1,17},{2,18},{3,19},{4,20},{5,21},{6,22},{7,23},{8,24},{9,... | collective-permute-start | bytes 393224 | tf_op jit(solution)/shard_map/ppermute | solution.py:569
  156.3 11.1 %collective-permute-start.48 = (bf16[4,192,128]{2,1,0:T(8,128)(2,1)S(1)}, bf16[4,192,128]{2,1,0:T(8,128)(2,1)S(1)}, u32[]{:S(2)}, u32[]{:S(2)}) collective-permute-start(bf16[4,192,128]{2,1,0:T(8,128)(2,1)S(1)} %get-tuple-element.123), channel_id=1, source_target_pairs={{0,8},{1,9},{2,10},{3,11},{4,12},{5,13},{6,14},{7,15},{8,0},{9,1},... | collective-permute-start | bytes 589832 | tf_op jit(solution)/shard_map/ppermute | solution.py:569
  156.9 13.0 %collective-permute-start.50 = (bf16[4,192,128]{2,1,0:T(8,128)(2,1)S(1)}, bf16[4,192,128]{2,1,0:T(8,128)(2,1)S(1)}, u32[]{:S(2)}, u32[]{:S(2)}) collective-permute-start(bf16[4,192,128]{2,1,0:T(8,128)(2,1)S(1)} %get-tuple-element.124), channel_id=1, source_target_pairs={{0,24},{1,25},{2,26},{3,27},{4,28},{5,29},{6,30},{7,31},{8,16},{9,... | collective-permute-start | bytes 589832 | tf_op jit(solution)/shard_map/ppermute | solution.py:569
  159.1 12.1 %collective-permute-start.49 = (bf16[4,192,128]{2,1,0:T(8,128)(2,1)S(1)}, bf16[4,192,128]{2,1,0:T(8,128)(2,1)S(1)}, u32[]{:S(2)}, u32[]{:S(2)}) collective-permute-start(bf16[4,192,128]{2,1,0:T(8,128)(2,1)S(1)} %get-tuple-element.125), channel_id=1, source_target_pairs={{0,16},{1,17},{2,18},{3,19},{4,20},{5,21},{6,22},{7,23},{8,24},{9,... | collective-permute-start | bytes 589832 | tf_op jit(solution)/shard_map/ppermute | solution.py:569
  163.8 11.0 %collective-permute-start.44 = (bf16[128,128]{1,0:T(8,128)(2,1)S(1)}, bf16[128,128]{1,0:T(8,128)(2,1)S(1)}, u32[]{:S(2)}, u32[]{:S(2)}) collective-permute-start(bf16[128,128]{1,0:T(8,128)(2,1)S(1)} %get-tuple-element.138), channel_id=1, source_target_pairs={{0,1},{1,0},{2,3},{3,2},{4,5},{5,4},{6,7},{7,6},{8,9},{9,8},{10,11... | collective-permute-start | bytes 98312 | tf_op jit(solution)/shard_map/ppermute | solution.py:569
  165.4 9.5 %collective-permute-start.46 = (bf16[128,128]{1,0:T(8,128)(2,1)S(1)}, bf16[128,128]{1,0:T(8,128)(2,1)S(1)}, u32[]{:S(2)}, u32[]{:S(2)}) collective-permute-start(bf16[128,128]{1,0:T(8,128)(2,1)S(1)} %get-tuple-element.139), channel_id=1, source_target_pairs={{0,3},{1,2},{2,1},{3,0},{4,7},{5,6},{6,5},{7,4},{8,11},{9,10},{10,... | collective-permute-start | bytes 98312 | tf_op jit(solution)/shard_map/ppermute | solution.py:569
  167.4 7.5 %collective-permute-start.45 = (bf16[128,128]{1,0:T(8,128)(2,1)S(1)}, bf16[128,128]{1,0:T(8,128)(2,1)S(1)}, u32[]{:S(2)}, u32[]{:S(2)}) collective-permute-start(bf16[128,128]{1,0:T(8,128)(2,1)S(1)} %get-tuple-element.140), channel_id=1, source_target_pairs={{0,2},{1,3},{2,0},{3,1},{4,6},{5,7},{6,4},{7,5},{8,10},{9,11},{10,... | collective-permute-start | bytes 98312 | tf_op jit(solution)/shard_map/ppermute | solution.py:569
  171.3 4.2 %collective-permute-start.51 = (bf16[192,128]{1,0:T(8,128)(2,1)S(1)}, bf16[192,128]{1,0:T(8,128)(2,1)S(1)}, u32[]{:S(2)}, u32[]{:S(2)}) collective-permute-start(bf16[192,128]{1,0:T(8,128)(2,1)S(1)} %get-tuple-element.129), channel_id=1, source_target_pairs={{0,1},{1,0},{2,3},{3,2},{4,5},{5,4},{6,7},{7,6},{8,9},{9,8},{10,11... | collective-permute-start | bytes 147464 | tf_op jit(solution)/shard_map/ppermute | solution.py:569
  172.9 5.9 %collective-permute-start.53 = (bf16[192,128]{1,0:T(8,128)(2,1)S(1)}, bf16[192,128]{1,0:T(8,128)(2,1)S(1)}, u32[]{:S(2)}, u32[]{:S(2)}) collective-permute-start(bf16[192,128]{1,0:T(8,128)(2,1)S(1)} %get-tuple-element.130), channel_id=1, source_target_pairs={{0,3},{1,2},{2,1},{3,0},{4,7},{5,6},{6,5},{7,4},{8,11},{9,10},{10,... | collective-permute-start | bytes 147464 | tf_op jit(solution)/shard_map/ppermute | solution.py:569
  174.9 5.0 %collective-permute-start.52 = (bf16[192,128]{1,0:T(8,128)(2,1)S(1)}, bf16[192,128]{1,0:T(8,128)(2,1)S(1)}, u32[]{:S(2)}, u32[]{:S(2)}) collective-permute-start(bf16[192,128]{1,0:T(8,128)(2,1)S(1)} %get-tuple-element.131), channel_id=1, source_target_pairs={{0,2},{1,3},{2,0},{3,1},{4,6},{5,7},{6,4},{7,5},{8,10},{9,11},{10,... | collective-permute-start | bytes 147464 | tf_op jit(solution)/shard_map/ppermute | solution.py:569
  179.9 13.6 %collective-permute-start.59 = (bf16[320,128]{1,0:T(8,128)(2,1)S(1)}, bf16[320,128]{1,0:T(8,128)(2,1)S(1)}, u32[]{:S(2)}, u32[]{:S(2)}) collective-permute-start(bf16[320,128]{1,0:T(8,128)(2,1)S(1)} %pad_maximum_fusion.1.refs_0_), channel_id=1, source_target_pairs={{0,24},{1,25},{2,26},{3,27},{4,28},{5,29},{6,30},{7,31},{8,16},{9,... | collective-permute-start | bytes 245768 | tf_op jit(solution)/shard_map/ppermute | solution.py:569
  181.5 12.5 %collective-permute-start.57 = (bf16[320,128]{1,0:T(8,128)(2,1)S(1)}, bf16[320,128]{1,0:T(8,128)(2,1)S(1)}, u32[]{:S(2)}, u32[]{:S(2)}) collective-permute-start(bf16[320,128]{1,0:T(8,128)(2,1)S(1)} %pad_maximum_fusion.1.refs_0_), channel_id=1, source_target_pairs={{0,16},{1,17},{2,18},{3,19},{4,20},{5,21},{6,22},{7,23},{8,24},{9,... | collective-permute-start | bytes 245768 | tf_op jit(solution)/shard_map/ppermute | solution.py:569
  182.4 11.7 %collective-permute-start.55 = (bf16[320,128]{1,0:T(8,128)(2,1)S(1)}, bf16[320,128]{1,0:T(8,128)(2,1)S(1)}, u32[]{:S(2)}, u32[]{:S(2)}) collective-permute-start(bf16[320,128]{1,0:T(8,128)(2,1)S(1)} %pad_maximum_fusion.1.refs_0_), channel_id=1, source_target_pairs={{0,8},{1,9},{2,10},{3,11},{4,12},{5,13},{6,14},{7,15},{8,0},{9,1},... | collective-permute-start | bytes 245768 | tf_op jit(solution)/shard_map/ppermute | solution.py:569
  193.5 2.4 %collective-permute-start.54 = (bf16[320,128]{1,0:T(8,128)(2,1)S(1)}, bf16[320,128]{1,0:T(8,128)(2,1)S(1)}, u32[]{:S(2)}, u32[]{:S(2)}) collective-permute-start(bf16[320,128]{1,0:T(8,128)(2,1)S(1)} %pad_maximum_fusion.1.refs_0_), channel_id=1, source_target_pairs={{0,4},{1,5},{2,6},{3,7},{4,0},{5,1},{6,2},{7,3},{8,12},{9,13},{10,... | collective-permute-start | bytes 245768 | tf_op jit(solution)/shard_map/ppermute | solution.py:569
  193.5 2.3 %collective-permute-start.60 = (bf16[320,128]{1,0:T(8,128)(2,1)S(1)}, bf16[320,128]{1,0:T(8,128)(2,1)S(1)}, u32[]{:S(2)}, u32[]{:S(2)}) collective-permute-start(bf16[320,128]{1,0:T(8,128)(2,1)S(1)} %collective-permute-done.59.refs_6_), channel_id=1, source_target_pairs={{0,4},{1,5},{2,6},{3,7},{4,0},{5,1},{6,2},{7,3},{8,12},{9,13},{10,... | collective-permute-start | bytes 245768 | tf_op jit(solution)/shard_map/ppermute | solution.py:569
  194.0 1.9 collective-permute-start.58
  194.1 1.8 collective-permute-start.56
  202.0 4.6 %collective-permute-start.62 = (f32[8,128]{1,0:T(8,128)S(1)}, f32[8,128]{1,0:T(8,128)S(1)}, u32[]{:S(2)}, u32[]{:S(2)}) collective-permute-start(f32[8,128]{1,0:T(8,128)S(1)} %broadcast_in_dim.3), channel_id=1, source_target_pairs={{0,2},{1,3},{2,0},{3,1},{4,6},{5,7},{6,4},{7,5},{8,10},{9,11},{10,... | collective-permute-start | bytes 12296 | tf_op jit(solution)/shard_map/ppermute | solution.py:569
  202.6 5.4 %collective-permute-start.63 = (f32[8,128]{1,0:T(8,128)S(1)}, f32[8,128]{1,0:T(8,128)S(1)}, u32[]{:S(2)}, u32[]{:S(2)}) collective-permute-start(f32[8,128]{1,0:T(8,128)S(1)} %broadcast_in_dim.3), channel_id=1, source_target_pairs={{0,3},{1,2},{2,1},{3,0},{4,7},{5,6},{6,5},{7,4},{8,11},{9,10},{10,... | collective-permute-start | bytes 12296 | tf_op jit(solution)/shard_map/ppermute | solution.py:569
  204.4 3.6 %collective-permute-start.61 = (f32[8,128]{1,0:T(8,128)S(1)}, f32[8,128]{1,0:T(8,128)S(1)}, u32[]{:S(2)}, u32[]{:S(2)}) collective-permute-start(f32[8,128]{1,0:T(8,128)S(1)} %broadcast_in_dim.3), channel_id=1, source_target_pairs={{0,1},{1,0},{2,3},{3,2},{4,5},{5,4},{6,7},{7,6},{8,9},{9,8},{10,11... | collective-permute-start | bytes 12296 | tf_op jit(solution)/shard_map/ppermute | solution.py:569
  (39 other events, 201.2 us)

commit v2 on v1

v2 whole, which is shorter than its diff:
```python
import functools
import math

import jax
import jax.numpy as jnp
from jax import lax
from jax.experimental import pallas as pl
from jax.experimental.pallas import tpu as pltpu
from jax.sharding import PartitionSpec as P

HEADS = 8
CLUSTERS = 4
STEP = 10
AXES = ("nodes", "shard")

norm_eps = 1e-05
beta_one = 0.9
beta_two = 0.999
learn_rate = 0.05
norm_rate = 0.5
decay_rate = 0.01
adam_eps = 1e-08
bf_type = jnp.bfloat16
fl_type = jnp.float32

GROUPS = 2
CHUNKS = GROUPS * CLUSTERS
PAD = 16


def dot_nn(a, b):
    return lax.dot_general(a, b, (((1,), (0,)), ((), ())), preferred_element_type=fl_type)


def dot_nt(a, b):
    return lax.dot_general(a, b, (((1,), (1,)), ((), ())), preferred_element_type=fl_type)


def dot_tn(a, b):
    return lax.dot_general(a, b, (((0,), (0,)), ((), ())), preferred_element_type=fl_type)


def whole(shape):
    return pl.BlockSpec(shape, lambda *_: (0,) * len(shape))


def smem():
    return pl.BlockSpec(memory_space=pltpu.SMEM)


def view(ref, kind, start, size):
    if kind == "lane":
        return ref.at[:, pl.ds(start, size)]
    if kind == "row":
        return ref.at[pl.ds(start, size), :]
    return ref


def call(kernel, steps, ins, in_kinds, outs, out_kinds, scratch, flops, name, block=0, vmem=16, piped=False):
    moved = sum(math.prod(a.shape) * a.dtype.itemsize for a in (*ins, *outs))
    arrays, kinds = [*ins, *outs], [*in_kinds, *out_kinds]

    def spec(array, kind):
        if kind == "smem":
            return smem()
        if isinstance(kind, pl.BlockSpec):
            return kind
        if piped and kind == "lane":
            return pl.BlockSpec((array.shape[0], block), lambda i: (0, i))
        if piped and kind == "row":
            return pl.BlockSpec((block, array.shape[1]), lambda i: (i, 0))
        return whole(array.shape)

    def body(*refs):
        if piped:
            kernel(pl.program_id(0), *refs)
            return
        if steps == 1:
            kernel(0, *refs)
            return

        def one(i, carry):
            start = pl.multiple_of(i * block, block)
            views = [view(r, k, start, block) for r, k in zip(refs, kinds)]
            kernel(i, *views, *refs[len(kinds) :])
            return carry

        lax.fori_loop(0, steps, one, 0)

    specs = [spec(a, k) for a, k in zip(arrays, kinds)]
    return pl.pallas_call(
        body,
        grid=(steps,) if piped else (),
        in_specs=specs[: len(ins)],
        out_specs=specs[len(ins) :],
        out_shape=outs,
        scratch_shapes=scratch,
        cost_estimate=pl.CostEstimate(flops=int(flops), transcendentals=0, bytes_accessed=int(moved)),
        compiler_params=pltpu.CompilerParams(vmem_limit_bytes=vmem * 1024 * 1024),
        name=name,
    )(*ins)


def out(shape, dtype):
    return jax.ShapeDtypeStruct(shape, dtype)


def prep_kernel(step, wp, wo, wn, message, other, query_all, stage):
    core = lax.bitwise_and(lax.axis_index("nodes"), 1)
    part = lax.bitwise_and(lax.axis_index("nodes"), 7)
    shard, width = wo.shape
    stage[0:width] = wp[:, width : 2 * width].T.astype(bf_type)
    stage[width : 2 * width] = wp[:, 2 * width : 3 * width].T.astype(bf_type)
    query_all[0:width] = wp[:, 0:width].T.astype(bf_type)
    query_all[width : 2 * width] = wp[:, 3 * width : 4 * width].T.astype(bf_type)
    query_all[2 * width : 3 * width] = wo[...].T.astype(bf_type)
    rest = query_all.shape[0] - 3 * width
    rows = jnp.concatenate([wn[...], jnp.zeros((rest - 2, shard), fl_type)], axis=0)
    query_all[3 * width :] = rows.astype(bf_type)
    message[0:width] = stage[pl.ds(pl.multiple_of(core * width, 16), width)]
    other[...] = stage[pl.ds(pl.multiple_of((1 - core) * width, 16), width)]
    height = query_all.shape[0] // 8
    message[width:] = query_all[pl.ds(pl.multiple_of(part * height, 16), height)]


def members(ids_ref):
    rows = ids_ref.shape[1]
    classes = lax.broadcasted_iota(jnp.int32, (PAD, rows), 0)
    return (classes == ids_ref[...]).astype(fl_type).astype(bf_type)


def valid_row(count, start, rows):
    slots = lax.broadcasted_iota(jnp.int32, (1, rows), 1) + start
    return slots < count


def put_chunks(acc, keep, send, node, extra):
    width = acc.shape[2]
    head = width // 4
    for g in range(GROUPS):
        for c in range(CLUSTERS):
            chunk = g * CLUSTERS + c
            distance = lax.bitwise_xor(node, chunk)
            slot = lax.shift_right_logical(distance, 1)
            lane_head = lax.broadcasted_iota(jnp.int32, (head, width), 1) // head
            body = jnp.zeros((head, width), fl_type)
            for h in range(4):
                rows = acc[g, c * width + h * head : c * width + (h + 1) * head, :]
                body = jnp.where(lane_head == h, rows, body)
            block = jnp.concatenate([body, extra(g, c)], axis=0)

            @pl.when(lax.bitwise_and(distance, 1) == 0)
            def _():
                keep[slot] = block

            @pl.when(lax.bitwise_and(distance, 1) == 1)
            def _():
                send[slot] = block.astype(bf_type)


def key_kernel(pieces, steps, step, place, x, ids, *refs):
    mine, other = refs[:pieces], refs[pieces : 2 * pieces]
    sig_key, value_out, keep, send, weights, masked, keys, acc = refs[2 * pieces :]
    core, node, count = place[0], place[1], place[3]
    width = x.shape[1]
    rows = x.shape[0]
    half = width // GROUPS

    @pl.when(step == 0)
    def _():
        span = mine[0].shape[1]
        for d in range(pieces):
            cols = slice(d * span, (d + 1) * span)
            weights[pl.ds(pl.multiple_of(core * width, 16), width), cols] = mine[d][0:width]
            weights[pl.ds(pl.multiple_of((1 - core) * width, 16), width), cols] = other[d][0:width]
        acc[...] = jnp.zeros_like(acc)

    table = members(ids)
    valid = valid_row(count, step * rows, rows)
    for g in range(GROUPS):
        sig = jax.nn.sigmoid(dot_nt(weights[g * half : (g + 1) * half, :], x[...]))
        sig_key[g * half : (g + 1) * half, :] = sig
        keys[...] = jnp.where(valid, sig, 0.0).astype(bf_type)
        value = dot_nt(weights[width + g * half : width + (g + 1) * half, :], x[...]).astype(bf_type)
        value_out[g * half : (g + 1) * half, :] = value
        for c in range(CLUSTERS):
            masked[c * half : (c + 1) * half, :] = value * table[c : c + 1, :]
        masked[CLUSTERS * half :, :] = table
        acc[g] += dot_nt(masked[...], keys[...])

    @pl.when(step == steps - 1)
    def _():
        def extra(g, c):
            row = acc[g, CLUSTERS * half + c : CLUSTERS * half + c + 1, :]
            return jnp.concatenate([row, jnp.zeros((PAD - 1, half), fl_type)], axis=0)

        put_chunks(acc, keep, send, node, extra)


def weights_kernel(pieces, step, place, own, *refs):
    near, far = refs[: 2 * (pieces - 1)], refs[2 * (pieces - 1) : 2 * (pieces - 1) + 6]
    query_weight, gate_weight, out_weight, gain, shift, full_query, full_gate, stage = refs[2 * (pieces - 1) + 6 :]
    node, shard = place[1], place[2]
    width = out_weight.shape[0]
    span = own.shape[1]
    height = own.shape[0] // 8

    def put(d, position, block):
        where = pl.multiple_of(lax.bitwise_xor(node, position) * height, 16)
        stage[d, pl.ds(where, height), :] = block

    stage[0] = own[...]
    for d in range(1, pieces):
        for core in range(2):
            put(d, core, near[core * (pieces - 1) + d - 1][width:])
            for e in range(3):
                put(d, 2 * (e + 1) + core, far[core * 3 + e][d - 1])
    norm_rows = []
    for z in range(pieces):
        where = lax.bitwise_xor(shard, z)
        cols = slice(z * span, (z + 1) * span)
        query_weight[:, cols] = stage[z, 0:width, :]
        gate_weight[:, cols] = stage[z, width : 2 * width, :]
        full_query[:, cols] = stage[where, 0:width, :]
        full_gate[:, cols] = stage[where, width : 2 * width, :]
        out_weight[cols, :] = stage[where, 2 * width : 3 * width, :].T
        norm_rows.append(stage[where, 3 * width : 3 * width + 16, :])
    turned = jnp.concatenate(norm_rows, axis=1).astype(fl_type).T
    gain[...] = jnp.broadcast_to(turned[:, 0:1], gain.shape)
    shift[...] = jnp.broadcast_to(turned[:, 1:2], shift.shape)


def key_weights_kernel(pieces, step, place, *refs):
    mine, other = refs[:pieces], refs[pieces : 2 * pieces]
    full, stage = refs[2 * pieces :]
    core = place[0]
    width, span = full.shape[1], mine[0].shape[1]
    for d in range(pieces):
        stage[d, pl.ds(pl.multiple_of(core * width, 16), width), :] = mine[d][0:width]
        stage[d, pl.ds(pl.multiple_of((1 - core) * width, 16), width), :] = other[d][0:width]
    for z in range(pieces):
        full[:, z * span : (z + 1) * span] = stage[lax.bitwise_xor(place[2], z)]


def query_kernel(step, place, x, weight, sig_query, query):
    sig = jax.nn.sigmoid(dot_nt(weight[...], x[...]))
    sig_query[...] = sig
    query[...] = sig.astype(bf_type)


def gate_kernel(step, place, x, weight, gate):
    gate[...] = dot_nt(weight[...], x[...])


def grad_prod_kernel(step, place, g, out_weight, grad_prod):
    rows = g.shape[0]
    valid = valid_row(place[3], step * rows, rows)
    grad_prod[...] = jnp.where(valid, dot_nt(out_weight[...], g[...]), 0.0)


def place_chunks(chunk_refs, place, stage):
    node = place[1]
    for d in range(CHUNKS):
        stage[lax.bitwise_xor(node, d)] = chunk_refs[d][...]


def head_rows(width, h, value):
    lane_head = lax.broadcasted_iota(jnp.int32, (1, width), 1) // (width // 4)
    return jnp.where(lane_head == h, value, jnp.zeros_like(value))


def middle_kernel(steps, lanes, step, place, ids, query, gate, grad_prod, gain, shift, *refs):
    chunk_refs = refs[:CHUNKS]
    prod_out, dgate_out, dnum_out, dden_out, keep, send = refs[CHUNKS : CHUNKS + 6]
    rest = refs[CHUNKS + 6 :]
    width, rows = query.shape
    parts = rows // lanes
    stage, left, acc, dgain, dshift = rest[:5]
    stacks, back_stacks, nums, normeds, dnormeds, dens, ddens = (
        rest[5 + i * parts : 5 + (i + 1) * parts] for i in range(7)
    )
    node, count = place[1], place[3]
    half = width // GROUPS
    head = half // 4

    @pl.when(step == 0)
    def _():
        place_chunks(chunk_refs, place, stage)
        for g in range(GROUPS):
            for c in range(CLUSTERS):
                chunk = stage[g * CLUSTERS + c].astype(fl_type)
                cols = slice(c * half, (c + 1) * half)
                for h in range(4):
                    left[g, h * head : (h + 1) * head, cols] = head_rows(half, h, chunk[:head]).astype(bf_type)
                sums = [head_rows(half, h, chunk[head : head + 1]) for h in range(4)]
                sums.append(jnp.zeros((PAD - 4, half), fl_type))
                left[g, half : half + PAD, cols] = jnp.concatenate(sums, axis=0).astype(bf_type)
        acc[...] = jnp.zeros_like(acc)
        dgain[...] = jnp.zeros_like(dgain)
        dshift[...] = jnp.zeros_like(dshift)

    def forward(part):
        cols = slice(part * lanes, (part + 1) * lanes)
        table = members(ids.at[:, cols])
        stack, num, den = stacks[part], nums[part], dens[part]
        for g in range(GROUPS):
            mine = query[g * half : (g + 1) * half, cols]
            for c in range(CLUSTERS):
                stack[g, c * half : (c + 1) * half, :] = mine * table[c : c + 1, :]
            both = dot_nn(left[g], stack[g])
            num[g * half : (g + 1) * half, :] = both[:half]
            den[g * 8 : g * 8 + 8, :] = 1.0 / both[half : half + 8]

    def norm(part):
        cols = slice(part * lanes, (part + 1) * lanes)
        num, normed, dnormed, den, dden = nums[part], normeds[part], dnormeds[part], dens[part], ddens[part]
        valid = valid_row(count, step * rows + part * lanes, lanes)
        total = jnp.zeros((8, lanes), fl_type)
        for h in range(HEADS):
            span = slice(h * head, (h + 1) * head)
            row = (h // 4) * 8 + h % 4
            att = num[span, :] * den[row : row + 1, :]
            num[span, :] = att
            total = total + fold_rows(att)
        mean = jnp.sum(total, axis=0, keepdims=True) * (1.0 / width)
        total = jnp.zeros((8, lanes), fl_type)
        for h in range(HEADS):
            centered = num[h * head : (h + 1) * head, :] - mean
            total = total + fold_rows(centered * centered)
        scale = lax.rsqrt(jnp.sum(total, axis=0, keepdims=True) * (1.0 / width) + norm_eps)
        first = jnp.zeros((8, lanes), fl_type)
        second = jnp.zeros((8, lanes), fl_type)
        for h in range(HEADS):
            span = slice(h * head, (h + 1) * head)
            ah = (num[span, :] - mean) * scale
            gamma = jnp.concatenate([gain[span, :]] * (lanes // 128), axis=1)
            beta = jnp.concatenate([shift[span, :]] * (lanes // 128), axis=1)
            u = ah * gamma + beta
            zg = gate[span, cols]
            dp = grad_prod[span, cols]
            prod_out[span, cols] = jnp.where(valid, u * zg, 0.0).astype(bf_type)
            du = dp * zg
            dgate_out[span, cols] = (dp * u).astype(bf_type)
            du_ah = du * ah
            dgain[span, :] += fold_lanes(du_ah)
            dshift[span, :] += fold_lanes(du)
            dah = gamma * du
            first = first + fold_rows(dah)
            second = second + fold_rows(dah * ah)
            normed[span, :] = ah
            dnormed[span, :] = dah
        first = jnp.sum(first, axis=0, keepdims=True) * (1.0 / width)
        second = jnp.sum(second, axis=0, keepdims=True) * (1.0 / width)
        for h in range(HEADS):
            span = slice(h * head, (h + 1) * head)
            row = (h // 4) * 8 + h % 4
            da = scale * (dnormed[span, :] - first - normed[span, :] * second)
            inverse = den[row : row + 1, :]
            dnum_out[span, cols] = (da * inverse).astype(bf_type)
            dden[row : row + 1, :] = -jnp.sum(da * num[span, :], axis=0, keepdims=True) * inverse
        dden_out[:, cols] = dden[...]

    def backward(part):
        cols = slice(part * lanes, (part + 1) * lanes)
        table = members(ids.at[:, cols])
        stack, dden = back_stacks[part], ddens[part]
        for g in range(GROUPS):
            mine = dnum_out[g * half : (g + 1) * half, cols]
            for c in range(CLUSTERS):
                stack[g, c * half : (c + 1) * half, :] = mine * table[c : c + 1, :]
            den_rows = dden[g * 8 : g * 8 + 4, :]
            high = den_rows.astype(bf_type)
            low = (den_rows - high.astype(fl_type)).astype(bf_type)
            four_high = jnp.concatenate([high * table[c : c + 1, :] for c in range(CLUSTERS)], axis=0)
            four_low = jnp.concatenate([low * table[c : c + 1, :] for c in range(CLUSTERS)], axis=0)
            stack[g, CLUSTERS * half :, :] = jnp.concatenate([four_high, four_low], axis=0)
            acc[g] += dot_nt(stack[g], query[g * half : (g + 1) * half, cols])

    for part in range(parts):
        forward(part)
    for part in range(parts):
        norm(part)
        backward(part)

    @pl.when(step == steps - 1)
    def _():
        gain_row = jnp.sum(dgain[...].T, axis=0, keepdims=True)
        shift_row = jnp.sum(dshift[...].T, axis=0, keepdims=True)

        def extra(g, c):
            base = CLUSTERS * half
            row = jnp.zeros((1, half), fl_type)
            for h in range(4):
                at = base + c * 4 + h
                row = row + head_rows(half, h, acc[g, at : at + 1, :] + acc[g, at + 16 : at + 17, :])
            cols = slice(g * half, (g + 1) * half)
            tail = [row]
            if c == 0:
                tail += [gain_row[:, cols], shift_row[:, cols]]
            tail.append(jnp.zeros((PAD - len(tail), half), fl_type))
            return jnp.concatenate(tail, axis=0)

        put_chunks(acc, keep, send, node, extra)


def fold_rows(block):
    return tree_sum([block[i * 8 : (i + 1) * 8] for i in range(block.shape[0] // 8)])


def fold_lanes(block):
    return tree_sum([block[:, i * 128 : (i + 1) * 128] for i in range(block.shape[1] // 128)])


def write_pieces(pieces, node, shard, span, keep, send, blocks):
    for chunk in range(8):
        distance = lax.bitwise_xor(node, chunk)
        slot = lax.shift_right_logical(distance, 1)
        even = lax.bitwise_and(distance, 1) == 0
        for z in range(pieces):
            block = blocks(z, chunk)

            @pl.when(even)
            def _():
                keep[slot, z] = block

            @pl.when(jnp.logical_not(even))
            def _():
                send[slot, z] = block.astype(bf_type)


def query_back_kernel(pieces, step, place, ids, dnum, dden, sig_query, x, *refs):
    chunk_refs = refs[:CHUNKS]
    dquery_out, grad_out = refs[CHUNKS : CHUNKS + 2]
    stage, left, sums, stack = refs[CHUNKS + 2 :]
    width, rows = dnum.shape
    half = width // GROUPS
    head = half // 4

    @pl.when(step == 0)
    def _():
        place_chunks(chunk_refs, place, stage)
        for gr in range(GROUPS):
            for c in range(CLUSTERS):
                chunk = stage[gr * CLUSTERS + c].astype(fl_type)
                block = jnp.concatenate([head_rows(half, h, chunk[:head]) for h in range(4)], axis=0)
                left[gr, :, c * half : (c + 1) * half] = block.T.astype(bf_type)
                column = chunk[head : head + 8].T
                sums[c, gr * half : (gr + 1) * half, :] = jnp.broadcast_to(column[:, 0:1], (half, 128))
        grad_out[...] = jnp.zeros_like(grad_out)

    table = members(ids)
    for gr in range(GROUPS):
        part = dnum[gr * half : (gr + 1) * half, :]
        for c in range(CLUSTERS):
            stack[c * half : (c + 1) * half, :] = part * table[c : c + 1, :]
        dq = dot_nn(left[gr], stack[...])
        for h in range(4):
            at = slice(gr * half + h * head, gr * half + (h + 1) * head)
            pick = pick_rows(sums, at, ids, rows)
            row = gr * 8 + h
            full = dq[h * head : (h + 1) * head] + dden[row : row + 1, :] * pick
            sig = sig_query[at, :]
            dquery_out[at, :] = (full * (sig * (1.0 - sig))).astype(bf_type)
    grad_out[...] += dot_nn(dquery_out[...], x[...])


def gate_back_kernel(step, place, dgate, prod, x, g, grad_gate, grad_out):
    @pl.when(step == 0)
    def _():
        grad_gate[...] = jnp.zeros_like(grad_gate)
        grad_out[...] = jnp.zeros_like(grad_out)

    grad_gate[...] += dot_nn(dgate[...], x[...])
    grad_out[...] += dot_nn(prod[...], g[...])


def fold(block, span):
    return jnp.concatenate(
        [block[:, i * span : (i + 1) * span] for i in range(block.shape[1] // span)], axis=0
    )


def pick_rows(sums, at, ids, rows):
    reps = rows // 128
    wide = [jnp.concatenate([sums[c, at, :]] * reps, axis=1) for c in range(CLUSTERS)]
    pick = wide[CLUSTERS - 1]
    for c in range(CLUSTERS - 1):
        pick = jnp.where(ids[...] == c, wide[c], pick)
    return pick


def output_kernel(step, place, x, prod, out_weight, result):
    result[...] = x[...].astype(fl_type) + dot_tn(prod[...], out_weight[...])


def key_back_kernel(pieces, steps, step, place, ids, sig_key, value, x, grad_query, grad_gate, grad_out, *refs):
    chunk_refs = refs[:CHUNKS]
    dkey_out, dvalue_out, norm_out, keep, send = refs[CHUNKS : CHUNKS + 5]
    stage, left_key, left_value, sums, stack, acc = refs[CHUNKS + 5 :]
    node, shard, count = place[1], place[2], place[3]
    width, rows = value.shape
    half = width // GROUPS
    head = half // 4
    span = width // pieces

    @pl.when(step == 0)
    def _():
        place_chunks(chunk_refs, place, stage)
        for gr in range(GROUPS):
            for c in range(CLUSTERS):
                chunk = stage[gr * CLUSTERS + c].astype(fl_type)
                block = jnp.concatenate([head_rows(half, h, chunk[:head]) for h in range(4)], axis=0)
                left_value[gr, :, c * half : (c + 1) * half] = block.astype(bf_type)
                left_key[gr, :, c * half : (c + 1) * half] = block.T.astype(bf_type)
                column = chunk[head : head + 8].T
                sums[c, gr * half : (gr + 1) * half, :] = jnp.broadcast_to(column[:, 0:1], (half, 128))
                if c == 0:
                    norm_out[:, gr * half : (gr + 1) * half] = chunk[head : head + 8]
        acc[...] = jnp.zeros_like(acc)

    table = members(ids)
    valid = valid_row(count, step * rows, rows)
    for gr in range(GROUPS):
        at = slice(gr * half, (gr + 1) * half)
        part = value[at, :]
        for c in range(CLUSTERS):
            stack[c * half : (c + 1) * half, :] = part * table[c : c + 1, :]
        dk = dot_nn(left_key[gr], stack[...])
        for h in range(4):
            sub = slice(gr * half + h * head, gr * half + (h + 1) * head)
            full = dk[h * head : (h + 1) * head] + pick_rows(sums, sub, ids, rows)
            sig = sig_key[sub, :]
            dkey_out[sub, :] = jnp.where(valid, full * (sig * (1.0 - sig)), 0.0).astype(bf_type)
        key = jnp.where(valid, sig_key[at, :], 0.0).astype(bf_type)
        for c in range(CLUSTERS):
            stack[c * half : (c + 1) * half, :] = key * table[c : c + 1, :]
        dvalue_out[at, :] = dot_nn(left_value[gr], stack[...]).astype(bf_type)
    acc[0:width] += dot_nn(dkey_out[...], x[...])
    acc[width : 2 * width] += dot_nn(dvalue_out[...], x[...])

    @pl.when(step == steps - 1)
    def _():
        tall = 2 * width // 8
        lanes = width // 4
        short = span // 2

        def blocks(z, chunk):
            cols = slice(z * span, (z + 1) * span)
            top = acc[chunk * tall : (chunk + 1) * tall, cols]
            source = grad_query if chunk < 4 else grad_gate
            center = source[(chunk % 4) * tall : (chunk % 4 + 1) * tall, cols]
            start = pl.multiple_of(lax.bitwise_xor(shard, z) * span + (chunk % 2) * short, 8)
            bottom = grad_out[pl.ds(start, short), (chunk // 2) * lanes : (chunk // 2 + 1) * lanes]
            return jnp.concatenate([top, center, fold(bottom, span)], axis=0)

        write_pieces(pieces, node, shard, span, keep, send, blocks)


def input_kernel(step, place, dquery, dkey, dvalue, dgate, full_query, full_key, full_gate, g, result):
    width = g.shape[1]
    total = g[...].astype(fl_type)
    total = total + dot_tn(dquery[...], full_query[...])
    total = total + dot_tn(dkey[...], full_key[0:width, :])
    total = total + dot_tn(dvalue[...], full_key[width:, :])
    total = total + dot_tn(dgate[...], full_gate[...])
    result[...] = total


def finish_kernel(step, *refs):
    parts, (sums, squares) = refs[:-2], refs[-2:]
    value = tree_sum([p[...].astype(fl_type) for p in parts]).astype(bf_type)
    sums[...] = value
    value = value.astype(fl_type)
    total = jnp.sum(value * value, axis=0, keepdims=True)
    squares[...] = jnp.broadcast_to(jnp.sum(total, axis=1, keepdims=True), squares.shape)


def with_squares_kernel(count, step, *refs):
    sums, squares, result = refs[0], refs[1 : 1 + count], refs[1 + count]
    span = sums.shape[1]
    result[0 : sums.shape[0]] = sums[...]
    value = tree_sum([q[...] for q in squares])[:, :span]
    high = value.astype(bf_type).astype(fl_type)
    rest = value - high
    middle = rest.astype(bf_type).astype(fl_type)
    low = rest - middle
    row = lax.broadcasted_iota(jnp.int32, value.shape, 0)
    terms = jnp.where(row == 0, high, jnp.where(row == 1, middle, jnp.where(row == 2, low, 0.0)))
    result[sums.shape[0] :] = jnp.concatenate([terms, jnp.zeros_like(terms)], axis=0).astype(bf_type)


def adam(master_w, moment_old, square_old, clipped, decay_coef, step_rate):
    moment_new = beta_one * moment_old + (1.0 - beta_one) * clipped
    square_new = beta_two * square_old + (1.0 - beta_two) * clipped * clipped
    moment_hat = moment_new * (1.0 / (1.0 - beta_one**STEP))
    square_hat = square_new * (1.0 / (1.0 - beta_two**STEP))
    master_new = master_w * (1.0 - step_rate * decay_coef) - step_rate * moment_hat / (
        jnp.sqrt(square_hat) + adam_eps
    )
    return moment_new, square_new, master_new


def update_kernel(pieces, step, place, *refs):
    parts, gn, pw, pm, ps, ow, om, osq, nw, nm, ns = refs[:CHUNKS], *refs[CHUNKS : CHUNKS + 10]
    size, p_m, p_s, p_w, p_c, o_m, o_s, o_w, o_c, n_g, n_m, n_s, n_w = refs[CHUNKS + 10 : CHUNKS + 23]
    stage, grad_out, factor = refs[CHUNKS + 23 :]
    node, shard = place[1], place[2]
    span, width = ow.shape
    tall = 2 * width // 8

    @pl.when(step == 0)
    def _():
        terms = []
        lanes = width // 4
        rows = span // 2
        for d in range(CHUNKS):
            chunk = lax.bitwise_xor(node, d)
            part = parts[d]
            stage[4 + chunk] = part[0:tall]
            stage[jnp.where(chunk < 4, chunk, chunk + 8)] = part[tall : 2 * tall]
            bottom = part[2 * tall : 2 * tall + rows * (lanes // span)].astype(fl_type)
            tail = part[2 * tall + rows * (lanes // span) :].astype(fl_type)
            terms.append((tail[2:3] + tail[1:2]) + tail[0:1])
            row_start = pl.multiple_of(lax.bitwise_and(chunk, 1) * rows, 8)
            quarter = lax.shift_right_logical(chunk, 1)
            for q in range(4):

                @pl.when(quarter == q)
                def _():
                    for i in range(lanes // span):
                        at = slice(q * lanes + i * span, q * lanes + (i + 1) * span)
                        grad_out[pl.ds(row_start, rows), at] = bottom[i * rows : (i + 1) * rows]

        norm_grad = gn[1:3, :]
        norm_square = jnp.sum(norm_grad * norm_grad, axis=0, keepdims=True)
        total = tree_sum(terms)[:, 0:1] + jnp.sum(norm_square, axis=1, keepdims=True)
        norm = jnp.sqrt(total)
        size[...] = norm
        clip_level = 0.5 * math.sqrt(5 * width * width + 2 * width)
        scale = jnp.minimum(1.0, clip_level / norm)
        factor[...] = jnp.broadcast_to(scale, factor.shape)
        o_m[...], o_s[...], new = adam(ow[...], om[...], osq[...], grad_out[...] * scale, decay_rate, learn_rate)
        o_w[...] = new
        o_c[...] = new.astype(bf_type)
        mine = norm_grad[:, 0:span]
        for z in range(1, pieces):
            mine = jnp.where(shard == z, norm_grad[:, z * span : (z + 1) * span], mine)
        clipped = mine * scale
        n_g[...] = clipped
        n_m[...], n_s[...], n_w[...] = adam(nw[...], nm[...], ns[...], clipped, 0.0, norm_rate)

    scale = factor[0:1, 0:1]
    for i in range(4):
        cols = slice(i * tall, (i + 1) * tall)
        grad = stage[step * 4 + i].astype(fl_type).T * scale
        p_m[:, cols], p_s[:, cols], new = adam(pw[:, cols], pm[:, cols], ps[:, cols], grad, decay_rate, learn_rate)
        p_w[:, cols] = new
        p_c[:, cols] = new.astype(bf_type)


def make_exchange(nodes, shards):
    count = nodes * shards

    def exchange(value, node_bits, shard_bits):
        pairs = [
            (i, ((i // shards) ^ node_bits) * shards + ((i % shards) ^ shard_bits)) for i in range(count)
        ]
        return lax.ppermute(value, AXES, pairs)

    return exchange


def tree_sum(parts):
    parts = list(parts)
    while len(parts) > 1:
        parts = [parts[i] + parts[i + 1] for i in range(0, len(parts), 2)]
    return parts[0]


def to_float(parts):
    return [p.astype(fl_type) for p in parts]


def tie(value, *others):
    return lax.optimization_barrier((value, *others))[0]


def tie(value, *others):
    return lax.optimization_barrier((value, *others))[0]


def local(nodes, shards, *args):
    (x, g, ids, counts, pw, pm, ps, ow, om, osq, nw, nm, ns) = args
    exchange = make_exchange(nodes, shards)
    outer = nodes // 8
    rows, width = x.shape
    half = width // GROUPS
    head = width // HEADS
    span = pw.shape[0]
    block = min(512, rows)
    steps = rows // block
    lanes = 256
    tall = 2 * width // 8
    part_rows = (3 * width + 2 + 127) // 128 * 16
    work = 2 * rows * width * width

    node = lax.axis_index("nodes").astype(jnp.int32)
    shard = lax.axis_index("shard").astype(jnp.int32)
    place = jnp.stack([lax.bitwise_and(node, 1), lax.bitwise_and(node, 7), shard, counts[0]])
    ids = ids.reshape(1, rows)
    chunk_shape = (4, head + PAD, half)

    def wide(dtype):
        return out((width, rows), dtype)

    def vmem(shape, dtype):
        return pltpu.VMEM(shape, dtype)

    message, kv_half, query_all = call(
        prep_kernel,
        1,
        (pw, ow, nw),
        [None] * 3,
        [
            out((width + part_rows, span), bf_type),
            out((width, span), bf_type),
            out((8 * part_rows, span), bf_type),
        ],
        [None] * 3,
        [vmem((2 * width, span), bf_type)],
        1e6,
        "prep",
    )
    mine, other = [message], [kv_half]
    for z in range(1, shards):
        mine.append(exchange(message, 0, z))
    for z in range(1, shards):
        other.append(exchange(mine[z], 1, 0))
    x_turned = jnp.concatenate(
        [
            lax.dynamic_slice(x, (0, lax.bitwise_xor(shard, z) * span), (rows, span))
            for z in range(shards)
        ],
        axis=1,
    )

    sig_key, value, keep, send = call(
        functools.partial(key_kernel, shards, steps),
        steps,
        (place, x_turned, ids, *mine, *other),
        ["smem", "row", "lane"] + [None] * (2 * shards),
        [wide(fl_type), wide(bf_type), out(chunk_shape, fl_type), out(chunk_shape, bf_type)],
        ["lane", "lane", None, None],
        [
            vmem((2 * width, width), bf_type),
            vmem((CLUSTERS * half + PAD, block), bf_type),
            vmem((half, block), bf_type),
            vmem((GROUPS, CLUSTERS * half + PAD, half), fl_type),
        ],
        4 * work,
        "keys",
        block,
    )

    def swap(pieces, peers, filler):
        got = [exchange(p, *at) for p, at in zip(pieces, peers)]
        if filler is not None:
            done = filler(pieces[0])
            got = list(tie(tuple(got), done))
        return to_float(got)

    plane = [(2 * e, 0) for e in range(1, 4)]
    along = [(0, z) for z in range(1, shards)]
    made = {}

    def reduce_chunks(keep, send, fillers):
        mine = keep + exchange(send, 1, 0).astype(fl_type)
        got = swap([mine[e].astype(bf_type) for e in range(1, 4)], plane, fillers[0])
        own = tree_sum([mine[0], *got]).astype(bf_type)
        got = swap([own] * (shards - 1), along, fillers[1])
        own = tree_sum([own.astype(fl_type), *got]).astype(bf_type)
        if outer > 1:
            got = swap([own] * (outer - 1), [(8 * o, 0) for o in range(1, outer)], None)
            own = tree_sum([own.astype(fl_type), *got]).astype(bf_type)
        return spread(own, fillers[2])

    def spread(own, filler=None):
        chunks = [own] + [None] * 7
        for e in range(1, 4):
            chunks[2 * e] = exchange(own, 2 * e, 0)
        chunks[1] = exchange(own, 1, 0)
        if filler is not None:
            done = filler(own)
            chunks[2], chunks[4], chunks[6] = tie((chunks[2], chunks[4], chunks[6]), done)
        for e in range(1, 4):
            chunks[2 * e + 1] = exchange(chunks[2 * e], 1, 0)
        return chunks

    def fill_weights(dep):
        made["weights"] = call(
            functools.partial(weights_kernel, shards),
            1,
            (tie(place, dep), query_all, *mine[1:], *other[1:], *far),
            ["smem", None] + [None] * (2 * (shards - 1) + 6),
            [
                out((width, width), bf_type),
                out((width, width), bf_type),
                out((width, width), bf_type),
                out((width, 128), fl_type),
                out((width, 128), fl_type),
                out((width, width), bf_type),
                out((width, width), bf_type),
            ],
            [None] * 7,
            [vmem((shards, 8 * part_rows, span), bf_type)],
            1e6,
            "weights",
        )
        return made["weights"][0]

    def fill_query(dep):
        made["query"] = call(
            query_kernel,
            steps,
            (tie(place, dep), x_turned, made["weights"][0]),
            ["smem", "row", None],
            [wide(fl_type), wide(bf_type)],
            ["lane"] * 2,
            [],
            work,
            "query",
            block,
            vmem=12,
        )
        return made["query"][1], fill_gate(dep)

    def fill_gate(dep):
        gate_weight = made["weights"][1]
        made["gate"] = call(
            gate_kernel,
            steps,
            (tie(place, dep), x_turned, gate_weight),
            ["smem", "row", None],
            [wide(fl_type)],
            ["lane"],
            [],
            work,
            "gate",
            block,
            vmem=12,
        )[0]
        return made["gate"]

    def fill_grad_prod(dep):
        out_weight = made["weights"][2]
        made["grad_prod"] = call(
            grad_prod_kernel,
            steps,
            (tie(place, dep), g, out_weight),
            ["smem", "row", None],
            [wide(fl_type)],
            ["lane"],
            [],
            work,
            "grad_prod",
            block,
            vmem=12,
        )[0]
        return made["grad_prod"]

    stack = jnp.stack([mine[z][width:] for z in range(1, shards)])
    far = [exchange(stack, *at) for at in plane]
    send = tie(send, *far)
    far = far + [exchange(f, 1, 0) for f in far]
    chunks = reduce_chunks(keep, send, (fill_weights, fill_query, fill_grad_prod))
    out_weight, gain, shift, full_query, full_gate = made["weights"][2:]
    sig_query, query = made["query"]

    parts = block // lanes
    prod, dgate, dnum, dden, keep, send = call(
        functools.partial(middle_kernel, steps, lanes),
        steps,
        (place, ids, query, made["gate"], made["grad_prod"], gain, shift, *chunks),
        ["smem", "lane", "lane", "lane", "lane", None, None] + [None] * CHUNKS,
        [
            wide(bf_type),
            wide(bf_type),
            wide(bf_type),
            out((16, rows), fl_type),
            out(chunk_shape, fl_type),
            out(chunk_shape, bf_type),
        ],
        ["lane", "lane", "lane", "lane", None, None],
        [
            vmem((CHUNKS, head + PAD, half), bf_type),
            vmem((GROUPS, half + PAD, CLUSTERS * half), bf_type),
            vmem((GROUPS, CLUSTERS * half + 32, half), fl_type),
            vmem((width, 128), fl_type),
            vmem((width, 128), fl_type),
        ]
        + [vmem((GROUPS, CLUSTERS * half, lanes), bf_type)] * parts
        + [vmem((GROUPS, CLUSTERS * half + 32, lanes), bf_type)] * parts
        + [vmem((width, lanes), fl_type)] * (3 * parts)
        + [vmem((16, lanes), fl_type)] * (2 * parts),
        6 * work,
        "middle",
        block,
    )

    def fill_gate_back(dep):
        made["gate_back"] = call(
            gate_back_kernel,
            steps,
            (tie(place, dep), dgate, prod, x_turned, g),
            ["smem", "lane", "lane", "row", "row"],
            [out((width, width), fl_type)] * 2,
            [None] * 2,
            [],
            2 * work,
            "gate_back",
            block,
            vmem=12,
        )
        return made["gate_back"][0]

    def fill_output(dep):
        made["output"] = call(
            output_kernel,
            steps,
            (tie(place, dep), x, prod, out_weight),
            ["smem", "row", "lane", None],
            [out((rows, width), fl_type)],
            ["row"],
            [],
            work,
            "output",
            block,
            piped=True,
        )[0]
        return made["output"]

    def fill_query_back(dep):
        made["query_back"] = call(
            functools.partial(query_back_kernel, shards),
            steps,
            (tie(place, dep), ids, dnum, dden, sig_query, x_turned, *chunks),
            ["smem", "lane", "lane", "lane", "lane", "row"] + [None] * CHUNKS,
            [wide(bf_type), out((width, width), fl_type)],
            ["lane", None],
            [
                vmem((CHUNKS, head + PAD, half), bf_type),
                vmem((GROUPS, half, CLUSTERS * half), bf_type),
                vmem((CLUSTERS, width, 128), fl_type),
                vmem((CLUSTERS * half, block), bf_type),
            ],
            3 * work,
            "query_back",
            block,
        )
        return made["query_back"][0]

    back_chunks = reduce_chunks(keep, send, (fill_gate_back, None, fill_query_back))
    dquery, grad_query = made["query_back"]

    height = 2 * tall + (span // 2) * (width // 4 // span)
    piece_shape = (4, shards, height, span)
    dkey, dvalue, norm_grad, keep, send = call(
        functools.partial(key_back_kernel, shards, steps),
        steps,
        (place, ids, sig_key, value, x_turned, grad_query, *made["gate_back"], *back_chunks),
        ["smem", "lane", "lane", "lane", "row"] + [None] * (3 + CHUNKS),
        [
            wide(bf_type),
            wide(bf_type),
            out((8, width), fl_type),
            out(piece_shape, fl_type),
            out(piece_shape, bf_type),
        ],
        ["lane", "lane", None, None, None],
        [
            vmem((CHUNKS, head + PAD, half), bf_type),
            vmem((GROUPS, half, CLUSTERS * half), bf_type),
            vmem((GROUPS, half, CLUSTERS * half), bf_type),
            vmem((CLUSTERS, width, 128), fl_type),
            vmem((CLUSTERS * half, block), bf_type),
            vmem((2 * width, width), fl_type),
        ],
        6 * work,
        "key_back",
        block,
    )

    full_key = call(
        functools.partial(key_weights_kernel, shards),
        1,
        (place, *mine, *other),
        ["smem"] + [None] * (2 * shards),
        [out((2 * width, width), bf_type)],
        [None],
        [vmem((shards, 2 * width, span), bf_type)],
        1e6,
        "key_weights",
        vmem=12,
    )[0]

    def fill_inputs(dep):
        made["inputs"] = call(
            input_kernel,
            steps,
            (tie(place, dep), dquery, dkey, dvalue, dgate, full_query, full_key, full_gate, g),
            ["smem"] + ["lane"] * 4 + [None] * 3 + ["row"],
            [out((rows, width), fl_type)],
            ["row"],
            [],
            4 * work,
            "inputs",
            block,
            piped=True,
        )[0]
        fill_output(dep)
        return made["inputs"], made["output"]

    mine_sum = keep + exchange(send, 1, 0).astype(fl_type)
    got = swap([mine_sum[e].astype(bf_type) for e in range(1, 4)], plane, fill_inputs)
    mine_sum = tree_sum([mine_sum[0], *got])
    got = [exchange(mine_sum[z].astype(bf_type), *along[z - 1]) for z in range(1, shards)]
    owned_parts = [mine_sum[0], *got]
    if outer > 1:
        own = tree_sum(to_float(owned_parts)).astype(bf_type)
        got = [own] + [exchange(own, 8 * o, 0) for o in range(1, outer)]
        owned_parts = [tree_sum(to_float(got))] + [jnp.zeros_like(own)] * (shards - 1)

    sums, squares = call(
        finish_kernel,
        1,
        owned_parts,
        [None] * shards,
        [out((height, span), bf_type), out((8, 128), fl_type)],
        [None] * 2,
        [],
        1e6,
        "finish",
        vmem=4,
    )
    squares = [squares] + [exchange(squares, 0, z) for z in range(1, shards)]
    owned = call(
        functools.partial(with_squares_kernel, shards),
        1,
        (sums, *squares),
        [None] * (1 + shards),
        [out((height + 16, span), bf_type)],
        [None],
        [],
        1e6,
        "with_squares",
        vmem=4,
    )[0]
    parts = spread(owned)
    states = (pw, pm, ps, ow, om, osq, nw, nm, ns)
    column = pl.BlockSpec((span, width), lambda i: (0, i))
    like = [pw] * 4 + [ow] * 4 + [nw] * 4
    kinds = [fl_type] * 3 + [bf_type] + [fl_type] * 3 + [bf_type] + [fl_type] * 4
    grad_size, *new = call(
        functools.partial(update_kernel, shards),
        4,
        (place, *parts, norm_grad, *states),
        ["smem"] + [None] * (CHUNKS + 1) + [column] * 3 + [None] * 6,
        [out((1, 1), fl_type)] + [out(s.shape, k) for s, k in zip(like, kinds)],
        [None] + [column] * 4 + [None] * 8,
        [
            vmem((16, tall, span), bf_type),
            vmem((span, width), fl_type),
            vmem((8, 128), fl_type),
        ],
        1e6,
        "update",
        piped=True,
    )
    return (made["output"], made["inputs"], grad_size.reshape(1), *new)


def solution(mesh):
    nodes, shards = mesh.shape["nodes"], mesh.shape["shard"]
    by_node = P(AXES, None)
    rows = P("shard", None)
    cols = P(None, "shard")
    return jax.shard_map(
        functools.partial(local, nodes, shards),
        mesh=mesh,
        in_specs=(by_node, by_node, P(AXES), P(AXES)) + (rows,) * 6 + (cols,) * 3,
        out_specs=(by_node, by_node, P()) + (rows,) * 8 + (cols,) * 4,
        check_vma=False,
    )
```

time: 218 us -> 163 us (0.75)
  Pallas kernels: 89 us -> 63 us
  starting transfers between devices: 63.4 us -> 52.9 us
  other arithmetic: 8.2 us -> 1.17 us
  waiting for transfers between devices: 43.6 us -> 39.5 us
  local copies, waits for them, and re-layouts: 8.42 us -> 4.74 us
  between operations: 4.46 us -> 1.79 us
    pallas_call x11 -> x16, Pallas kernels: 89 us -> 63 us  [call(): pl.pallas_call(body, grid=(steps,) if piped else (), in_specs=specs[:len(...]
    ppermute x64 -> x57, starting transfers between devices: 63.4 us -> 52.9 us  [exchange(): return lax.ppermute(value, AXES, pairs)]
    ppermute x64 -> x57, waiting for transfers between devices: 43.6 us -> 39.5 us  [exchange(): return lax.ppermute(value, AXES, pairs)]
    another operation x7 -> x6, other arithmetic: 3.28 us -> 0.84 us
    unnamed x78 -> x30, local copies, waits for them, and re-layouts: 4.92 us -> 2.91 us
  transfers between devices with their start and end apart: 64 -> 57, of which waited for: 25 -> 30; matrix products, arithmetic and copies ran while one was open for 3% -> 1% of each run, Pallas kernels for 25% -> 22%
where the time goes in v2:
time: 163 us
  Pallas kernels  63 us (39%)
  starting transfers between devices  52.9 us (32%)
  waiting for transfers between devices  39.5 us (24%)
  local copies, waits for them, and re-layouts  4.74 us (3%)
  between operations  1.79 us (1%)
    pallas_call x16, Pallas kernels, call(): pl.pallas_call(body, grid=(steps,) if piped else (), in_specs=specs[:len(...  63 us
    ppermute x57, starting transfers between devices, exchange(): return lax.ppermute(value, AXES, pairs)  52.9 us
    ppermute x57, waiting for transfers between devices, exchange(): return lax.ppermute(value, AXES, pairs)  39.5 us
  transfers between devices with their start and end apart: 57, of which 30 were waited for; matrix products, arithmetic and copies ran while one was open for 1% of the time, Pallas kernels for 22%

profile of v2, /device:TPU:0, one launch (start us, length us, event | category | flops | bytes accessed | tf_op | source)
XLA Modules:
  0.0 163.2 jit_solution(5711529823459499491)
XLA Ops:
  0.7 1.2 copy-done.2
  1.9 0.9 copy-done.6
  2.8 0.7 copy-done.10
  3.8 5.1 %collective-permute-start.2 = (bf16[720,128]{1,0:T(8,128)(2,1)S(1)}, bf16[720,128]{1,0:T(8,128)(2,1)S(1)}, u32[]{:S(2)}, u32[]{:S(2)}) collective-permute-start(bf16[720,128]{1,0:T(8,128)(2,1)S(1)} %get-tuple-element.86.refs_3_.refs_1_), channel_id=1, source_target_pairs={{0,3},{1,2},{2,1},{3,0},{4,7},{5,6},{6,5},{7,4},{8,11},{9,10},{10,... | collective-permute-start | bytes 552968 | tf_op jit(solution)/shard_map/ppermute | solution.py:668
  8.9 0.6 collective-permute-start
  9.6 1.7 %constant_dynamic-slice_fusion.3 = (bf16[2048,128]{1,0:T(8,128)(2,1)S(1)}, bf16[2048,128]{1,0:T(8,128)(2,1)S(1)}, bf16[2048,128]{1,0:T(8,128)(2,1)S(1)}, bf16[2048,128]{1,0:T(8,128)(2,1)S(1)}) fusion(bf16[2048,512]{1,0:T(8,128)(2,1)} %refs_1_.5, s32[]{:T(128)S(6)} %select_n.12, s32[]{:T(128)S(6)} %select_n.14, s32[]{:T(128)S(6)} %select_n.13, s32[]{:T(128)S(6)} %select_n.15), kind=kLoop, calls=%fused_computation.37 | loop fusion | bytes 4194320 | tf_op jit(solution)/shard_map/dynamic_slice | solution.py:741
  12.2 2.3 %collective-permute-done.2.refs_6_.refs_4_ = bf16[720,128]{1,0:T(8,128)(2,1)S(1)} collective-permute-done((bf16[720,128]{1,0:T(8,128)(2,1)S(1)}, bf16[720,128]{1,0:T(8,128)(2,1)S(1)}, u32[]{:S(2)}, u32[]{:S(2)}) %collective-permute-start.2) | collective-permute-done | bytes 184352 | tf_op jit(solution)/shard_map/ppermute | solution.py:668
  14.5 10.0 %collective-permute-done.1.refs_5_.refs_3_ = bf16[720,128]{1,0:T(8,128)(2,1)S(1)} collective-permute-done((bf16[720,128]{1,0:T(8,128)(2,1)S(1)}, bf16[720,128]{1,0:T(8,128)(2,1)S(1)}, u32[]{:S(2)}, u32[]{:S(2)}) %collective-permute-start.1) | collective-permute-done | bytes 184352 | tf_op jit(solution)/shard_map/ppermute | solution.py:668
  25.2 2.5 %collective-permute-start.8 = (bf16[3,208,128]{2,1,0:T(8,128)(2,1)S(1)}, bf16[3,208,128]{2,1,0:T(8,128)(2,1)S(1)}, u32[]{:S(2)}, u32[]{:S(2)}) collective-permute-start(bf16[3,208,128]{2,1,0:T(8,128)(2,1)S(1)} %pad_maximum_fusion.1), channel_id=1, source_target_pairs={{0,24},{1,25},{2,26},{3,27},{4,28},{5,29},{6,30},{7,31},{8,16},{9,... | collective-permute-start | bytes 479240 | tf_op jit(solution)/shard_map/ppermute | solution.py:668
  28.7 6.5 %keys.1 = (f32[512,2048]{1,0:T(8,128)S(1)}, bf16[512,2048]{1,0:T(8,128)(2,1)S(1)}, f32[4,80,256]{2,1,0:T(8,128)S(1)}, bf16[4,80,256]{2,1,0:T(8,128)(2,1)S(1)}) custom-call(s32[4]{0:T(128)S(1)} %pad_add_fusion.refs_0_, bf16[2048,512]{1,0:T(8,128)(2,1)S(1)} %pad_maximum_fusion.refs_1_.refs_3_.refs_5_.refs_4_, s32[1,2048]{1,0:T(1,128)S(1)} %bitcast.60, ...), custom_call_target="tpu_custom_call" | custom-call | flops 4294967296 | bytes 10309648 | tf_op jit(solution)/shard_map/keys/pallas_call | solution.py:91
  37.2 2.1 %collective-permute-start.12 = (bf16[80,256]{1,0:T(8,128)(2,1)S(1)}, bf16[80,256]{1,0:T(8,128)(2,1)S(1)}, u32[]{:S(2)}, u32[]{:S(2)}) collective-permute-start(bf16[80,256]{1,0:T(8,128)(2,1)S(1)} %get-tuple-element.178), channel_id=1, source_target_pairs={{0,24},{1,25},{2,26},{3,27},{4,28},{5,29},{6,30},{7,31},{8,16},{9,... | collective-permute-start | bytes 122888 | tf_op jit(solution)/shard_map/ppermute | solution.py:668
  39.3 0.9 collective-permute-start.11
  40.7 1.3 weights.1
  42.2 1.1 collective-permute-done.11
  43.3 0.9 collective-permute-done.10
  44.2 2.5 %collective-permute-start.18 = (bf16[80,256]{1,0:T(8,128)(2,1)S(1)}, bf16[80,256]{1,0:T(8,128)(2,1)S(1)}, u32[]{:S(2)}, u32[]{:S(2)}) collective-permute-start(bf16[80,256]{1,0:T(8,128)(2,1)S(1)} %fusion.7), channel_id=1, source_target_pairs={{0,3},{1,2},{2,1},{3,0},{4,7},{5,6},{6,5},{7,4},{8,11},{9,10},{10,... | collective-permute-start | bytes 122888 | tf_op jit(solution)/shard_map/ppermute | solution.py:668
  46.8 1.9 %collective-permute-start.16 = (bf16[80,256]{1,0:T(8,128)(2,1)S(1)}, bf16[80,256]{1,0:T(8,128)(2,1)S(1)}, u32[]{:S(2)}, u32[]{:S(2)}) collective-permute-start(bf16[80,256]{1,0:T(8,128)(2,1)S(1)} %fusion.7), channel_id=1, source_target_pairs={{0,1},{1,0},{2,3},{3,2},{4,5},{5,4},{6,7},{7,6},{8,9},{9,8},{10,11... | collective-permute-start | bytes 122888 | tf_op jit(solution)/shard_map/ppermute | solution.py:668
  48.7 2.5 %query.1 = (f32[512,2048]{1,0:T(8,128)S(1)}, bf16[512,2048]{1,0:T(8,128)(2,1)S(1)}) custom-call(s32[4]{0:T(128)S(1)} %pad_add_fusion.refs_0_, bf16[2048,512]{1,0:T(8,128)(2,1)S(1)} %pad_maximum_fusion.refs_1_.refs_3_.refs_5_.refs_4_, bf16[512,512]{1,0:T(8,128)(2,1)S(1)} %get-tuple-element.95.refs_2_), custom_call_target="tpu_custom_call" | custom-call | flops 1073741824 | bytes 8912912 | tf_op jit(solution)/shard_map/query/pallas_call | solution.py:91
  51.2 2.4 %gate.1.refs_3_ = f32[512,2048]{1,0:T(8,128)S(1)} custom-call(s32[4]{0:T(128)S(1)} %pad_add_fusion.refs_0_, bf16[2048,512]{1,0:T(8,128)(2,1)S(1)} %pad_maximum_fusion.refs_1_.refs_3_.refs_5_.refs_4_, bf16[512,512]{1,0:T(8,128)(2,1)S(1)} %get-tuple-element.101.refs_2_), custom_call_target="tpu_custom_call" | custom-call | flops 1073741824 | bytes 6815760 | tf_op jit(solution)/shard_map/gate/pallas_call | solution.py:91
  53.6 1.5 collective-permute-start.22
  55.1 0.6 collective-permute-start.21
  55.7 1.5 collective-permute-start.20
  57.2 2.4 %grad_prod.1.refs_4_ = f32[512,2048]{1,0:T(8,128)S(1)} custom-call(s32[4]{0:T(128)S(1)} %pad_add_fusion.refs_0_, bf16[2048,512]{1,0:T(8,128)(2,1)S(1)} %copy-done, bf16[512,512]{1,0:T(8,128)(2,1)S(1)} %get-tuple-element.106.refs_2_.refs_3_), custom_call_target="tpu_custom_call" | custom-call | flops 1073741824 | bytes 6815760 | tf_op jit(solution)/shard_map/grad_prod/pallas_call | solution.py:91
  61.6 11.2 %middle.1 = (bf16[512,2048]{1,0:T(8,128)(2,1)S(1)}, bf16[512,2048]{1,0:T(8,128)(2,1)S(1)}, bf16[512,2048]{1,0:T(8,128)(2,1)S(1)}, f32[16,2048]{1,0:T(8,128)S(1)}...) custom-call(s32[4]{0:T(128)S(1)} %pad_add_fusion.refs_0_, s32[1,2048]{1,0:T(1,128)S(1)} %bitcast.61, ...), custom_call_target="tpu_custom_call" | custom-call | flops 6442450944 | bytes 18259984 | tf_op jit(solution)/shard_map/middle/pallas_call | solution.py:91
  73.3 1.1 collective-permute-done.26
  74.4 1.4 collective-permute-start.27
  75.7 1.4 collective-permute-start.29
  77.1 0.8 collective-permute-start.28
  77.9 3.5 %gate_back.1 = (f32[512,512]{1,0:T(8,128)S(1)}, f32[512,512]{1,0:T(8,128)S(1)}) custom-call(s32[4]{0:T(128)S(1)} %pad_add_fusion.refs_0_, bf16[512,2048]{1,0:T(8,128)(2,1)S(1)} %get-tuple-element.115.refs_1_.refs_4_, bf16[512,2048]{1,0:T(8,128)(2,1)S(1)} %get-tuple-element.116.refs_2_, bf16[2048,512]{1,0:T(8,128)(2,1)S(1)} %pad_maximum_fusion.refs_1_.refs_3_.refs_5_.refs_4_, ...), custom_call_target="tpu_custom_call" | custom-call | flops 2147483648 | bytes 10485776 | tf_op jit(solution)/shard_map/gate_back/pallas_call | solution.py:91
  81.6 2.5 %collective-permute-start.32 = (bf16[80,256]{1,0:T(8,128)(2,1)S(1)}, bf16[80,256]{1,0:T(8,128)(2,1)S(1)}, u32[]{:S(2)}, u32[]{:S(2)}) collective-permute-start(bf16[80,256]{1,0:T(8,128)(2,1)S(1)} %fusion.4), channel_id=1, source_target_pairs={{0,3},{1,2},{2,1},{3,0},{4,7},{5,6},{6,5},{7,4},{8,11},{9,10},{10,... | collective-permute-start | bytes 122888 | tf_op jit(solution)/shard_map/ppermute | solution.py:668
  84.1 1.9 %collective-permute-start.30 = (bf16[80,256]{1,0:T(8,128)(2,1)S(1)}, bf16[80,256]{1,0:T(8,128)(2,1)S(1)}, u32[]{:S(2)}, u32[]{:S(2)}) collective-permute-start(bf16[80,256]{1,0:T(8,128)(2,1)S(1)} %fusion.4), channel_id=1, source_target_pairs={{0,1},{1,0},{2,3},{3,2},{4,5},{5,4},{6,7},{7,6},{8,9},{9,8},{10,11... | collective-permute-start | bytes 122888 | tf_op jit(solution)/shard_map/ppermute | solution.py:668
  86.0 1.5 collective-permute-done.32
  87.5 1.5 collective-permute-done.31
  89.0 1.9 %collective-permute-start.36 = (bf16[80,256]{1,0:T(8,128)(2,1)S(1)}, bf16[80,256]{1,0:T(8,128)(2,1)S(1)}, u32[]{:S(2)}, u32[]{:S(2)}) collective-permute-start(bf16[80,256]{1,0:T(8,128)(2,1)S(1)} %add_convert_fusion.refs_8_), channel_id=1, source_target_pairs={{0,24},{1,25},{2,26},{3,27},{4,28},{5,29},{6,30},{7,31},{8,16},{9,... | collective-permute-start | bytes 122888 | tf_op jit(solution)/shard_map/ppermute | solution.py:668
  91.0 0.9 collective-permute-start.35
  91.9 0.7 collective-permute-start.34
  92.6 5.8 %query_back.1 = (bf16[512,2048]{1,0:T(8,128)(2,1)S(1)}, f32[512,512]{1,0:T(8,128)S(1)}) custom-call(s32[4]{0:T(128)S(1)} %pad_add_fusion.refs_0_, s32[1,2048]{1,0:T(1,128)S(1)} %bitcast.62, bf16[512,2048]{1,0:T(8,128)(2,1)S(1)} %get-tuple-element.122.refs_2_, f32[16,2048]{1,0:T(8,128)S(1)} %get-tuple-element.123.refs_3_, ...), custom_call_target="tpu_custom_call" | custom-call | flops 3221225472 | bytes 12001296 | tf_op jit(solution)/shard_map/query_back/pallas_call | solution.py:91
  98.5 0.6 collective-permute-start.37
  100.4 10.3 %key_back.1 = (bf16[512,2048]{1,0:T(8,128)(2,1)S(1)}, bf16[512,2048]{1,0:T(8,128)(2,1)S(1)}, f32[8,512]{1,0:T(8,128)S(1)}, f32[4,4,320,128]{3,2,1,0:T(8,128)S(1)}, bf16[4,4,320,128]{3,2,1,0:T(8,128)(2,1)S(1)}) custom-call(s32[4]{0:T(128)S(1)} %pad_add_fusion.refs_0_, s32[1,2048]{1,0:T(1,128)S(1)} %bitcast.63, f32[512,2048]{1,0:T(8,128)S(1)} %get-tuple-element.88.refs_2_, ...), custom_call_target="tpu_custom_call" | custom-call | flops 6442450944 | bytes 20013072 | tf_op jit(solution)/shard_map/key_back/pallas_call | solution.py:91
  111.1 0.8 key_weights.1.refs_6_
  111.9 1.9 %collective-permute-done.40 = bf16[4,4,320,128]{3,2,1,0:T(8,128)(2,1)S(1)} collective-permute-done((bf16[4,4,320,128]{3,2,1,0:T(8,128)(2,1)S(1)}, bf16[4,4,320,128]{3,2,1,0:T(8,128)(2,1)S(1)}, u32[]{:S(2)}, u32[]{:S(2)}) %collective-permute-start.40) | collective-permute-done | bytes 1310752 | tf_op jit(solution)/shard_map/ppermute | solution.py:668
  114.4 1.4 collective-permute-start.41
  115.8 1.4 collective-permute-start.43
  117.1 0.8 collective-permute-start.42
  117.9 4.0 %output.1 = f32[2048,512]{1,0:T(8,128)} custom-call(s32[4]{0:T(128)S(1)} %pad_add_fusion.refs_0_, bf16[2048,512]{1,0:T(8,128)(2,1)S(1)} %copy-done.1, bf16[512,2048]{1,0:T(8,128)(2,1)S(1)} %get-tuple-element.116.refs_2_, bf16[512,512]{1,0:T(8,128)(2,1)S(1)} %get-tuple-element.106.refs_2_.refs_3_), custom_call_target="tpu_custom_call" | custom-call | flops 1073741824 | bytes 8912912 | tf_op jit(solution)/shard_map/output/pallas_call | solution.py:91
  122.0 7.2 %inputs.1 = f32[2048,512]{1,0:T(8,128)} custom-call(s32[4]{0:T(128)S(1)} %pad_add_fusion.refs_0_, bf16[512,2048]{1,0:T(8,128)(2,1)S(1)} %get-tuple-element.127.refs_1_, bf16[512,2048]{1,0:T(8,128)(2,1)S(1)} %get-tuple-element.134.refs_2_, bf16[512,2048]{1,0:T(8,128)(2,1)S(1)} %get-tuple-element.135.refs_3_, ...), custom_call_target="tpu_custom_call" | custom-call | flops 4294967296 | bytes 16777232 | tf_op jit(solution)/shard_map/inputs/pallas_call | solution.py:91
  129.3 2.9 %collective-permute-done.43 = bf16[4,320,128]{2,1,0:T(8,128)(2,1)S(1)} collective-permute-done((bf16[4,320,128]{2,1,0:T(8,128)(2,1)S(1)}, bf16[4,320,128]{2,1,0:T(8,128)(2,1)S(1)}, u32[]{:S(2)}, u32[]{:S(2)}) %collective-permute-start.43) | collective-permute-done | bytes 327712 | tf_op jit(solution)/shard_map/ppermute | solution.py:668
  132.2 1.4 collective-permute-done.42
  133.8 2.1 %collective-permute-start.46 = (bf16[320,128]{1,0:T(8,128)(2,1)S(1)}, bf16[320,128]{1,0:T(8,128)(2,1)S(1)}, u32[]{:S(2)}, u32[]{:S(2)}) collective-permute-start(bf16[320,128]{1,0:T(8,128)(2,1)S(1)} %get-tuple-element.172), channel_id=1, source_target_pairs={{0,3},{1,2},{2,1},{3,0},{4,7},{5,6},{6,5},{7,4},{8,11},{9,10},{10,... | collective-permute-start | bytes 245768 | tf_op jit(solution)/shard_map/ppermute | solution.py:668
  136.3 1.9 %collective-permute-start.44 = (bf16[320,128]{1,0:T(8,128)(2,1)S(1)}, bf16[320,128]{1,0:T(8,128)(2,1)S(1)}, u32[]{:S(2)}, u32[]{:S(2)}) collective-permute-start(bf16[320,128]{1,0:T(8,128)(2,1)S(1)} %get-tuple-element.174), channel_id=1, source_target_pairs={{0,1},{1,0},{2,3},{3,2},{4,5},{5,4},{6,7},{7,6},{8,9},{9,8},{10,11... | collective-permute-start | bytes 245768 | tf_op jit(solution)/shard_map/ppermute | solution.py:668
  138.2 2.6 %collective-permute-done.46.refs_3_ = bf16[320,128]{1,0:T(8,128)(2,1)S(1)} collective-permute-done((bf16[320,128]{1,0:T(8,128)(2,1)S(1)}, bf16[320,128]{1,0:T(8,128)(2,1)S(1)}, u32[]{:S(2)}, u32[]{:S(2)}) %collective-permute-start.46) | collective-permute-done | bytes 81952 | tf_op jit(solution)/shard_map/ppermute | solution.py:668
  140.9 2.4 %collective-permute-done.45.refs_2_ = bf16[320,128]{1,0:T(8,128)(2,1)S(1)} collective-permute-done((bf16[320,128]{1,0:T(8,128)(2,1)S(1)}, bf16[320,128]{1,0:T(8,128)(2,1)S(1)}, u32[]{:S(2)}, u32[]{:S(2)}) %collective-permute-start.45) | collective-permute-done | bytes 81952 | tf_op jit(solution)/shard_map/ppermute | solution.py:668
  143.5 2.0 %collective-permute-start.49 = (f32[8,128]{1,0:T(8,128)S(1)}, f32[8,128]{1,0:T(8,128)S(1)}, u32[]{:S(2)}, u32[]{:S(2)}) collective-permute-start(f32[8,128]{1,0:T(8,128)S(1)} %get-tuple-element.142.refs_1_), channel_id=1, source_target_pairs={{0,3},{1,2},{2,1},{3,0},{4,7},{5,6},{6,5},{7,4},{8,11},{9,10},{10,... | collective-permute-start | bytes 12296 | tf_op jit(solution)/shard_map/ppermute | solution.py:668
  145.5 2.4 %collective-permute-start.47 = (f32[8,128]{1,0:T(8,128)S(1)}, f32[8,128]{1,0:T(8,128)S(1)}, u32[]{:S(2)}, u32[]{:S(2)}) collective-permute-start(f32[8,128]{1,0:T(8,128)S(1)} %get-tuple-element.142.refs_1_), channel_id=1, source_target_pairs={{0,1},{1,0},{2,3},{3,2},{4,5},{5,4},{6,7},{7,6},{8,9},{9,8},{10,11... | collective-permute-start | bytes 12296 | tf_op jit(solution)/shard_map/ppermute | solution.py:668
  147.8 1.0 collective-permute-done.49.refs_4_
  148.9 1.1 collective-permute-done.48.refs_3_
  150.0 1.6 collective-permute-start.55
  151.6 1.1 collective-permute-start.53
  152.7 0.8 collective-permute-start.51
  153.6 1.9 %collective-permute-done.55.refs_7_ = bf16[336,128]{1,0:T(8,128)(2,1)S(1)} collective-permute-done((bf16[336,128]{1,0:T(8,128)(2,1)S(1)}, bf16[336,128]{1,0:T(8,128)(2,1)S(1)}, u32[]{:S(2)}, u32[]{:S(2)}) %collective-permute-start.55) | collective-permute-done | bytes 86048 | tf_op jit(solution)/shard_map/ppermute | solution.py:668
  155.5 0.9 collective-permute-done.53.refs_5_
  156.4 0.8 collective-permute-done.51.refs_3_
  157.7 0.9 collective-permute-done.52.refs_4_
  158.6 4.5 %update.1 = (f32[1,1]{1,0:T(1,128)}, f32[128,2048]{1,0:T(8,128)}, f32[128,2048]{1,0:T(8,128)}, f32[128,2048]{1,0:T(8,128)}, bf16[128,2048]{1,0:T(8,128)(2,1)}, /...) custom-call(s32[4]{0:T(128)S(1)} %pad_add_fusion.refs_0_, ...), custom_call_target="tpu_custom_call" | custom-call | flops 1000000 | bytes 9231380 | tf_op jit(solution)/shard_map/update/pallas_call | solution.py:91
  (116 shorter events, 11.2 us)
Async XLA Ops:
  3.8 10.7 %collective-permute-start.2 = (bf16[720,128]{1,0:T(8,128)(2,1)S(1)}, bf16[720,128]{1,0:T(8,128)(2,1)S(1)}, u32[]{:S(2)}, u32[]{:S(2)}) collective-permute-start(bf16[720,128]{1,0:T(8,128)(2,1)S(1)} %get-tuple-element.86.refs_3_.refs_1_), channel_id=1, source_target_pairs={{0,3},{1,2},{2,1},{3,0},{4,7},{5,6},{6,5},{7,4},{8,11},{9,10},{10,... | collective-permute-start | bytes 552968 | tf_op jit(solution)/shard_map/ppermute | solution.py:668
  8.9 15.6 %collective-permute-start.1 = (bf16[720,128]{1,0:T(8,128)(2,1)S(1)}, bf16[720,128]{1,0:T(8,128)(2,1)S(1)}, u32[]{:S(2)}, u32[]{:S(2)}) collective-permute-start(bf16[720,128]{1,0:T(8,128)(2,1)S(1)} %get-tuple-element.86.refs_3_.refs_1_), channel_id=1, source_target_pairs={{0,2},{1,3},{2,0},{3,1},{4,6},{5,7},{6,4},{7,5},{8,10},{9,11},{10,... | collective-permute-start | bytes 552968 | tf_op jit(solution)/shard_map/ppermute | solution.py:668
  8.9 15.7 %collective-permute-start = (bf16[720,128]{1,0:T(8,128)(2,1)S(1)}, bf16[720,128]{1,0:T(8,128)(2,1)S(1)}, u32[]{:S(2)}, u32[]{:S(2)}) collective-permute-start(bf16[720,128]{1,0:T(8,128)(2,1)S(1)} %get-tuple-element.86.refs_3_.refs_1_), channel_id=1, source_target_pairs={{0,1},{1,0},{2,3},{3,2},{4,5},{5,4},{6,7},{7,6},{8,9},{9,8},{10,11... | collective-permute-start | bytes 552968 | tf_op jit(solution)/shard_map/ppermute | solution.py:668
  14.5 13.7 %collective-permute-start.5 = (bf16[720,128]{1,0:T(8,128)(2,1)S(1)}, bf16[720,128]{1,0:T(8,128)(2,1)S(1)}, u32[]{:S(2)}, u32[]{:S(2)}) collective-permute-start(bf16[720,128]{1,0:T(8,128)(2,1)S(1)} %collective-permute-done.2.refs_6_.refs_4_), channel_id=1, source_target_pairs={{0,4},{1,5},{2,6},{3,7},{4,0},{5,1},{6,2},{7,3},{8,12},{9,13},{10,... | collective-permute-start | bytes 552968 | tf_op jit(solution)/shard_map/ppermute | solution.py:668
  24.6 4.2 %collective-permute-start.4 = (bf16[720,128]{1,0:T(8,128)(2,1)S(1)}, bf16[720,128]{1,0:T(8,128)(2,1)S(1)}, u32[]{:S(2)}, u32[]{:S(2)}) collective-permute-start(bf16[720,128]{1,0:T(8,128)(2,1)S(1)} %collective-permute-done.1.refs_5_.refs_3_), channel_id=1, source_target_pairs={{0,4},{1,5},{2,6},{3,7},{4,0},{5,1},{6,2},{7,3},{8,12},{9,13},{10,... | collective-permute-start | bytes 552968 | tf_op jit(solution)/shard_map/ppermute | solution.py:668
  24.6 4.2 %collective-permute-start.3 = (bf16[720,128]{1,0:T(8,128)(2,1)S(1)}, bf16[720,128]{1,0:T(8,128)(2,1)S(1)}, u32[]{:S(2)}, u32[]{:S(2)}) collective-permute-start(bf16[720,128]{1,0:T(8,128)(2,1)S(1)} %collective-permute-done.refs_4_.refs_2_), channel_id=1, source_target_pairs={{0,4},{1,5},{2,6},{3,7},{4,0},{5,1},{6,2},{7,3},{8,12},{9,13},{10,... | collective-permute-start | bytes 552968 | tf_op jit(solution)/shard_map/ppermute | solution.py:668
  25.2 10.0 %collective-permute-start.8 = (bf16[3,208,128]{2,1,0:T(8,128)(2,1)S(1)}, bf16[3,208,128]{2,1,0:T(8,128)(2,1)S(1)}, u32[]{:S(2)}, u32[]{:S(2)}) collective-permute-start(bf16[3,208,128]{2,1,0:T(8,128)(2,1)S(1)} %pad_maximum_fusion.1), channel_id=1, source_target_pairs={{0,24},{1,25},{2,26},{3,27},{4,28},{5,29},{6,30},{7,31},{8,16},{9,... | collective-permute-start | bytes 479240 | tf_op jit(solution)/shard_map/ppermute | solution.py:668
  27.7 7.9 %collective-permute-start.7 = (bf16[3,208,128]{2,1,0:T(8,128)(2,1)S(1)}, bf16[3,208,128]{2,1,0:T(8,128)(2,1)S(1)}, u32[]{:S(2)}, u32[]{:S(2)}) collective-permute-start(bf16[3,208,128]{2,1,0:T(8,128)(2,1)S(1)} %pad_maximum_fusion.1), channel_id=1, source_target_pairs={{0,16},{1,17},{2,18},{3,19},{4,20},{5,21},{6,22},{7,23},{8,24},{9,... | collective-permute-start | bytes 479240 | tf_op jit(solution)/shard_map/ppermute | solution.py:668
  28.2 7.5 %collective-permute-start.6 = (bf16[3,208,128]{2,1,0:T(8,128)(2,1)S(1)}, bf16[3,208,128]{2,1,0:T(8,128)(2,1)S(1)}, u32[]{:S(2)}, u32[]{:S(2)}) collective-permute-start(bf16[3,208,128]{2,1,0:T(8,128)(2,1)S(1)} %pad_maximum_fusion.1), channel_id=1, source_target_pairs={{0,8},{1,9},{2,10},{3,11},{4,12},{5,13},{6,14},{7,15},{8,0},{9,1},... | collective-permute-start | bytes 479240 | tf_op jit(solution)/shard_map/ppermute | solution.py:668
  35.7 1.4 collective-permute-start.9
  35.7 4.5 %collective-permute-start.15 = (bf16[3,208,128]{2,1,0:T(8,128)(2,1)S(1)}, bf16[3,208,128]{2,1,0:T(8,128)(2,1)S(1)}, u32[]{:S(2)}, u32[]{:S(2)}) collective-permute-start(bf16[3,208,128]{2,1,0:T(8,128)(2,1)S(1)} %collective-permute-done.8.refs_10_), channel_id=1, source_target_pairs={{0,4},{1,5},{2,6},{3,7},{4,0},{5,1},{6,2},{7,3},{8,12},{9,13},{10,... | collective-permute-start | bytes 479240 | tf_op jit(solution)/shard_map/ppermute | solution.py:668
  36.2 4.5 %collective-permute-start.14 = (bf16[3,208,128]{2,1,0:T(8,128)(2,1)S(1)}, bf16[3,208,128]{2,1,0:T(8,128)(2,1)S(1)}, u32[]{:S(2)}, u32[]{:S(2)}) collective-permute-start(bf16[3,208,128]{2,1,0:T(8,128)(2,1)S(1)} %collective-permute-done.7.refs_9_), channel_id=1, source_target_pairs={{0,4},{1,5},{2,6},{3,7},{4,0},{5,1},{6,2},{7,3},{8,12},{9,13},{10,... | collective-permute-start | bytes 479240 | tf_op jit(solution)/shard_map/ppermute | solution.py:668
  36.2 4.5 %collective-permute-start.13 = (bf16[3,208,128]{2,1,0:T(8,128)(2,1)S(1)}, bf16[3,208,128]{2,1,0:T(8,128)(2,1)S(1)}, u32[]{:S(2)}, u32[]{:S(2)}) collective-permute-start(bf16[3,208,128]{2,1,0:T(8,128)(2,1)S(1)} %collective-permute-done.6.refs_8_), channel_id=1, source_target_pairs={{0,4},{1,5},{2,6},{3,7},{4,0},{5,1},{6,2},{7,3},{8,12},{9,13},{10,... | collective-permute-start | bytes 479240 | tf_op jit(solution)/shard_map/ppermute | solution.py:668
  37.2 5.0 %collective-permute-start.12 = (bf16[80,256]{1,0:T(8,128)(2,1)S(1)}, bf16[80,256]{1,0:T(8,128)(2,1)S(1)}, u32[]{:S(2)}, u32[]{:S(2)}) collective-permute-start(bf16[80,256]{1,0:T(8,128)(2,1)S(1)} %get-tuple-element.178), channel_id=1, source_target_pairs={{0,24},{1,25},{2,26},{3,27},{4,28},{5,29},{6,30},{7,31},{8,16},{9,... | collective-permute-start | bytes 122888 | tf_op jit(solution)/shard_map/ppermute | solution.py:668
  39.3 4.0 %collective-permute-start.11 = (bf16[80,256]{1,0:T(8,128)(2,1)S(1)}, bf16[80,256]{1,0:T(8,128)(2,1)S(1)}, u32[]{:S(2)}, u32[]{:S(2)}) collective-permute-start(bf16[80,256]{1,0:T(8,128)(2,1)S(1)} %get-tuple-element.179), channel_id=1, source_target_pairs={{0,16},{1,17},{2,18},{3,19},{4,20},{5,21},{6,22},{7,23},{8,24},{9,... | collective-permute-start | bytes 122888 | tf_op jit(solution)/shard_map/ppermute | solution.py:668
  40.2 4.0 %collective-permute-start.10 = (bf16[80,256]{1,0:T(8,128)(2,1)S(1)}, bf16[80,256]{1,0:T(8,128)(2,1)S(1)}, u32[]{:S(2)}, u32[]{:S(2)}) collective-permute-start(bf16[80,256]{1,0:T(8,128)(2,1)S(1)} %get-tuple-element.180), channel_id=1, source_target_pairs={{0,8},{1,9},{2,10},{3,11},{4,12},{5,13},{6,14},{7,15},{8,0},{9,1},... | collective-permute-start | bytes 122888 | tf_op jit(solution)/shard_map/ppermute | solution.py:668
  44.2 9.4 %collective-permute-start.18 = (bf16[80,256]{1,0:T(8,128)(2,1)S(1)}, bf16[80,256]{1,0:T(8,128)(2,1)S(1)}, u32[]{:S(2)}, u32[]{:S(2)}) collective-permute-start(bf16[80,256]{1,0:T(8,128)(2,1)S(1)} %fusion.7), channel_id=1, source_target_pairs={{0,3},{1,2},{2,1},{3,0},{4,7},{5,6},{6,5},{7,4},{8,11},{9,10},{10,... | collective-permute-start | bytes 122888 | tf_op jit(solution)/shard_map/ppermute | solution.py:668
  46.8 6.8 %collective-permute-start.17 = (bf16[80,256]{1,0:T(8,128)(2,1)S(1)}, bf16[80,256]{1,0:T(8,128)(2,1)S(1)}, u32[]{:S(2)}, u32[]{:S(2)}) collective-permute-start(bf16[80,256]{1,0:T(8,128)(2,1)S(1)} %fusion.7), channel_id=1, source_target_pairs={{0,2},{1,3},{2,0},{3,1},{4,6},{5,7},{6,4},{7,5},{8,10},{9,11},{10,... | collective-permute-start | bytes 122888 | tf_op jit(solution)/shard_map/ppermute | solution.py:668
  46.8 6.8 %collective-permute-start.16 = (bf16[80,256]{1,0:T(8,128)(2,1)S(1)}, bf16[80,256]{1,0:T(8,128)(2,1)S(1)}, u32[]{:S(2)}, u32[]{:S(2)}) collective-permute-start(bf16[80,256]{1,0:T(8,128)(2,1)S(1)} %fusion.7), channel_id=1, source_target_pairs={{0,1},{1,0},{2,3},{3,2},{4,5},{5,4},{6,7},{7,6},{8,9},{9,8},{10,11... | collective-permute-start | bytes 122888 | tf_op jit(solution)/shard_map/ppermute | solution.py:668
  53.6 6.0 %collective-permute-start.22 = (bf16[80,256]{1,0:T(8,128)(2,1)S(1)}, bf16[80,256]{1,0:T(8,128)(2,1)S(1)}, u32[]{:S(2)}, u32[]{:S(2)}) collective-permute-start(bf16[80,256]{1,0:T(8,128)(2,1)S(1)} %add_convert_fusion.1.refs_7_.refs_6_), channel_id=1, source_target_pairs={{0,24},{1,25},{2,26},{3,27},{4,28},{5,29},{6,30},{7,31},{8,16},{9,... | collective-permute-start | bytes 122888 | tf_op jit(solution)/shard_map/ppermute | solution.py:668
  55.1 4.5 %collective-permute-start.21 = (bf16[80,256]{1,0:T(8,128)(2,1)S(1)}, bf16[80,256]{1,0:T(8,128)(2,1)S(1)}, u32[]{:S(2)}, u32[]{:S(2)}) collective-permute-start(bf16[80,256]{1,0:T(8,128)(2,1)S(1)} %add_convert_fusion.1.refs_7_.refs_6_), channel_id=1, source_target_pairs={{0,16},{1,17},{2,18},{3,19},{4,20},{5,21},{6,22},{7,23},{8,24},{9,... | collective-permute-start | bytes 122888 | tf_op jit(solution)/shard_map/ppermute | solution.py:668
  55.7 4.0 %collective-permute-start.20 = (bf16[80,256]{1,0:T(8,128)(2,1)S(1)}, bf16[80,256]{1,0:T(8,128)(2,1)S(1)}, u32[]{:S(2)}, u32[]{:S(2)}) collective-permute-start(bf16[80,256]{1,0:T(8,128)(2,1)S(1)} %add_convert_fusion.1.refs_7_.refs_6_), channel_id=1, source_target_pairs={{0,8},{1,9},{2,10},{3,11},{4,12},{5,13},{6,14},{7,15},{8,0},{9,1},... | collective-permute-start | bytes 122888 | tf_op jit(solution)/shard_map/ppermute | solution.py:668
  57.2 3.6 %collective-permute-start.19 = (bf16[80,256]{1,0:T(8,128)(2,1)S(1)}, bf16[80,256]{1,0:T(8,128)(2,1)S(1)}, u32[]{:S(2)}, u32[]{:S(2)}) collective-permute-start(bf16[80,256]{1,0:T(8,128)(2,1)S(1)} %add_convert_fusion.1.refs_7_.refs_6_), channel_id=1, source_target_pairs={{0,4},{1,5},{2,6},{3,7},{4,0},{5,1},{6,2},{7,3},{8,12},{9,13},{10,... | collective-permute-start | bytes 122888 | tf_op jit(solution)/shard_map/ppermute | solution.py:668
  59.7 1.4 collective-permute-start.23
  60.2 1.2 collective-permute-start.24
  60.3 1.3 collective-permute-start.25
  72.8 1.5 collective-permute-start.26
  74.4 7.1 %collective-permute-start.27 = (bf16[80,256]{1,0:T(8,128)(2,1)S(1)}, bf16[80,256]{1,0:T(8,128)(2,1)S(1)}, u32[]{:S(2)}, u32[]{:S(2)}) collective-permute-start(bf16[80,256]{1,0:T(8,128)(2,1)S(1)} %get-tuple-element.177), channel_id=1, source_target_pairs={{0,8},{1,9},{2,10},{3,11},{4,12},{5,13},{6,14},{7,15},{8,0},{9,1},... | collective-permute-start | bytes 122888 | tf_op jit(solution)/shard_map/ppermute | solution.py:668
  75.7 5.8 %collective-permute-start.29 = (bf16[80,256]{1,0:T(8,128)(2,1)S(1)}, bf16[80,256]{1,0:T(8,128)(2,1)S(1)}, u32[]{:S(2)}, u32[]{:S(2)}) collective-permute-start(bf16[80,256]{1,0:T(8,128)(2,1)S(1)} %get-tuple-element.175), channel_id=1, source_target_pairs={{0,24},{1,25},{2,26},{3,27},{4,28},{5,29},{6,30},{7,31},{8,16},{9,... | collective-permute-start | bytes 122888 | tf_op jit(solution)/shard_map/ppermute | solution.py:668
  77.1 4.4 %collective-permute-start.28 = (bf16[80,256]{1,0:T(8,128)(2,1)S(1)}, bf16[80,256]{1,0:T(8,128)(2,1)S(1)}, u32[]{:S(2)}, u32[]{:S(2)}) collective-permute-start(bf16[80,256]{1,0:T(8,128)(2,1)S(1)} %get-tuple-element.176), channel_id=1, source_target_pairs={{0,16},{1,17},{2,18},{3,19},{4,20},{5,21},{6,22},{7,23},{8,24},{9,... | collective-permute-start | bytes 122888 | tf_op jit(solution)/shard_map/ppermute | solution.py:668
  81.6 6.0 %collective-permute-start.32 = (bf16[80,256]{1,0:T(8,128)(2,1)S(1)}, bf16[80,256]{1,0:T(8,128)(2,1)S(1)}, u32[]{:S(2)}, u32[]{:S(2)}) collective-permute-start(bf16[80,256]{1,0:T(8,128)(2,1)S(1)} %fusion.4), channel_id=1, source_target_pairs={{0,3},{1,2},{2,1},{3,0},{4,7},{5,6},{6,5},{7,4},{8,11},{9,10},{10,... | collective-permute-start | bytes 122888 | tf_op jit(solution)/shard_map/ppermute | solution.py:668
  84.1 4.9 %collective-permute-start.31 = (bf16[80,256]{1,0:T(8,128)(2,1)S(1)}, bf16[80,256]{1,0:T(8,128)(2,1)S(1)}, u32[]{:S(2)}, u32[]{:S(2)}) collective-permute-start(bf16[80,256]{1,0:T(8,128)(2,1)S(1)} %fusion.4), channel_id=1, source_target_pairs={{0,2},{1,3},{2,0},{3,1},{4,6},{5,7},{6,4},{7,5},{8,10},{9,11},{10,... | collective-permute-start | bytes 122888 | tf_op jit(solution)/shard_map/ppermute | solution.py:668
  84.1 4.9 %collective-permute-start.30 = (bf16[80,256]{1,0:T(8,128)(2,1)S(1)}, bf16[80,256]{1,0:T(8,128)(2,1)S(1)}, u32[]{:S(2)}, u32[]{:S(2)}) collective-permute-start(bf16[80,256]{1,0:T(8,128)(2,1)S(1)} %fusion.4), channel_id=1, source_target_pairs={{0,1},{1,0},{2,3},{3,2},{4,5},{5,4},{6,7},{7,6},{8,9},{9,8},{10,11... | collective-permute-start | bytes 122888 | tf_op jit(solution)/shard_map/ppermute | solution.py:668
  89.0 9.4 %collective-permute-start.36 = (bf16[80,256]{1,0:T(8,128)(2,1)S(1)}, bf16[80,256]{1,0:T(8,128)(2,1)S(1)}, u32[]{:S(2)}, u32[]{:S(2)}) collective-permute-start(bf16[80,256]{1,0:T(8,128)(2,1)S(1)} %add_convert_fusion.refs_8_), channel_id=1, source_target_pairs={{0,24},{1,25},{2,26},{3,27},{4,28},{5,29},{6,30},{7,31},{8,16},{9,... | collective-permute-start | bytes 122888 | tf_op jit(solution)/shard_map/ppermute | solution.py:668
  91.0 7.5 %collective-permute-start.35 = (bf16[80,256]{1,0:T(8,128)(2,1)S(1)}, bf16[80,256]{1,0:T(8,128)(2,1)S(1)}, u32[]{:S(2)}, u32[]{:S(2)}) collective-permute-start(bf16[80,256]{1,0:T(8,128)(2,1)S(1)} %add_convert_fusion.refs_8_), channel_id=1, source_target_pairs={{0,16},{1,17},{2,18},{3,19},{4,20},{5,21},{6,22},{7,23},{8,24},{9,... | collective-permute-start | bytes 122888 | tf_op jit(solution)/shard_map/ppermute | solution.py:668
  91.9 6.6 %collective-permute-start.34 = (bf16[80,256]{1,0:T(8,128)(2,1)S(1)}, bf16[80,256]{1,0:T(8,128)(2,1)S(1)}, u32[]{:S(2)}, u32[]{:S(2)}) collective-permute-start(bf16[80,256]{1,0:T(8,128)(2,1)S(1)} %add_convert_fusion.refs_8_), channel_id=1, source_target_pairs={{0,8},{1,9},{2,10},{3,11},{4,12},{5,13},{6,14},{7,15},{8,0},{9,1},... | collective-permute-start | bytes 122888 | tf_op jit(solution)/shard_map/ppermute | solution.py:668
  92.6 7.0 %collective-permute-start.33 = (bf16[80,256]{1,0:T(8,128)(2,1)S(1)}, bf16[80,256]{1,0:T(8,128)(2,1)S(1)}, u32[]{:S(2)}, u32[]{:S(2)}) collective-permute-start(bf16[80,256]{1,0:T(8,128)(2,1)S(1)} %add_convert_fusion.refs_8_), channel_id=1, source_target_pairs={{0,4},{1,5},{2,6},{3,7},{4,0},{5,1},{6,2},{7,3},{8,12},{9,13},{10,... | collective-permute-start | bytes 122888 | tf_op jit(solution)/shard_map/ppermute | solution.py:668
  98.5 1.4 collective-permute-start.37
  99.0 1.2 collective-permute-start.38
  99.1 1.3 collective-permute-start.39
  110.7 3.1 %collective-permute-start.40 = (bf16[4,4,320,128]{3,2,1,0:T(8,128)(2,1)S(1)}, bf16[4,4,320,128]{3,2,1,0:T(8,128)(2,1)S(1)}, u32[]{:S(2)}, u32[]{:S(2)}) collective-permute-start(bf16[4,4,320,128]{3,2,1,0:T(8,128)(2,1)S(1)} %get-tuple-element.132), channel_id=1, source_target_pairs={{0,4},{1,5},{2,6},{3,7},{4,0},{5,1},{6,2},{7,3},{8,12},{9,13},{10,... | collective-permute-start | bytes 3932168 | tf_op jit(solution)/shard_map/ppermute | solution.py:668
  114.4 19.2 %collective-permute-start.41 = (bf16[4,320,128]{2,1,0:T(8,128)(2,1)S(1)}, bf16[4,320,128]{2,1,0:T(8,128)(2,1)S(1)}, u32[]{:S(2)}, u32[]{:S(2)}) collective-permute-start(bf16[4,320,128]{2,1,0:T(8,128)(2,1)S(1)} %get-tuple-element.171), channel_id=1, source_target_pairs={{0,8},{1,9},{2,10},{3,11},{4,12},{5,13},{6,14},{7,15},{8,0},{9,1},... | collective-permute-start | bytes 983048 | tf_op jit(solution)/shard_map/ppermute | solution.py:668
  115.8 16.5 %collective-permute-start.43 = (bf16[4,320,128]{2,1,0:T(8,128)(2,1)S(1)}, bf16[4,320,128]{2,1,0:T(8,128)(2,1)S(1)}, u32[]{:S(2)}, u32[]{:S(2)}) collective-permute-start(bf16[4,320,128]{2,1,0:T(8,128)(2,1)S(1)} %get-tuple-element.169), channel_id=1, source_target_pairs={{0,24},{1,25},{2,26},{3,27},{4,28},{5,29},{6,30},{7,31},{8,16},{9,... | collective-permute-start | bytes 983048 | tf_op jit(solution)/shard_map/ppermute | solution.py:668
  117.1 16.4 %collective-permute-start.42 = (bf16[4,320,128]{2,1,0:T(8,128)(2,1)S(1)}, bf16[4,320,128]{2,1,0:T(8,128)(2,1)S(1)}, u32[]{:S(2)}, u32[]{:S(2)}) collective-permute-start(bf16[4,320,128]{2,1,0:T(8,128)(2,1)S(1)} %get-tuple-element.170), channel_id=1, source_target_pairs={{0,16},{1,17},{2,18},{3,19},{4,20},{5,21},{6,22},{7,23},{8,24},{9,... | collective-permute-start | bytes 983048 | tf_op jit(solution)/shard_map/ppermute | solution.py:668
  129.2 29.3 %copy-start.4 = (f32[128,2048]{1,0:T(8,128)S(1)}, f32[128,2048]{1,0:T(8,128)}, u32[]{:S(2)}) copy-start(f32[128,2048]{1,0:T(8,128)} %refs_11_.1) | copy-start | bytes 3145732
  129.2 29.3 %copy-start.5 = (f32[128,2048]{1,0:T(8,128)S(1)}, f32[128,2048]{1,0:T(8,128)}, u32[]{:S(2)}) copy-start(f32[128,2048]{1,0:T(8,128)} %refs_12_.1) | copy-start | bytes 3145732
  129.2 29.3 %copy-start.7 = (f32[128,512]{1,0:T(8,128)S(1)}, f32[128,512]{1,0:T(8,128)}, u32[]{:S(2)}) copy-start(f32[128,512]{1,0:T(8,128)} %refs_13_.1) | copy-start | bytes 786436
  129.2 29.3 %copy-start.8 = (f32[128,512]{1,0:T(8,128)S(1)}, f32[128,512]{1,0:T(8,128)}, u32[]{:S(2)}) copy-start(f32[128,512]{1,0:T(8,128)} %refs_14_.1) | copy-start | bytes 786436
  129.2 29.3 %copy-start.9 = (f32[128,512]{1,0:T(8,128)S(1)}, f32[128,512]{1,0:T(8,128)}, u32[]{:S(2)}) copy-start(f32[128,512]{1,0:T(8,128)} %refs_15_.1) | copy-start | bytes 786436
  129.2 29.3 %copy-start.11 = (f32[2,128]{1,0:T(2,128)S(1)}, f32[2,128]{1,0:T(2,128)}, u32[]{:S(2)}) copy-start(f32[2,128]{1,0:T(2,128)} %refs_16_.1) | copy-start | bytes 3076
  129.2 29.3 %copy-start.12 = (f32[2,128]{1,0:T(2,128)S(1)}, f32[2,128]{1,0:T(2,128)}, u32[]{:S(2)}) copy-start(f32[2,128]{1,0:T(2,128)} %refs_17_.1) | copy-start | bytes 3076
  133.8 7.1 %collective-permute-start.46 = (bf16[320,128]{1,0:T(8,128)(2,1)S(1)}, bf16[320,128]{1,0:T(8,128)(2,1)S(1)}, u32[]{:S(2)}, u32[]{:S(2)}) collective-permute-start(bf16[320,128]{1,0:T(8,128)(2,1)S(1)} %get-tuple-element.172), channel_id=1, source_target_pairs={{0,3},{1,2},{2,1},{3,0},{4,7},{5,6},{6,5},{7,4},{8,11},{9,10},{10,... | collective-permute-start | bytes 245768 | tf_op jit(solution)/shard_map/ppermute | solution.py:668
  135.8 7.5 %collective-permute-start.45 = (bf16[320,128]{1,0:T(8,128)(2,1)S(1)}, bf16[320,128]{1,0:T(8,128)(2,1)S(1)}, u32[]{:S(2)}, u32[]{:S(2)}) collective-permute-start(bf16[320,128]{1,0:T(8,128)(2,1)S(1)} %get-tuple-element.173), channel_id=1, source_target_pairs={{0,2},{1,3},{2,0},{3,1},{4,6},{5,7},{6,4},{7,5},{8,10},{9,11},{10,... | collective-permute-start | bytes 245768 | tf_op jit(solution)/shard_map/ppermute | solution.py:668
  136.3 7.0 %collective-permute-start.44 = (bf16[320,128]{1,0:T(8,128)(2,1)S(1)}, bf16[320,128]{1,0:T(8,128)(2,1)S(1)}, u32[]{:S(2)}, u32[]{:S(2)}) collective-permute-start(bf16[320,128]{1,0:T(8,128)(2,1)S(1)} %get-tuple-element.174), channel_id=1, source_target_pairs={{0,1},{1,0},{2,3},{3,2},{4,5},{5,4},{6,7},{7,6},{8,9},{9,8},{10,11... | collective-permute-start | bytes 245768 | tf_op jit(solution)/shard_map/ppermute | solution.py:668
  143.5 5.4 %collective-permute-start.49 = (f32[8,128]{1,0:T(8,128)S(1)}, f32[8,128]{1,0:T(8,128)S(1)}, u32[]{:S(2)}, u32[]{:S(2)}) collective-permute-start(f32[8,128]{1,0:T(8,128)S(1)} %get-tuple-element.142.refs_1_), channel_id=1, source_target_pairs={{0,3},{1,2},{2,1},{3,0},{4,7},{5,6},{6,5},{7,4},{8,11},{9,10},{10,... | collective-permute-start | bytes 12296 | tf_op jit(solution)/shard_map/ppermute | solution.py:668
  145.5 4.5 %collective-permute-start.48 = (f32[8,128]{1,0:T(8,128)S(1)}, f32[8,128]{1,0:T(8,128)S(1)}, u32[]{:S(2)}, u32[]{:S(2)}) collective-permute-start(f32[8,128]{1,0:T(8,128)S(1)} %get-tuple-element.142.refs_1_), channel_id=1, source_target_pairs={{0,2},{1,3},{2,0},{3,1},{4,6},{5,7},{6,4},{7,5},{8,10},{9,11},{10,... | collective-permute-start | bytes 12296 | tf_op jit(solution)/shard_map/ppermute | solution.py:668
  145.5 4.5 %collective-permute-start.47 = (f32[8,128]{1,0:T(8,128)S(1)}, f32[8,128]{1,0:T(8,128)S(1)}, u32[]{:S(2)}, u32[]{:S(2)}) collective-permute-start(f32[8,128]{1,0:T(8,128)S(1)} %get-tuple-element.142.refs_1_), channel_id=1, source_target_pairs={{0,1},{1,0},{2,3},{3,2},{4,5},{5,4},{6,7},{7,6},{8,9},{9,8},{10,11... | collective-permute-start | bytes 12296 | tf_op jit(solution)/shard_map/ppermute | solution.py:668
  150.0 5.5 %collective-permute-start.55 = (bf16[336,128]{1,0:T(8,128)(2,1)S(1)}, bf16[336,128]{1,0:T(8,128)(2,1)S(1)}, u32[]{:S(2)}, u32[]{:S(2)}) collective-permute-start(bf16[336,128]{1,0:T(8,128)(2,1)S(1)} %with_squares.1.refs_1_), channel_id=1, source_target_pairs={{0,24},{1,25},{2,26},{3,27},{4,28},{5,29},{6,30},{7,31},{8,16},{9,... | collective-permute-start | bytes 258056 | tf_op jit(solution)/shard_map/ppermute | solution.py:668
  151.6 4.8 %collective-permute-start.53 = (bf16[336,128]{1,0:T(8,128)(2,1)S(1)}, bf16[336,128]{1,0:T(8,128)(2,1)S(1)}, u32[]{:S(2)}, u32[]{:S(2)}) collective-permute-start(bf16[336,128]{1,0:T(8,128)(2,1)S(1)} %with_squares.1.refs_1_), channel_id=1, source_target_pairs={{0,16},{1,17},{2,18},{3,19},{4,20},{5,21},{6,22},{7,23},{8,24},{9,... | collective-permute-start | bytes 258056 | tf_op jit(solution)/shard_map/ppermute | solution.py:668
  152.7 4.5 %collective-permute-start.51 = (bf16[336,128]{1,0:T(8,128)(2,1)S(1)}, bf16[336,128]{1,0:T(8,128)(2,1)S(1)}, u32[]{:S(2)}, u32[]{:S(2)}) collective-permute-start(bf16[336,128]{1,0:T(8,128)(2,1)S(1)} %with_squares.1.refs_1_), channel_id=1, source_target_pairs={{0,8},{1,9},{2,10},{3,11},{4,12},{5,13},{6,14},{7,15},{8,0},{9,1},... | collective-permute-start | bytes 258056 | tf_op jit(solution)/shard_map/ppermute | solution.py:668
  153.6 3.7 %collective-permute-start.50 = (bf16[336,128]{1,0:T(8,128)(2,1)S(1)}, bf16[336,128]{1,0:T(8,128)(2,1)S(1)}, u32[]{:S(2)}, u32[]{:S(2)}) collective-permute-start(bf16[336,128]{1,0:T(8,128)(2,1)S(1)} %with_squares.1.refs_1_), channel_id=1, source_target_pairs={{0,4},{1,5},{2,6},{3,7},{4,0},{5,1},{6,2},{7,3},{8,12},{9,13},{10,... | collective-permute-start | bytes 258056 | tf_op jit(solution)/shard_map/ppermute | solution.py:668
  155.5 1.8 %collective-permute-start.56 = (bf16[336,128]{1,0:T(8,128)(2,1)S(1)}, bf16[336,128]{1,0:T(8,128)(2,1)S(1)}, u32[]{:S(2)}, u32[]{:S(2)}) collective-permute-start(bf16[336,128]{1,0:T(8,128)(2,1)S(1)} %collective-permute-done.55.refs_7_), channel_id=1, source_target_pairs={{0,4},{1,5},{2,6},{3,7},{4,0},{5,1},{6,2},{7,3},{8,12},{9,13},{10,... | collective-permute-start | bytes 258056 | tf_op jit(solution)/shard_map/ppermute | solution.py:668
  156.4 1.3 collective-permute-start.54
  157.2 1.3 collective-permute-start.52
  (8 other events, 89.2 us)

commit v3 on v2

--- a/solution.py
+++ b/solution.py
@@ -24,6 +24,7 @@
 fl_type = jnp.float32
 
 GROUPS = 2
+PAIRS = HEADS // 2
 CHUNKS = GROUPS * CLUSTERS
 PAD = 16
 
@@ -63,6 +64,8 @@
     def spec(array, kind):
         if kind == "smem":
             return smem()
+        if kind == "hbm":
+            return pl.BlockSpec(memory_space=pltpu.HBM)
         if isinstance(kind, pl.BlockSpec):
             return kind
         if piped and kind == "lane":
@@ -105,22 +108,36 @@
     return jax.ShapeDtypeStruct(shape, dtype)
 
 
-def prep_kernel(step, wp, wo, wn, message, other, query_all, stage):
+def fetch(copies):
+    copies = [pltpu.make_async_copy(*c) for c in copies]
+    for c in copies:
+        c.start()
+    return copies
+
+
+def prep_kernel(step, wp, wo, wn, key_message, key_other, message, query_all, block, rows, stage, sems):
     core = lax.bitwise_and(lax.axis_index("nodes"), 1)
     part = lax.bitwise_and(lax.axis_index("nodes"), 7)
     shard, width = wo.shape
-    stage[0:width] = wp[:, width : 2 * width].T.astype(bf_type)
-    stage[width : 2 * width] = wp[:, 2 * width : 3 * width].T.astype(bf_type)
-    query_all[0:width] = wp[:, 0:width].T.astype(bf_type)
-    query_all[width : 2 * width] = wp[:, 3 * width : 4 * width].T.astype(bf_type)
-    query_all[2 * width : 3 * width] = wo[...].T.astype(bf_type)
+    columns = [wp.at[:, i * width : (i + 1) * width] for i in (1, 2, 0, 3)]
+    sources = [*columns, wo]
+    copies = fetch(
+        [(sources[i], block.at[i], sems.at[i]) for i in range(5)] + [(wn, rows, sems.at[5])]
+    )
+    for i in range(2):
+        copies[i].wait()
+        stage[i] = block[i].T.astype(bf_type)
+    key_message[...] = stage[core]
+    key_other[...] = stage[1 - core]
+    for i in range(3):
+        copies[2 + i].wait()
+        query_all[i * width : (i + 1) * width] = block[2 + i].T.astype(bf_type)
+    copies[5].wait()
     rest = query_all.shape[0] - 3 * width
-    rows = jnp.concatenate([wn[...], jnp.zeros((rest - 2, shard), fl_type)], axis=0)
-    query_all[3 * width :] = rows.astype(bf_type)
-    message[0:width] = stage[pl.ds(pl.multiple_of(core * width, 16), width)]
-    other[...] = stage[pl.ds(pl.multiple_of((1 - core) * width, 16), width)]
+    tail = jnp.concatenate([rows[...], jnp.zeros((rest - 2, shard), fl_type)], axis=0)
+    query_all[3 * width :] = tail.astype(bf_type)
     height = query_all.shape[0] // 8
-    message[width:] = query_all[pl.ds(pl.multiple_of(part * height, 16), height)]
+    message[...] = query_all[pl.ds(pl.multiple_of(part * height, 16), height)]
 
 
 def members(ids_ref):
@@ -160,7 +177,7 @@
 
 def key_kernel(pieces, steps, step, place, x, ids, *refs):
     mine, other = refs[:pieces], refs[pieces : 2 * pieces]
-    sig_key, value_out, keep, send, weights, masked, keys, acc = refs[2 * pieces :]
+    key_slope, key_out, value_out, keep, send, weights, masked, acc = refs[2 * pieces :]
     core, node, count = place[0], place[1], place[3]
     width = x.shape[1]
     rows = x.shape[0]
@@ -179,14 +196,16 @@
     valid = valid_row(count, step * rows, rows)
     for g in range(GROUPS):
         sig = jax.nn.sigmoid(dot_nt(weights[g * half : (g + 1) * half, :], x[...]))
-        sig_key[g * half : (g + 1) * half, :] = sig
-        keys[...] = jnp.where(valid, sig, 0.0).astype(bf_type)
+        kept = jnp.where(valid, sig, 0.0)
+        key_slope[g * half : (g + 1) * half, :] = kept * (1.0 - sig)
+        keys = kept.astype(bf_type)
+        key_out[g * half : (g + 1) * half, :] = keys
         value = dot_nt(weights[width + g * half : width + (g + 1) * half, :], x[...]).astype(bf_type)
         value_out[g * half : (g + 1) * half, :] = value
         for c in range(CLUSTERS):
             masked[c * half : (c + 1) * half, :] = value * table[c : c + 1, :]
         masked[CLUSTERS * half :, :] = table
-        acc[g] += dot_nt(masked[...], keys[...])
+        acc[g] += dot_nt(masked[...], keys)
 
     @pl.when(step == steps - 1)
     def _():
@@ -198,23 +217,17 @@
 
 
 def weights_kernel(pieces, step, place, own, *refs):
-    near, far = refs[: 2 * (pieces - 1)], refs[2 * (pieces - 1) : 2 * (pieces - 1) + 6]
-    query_weight, gate_weight, out_weight, gain, shift, full_query, full_gate, stage = refs[2 * (pieces - 1) + 6 :]
+    stacks = refs[:8]
+    query_weight, gate_weight, out_weight, gain, shift, full_query, full_gate, stage = refs[8:]
     node, shard = place[1], place[2]
     width = out_weight.shape[0]
     span = own.shape[1]
     height = own.shape[0] // 8
-
-    def put(d, position, block):
+    stage[0] = own[...]
+    for position in range(8):
         where = pl.multiple_of(lax.bitwise_xor(node, position) * height, 16)
-        stage[d, pl.ds(where, height), :] = block
-
-    stage[0] = own[...]
-    for d in range(1, pieces):
-        for core in range(2):
-            put(d, core, near[core * (pieces - 1) + d - 1][width:])
-            for e in range(3):
-                put(d, 2 * (e + 1) + core, far[core * 3 + e][d - 1])
+        for d in range(1, pieces):
+            stage[d, pl.ds(where, height), :] = stacks[position][d - 1]
     norm_rows = []
     for z in range(pieces):
         where = lax.bitwise_xor(shard, z)
@@ -242,14 +255,16 @@
         full[:, z * span : (z + 1) * span] = stage[lax.bitwise_xor(place[2], z)]
 
 
-def query_kernel(step, place, x, weight, sig_query, query):
+def query_kernel(step, place, x, weight, query_slope, query):
     sig = jax.nn.sigmoid(dot_nt(weight[...], x[...]))
-    sig_query[...] = sig
+    query_slope[...] = sig * (1.0 - sig)
     query[...] = sig.astype(bf_type)
 
 
 def gate_kernel(step, place, x, weight, gate):
-    gate[...] = dot_nt(weight[...], x[...])
+    rows = x.shape[0]
+    valid = valid_row(place[3], step * rows, rows)
+    gate[...] = jnp.where(valid, dot_nt(weight[...], x[...]), 0.0)
 
 
 def grad_prod_kernel(step, place, g, out_weight, grad_prod):
@@ -262,6 +277,16 @@
     node = place[1]
     for d in range(CHUNKS):
         stage[lax.bitwise_xor(node, d)] = chunk_refs[d][...]
+
+
+def pair_rows(h, value):
+    lane_head = lax.broadcasted_iota(jnp.int32, (1, value.shape[1]), 1) // (value.shape[1] // 2)
+    return jnp.where(lane_head == h, value, jnp.zeros_like(value))
+
+
+def pair_block(chunk, p, head):
+    mine = chunk[:head, p * 2 * head : (p + 1) * 2 * head]
+    return jnp.concatenate([pair_rows(0, mine), pair_rows(1, mine)], axis=0)
 
 
 def head_rows(width, h, value):
@@ -289,12 +314,15 @@
         for g in range(GROUPS):
             for c in range(CLUSTERS):
                 chunk = stage[g * CLUSTERS + c].astype(fl_type)
-                cols = slice(c * half, (c + 1) * half)
-                for h in range(4):
-                    left[g, h * head : (h + 1) * head, cols] = head_rows(half, h, chunk[:head]).astype(bf_type)
-                sums = [head_rows(half, h, chunk[head : head + 1]) for h in range(4)]
-                sums.append(jnp.zeros((PAD - 4, half), fl_type))
-                left[g, half : half + PAD, cols] = jnp.concatenate(sums, axis=0).astype(bf_type)
+                cols = slice(c * 2 * head, (c + 1) * 2 * head)
+                for p in range(2):
+                    mine = chunk[:, p * 2 * head : (p + 1) * 2 * head]
+                    for h in range(2):
+                        at = slice(h * head, (h + 1) * head)
+                        left[g * 2 + p, at, cols] = pair_rows(h, mine[:head]).astype(bf_type)
+                    sums = [pair_rows(h, mine[head : head + 1]) for h in range(2)]
+                    sums.append(jnp.zeros((PAD - 2, 2 * head), fl_type))
+                    left[g * 2 + p, 2 * head :, cols] = jnp.concatenate(sums, axis=0).astype(bf_type)
         acc[...] = jnp.zeros_like(acc)
         dgain[...] = jnp.zeros_like(dgain)
         dshift[...] = jnp.zeros_like(dshift)
@@ -303,61 +331,63 @@
         cols = slice(part * lanes, (part + 1) * lanes)
         table = members(ids.at[:, cols])
         stack, num, den = stacks[part], nums[part], dens[part]
-        for g in range(GROUPS):
-            mine = query[g * half : (g + 1) * half, cols]
+        for p in range(PAIRS):
+            at = slice(p * 2 * head, (p + 1) * 2 * head)
+            mine = query[at, cols]
             for c in range(CLUSTERS):
-                stack[g, c * half : (c + 1) * half, :] = mine * table[c : c + 1, :]
-            both = dot_nn(left[g], stack[g])
-            num[g * half : (g + 1) * half, :] = both[:half]
-            den[g * 8 : g * 8 + 8, :] = 1.0 / both[half : half + 8]
+                stack[p, c * 2 * head : (c + 1) * 2 * head, :] = mine * table[c : c + 1, :]
+            both = dot_nn(left[p], stack[p])
+            num[at, :] = both[: 2 * head]
+            row = (p // 2) * 8 + (p % 2) * 2
+            den[row : row + 2, :] = 1.0 / both[2 * head : 2 * head + 2]
 
     def norm(part):
         cols = slice(part * lanes, (part + 1) * lanes)
-        num, normed, dnormed, den, dden = nums[part], normeds[part], dnormeds[part], dens[part], ddens[part]
-        valid = valid_row(count, step * rows + part * lanes, lanes)
-        total = jnp.zeros((8, lanes), fl_type)
+        num, dnormed, den, dden = nums[part], dnormeds[part], dens[part], ddens[part]
+        spans = [slice(h * head, (h + 1) * head) for h in range(HEADS)]
+        inverse = [den[(h // 4) * 8 + h % 4 : (h // 4) * 8 + h % 4 + 1, :] for h in range(HEADS)]
+
+        def mean_of(blocks):
+            return jnp.sum(tree_sum(blocks), axis=0, keepdims=True) * (1.0 / width)
+
+        mean = mean_of([fold_rows(num[spans[h], :]) * inverse[h] for h in range(HEADS)])
+        squares = []
         for h in range(HEADS):
-            span = slice(h * head, (h + 1) * head)
-            row = (h // 4) * 8 + h % 4
-            att = num[span, :] * den[row : row + 1, :]
-            num[span, :] = att
-            total = total + fold_rows(att)
-        mean = jnp.sum(total, axis=0, keepdims=True) * (1.0 / width)
-        total = jnp.zeros((8, lanes), fl_type)
+            centered = num[spans[h], :] * inverse[h] - mean
+            num[spans[h], :] = centered
+            squares.append(fold_rows(centered * centered))
+        scale = lax.rsqrt(mean_of(squares) + norm_eps)
+        first, second = [], []
         for h in range(HEADS):
-            centered = num[h * head : (h + 1) * head, :] - mean
-            total = total + fold_rows(centered * centered)
-        scale = lax.rsqrt(jnp.sum(total, axis=0, keepdims=True) * (1.0 / width) + norm_eps)
-        first = jnp.zeros((8, lanes), fl_type)
-        second = jnp.zeros((8, lanes), fl_type)
-        for h in range(HEADS):
-            span = slice(h * head, (h + 1) * head)
-            ah = (num[span, :] - mean) * scale
+            span = spans[h]
+            ah = num[span, :] * scale
+            num[span, :] = ah
             gamma = jnp.concatenate([gain[span, :]] * (lanes // 128), axis=1)
             beta = jnp.concatenate([shift[span, :]] * (lanes // 128), axis=1)
             u = ah * gamma + beta
             zg = gate[span, cols]
             dp = grad_prod[span, cols]
-            prod_out[span, cols] = jnp.where(valid, u * zg, 0.0).astype(bf_type)
+            prod_out[span, cols] = (u * zg).astype(bf_type)
             du = dp * zg
             dgate_out[span, cols] = (dp * u).astype(bf_type)
             du_ah = du * ah
             dgain[span, :] += fold_lanes(du_ah)
             dshift[span, :] += fold_lanes(du)
             dah = gamma * du
-            first = first + fold_rows(dah)
-            second = second + fold_rows(dah * ah)
-            normed[span, :] = ah
+            first.append(fold_rows(dah))
+            second.append(fold_rows(gamma * du_ah))
             dnormed[span, :] = dah
-        first = jnp.sum(first, axis=0, keepdims=True) * (1.0 / width)
-        second = jnp.sum(second, axis=0, keepdims=True) * (1.0 / width)
+        first = mean_of(first)
+        second = mean_of(second)
+        shifted = mean * scale
         for h in range(HEADS):
-            span = slice(h * head, (h + 1) * head)
+            span = spans[h]
+            ah = num[span, :]
+            rest = dnormed[span, :] - ah * second - first
+            dnum_out[span, cols] = (rest * (scale * inverse[h])).astype(bf_type)
+            inner = fold_rows(rest * ah) + shifted * fold_rows(rest)
             row = (h // 4) * 8 + h % 4
-            da = scale * (dnormed[span, :] - first - normed[span, :] * second)
-            inverse = den[row : row + 1, :]
-            dnum_out[span, cols] = (da * inverse).astype(bf_type)
-            dden[row : row + 1, :] = -jnp.sum(da * num[span, :], axis=0, keepdims=True) * inverse
+            dden[row : row + 1, :] = -jnp.sum(inner, axis=0, keepdims=True) * inverse[h]
         dden_out[:, cols] = dden[...]
 
     def backward(part):
@@ -428,10 +458,10 @@
                 send[slot, z] = block.astype(bf_type)
 
 
-def query_back_kernel(pieces, step, place, ids, dnum, dden, sig_query, x, *refs):
+def query_back_kernel(step, place, ids, dnum, dden, query_slope, *refs):
     chunk_refs = refs[:CHUNKS]
-    dquery_out, grad_out = refs[CHUNKS : CHUNKS + 2]
-    stage, left, sums, stack = refs[CHUNKS + 2 :]
+    dquery_out = refs[CHUNKS]
+    stage, left, sums, stack = refs[CHUNKS + 1 :]
     width, rows = dnum.shape
     half = width // GROUPS
     head = half // 4
@@ -442,26 +472,32 @@
         for gr in range(GROUPS):
             for c in range(CLUSTERS):
                 chunk = stage[gr * CLUSTERS + c].astype(fl_type)
-                block = jnp.concatenate([head_rows(half, h, chunk[:head]) for h in range(4)], axis=0)
-                left[gr, :, c * half : (c + 1) * half] = block.T.astype(bf_type)
+                for p in range(2):
+                    cols = slice(c * 2 * head, (c + 1) * 2 * head)
+                    left[gr * 2 + p, :, cols] = pair_block(chunk, p, head).T.astype(bf_type)
                 column = chunk[head : head + 8].T
                 sums[c, gr * half : (gr + 1) * half, :] = jnp.broadcast_to(column[:, 0:1], (half, 128))
-        grad_out[...] = jnp.zeros_like(grad_out)
 
     table = members(ids)
-    for gr in range(GROUPS):
-        part = dnum[gr * half : (gr + 1) * half, :]
+    for p in range(PAIRS):
+        part = dnum[p * 2 * head : (p + 1) * 2 * head, :]
         for c in range(CLUSTERS):
-            stack[c * half : (c + 1) * half, :] = part * table[c : c + 1, :]
-        dq = dot_nn(left[gr], stack[...])
-        for h in range(4):
-            at = slice(gr * half + h * head, gr * half + (h + 1) * head)
+            stack[p, c * 2 * head : (c + 1) * 2 * head, :] = part * table[c : c + 1, :]
+        dq = dot_nn(left[p], stack[p])
+        for h in range(2):
+            at = slice((p * 2 + h) * head, (p * 2 + h + 1) * head)
             pick = pick_rows(sums, at, ids, rows)
-            row = gr * 8 + h
+            row = (p // 2) * 8 + (p % 2) * 2 + h
             full = dq[h * head : (h + 1) * head] + dden[row : row + 1, :] * pick
-            sig = sig_query[at, :]
-            dquery_out[at, :] = (full * (sig * (1.0 - sig))).astype(bf_type)
-    grad_out[...] += dot_nn(dquery_out[...], x[...])
+            dquery_out[at, :] = (full * query_slope[at, :]).astype(bf_type)
+
+
+def grad_query_kernel(step, place, dquery, x, grad_query):
+    @pl.when(step == 0)
+    def _():
+        grad_query[...] = jnp.zeros_like(grad_query)
+
+    grad_query[...] += dot_nn(dquery[...], x[...])
 
 
 def gate_back_kernel(step, place, dgate, prod, x, g, grad_gate, grad_out):
@@ -493,10 +529,10 @@
     result[...] = x[...].astype(fl_type) + dot_tn(prod[...], out_weight[...])
 
 
-def key_back_kernel(pieces, steps, step, place, ids, sig_key, value, x, grad_query, grad_gate, grad_out, *refs):
+def key_back_kernel(pieces, steps, step, place, ids, key_slope, key, value, x, grad_query, grad_gate, grad_out, *refs):
     chunk_refs = refs[:CHUNKS]
     dkey_out, dvalue_out, norm_out, keep, send = refs[CHUNKS : CHUNKS + 5]
-    stage, left_key, left_value, sums, stack, acc = refs[CHUNKS + 5 :]
+    stage, left_key, left_value, sums, stack, key_stack, acc = refs[CHUNKS + 5 :]
     node, shard, count = place[1], place[2], place[3]
     width, rows = value.shape
     half = width // GROUPS
@@ -509,9 +545,11 @@
         for gr in range(GROUPS):
             for c in range(CLUSTERS):
                 chunk = stage[gr * CLUSTERS + c].astype(fl_type)
-                block = jnp.concatenate([head_rows(half, h, chunk[:head]) for h in range(4)], axis=0)
-                left_value[gr, :, c * half : (c + 1) * half] = block.astype(bf_type)
-                left_key[gr, :, c * half : (c + 1) * half] = block.T.astype(bf_type)
+                for p in range(2):
+                    cols = slice(c * 2 * head, (c + 1) * 2 * head)
+                    pair = pair_block(chunk, p, head)
+                    left_value[gr * 2 + p, :, cols] = pair.astype(bf_type)
+                    left_key[gr * 2 + p, :, cols] = pair.T.astype(bf_type)
                 column = chunk[head : head + 8].T
                 sums[c, gr * half : (gr + 1) * half, :] = jnp.broadcast_to(column[:, 0:1], (half, 128))
                 if c == 0:
@@ -520,21 +558,20 @@
 
     table = members(ids)
     valid = valid_row(count, step * rows, rows)
-    for gr in range(GROUPS):
-        at = slice(gr * half, (gr + 1) * half)
+    for p in range(PAIRS):
+        at = slice(p * 2 * head, (p + 1) * 2 * head)
         part = value[at, :]
         for c in range(CLUSTERS):
-            stack[c * half : (c + 1) * half, :] = part * table[c : c + 1, :]
-        dk = dot_nn(left_key[gr], stack[...])
-        for h in range(4):
-            sub = slice(gr * half + h * head, gr * half + (h + 1) * head)
+            stack[p, c * 2 * head : (c + 1) * 2 * head, :] = part * table[c : c + 1, :]
+        dk = dot_nn(left_key[p], stack[p])
+        for h in range(2):
+            sub = slice((p * 2 + h) * head, (p * 2 + h + 1) * head)
             full = dk[h * head : (h + 1) * head] + pick_rows(sums, sub, ids, rows)
-            sig = sig_key[sub, :]
-            dkey_out[sub, :] = jnp.where(valid, full * (sig * (1.0 - sig)), 0.0).astype(bf_type)
-        key = jnp.where(valid, sig_key[at, :], 0.0).astype(bf_type)
+            dkey_out[sub, :] = (full * key_slope[sub, :]).astype(bf_type)
+        part = key[at, :]
         for c in range(CLUSTERS):
-            stack[c * half : (c + 1) * half, :] = key * table[c : c + 1, :]
-        dvalue_out[at, :] = dot_nn(left_value[gr], stack[...]).astype(bf_type)
+            key_stack[p, c * 2 * head : (c + 1) * 2 * head, :] = part * table[c : c + 1, :]
+        dvalue_out[at, :] = dot_nn(left_value[p], key_stack[p]).astype(bf_type)
     acc[0:width] += dot_nn(dkey_out[...], x[...])
     acc[width : 2 * width] += dot_nn(dvalue_out[...], x[...])
 
@@ -567,26 +604,39 @@
 
 
 def finish_kernel(step, *refs):
-    parts, (sums, squares) = refs[:-2], refs[-2:]
-    value = tree_sum([p[...].astype(fl_type) for p in parts]).astype(bf_type)
-    sums[...] = value
-    value = value.astype(fl_type)
-    total = jnp.sum(value * value, axis=0, keepdims=True)
+    parts, sums = refs[:-1], refs[-1]
+    sums[...] = tree_sum([p[...].astype(fl_type) for p in parts]).astype(bf_type)
+
+
+def squares_kernel(step, *refs):
+    parts, squares = refs[:-1], refs[-1]
+    totals = []
+    for part in parts:
+        value = part[...].astype(fl_type)
+        totals.append(fold_rows(value * value))
+    total = jnp.sum(tree_sum(totals), axis=0, keepdims=True)
     squares[...] = jnp.broadcast_to(jnp.sum(total, axis=1, keepdims=True), squares.shape)
 
 
-def with_squares_kernel(count, step, *refs):
-    sums, squares, result = refs[0], refs[1 : 1 + count], refs[1 + count]
-    span = sums.shape[1]
-    result[0 : sums.shape[0]] = sums[...]
-    value = tree_sum([q[...] for q in squares])[:, :span]
-    high = value.astype(bf_type).astype(fl_type)
-    rest = value - high
-    middle = rest.astype(bf_type).astype(fl_type)
-    low = rest - middle
-    row = lax.broadcasted_iota(jnp.int32, value.shape, 0)
-    terms = jnp.where(row == 0, high, jnp.where(row == 1, middle, jnp.where(row == 2, low, 0.0)))
-    result[sums.shape[0] :] = jnp.concatenate([terms, jnp.zeros_like(terms)], axis=0).astype(bf_type)
+def assemble_kernel(step, place, *refs):
+    parts, (grad_proj, grad_out, stage) = refs[:CHUNKS], refs[CHUNKS:]
+    node = place[1]
+    span, width = grad_out.shape
+    tall = 2 * width // 8
+    lanes = width // 4
+    rows = span // 2
+    folds = lanes // span
+    for d in range(CHUNKS):
+        chunk = lax.bitwise_xor(node, d)
+        stage[chunk] = parts[d][...].astype(fl_type)
+    for chunk in range(CHUNKS):
+        query_at = (0 if chunk < 4 else 3 * width) + (chunk % 4) * tall
+        grad_proj[:, width + chunk * tall : width + (chunk + 1) * tall] = stage[chunk, 0:tall].T
+        grad_proj[:, query_at : query_at + tall] = stage[chunk, tall : 2 * tall].T
+        for i in range(folds):
+            at = slice((chunk // 2) * lanes + i * span, (chunk // 2) * lanes + (i + 1) * span)
+            block = stage[chunk, 2 * tall + i * rows : 2 * tall + (i + 1) * rows]
+            grad_out[(chunk % 2) * rows : (chunk % 2 + 1) * rows, at] = block
 
 
 def adam(master_w, moment_old, square_old, clipped, decay_coef, step_rate):
@@ -601,61 +651,55 @@
 
 
 def update_kernel(pieces, step, place, *refs):
-    parts, gn, pw, pm, ps, ow, om, osq, nw, nm, ns = refs[:CHUNKS], *refs[CHUNKS : CHUNKS + 10]
-    size, p_m, p_s, p_w, p_c, o_m, o_s, o_w, o_c, n_g, n_m, n_s, n_w = refs[CHUNKS + 10 : CHUNKS + 23]
-    stage, grad_out, factor = refs[CHUNKS + 23 :]
-    node, shard = place[1], place[2]
+    squares, (gp, go, gn, pw, pm, ps, ow, om, osq, nw, nm, ns) = refs[:pieces], refs[pieces : pieces + 12]
+    size, *results = refs[pieces + 12 : pieces + 25]
+    p_out, o_out, n_out = results[0:4], results[4:8], results[8:12]
+    new_p, new_pc, new_o, new_oc, new_n, sems = refs[pieces + 25 :]
+    shard = place[2]
     span, width = ow.shape
-    tall = 2 * width // 8
-
-    @pl.when(step == 0)
-    def _():
-        terms = []
-        lanes = width // 4
-        rows = span // 2
-        for d in range(CHUNKS):
-            chunk = lax.bitwise_xor(node, d)
-            part = parts[d]
-            stage[4 + chunk] = part[0:tall]
-            stage[jnp.where(chunk < 4, chunk, chunk + 8)] = part[tall : 2 * tall]
-            bottom = part[2 * tall : 2 * tall + rows * (lanes // span)].astype(fl_type)
-            tail = part[2 * tall + rows * (lanes // span) :].astype(fl_type)
-            terms.append((tail[2:3] + tail[1:2]) + tail[0:1])
-            row_start = pl.multiple_of(lax.bitwise_and(chunk, 1) * rows, 8)
-            quarter = lax.shift_right_logical(chunk, 1)
-            for q in range(4):
-
-                @pl.when(quarter == q)
-                def _():
-                    for i in range(lanes // span):
-                        at = slice(q * lanes + i * span, q * lanes + (i + 1) * span)
-                        grad_out[pl.ds(row_start, rows), at] = bottom[i * rows : (i + 1) * rows]
-
-        norm_grad = gn[1:3, :]
-        norm_square = jnp.sum(norm_grad * norm_grad, axis=0, keepdims=True)
-        total = tree_sum(terms)[:, 0:1] + jnp.sum(norm_square, axis=1, keepdims=True)
-        norm = jnp.sqrt(total)
-        size[...] = norm
-        clip_level = 0.5 * math.sqrt(5 * width * width + 2 * width)
-        scale = jnp.minimum(1.0, clip_level / norm)
-        factor[...] = jnp.broadcast_to(scale, factor.shape)
-        o_m[...], o_s[...], new = adam(ow[...], om[...], osq[...], grad_out[...] * scale, decay_rate, learn_rate)
-        o_w[...] = new
-        o_c[...] = new.astype(bf_type)
-        mine = norm_grad[:, 0:span]
-        for z in range(1, pieces):
-            mine = jnp.where(shard == z, norm_grad[:, z * span : (z + 1) * span], mine)
-        clipped = mine * scale
-        n_g[...] = clipped
-        n_m[...], n_s[...], n_w[...] = adam(nw[...], nm[...], ns[...], clipped, 0.0, norm_rate)
-
-    scale = factor[0:1, 0:1]
+    norm_grad = gn[1:3, :]
+    norm_square = jnp.sum(norm_grad * norm_grad, axis=0, keepdims=True)
+    total = tree_sum([q[0:1, 0:1] for q in squares]) + jnp.sum(norm_square, axis=1, keepdims=True)
+    norm = jnp.sqrt(total)
+    size[...] = norm
+    clip_level = 0.5 * math.sqrt(5 * width * width + 2 * width)
+    scale = jnp.minimum(1.0, clip_level / norm)
+    copies = []
+
+    def send(source, target):
+        copies.append(pltpu.make_async_copy(source, target, sems.at[len(copies)]))
+        copies[-1].start()
+
+    scale = jnp.broadcast_to(scale, (1, width))
+
+    def step_block(at, cols, w, m, s, grad, new, new_copy):
+        results = adam(w[at, cols], m[at, cols], s[at, cols], grad[at, cols] * scale, decay_rate, learn_rate)
+        for j, value in zip((2, 0, 1), (results[2], *results[:2])):
+            new[j, at, :] = value
+        new_copy[at, :] = results[2].astype(bf_type)
+
+    blocks = [slice(r, r + 16) for r in range(0, span, 16)]
     for i in range(4):
-        cols = slice(i * tall, (i + 1) * tall)
-        grad = stage[step * 4 + i].astype(fl_type).T * scale
-        p_m[:, cols], p_s[:, cols], new = adam(pw[:, cols], pm[:, cols], ps[:, cols], grad, decay_rate, learn_rate)
-        p_w[:, cols] = new
-        p_c[:, cols] = new.astype(bf_type)
+        cols = slice(i * width, (i + 1) * width)
+        for at in blocks:
+            step_block(at, cols, pw, pm, ps, gp, new_p.at[:, i], new_pc.at[i])
+        for j in range(3):
+            send(new_p.at[j, i], p_out[j].at[:, cols])
+        send(new_pc.at[i], p_out[3].at[:, cols])
+    for at in blocks:
+        step_block(at, slice(0, width), ow, om, osq, go, new_o, new_oc)
+    for j in range(3):
+        send(new_o.at[j], o_out[j])
+    send(new_oc, o_out[3])
+    mine = norm_grad[:, 0:span]
+    for z in range(1, pieces):
+        mine = jnp.where(shard == z, norm_grad[:, z * span : (z + 1) * span], mine)
+    clipped = mine * scale[:, 0:span]
+    for j, value in enumerate((clipped, *adam(nw[...], nm[...], ns[...], clipped, 0.0, norm_rate))):
+        new_n[j] = value
+        send(new_n.at[j], n_out[j])
+    for copy in copies:
+        copy.wait()
 
 
 def make_exchange(nodes, shards):
@@ -673,7 +717,8 @@
 def tree_sum(parts):
     parts = list(parts)
     while len(parts) > 1:
-        parts = [parts[i] + parts[i + 1] for i in range(0, len(parts), 2)]
+        pairs = [parts[i] + parts[i + 1] for i in range(0, len(parts) - 1, 2)]
+        parts = pairs + parts[len(parts) - len(parts) % 2 :]
     return parts[0]
 
 
@@ -697,7 +742,7 @@
     half = width // GROUPS
     head = width // HEADS
     span = pw.shape[0]
-    block = min(512, rows)
+    block = min(1024, rows)
     steps = rows // block
     lanes = 256
     tall = 2 * width // 8
@@ -716,26 +761,37 @@
     def vmem(shape, dtype):
         return pltpu.VMEM(shape, dtype)
 
-    message, kv_half, query_all = call(
+    message, kv_half, part, query_all = call(
         prep_kernel,
         1,
         (pw, ow, nw),
-        [None] * 3,
+        ["hbm"] * 3,
         [
-            out((width + part_rows, span), bf_type),
             out((width, span), bf_type),
+            out((width, span), bf_type),
+            out((part_rows, span), bf_type),
             out((8 * part_rows, span), bf_type),
         ],
-        [None] * 3,
-        [vmem((2 * width, span), bf_type)],
+        [None] * 4,
+        [
+            vmem((5, span, width), fl_type),
+            vmem((2, span), fl_type),
+            vmem((2, width, span), bf_type),
+            pltpu.SemaphoreType.DMA((6,)),
+        ],
         1e6,
         "prep",
+        vmem=60,
     )
     mine, other = [message], [kv_half]
     for z in range(1, shards):
         mine.append(exchange(message, 0, z))
+    stack = jnp.stack([exchange(part, 0, z) for z in range(1, shards)])
+    stacks = [stack] + [None] * 7
+    for e in range(1, 4):
+        stacks[2 * e] = exchange(stack, 2 * e, 0)
     for z in range(1, shards):
-        other.append(exchange(mine[z], 1, 0))
+        other.append(exchange(tie(mine[z], stack), 1, 0))
     x_turned = jnp.concatenate(
         [
             lax.dynamic_slice(x, (0, lax.bitwise_xor(shard, z) * span), (rows, span))
@@ -744,20 +800,19 @@
         axis=1,
     )
 
-    sig_key, value, keep, send = call(
+    key_slope, key, value, keep, send = call(
         functools.partial(key_kernel, shards, steps),
         steps,
         (place, x_turned, ids, *mine, *other),
         ["smem", "row", "lane"] + [None] * (2 * shards),
-        [wide(fl_type), wide(bf_type), out(chunk_shape, fl_type), out(chunk_shape, bf_type)],
-        ["lane", "lane", None, None],
+        [wide(fl_type), wide(bf_type), wide(bf_type), out(chunk_shape, fl_type), out(chunk_shape, bf_type)],
+        ["lane", "lane", "lane", None, None],
         [
             vmem((2 * width, width), bf_type),
             vmem((CLUSTERS * half + PAD, block), bf_type),
-            vmem((half, block), bf_type),
             vmem((GROUPS, CLUSTERS * half + PAD, half), fl_type),
         ],
-        4 * work,
+        1e3,
         "keys",
         block,
     )
@@ -800,8 +855,8 @@
         made["weights"] = call(
             functools.partial(weights_kernel, shards),
             1,
-            (tie(place, dep), query_all, *mine[1:], *other[1:], *far),
-            ["smem", None] + [None] * (2 * (shards - 1) + 6),
+            (tie(place, dep), query_all, *stacks),
+            ["smem", None] + [None] * 8,
             [
                 out((width, width), bf_type),
                 out((width, width), bf_type),
@@ -821,7 +876,7 @@
     def fill_query(dep):
         made["query"] = call(
             query_kernel,
-            steps,
+            1,
             (tie(place, dep), x_turned, made["weights"][0]),
             ["smem", "row", None],
             [wide(fl_type), wide(bf_type)],
@@ -829,8 +884,8 @@
             [],
             work,
             "query",
-            block,
-            vmem=12,
+            rows,
+            vmem=16,
         )
         return made["query"][1], fill_gate(dep)
 
@@ -838,7 +893,7 @@
         gate_weight = made["weights"][1]
         made["gate"] = call(
             gate_kernel,
-            steps,
+            1,
             (tie(place, dep), x_turned, gate_weight),
             ["smem", "row", None],
             [wide(fl_type)],
@@ -846,8 +901,8 @@
             [],
             work,
             "gate",
-            block,
-            vmem=12,
+            rows,
+            vmem=16,
         )[0]
         return made["gate"]
 
@@ -855,7 +910,7 @@
         out_weight = made["weights"][2]
         made["grad_prod"] = call(
             grad_prod_kernel,
-            steps,
+            1,
             (tie(place, dep), g, out_weight),
             ["smem", "row", None],
             [wide(fl_type)],
@@ -863,18 +918,17 @@
             [],
             work,
             "grad_prod",
-            block,
-            vmem=12,
+            rows,
+            vmem=16,
         )[0]
         return made["grad_prod"]
 
-    stack = jnp.stack([mine[z][width:] for z in range(1, shards)])
-    far = [exchange(stack, *at) for at in plane]
-    send = tie(send, *far)
-    far = far + [exchange(f, 1, 0) for f in far]
+    send = tie(send, *stacks[2::2])
+    for e in range(4):
+        stacks[2 * e + 1] = exchange(stacks[2 * e], 1, 0)
     chunks = reduce_chunks(keep, send, (fill_weights, fill_query, fill_grad_prod))
     out_weight, gain, shift, full_query, full_gate = made["weights"][2:]
-    sig_query, query = made["query"]
+    query_slope, query = made["query"]
 
     parts = block // lanes
     prod, dgate, dnum, dden, keep, send = call(
@@ -893,12 +947,12 @@
         ["lane", "lane", "lane", "lane", None, None],
         [
             vmem((CHUNKS, head + PAD, half), bf_type),
-            vmem((GROUPS, half + PAD, CLUSTERS * half), bf_type),
+            vmem((PAIRS, 2 * head + PAD, CLUSTERS * 2 * head), bf_type),
             vmem((GROUPS, CLUSTERS * half + 32, half), fl_type),
             vmem((width, 128), fl_type),
             vmem((width, 128), fl_type),
         ]
-        + [vmem((GROUPS, CLUSTERS * half, lanes), bf_type)] * parts
+        + [vmem((PAIRS, CLUSTERS * 2 * head, lanes), bf_type)] * parts
         + [vmem((GROUPS, CLUSTERS * half + 32, lanes), bf_type)] * parts
         + [vmem((width, lanes), fl_type)] * (3 * parts)
         + [vmem((16, lanes), fl_type)] * (2 * parts),
@@ -910,7 +964,7 @@
     def fill_gate_back(dep):
         made["gate_back"] = call(
             gate_back_kernel,
-            steps,
+            1,
             (tie(place, dep), dgate, prod, x_turned, g),
             ["smem", "lane", "lane", "row", "row"],
             [out((width, width), fl_type)] * 2,
@@ -918,8 +972,8 @@
             [],
             2 * work,
             "gate_back",
-            block,
-            vmem=12,
+            rows,
+            vmem=16,
         )
         return made["gate_back"][0]
 
@@ -940,35 +994,50 @@
         return made["output"]
 
     def fill_query_back(dep):
-        made["query_back"] = call(
-            functools.partial(query_back_kernel, shards),
+        made["dquery"] = call(
+            query_back_kernel,
             steps,
-            (tie(place, dep), ids, dnum, dden, sig_query, x_turned, *chunks),
-            ["smem", "lane", "lane", "lane", "lane", "row"] + [None] * CHUNKS,
-            [wide(bf_type), out((width, width), fl_type)],
-            ["lane", None],
+            (tie(place, dep), ids, dnum, dden, query_slope, *chunks),
+            ["smem", "lane", "lane", "lane", "lane"] + [None] * CHUNKS,
+            [wide(bf_type)],
+            ["lane"],
             [
                 vmem((CHUNKS, head + PAD, half), bf_type),
-                vmem((GROUPS, half, CLUSTERS * half), bf_type),
+                vmem((PAIRS, 2 * head, CLUSTERS * 2 * head), bf_type),
                 vmem((CLUSTERS, width, 128), fl_type),
-                vmem((CLUSTERS * half, block), bf_type),
+                vmem((PAIRS, CLUSTERS * 2 * head, block), bf_type),
             ],
-            3 * work,
+            2 * work,
             "query_back",
             block,
-        )
-        return made["query_back"][0]
-
-    back_chunks = reduce_chunks(keep, send, (fill_gate_back, None, fill_query_back))
-    dquery, grad_query = made["query_back"]
+        )[0]
+        return made["dquery"]
+
+    def fill_grad_query(dep):
+        made["grad_query"] = call(
+            grad_query_kernel,
+            1,
+            (tie(place, dep), made["dquery"], x_turned),
+            ["smem", None, None],
+            [out((width, width), fl_type)],
+            [None],
+            [],
+            work,
+            "grad_query",
+            vmem=12,
+        )[0]
+        return made["grad_query"]
+
+    back_chunks = reduce_chunks(keep, send, (fill_gate_back, fill_query_back, fill_grad_query))
+    dquery, grad_query = made["dquery"], made["grad_query"]
 
     height = 2 * tall + (span // 2) * (width // 4 // span)
     piece_shape = (4, shards, height, span)
     dkey, dvalue, norm_grad, keep, send = call(
         functools.partial(key_back_kernel, shards, steps),
         steps,
-        (place, ids, sig_key, value, x_turned, grad_query, *made["gate_back"], *back_chunks),
-        ["smem", "lane", "lane", "lane", "row"] + [None] * (3 + CHUNKS),
+        (place, ids, key_slope, key, value, x_turned, grad_query, *made["gate_back"], *back_chunks),
+        ["smem", "lane", "lane", "lane", "lane", "row"] + [None] * (3 + CHUNKS),
         [
             wide(bf_type),
             wide(bf_type),
@@ -979,10 +1048,11 @@
         ["lane", "lane", None, None, None],
         [
             vmem((CHUNKS, head + PAD, half), bf_type),
-            vmem((GROUPS, half, CLUSTERS * half), bf_type),
-            vmem((GROUPS, half, CLUSTERS * half), bf_type),
+            vmem((PAIRS, 2 * head, CLUSTERS * 2 * head), bf_type),
+            vmem((PAIRS, 2 * head, CLUSTERS * 2 * head), bf_type),
             vmem((CLUSTERS, width, 128), fl_type),
-            vmem((CLUSTERS * half, block), bf_type),
+            vmem((PAIRS, CLUSTERS * 2 * head, block), bf_type),
+            vmem((PAIRS, CLUSTERS * 2 * head, block), bf_type),
             vmem((2 * width, width), fl_type),
         ],
         6 * work,
@@ -1030,51 +1100,68 @@
         got = [own] + [exchange(own, 8 * o, 0) for o in range(1, outer)]
         owned_parts = [tree_sum(to_float(got))] + [jnp.zeros_like(own)] * (shards - 1)
 
-    sums, squares = call(
+    sums = call(
         finish_kernel,
         1,
         owned_parts,
         [None] * shards,
-        [out((height, span), bf_type), out((8, 128), fl_type)],
-        [None] * 2,
+        [out((height, span), bf_type)],
+        [None],
         [],
         1e6,
         "finish",
         vmem=4,
-    )
-    squares = [squares] + [exchange(squares, 0, z) for z in range(1, shards)]
-    owned = call(
-        functools.partial(with_squares_kernel, shards),
+    )[0]
+    parts = spread(sums)
+    squares = call(
+        squares_kernel,
         1,
-        (sums, *squares),
-        [None] * (1 + shards),
-        [out((height + 16, span), bf_type)],
+        parts,
+        [None] * CHUNKS,
+        [out((8, 128), fl_type)],
         [None],
         [],
         1e6,
-        "with_squares",
+        "squares",
         vmem=4,
     )[0]
-    parts = spread(owned)
+
+    def fill_assemble(dep):
+        made["grads"] = call(
+            assemble_kernel,
+            1,
+            (tie(place, dep), *parts),
+            ["smem"] + [None] * CHUNKS,
+            [out((span, 4 * width), fl_type), out((span, width), fl_type)],
+            [None] * 2,
+            [vmem((CHUNKS, height, span), fl_type)],
+            1e6,
+            "assemble",
+            vmem=8,
+        )
+        return made["grads"][0]
+
+    squares = [squares, *swap([squares] * (shards - 1), along, fill_assemble)]
     states = (pw, pm, ps, ow, om, osq, nw, nm, ns)
-    column = pl.BlockSpec((span, width), lambda i: (0, i))
     like = [pw] * 4 + [ow] * 4 + [nw] * 4
     kinds = [fl_type] * 3 + [bf_type] + [fl_type] * 3 + [bf_type] + [fl_type] * 4
     grad_size, *new = call(
         functools.partial(update_kernel, shards),
-        4,
-        (place, *parts, norm_grad, *states),
-        ["smem"] + [None] * (CHUNKS + 1) + [column] * 3 + [None] * 6,
+        1,
+        (place, *squares, *made["grads"], norm_grad, *states),
+        ["smem"] + [None] * (shards + 12),
         [out((1, 1), fl_type)] + [out(s.shape, k) for s, k in zip(like, kinds)],
-        [None] + [column] * 4 + [None] * 8,
+        [None] + ["hbm"] * 12,
         [
-            vmem((16, tall, span), bf_type),
-            vmem((span, width), fl_type),
-            vmem((8, 128), fl_type),
+            vmem((3, 4, span, width), fl_type),
+            vmem((4, span, width), bf_type),
+            vmem((3, span, width), fl_type),
+            vmem((span, width), bf_type),
+            vmem((4, 2, span), fl_type),
+            pltpu.SemaphoreType.DMA((24,)),
         ],
         1e6,
         "update",
-        piped=True,
     )
     return (made["output"], made["inputs"], grad_size.reshape(1), *new)
 

time: 163 us -> 151 us (0.926)
  waiting for transfers between devices: 39.5 us -> 31.3 us
  Pallas kernels: 63 us -> 57 us
  starting transfers between devices: 52.9 us -> 57.6 us
  local copies, waits for them, and re-layouts: 4.74 us -> 1.9 us
    ppermute x57 -> x61, waiting for transfers between devices: 39.5 us -> 31.3 us  [exchange(): return lax.ppermute(value, AXES, pairs)]
    pallas_call x16 -> x18, Pallas kernels: 63 us -> 57 us  [call(): pl.pallas_call(body, grid=(steps,) if piped else (), in_specs=specs[:len(...]
    ppermute x57 -> x61, starting transfers between devices: 52.9 us -> 57.6 us  [exchange(): return lax.ppermute(value, AXES, pairs)]
    unnamed x30, local copies, waits for them, and re-layouts: 2.91 us -> 0.08 us
  transfers between devices with their start and end apart: 57 -> 61, of which waited for: 30 -> 30; matrix products, arithmetic and copies ran while one was open for 1% -> 1% of each run, Pallas kernels for 22% -> 22%
where the time goes in v3:
time: 151 us
  starting transfers between devices  57.6 us (38%)
  Pallas kernels  57 us (38%)
  waiting for transfers between devices  31.3 us (21%)
  between operations  1.95 us (1%)
  local copies, waits for them, and re-layouts  1.9 us (1%)
    ppermute x61, starting transfers between devices, exchange(): return lax.ppermute(value, AXES, pairs)  57.6 us
    pallas_call x18, Pallas kernels, call(): pl.pallas_call(body, grid=(steps,) if piped else (), in_specs=specs[:len(...  57 us
    ppermute x61, waiting for transfers between devices, exchange(): return lax.ppermute(value, AXES, pairs)  31.3 us
  transfers between devices with their start and end apart: 61, of which 30 were waited for; matrix products, arithmetic and copies ran while one was open for 1% of the time, Pallas kernels for 22%

profile of v3, /device:TPU:0, one launch (start us, length us, event | category | flops | bytes accessed | tf_op | source)
XLA Modules:
  0.0 150.9 jit_solution(13121913171691388016)
XLA Ops:
  0.6 2.4 %prep.1 = (bf16[512,128]{1,0:T(8,128)(2,1)}, bf16[512,128]{1,0:T(8,128)(2,1)}, bf16[208,128]{1,0:T(8,128)(2,1)}, bf16[1664,128]{1,0:T(8,128)(2,1)}) custom-call(f32[128,2048]{1,0:T(8,128)} %refs_8_.3, f32[128,512]{1,0:T(8,128)} %refs_11_.1, f32[2,128]{1,0:T(2,128)} %refs_14_.1), custom_call_target="tpu_custom_call" | custom-call | flops 1000000 | bytes 2053120 | tf_op jit(solution)/shard_map/prep/pallas_call | solution.py:94
  3.1 5.1 %collective-permute-start.5 = (bf16[208,128]{1,0:T(8,128)(2,1)}, bf16[208,128]{1,0:T(8,128)(2,1)S(1)}, u32[]{:S(2)}, u32[]{:S(2)}) collective-permute-start(bf16[208,128]{1,0:T(8,128)(2,1)} %get-tuple-element.99), channel_id=1, source_target_pairs={{0,3},{1,2},{2,1},{3,0},{4,7},{5,6},{6,5},{7,4},{8,11},{9,10},{10,... | collective-permute-start | bytes 159752 | tf_op jit(solution)/shard_map/ppermute | solution.py:712
  8.2 0.6 collective-permute-start.3
  8.8 3.7 %collective-permute-start.2 = (bf16[512,128]{1,0:T(8,128)(2,1)}, bf16[512,128]{1,0:T(8,128)(2,1)S(1)}, u32[]{:S(2)}, u32[]{:S(2)}) collective-permute-start(bf16[512,128]{1,0:T(8,128)(2,1)} %get-tuple-element.97.refs_3_.refs_1_), channel_id=1, source_target_pairs={{0,3},{1,2},{2,1},{3,0},{4,7},{5,6},{6,5},{7,4},{8,11},{9,10},{10,... | collective-permute-start | bytes 393224 | tf_op jit(solution)/shard_map/ppermute | solution.py:712
  12.6 0.6 collective-permute-start
  13.2 5.0 %collective-permute-done.4 = bf16[208,128]{1,0:T(8,128)(2,1)S(1)} collective-permute-done((bf16[208,128]{1,0:T(8,128)(2,1)}, bf16[208,128]{1,0:T(8,128)(2,1)S(1)}, u32[]{:S(2)}, u32[]{:S(2)}) %collective-permute-start.4) | collective-permute-done | bytes 53280 | tf_op jit(solution)/shard_map/ppermute | solution.py:712
  18.3 1.7 %constant_dynamic-slice_fusion.3 = (bf16[2048,128]{1,0:T(8,128)(2,1)S(1)}, bf16[2048,128]{1,0:T(8,128)(2,1)S(1)}, bf16[2048,128]{1,0:T(8,128)(2,1)S(1)}, bf16[2048,128]{1,0:T(8,128)(2,1)S(1)}) fusion(bf16[2048,512]{1,0:T(8,128)(2,1)} %refs_1_.5, s32[]{:T(128)S(6)} %select_n.12, s32[]{:T(128)S(6)} %select_n.14, s32[]{:T(128)S(6)} %select_n.13, s32[]{:T(128)S(6)} %select_n.15), kind=kLoop, calls=%fused_computation.34 | loop fusion | bytes 4194320 | tf_op jit(solution)/shard_map/dynamic_slice | solution.py:797
  20.1 2.5 %collective-permute-start.11 = (bf16[3,208,128]{2,1,0:T(8,128)(2,1)S(1)}, bf16[3,208,128]{2,1,0:T(8,128)(2,1)S(1)}, u32[]{:S(2)}, u32[]{:S(2)}) collective-permute-start(bf16[3,208,128]{2,1,0:T(8,128)(2,1)S(1)} %pad_maximum_fusion.1.refs_2_), channel_id=1, source_target_pairs={{0,24},{1,25},{2,26},{3,27},{4,28},{5,29},{6,30},{7,31},{8,16},{9,... | collective-permute-start | bytes 479240 | tf_op jit(solution)/shard_map/ppermute | solution.py:712
  23.1 1.3 collective-permute-done.1.refs_5_.refs_3_
  24.4 1.5 collective-permute-start.9
  27.5 5.9 %keys.1 = (f32[512,2048]{1,0:T(8,128)S(1)}, bf16[512,2048]{1,0:T(8,128)(2,1)S(1)}, bf16[512,2048]{1,0:T(8,128)(2,1)S(1)}, f32[4,80,256]{2,1,0:T(8,128)S(1)}, bf16[4,80,256]{2,1,0:T(8,128)(2,1)S(1)}) custom-call(s32[4]{0:T(128)S(1)} %pad_add_fusion.refs_0_, bf16[2048,512]{1,0:T(8,128)(2,1)S(1)} %pad_maximum_fusion.refs_1_.refs_3_.refs_2_.refs_5_, ...), custom_call_target="tpu_custom_call" | custom-call | flops 1000 | bytes 12034064 | tf_op jit(solution)/shard_map/keys/pallas_call | solution.py:94
  34.9 1.6 %collective-permute-start.15 = (bf16[80,256]{1,0:T(8,128)(2,1)S(1)}, bf16[80,256]{1,0:T(8,128)(2,1)S(1)}, u32[]{:S(2)}, u32[]{:S(2)}) collective-permute-start(bf16[80,256]{1,0:T(8,128)(2,1)S(1)} %get-tuple-element.200), channel_id=1, source_target_pairs={{0,24},{1,25},{2,26},{3,27},{4,28},{5,29},{6,30},{7,31},{8,16},{9,... | collective-permute-start | bytes 122888 | tf_op jit(solution)/shard_map/ppermute | solution.py:712
  37.0 1.5 collective-permute-start.13
  38.5 1.8 %weights.1 = (bf16[512,512]{1,0:T(8,128)(2,1)S(1)}, bf16[512,512]{1,0:T(8,128)(2,1)S(1)}, bf16[512,512]{1,0:T(8,128)(2,1)S(1)}, f32[512,128]{1,0:T(8,128)S(1)}, ...) custom-call(s32[4]{0:T(128)S(1)} %pad_add_fusion.refs_0_, ...), custom_call_target="tpu_custom_call" | custom-call | flops 1000000 | bytes 4849680 | tf_op jit(solution)/shard_map/weights/pallas_call | solution.py:94
  41.0 2.7 %collective-permute-start.22 = (bf16[80,256]{1,0:T(8,128)(2,1)S(1)}, bf16[80,256]{1,0:T(8,128)(2,1)S(1)}, u32[]{:S(2)}, u32[]{:S(2)}) collective-permute-start(bf16[80,256]{1,0:T(8,128)(2,1)S(1)} %fusion.7), channel_id=1, source_target_pairs={{0,3},{1,2},{2,1},{3,0},{4,7},{5,6},{6,5},{7,4},{8,11},{9,10},{10,... | collective-permute-start | bytes 122888 | tf_op jit(solution)/shard_map/ppermute | solution.py:712
  43.7 2.2 %collective-permute-start.21 = (bf16[80,256]{1,0:T(8,128)(2,1)S(1)}, bf16[80,256]{1,0:T(8,128)(2,1)S(1)}, u32[]{:S(2)}, u32[]{:S(2)}) collective-permute-start(bf16[80,256]{1,0:T(8,128)(2,1)S(1)} %fusion.7), channel_id=1, source_target_pairs={{0,2},{1,3},{2,0},{3,1},{4,6},{5,7},{6,4},{7,5},{8,10},{9,11},{10,... | collective-permute-start | bytes 122888 | tf_op jit(solution)/shard_map/ppermute | solution.py:712
  45.9 1.9 %query.1 = (f32[512,2048]{1,0:T(8,128)S(1)}, bf16[512,2048]{1,0:T(8,128)(2,1)S(1)}) custom-call(s32[4]{0:T(128)S(1)} %pad_add_fusion.refs_0_, bf16[2048,512]{1,0:T(8,128)(2,1)S(1)} %pad_maximum_fusion.refs_1_.refs_3_.refs_2_.refs_5_, bf16[512,512]{1,0:T(8,128)(2,1)S(1)} %get-tuple-element.111.refs_2_), custom_call_target="tpu_custom_call" | custom-call | flops 1073741824 | bytes 8912912 | tf_op jit(solution)/shard_map/query/pallas_call | solution.py:94
  47.9 1.9 %gate.1.refs_3_ = f32[512,2048]{1,0:T(8,128)S(1)} custom-call(s32[4]{0:T(128)S(1)} %pad_add_fusion.refs_0_, bf16[2048,512]{1,0:T(8,128)(2,1)S(1)} %pad_maximum_fusion.refs_1_.refs_3_.refs_2_.refs_5_, bf16[512,512]{1,0:T(8,128)(2,1)S(1)} %get-tuple-element.117.refs_2_), custom_call_target="tpu_custom_call" | custom-call | flops 1073741824 | bytes 6815760 | tf_op jit(solution)/shard_map/gate/pallas_call | solution.py:94
  50.0 1.9 %collective-permute-start.26 = (bf16[80,256]{1,0:T(8,128)(2,1)S(1)}, bf16[80,256]{1,0:T(8,128)(2,1)S(1)}, u32[]{:S(2)}, u32[]{:S(2)}) collective-permute-start(bf16[80,256]{1,0:T(8,128)(2,1)S(1)} %add_convert_fusion.1.refs_7_.refs_5_), channel_id=1, source_target_pairs={{0,24},{1,25},{2,26},{3,27},{4,28},{5,29},{6,30},{7,31},{8,16},{9,... | collective-permute-start | bytes 122888 | tf_op jit(solution)/shard_map/ppermute | solution.py:712
  52.4 1.1 collective-permute-start.24
  53.5 1.8 %grad_prod.1.refs_4_ = f32[512,2048]{1,0:T(8,128)S(1)} custom-call(s32[4]{0:T(128)S(1)} %pad_add_fusion.refs_0_, bf16[2048,512]{1,0:T(8,128)(2,1)S(1)} %copy-done, bf16[512,512]{1,0:T(8,128)(2,1)S(1)} %get-tuple-element.122.refs_2_.refs_3_), custom_call_target="tpu_custom_call" | custom-call | flops 1073741824 | bytes 6815760 | tf_op jit(solution)/shard_map/grad_prod/pallas_call | solution.py:94
  56.9 0.7 collective-permute-done.27.refs_10_.refs_8_
  58.1 9.5 %middle.1 = (bf16[512,2048]{1,0:T(8,128)(2,1)S(1)}, bf16[512,2048]{1,0:T(8,128)(2,1)S(1)}, bf16[512,2048]{1,0:T(8,128)(2,1)S(1)}, f32[16,2048]{1,0:T(8,128)S(1)}...) custom-call(s32[4]{0:T(128)S(1)} %pad_add_fusion.refs_0_, s32[1,2048]{1,0:T(1,128)S(1)} %bitcast.58, ...), custom_call_target="tpu_custom_call" | custom-call | flops 6442450944 | bytes 18259984 | tf_op jit(solution)/shard_map/middle/pallas_call | solution.py:94
  67.9 1.2 collective-permute-done.30
  69.2 1.2 collective-permute-start.31
  70.4 1.8 %collective-permute-start.33 = (bf16[80,256]{1,0:T(8,128)(2,1)S(1)}, bf16[80,256]{1,0:T(8,128)(2,1)S(1)}, u32[]{:S(2)}, u32[]{:S(2)}) collective-permute-start(bf16[80,256]{1,0:T(8,128)(2,1)S(1)} %get-tuple-element.197), channel_id=1, source_target_pairs={{0,24},{1,25},{2,26},{3,27},{4,28},{5,29},{6,30},{7,31},{8,16},{9,... | collective-permute-start | bytes 122888 | tf_op jit(solution)/shard_map/ppermute | solution.py:712
  72.7 2.9 %gate_back.1 = (f32[512,512]{1,0:T(8,128)S(1)}, f32[512,512]{1,0:T(8,128)S(1)}) custom-call(s32[4]{0:T(128)S(1)} %pad_add_fusion.refs_0_, bf16[512,2048]{1,0:T(8,128)(2,1)S(1)} %get-tuple-element.131.refs_1_.refs_4_, bf16[512,2048]{1,0:T(8,128)(2,1)S(1)} %get-tuple-element.132.refs_2_, bf16[2048,512]{1,0:T(8,128)(2,1)S(1)} %pad_maximum_fusion.refs_1_.refs_3_.refs_2_.refs_5_, ...), custom_call_target="tpu_custom_call" | custom-call | flops 2147483648 | bytes 10485776 | tf_op jit(solution)/shard_map/gate_back/pallas_call | solution.py:94
  75.6 0.6 collective-permute-done.32
  76.2 2.7 %collective-permute-start.36 = (bf16[80,256]{1,0:T(8,128)(2,1)S(1)}, bf16[80,256]{1,0:T(8,128)(2,1)S(1)}, u32[]{:S(2)}, u32[]{:S(2)}) collective-permute-start(bf16[80,256]{1,0:T(8,128)(2,1)S(1)} %fusion.4), channel_id=1, source_target_pairs={{0,3},{1,2},{2,1},{3,0},{4,7},{5,6},{6,5},{7,4},{8,11},{9,10},{10,... | collective-permute-start | bytes 122888 | tf_op jit(solution)/shard_map/ppermute | solution.py:712
  79.3 1.4 collective-permute-start.34
  80.7 3.4 %query_back.1.refs_1_ = bf16[512,2048]{1,0:T(8,128)(2,1)S(1)} custom-call(s32[4]{0:T(128)S(1)} %pad_add_fusion.refs_0_, s32[1,2048]{1,0:T(1,128)S(1)} %bitcast.59, bf16[512,2048]{1,0:T(8,128)(2,1)S(1)} %get-tuple-element.138.refs_2_, f32[16,2048]{1,0:T(8,128)S(1)} %get-tuple-element.139.refs_3_, f32[512,2048]{1,0:T(8,128)S(1)} %get-tuple-element.140.refs_4_, ...), custom_call_target="tpu_custom_call" | custom-call | flops 2147483648 | bytes 8855568 | tf_op jit(solution)/shard_map/query_back/pallas_call | solution.py:94
  84.1 1.6 %collective-permute-start.40 = (bf16[80,256]{1,0:T(8,128)(2,1)S(1)}, bf16[80,256]{1,0:T(8,128)(2,1)S(1)}, u32[]{:S(2)}, u32[]{:S(2)}) collective-permute-start(bf16[80,256]{1,0:T(8,128)(2,1)S(1)} %add_convert_fusion.refs_9_), channel_id=1, source_target_pairs={{0,24},{1,25},{2,26},{3,27},{4,28},{5,29},{6,30},{7,31},{8,16},{9,... | collective-permute-start | bytes 122888 | tf_op jit(solution)/shard_map/ppermute | solution.py:712
  85.7 1.1 collective-permute-start.39
  86.8 0.9 collective-permute-start.38
  87.7 1.8 %grad_query.1.refs_6_ = f32[512,512]{1,0:T(8,128)S(1)} custom-call(s32[4]{0:T(128)S(1)} %pad_add_fusion.refs_0_, bf16[512,2048]{1,0:T(8,128)(2,1)S(1)} %query_back.1.refs_1_, bf16[2048,512]{1,0:T(8,128)(2,1)S(1)} %pad_maximum_fusion.refs_1_.refs_3_.refs_2_.refs_5_), custom_call_target="tpu_custom_call" | custom-call | flops 1073741824 | bytes 5242896 | tf_op jit(solution)/shard_map/grad_query/pallas_call | solution.py:94
  89.7 1.1 collective-permute-done.38.refs_11_
  91.3 0.7 collective-permute-done.41.refs_12_
  92.5 7.5 %key_back.1 = (bf16[512,2048]{1,0:T(8,128)(2,1)S(1)}, bf16[512,2048]{1,0:T(8,128)(2,1)S(1)}, f32[8,512]{1,0:T(8,128)S(1)}, f32[4,4,320,128]{3,2,1,0:T(8,128)S(1)}, bf16[4,4,320,128]{3,2,1,0:T(8,128)(2,1)S(1)}) custom-call(s32[4]{0:T(128)S(1)} %pad_add_fusion.refs_0_, s32[1,2048]{1,0:T(1,128)S(1)} %bitcast.60, f32[512,2048]{1,0:T(8,128)S(1)} %get-tuple-element.103.refs_2_, ...), custom_call_target="tpu_custom_call" | custom-call | flops 6442450944 | bytes 22110224 | tf_op jit(solution)/shard_map/key_back/pallas_call | solution.py:94
  100.3 0.8 key_weights.1.refs_6_
  101.1 2.1 %collective-permute-done.44 = bf16[4,4,320,128]{3,2,1,0:T(8,128)(2,1)S(1)} collective-permute-done((bf16[4,4,320,128]{3,2,1,0:T(8,128)(2,1)S(1)}, bf16[4,4,320,128]{3,2,1,0:T(8,128)(2,1)S(1)}, u32[]{:S(2)}, u32[]{:S(2)}) %collective-permute-start.44) | collective-permute-done | bytes 1310752 | tf_op jit(solution)/shard_map/ppermute | solution.py:712
  103.8 0.9 collective-permute-start.45
  104.7 1.5 %collective-permute-start.47 = (bf16[4,320,128]{2,1,0:T(8,128)(2,1)S(1)}, bf16[4,320,128]{2,1,0:T(8,128)(2,1)S(1)}, u32[]{:S(2)}, u32[]{:S(2)}) collective-permute-start(bf16[4,320,128]{2,1,0:T(8,128)(2,1)S(1)} %get-tuple-element.191), channel_id=1, source_target_pairs={{0,24},{1,25},{2,26},{3,27},{4,28},{5,29},{6,30},{7,31},{8,16},{9,... | collective-permute-start | bytes 983048 | tf_op jit(solution)/shard_map/ppermute | solution.py:712
  106.2 1.1 collective-permute-start.46
  107.3 3.5 %output.1 = f32[2048,512]{1,0:T(8,128)} custom-call(s32[4]{0:T(128)S(1)} %pad_add_fusion.refs_0_, bf16[2048,512]{1,0:T(8,128)(2,1)S(1)} %copy-done.1, bf16[512,2048]{1,0:T(8,128)(2,1)S(1)} %get-tuple-element.132.refs_2_, bf16[512,512]{1,0:T(8,128)(2,1)S(1)} %get-tuple-element.122.refs_2_.refs_3_), custom_call_target="tpu_custom_call" | custom-call | flops 1073741824 | bytes 8912912 | tf_op jit(solution)/shard_map/output/pallas_call | solution.py:94
  110.8 6.9 %inputs.1 = f32[2048,512]{1,0:T(8,128)} custom-call(s32[4]{0:T(128)S(1)} %pad_add_fusion.refs_0_, bf16[512,2048]{1,0:T(8,128)(2,1)S(1)} %query_back.1.refs_1_, bf16[512,2048]{1,0:T(8,128)(2,1)S(1)} %get-tuple-element.152.refs_2_, bf16[512,2048]{1,0:T(8,128)(2,1)S(1)} %get-tuple-element.153.refs_3_, bf16[512,2048]{1,0:T(8,128)(2,1)S(1)} %get-tuple-element.131.refs_1_.refs_4_, ...), custom_call_target="tpu_custom_call" | custom-call | flops 4294967296 | bytes 16777232 | tf_op jit(solution)/shard_map/inputs/pallas_call | solution.py:94
  117.7 3.4 %collective-permute-done.47 = bf16[4,320,128]{2,1,0:T(8,128)(2,1)S(1)} collective-permute-done((bf16[4,320,128]{2,1,0:T(8,128)(2,1)S(1)}, bf16[4,320,128]{2,1,0:T(8,128)(2,1)S(1)}, u32[]{:S(2)}, u32[]{:S(2)}) %collective-permute-start.47) | collective-permute-done | bytes 327712 | tf_op jit(solution)/shard_map/ppermute | solution.py:712
  121.1 1.4 collective-permute-done.46
  122.7 2.4 %collective-permute-start.50 = (bf16[320,128]{1,0:T(8,128)(2,1)S(1)}, bf16[320,128]{1,0:T(8,128)(2,1)S(1)}, u32[]{:S(2)}, u32[]{:S(2)}) collective-permute-start(bf16[320,128]{1,0:T(8,128)(2,1)S(1)} %get-tuple-element.194), channel_id=1, source_target_pairs={{0,3},{1,2},{2,1},{3,0},{4,7},{5,6},{6,5},{7,4},{8,11},{9,10},{10,... | collective-permute-start | bytes 245768 | tf_op jit(solution)/shard_map/ppermute | solution.py:712
  125.2 2.0 %collective-permute-start.48 = (bf16[320,128]{1,0:T(8,128)(2,1)S(1)}, bf16[320,128]{1,0:T(8,128)(2,1)S(1)}, u32[]{:S(2)}, u32[]{:S(2)}) collective-permute-start(bf16[320,128]{1,0:T(8,128)(2,1)S(1)} %get-tuple-element.196), channel_id=1, source_target_pairs={{0,1},{1,0},{2,3},{3,2},{4,5},{5,4},{6,7},{7,6},{8,9},{9,8},{10,11... | collective-permute-start | bytes 245768 | tf_op jit(solution)/shard_map/ppermute | solution.py:712
  127.2 2.1 %collective-permute-done.50.refs_3_ = bf16[320,128]{1,0:T(8,128)(2,1)S(1)} collective-permute-done((bf16[320,128]{1,0:T(8,128)(2,1)S(1)}, bf16[320,128]{1,0:T(8,128)(2,1)S(1)}, u32[]{:S(2)}, u32[]{:S(2)}) %collective-permute-start.50) | collective-permute-done | bytes 81952 | tf_op jit(solution)/shard_map/ppermute | solution.py:712
  129.3 1.9 %collective-permute-done.49.refs_2_ = bf16[320,128]{1,0:T(8,128)(2,1)S(1)} collective-permute-done((bf16[320,128]{1,0:T(8,128)(2,1)S(1)}, bf16[320,128]{1,0:T(8,128)(2,1)S(1)}, u32[]{:S(2)}, u32[]{:S(2)}) %collective-permute-start.49) | collective-permute-done | bytes 81952 | tf_op jit(solution)/shard_map/ppermute | solution.py:712
  131.3 1.5 collective-permute-start.56
  132.8 0.9 collective-permute-start.54
  133.8 1.1 collective-permute-start.52
  134.9 1.9 %collective-permute-done.56.refs_6_.refs_7_ = bf16[320,128]{1,0:T(8,128)(2,1)S(1)} collective-permute-done((bf16[320,128]{1,0:T(8,128)(2,1)S(1)}, bf16[320,128]{1,0:T(8,128)(2,1)S(1)}, u32[]{:S(2)}, u32[]{:S(2)}) %collective-permute-start.56) | collective-permute-done | bytes 81952 | tf_op jit(solution)/shard_map/ppermute | solution.py:712
  136.8 0.8 collective-permute-done.54.refs_4_.refs_5_
  137.6 0.6 collective-permute-done.52.refs_2_.refs_3_
  138.2 0.7 collective-permute-done.55.refs_5_.refs_6_
  138.9 0.6 collective-permute-done.53.refs_3_.refs_4_
  139.7 2.6 %collective-permute-start.60 = (f32[8,128]{1,0:T(8,128)S(1)}, f32[8,128]{1,0:T(8,128)S(1)}, u32[]{:S(2)}, u32[]{:S(2)}) collective-permute-start(f32[8,128]{1,0:T(8,128)S(1)} %squares.1.refs_1_), channel_id=1, source_target_pairs={{0,3},{1,2},{2,1},{3,0},{4,7},{5,6},{6,5},{7,4},{8,11},{9,10},{10,... | collective-permute-start | bytes 12296 | tf_op jit(solution)/shard_map/ppermute | solution.py:712
  142.3 1.8 %collective-permute-start.58 = (f32[8,128]{1,0:T(8,128)S(1)}, f32[8,128]{1,0:T(8,128)S(1)}, u32[]{:S(2)}, u32[]{:S(2)}) collective-permute-start(f32[8,128]{1,0:T(8,128)S(1)} %squares.1.refs_1_), channel_id=1, source_target_pairs={{0,1},{1,0},{2,3},{3,2},{4,5},{5,4},{6,7},{7,6},{8,9},{9,8},{10,11... | collective-permute-start | bytes 12296 | tf_op jit(solution)/shard_map/ppermute | solution.py:712
  144.1 1.0 assemble.1
  145.1 1.7 %collective-permute-done.59.refs_3_ = f32[8,128]{1,0:T(8,128)S(1)} collective-permute-done((f32[8,128]{1,0:T(8,128)S(1)}, f32[8,128]{1,0:T(8,128)S(1)}, u32[]{:S(2)}, u32[]{:S(2)}) %collective-permute-start.59) | collective-permute-done | bytes 4128 | tf_op jit(solution)/shard_map/ppermute | solution.py:712
  146.9 3.8 %update.1 = (f32[1,1]{1,0:T(1,128)}, f32[128,2048]{1,0:T(8,128)}, f32[128,2048]{1,0:T(8,128)}, f32[128,2048]{1,0:T(8,128)}, bf16[128,2048]{1,0:T(8,128)(2,1)}, /...) custom-call(s32[4]{0:T(128)S(1)} %pad_add_fusion.refs_0_, ...), custom_call_target="tpu_custom_call" | custom-call | flops 1000000 | bytes 9870356 | tf_op jit(solution)/shard_map/update/pallas_call | solution.py:94
  (123 shorter events, 10.9 us)
Async XLA Ops:
  3.1 9.5 %collective-permute-start.5 = (bf16[208,128]{1,0:T(8,128)(2,1)}, bf16[208,128]{1,0:T(8,128)(2,1)S(1)}, u32[]{:S(2)}, u32[]{:S(2)}) collective-permute-start(bf16[208,128]{1,0:T(8,128)(2,1)} %get-tuple-element.99), channel_id=1, source_target_pairs={{0,3},{1,2},{2,1},{3,0},{4,7},{5,6},{6,5},{7,4},{8,11},{9,10},{10,... | collective-permute-start | bytes 159752 | tf_op jit(solution)/shard_map/ppermute | solution.py:712
  8.2 10.0 %collective-permute-start.4 = (bf16[208,128]{1,0:T(8,128)(2,1)}, bf16[208,128]{1,0:T(8,128)(2,1)S(1)}, u32[]{:S(2)}, u32[]{:S(2)}) collective-permute-start(bf16[208,128]{1,0:T(8,128)(2,1)} %get-tuple-element.99), channel_id=1, source_target_pairs={{0,2},{1,3},{2,0},{3,1},{4,6},{5,7},{6,4},{7,5},{8,10},{9,11},{10,... | collective-permute-start | bytes 159752 | tf_op jit(solution)/shard_map/ppermute | solution.py:712
  8.2 10.0 %collective-permute-start.3 = (bf16[208,128]{1,0:T(8,128)(2,1)}, bf16[208,128]{1,0:T(8,128)(2,1)S(1)}, u32[]{:S(2)}, u32[]{:S(2)}) collective-permute-start(bf16[208,128]{1,0:T(8,128)(2,1)} %get-tuple-element.99), channel_id=1, source_target_pairs={{0,1},{1,0},{2,3},{3,2},{4,5},{5,4},{6,7},{7,6},{8,9},{9,8},{10,11... | collective-permute-start | bytes 159752 | tf_op jit(solution)/shard_map/ppermute | solution.py:712
  8.8 9.5 %collective-permute-start.2 = (bf16[512,128]{1,0:T(8,128)(2,1)}, bf16[512,128]{1,0:T(8,128)(2,1)S(1)}, u32[]{:S(2)}, u32[]{:S(2)}) collective-permute-start(bf16[512,128]{1,0:T(8,128)(2,1)} %get-tuple-element.97.refs_3_.refs_1_), channel_id=1, source_target_pairs={{0,3},{1,2},{2,1},{3,0},{4,7},{5,6},{6,5},{7,4},{8,11},{9,10},{10,... | collective-permute-start | bytes 393224 | tf_op jit(solution)/shard_map/ppermute | solution.py:712
  12.6 11.8 %collective-permute-start.1 = (bf16[512,128]{1,0:T(8,128)(2,1)}, bf16[512,128]{1,0:T(8,128)(2,1)S(1)}, u32[]{:S(2)}, u32[]{:S(2)}) collective-permute-start(bf16[512,128]{1,0:T(8,128)(2,1)} %get-tuple-element.97.refs_3_.refs_1_), channel_id=1, source_target_pairs={{0,2},{1,3},{2,0},{3,1},{4,6},{5,7},{6,4},{7,5},{8,10},{9,11},{10,... | collective-permute-start | bytes 393224 | tf_op jit(solution)/shard_map/ppermute | solution.py:712
  12.6 13.3 %collective-permute-start = (bf16[512,128]{1,0:T(8,128)(2,1)}, bf16[512,128]{1,0:T(8,128)(2,1)S(1)}, u32[]{:S(2)}, u32[]{:S(2)}) collective-permute-start(bf16[512,128]{1,0:T(8,128)(2,1)} %get-tuple-element.97.refs_3_.refs_1_), channel_id=1, source_target_pairs={{0,1},{1,0},{2,3},{3,2},{4,5},{5,4},{6,7},{7,6},{8,9},{9,8},{10,11... | collective-permute-start | bytes 393224 | tf_op jit(solution)/shard_map/ppermute | solution.py:712
  18.3 7.6 %collective-permute-start.8 = (bf16[512,128]{1,0:T(8,128)(2,1)S(1)}, bf16[512,128]{1,0:T(8,128)(2,1)S(1)}, u32[]{:S(2)}, u32[]{:S(2)}) collective-permute-start(bf16[512,128]{1,0:T(8,128)(2,1)S(1)} %collective-permute-done.2.refs_6_.refs_4_), channel_id=1, source_target_pairs={{0,4},{1,5},{2,6},{3,7},{4,0},{5,1},{6,2},{7,3},{8,12},{9,13},{10,... | collective-permute-start | bytes 393224 | tf_op jit(solution)/shard_map/ppermute | solution.py:712
  20.1 13.3 %collective-permute-start.11 = (bf16[3,208,128]{2,1,0:T(8,128)(2,1)S(1)}, bf16[3,208,128]{2,1,0:T(8,128)(2,1)S(1)}, u32[]{:S(2)}, u32[]{:S(2)}) collective-permute-start(bf16[3,208,128]{2,1,0:T(8,128)(2,1)S(1)} %pad_maximum_fusion.1.refs_2_), channel_id=1, source_target_pairs={{0,24},{1,25},{2,26},{3,27},{4,28},{5,29},{6,30},{7,31},{8,16},{9,... | collective-permute-start | bytes 479240 | tf_op jit(solution)/shard_map/ppermute | solution.py:712
  22.6 10.8 %collective-permute-start.10 = (bf16[3,208,128]{2,1,0:T(8,128)(2,1)S(1)}, bf16[3,208,128]{2,1,0:T(8,128)(2,1)}, u32[]{:S(2)}, u32[]{:S(2)}) collective-permute-start(bf16[3,208,128]{2,1,0:T(8,128)(2,1)S(1)} %pad_maximum_fusion.1.refs_2_), channel_id=1, source_target_pairs={{0,16},{1,17},{2,18},{3,19},{4,20},{5,21},{6,22},{7,23},{8,24},{9,... | collective-permute-start | bytes 479240 | tf_op jit(solution)/shard_map/ppermute | solution.py:712
  24.4 9.0 %collective-permute-start.9 = (bf16[3,208,128]{2,1,0:T(8,128)(2,1)S(1)}, bf16[3,208,128]{2,1,0:T(8,128)(2,1)}, u32[]{:S(2)}, u32[]{:S(2)}) collective-permute-start(bf16[3,208,128]{2,1,0:T(8,128)(2,1)S(1)} %pad_maximum_fusion.1.refs_2_), channel_id=1, source_target_pairs={{0,8},{1,9},{2,10},{3,11},{4,12},{5,13},{6,14},{7,15},{8,0},{9,1},... | collective-permute-start | bytes 479240 | tf_op jit(solution)/shard_map/ppermute | solution.py:712
  25.9 1.5 collective-permute-start.7
  25.9 1.5 %collective-permute-start.6 = (bf16[512,128]{1,0:T(8,128)(2,1)S(1)}, bf16[512,128]{1,0:T(8,128)(2,1)S(1)}, u32[]{:S(2)}, u32[]{:S(2)}) collective-permute-start(bf16[512,128]{1,0:T(8,128)(2,1)S(1)} %collective-permute-done.refs_4_.refs_2_), channel_id=1, source_target_pairs={{0,4},{1,5},{2,6},{3,7},{4,0},{5,1},{6,2},{7,3},{8,12},{9,13},{10,... | collective-permute-start | bytes 393224 | tf_op jit(solution)/shard_map/ppermute | solution.py:712
  33.4 1.5 collective-permute-start.12
  33.8 2.7 %collective-permute-start.16 = (bf16[3,208,128]{2,1,0:T(8,128)(2,1)S(1)}, bf16[3,208,128]{2,1,0:T(8,128)(2,1)S(1)}, u32[]{:S(2)}, u32[]{:S(2)}) collective-permute-start(bf16[3,208,128]{2,1,0:T(8,128)(2,1)S(1)} %pad_maximum_fusion.1.refs_2_), channel_id=1, source_target_pairs={{0,4},{1,5},{2,6},{3,7},{4,0},{5,1},{6,2},{7,3},{8,12},{9,13},{10,... | collective-permute-start | bytes 479240 | tf_op jit(solution)/shard_map/ppermute | solution.py:712
  34.0 3.0 %collective-permute-start.19 = (bf16[3,208,128]{2,1,0:T(8,128)(2,1)S(1)}, bf16[3,208,128]{2,1,0:T(8,128)(2,1)S(1)}, u32[]{:S(2)}, u32[]{:S(2)}) collective-permute-start(bf16[3,208,128]{2,1,0:T(8,128)(2,1)S(1)} %collective-permute-done.11.refs_8_), channel_id=1, source_target_pairs={{0,4},{1,5},{2,6},{3,7},{4,0},{5,1},{6,2},{7,3},{8,12},{9,13},{10,... | collective-permute-start | bytes 479240 | tf_op jit(solution)/shard_map/ppermute | solution.py:712
  34.3 4.2 %collective-permute-start.18 = (bf16[3,208,128]{2,1,0:T(8,128)(2,1)}, bf16[3,208,128]{2,1,0:T(8,128)(2,1)S(1)}, u32[]{:S(2)}, u32[]{:S(2)}) collective-permute-start(bf16[3,208,128]{2,1,0:T(8,128)(2,1)} %collective-permute-done.10.refs_6_), channel_id=1, source_target_pairs={{0,4},{1,5},{2,6},{3,7},{4,0},{5,1},{6,2},{7,3},{8,12},{9,13},{10,... | collective-permute-start | bytes 479240 | tf_op jit(solution)/shard_map/ppermute | solution.py:712
  34.5 4.0 %collective-permute-start.17 = (bf16[3,208,128]{2,1,0:T(8,128)(2,1)}, bf16[3,208,128]{2,1,0:T(8,128)(2,1)S(1)}, u32[]{:S(2)}, u32[]{:S(2)}) collective-permute-start(bf16[3,208,128]{2,1,0:T(8,128)(2,1)} %collective-permute-done.9.refs_4_), channel_id=1, source_target_pairs={{0,4},{1,5},{2,6},{3,7},{4,0},{5,1},{6,2},{7,3},{8,12},{9,13},{10,... | collective-permute-start | bytes 479240 | tf_op jit(solution)/shard_map/ppermute | solution.py:712
  34.9 5.4 %collective-permute-start.15 = (bf16[80,256]{1,0:T(8,128)(2,1)S(1)}, bf16[80,256]{1,0:T(8,128)(2,1)S(1)}, u32[]{:S(2)}, u32[]{:S(2)}) collective-permute-start(bf16[80,256]{1,0:T(8,128)(2,1)S(1)} %get-tuple-element.200), channel_id=1, source_target_pairs={{0,24},{1,25},{2,26},{3,27},{4,28},{5,29},{6,30},{7,31},{8,16},{9,... | collective-permute-start | bytes 122888 | tf_op jit(solution)/shard_map/ppermute | solution.py:712
  36.5 4.1 %collective-permute-start.14 = (bf16[80,256]{1,0:T(8,128)(2,1)S(1)}, bf16[80,256]{1,0:T(8,128)(2,1)S(1)}, u32[]{:S(2)}, u32[]{:S(2)}) collective-permute-start(bf16[80,256]{1,0:T(8,128)(2,1)S(1)} %get-tuple-element.201), channel_id=1, source_target_pairs={{0,16},{1,17},{2,18},{3,19},{4,20},{5,21},{6,22},{7,23},{8,24},{9,... | collective-permute-start | bytes 122888 | tf_op jit(solution)/shard_map/ppermute | solution.py:712
  37.0 4.0 %collective-permute-start.13 = (bf16[80,256]{1,0:T(8,128)(2,1)S(1)}, bf16[80,256]{1,0:T(8,128)(2,1)S(1)}, u32[]{:S(2)}, u32[]{:S(2)}) collective-permute-start(bf16[80,256]{1,0:T(8,128)(2,1)S(1)} %get-tuple-element.202), channel_id=1, source_target_pairs={{0,8},{1,9},{2,10},{3,11},{4,12},{5,13},{6,14},{7,15},{8,0},{9,1},... | collective-permute-start | bytes 122888 | tf_op jit(solution)/shard_map/ppermute | solution.py:712
  41.0 8.7 %collective-permute-start.22 = (bf16[80,256]{1,0:T(8,128)(2,1)S(1)}, bf16[80,256]{1,0:T(8,128)(2,1)S(1)}, u32[]{:S(2)}, u32[]{:S(2)}) collective-permute-start(bf16[80,256]{1,0:T(8,128)(2,1)S(1)} %fusion.7), channel_id=1, source_target_pairs={{0,3},{1,2},{2,1},{3,0},{4,7},{5,6},{6,5},{7,4},{8,11},{9,10},{10,... | collective-permute-start | bytes 122888 | tf_op jit(solution)/shard_map/ppermute | solution.py:712
  43.7 6.0 %collective-permute-start.21 = (bf16[80,256]{1,0:T(8,128)(2,1)S(1)}, bf16[80,256]{1,0:T(8,128)(2,1)S(1)}, u32[]{:S(2)}, u32[]{:S(2)}) collective-permute-start(bf16[80,256]{1,0:T(8,128)(2,1)S(1)} %fusion.7), channel_id=1, source_target_pairs={{0,2},{1,3},{2,0},{3,1},{4,6},{5,7},{6,4},{7,5},{8,10},{9,11},{10,... | collective-permute-start | bytes 122888 | tf_op jit(solution)/shard_map/ppermute | solution.py:712
  45.9 4.0 %collective-permute-start.20 = (bf16[80,256]{1,0:T(8,128)(2,1)S(1)}, bf16[80,256]{1,0:T(8,128)(2,1)S(1)}, u32[]{:S(2)}, u32[]{:S(2)}) collective-permute-start(bf16[80,256]{1,0:T(8,128)(2,1)S(1)} %fusion.7), channel_id=1, source_target_pairs={{0,1},{1,0},{2,3},{3,2},{4,5},{5,4},{6,7},{7,6},{8,9},{9,8},{10,11... | collective-permute-start | bytes 122888 | tf_op jit(solution)/shard_map/ppermute | solution.py:712
  50.0 5.4 %collective-permute-start.26 = (bf16[80,256]{1,0:T(8,128)(2,1)S(1)}, bf16[80,256]{1,0:T(8,128)(2,1)S(1)}, u32[]{:S(2)}, u32[]{:S(2)}) collective-permute-start(bf16[80,256]{1,0:T(8,128)(2,1)S(1)} %add_convert_fusion.1.refs_7_.refs_5_), channel_id=1, source_target_pairs={{0,24},{1,25},{2,26},{3,27},{4,28},{5,29},{6,30},{7,31},{8,16},{9,... | collective-permute-start | bytes 122888 | tf_op jit(solution)/shard_map/ppermute | solution.py:712
  51.8 4.0 %collective-permute-start.25 = (bf16[80,256]{1,0:T(8,128)(2,1)S(1)}, bf16[80,256]{1,0:T(8,128)(2,1)S(1)}, u32[]{:S(2)}, u32[]{:S(2)}) collective-permute-start(bf16[80,256]{1,0:T(8,128)(2,1)S(1)} %add_convert_fusion.1.refs_7_.refs_5_), channel_id=1, source_target_pairs={{0,16},{1,17},{2,18},{3,19},{4,20},{5,21},{6,22},{7,23},{8,24},{9,... | collective-permute-start | bytes 122888 | tf_op jit(solution)/shard_map/ppermute | solution.py:712
  52.4 4.0 %collective-permute-start.24 = (bf16[80,256]{1,0:T(8,128)(2,1)S(1)}, bf16[80,256]{1,0:T(8,128)(2,1)S(1)}, u32[]{:S(2)}, u32[]{:S(2)}) collective-permute-start(bf16[80,256]{1,0:T(8,128)(2,1)S(1)} %add_convert_fusion.1.refs_7_.refs_5_), channel_id=1, source_target_pairs={{0,8},{1,9},{2,10},{3,11},{4,12},{5,13},{6,14},{7,15},{8,0},{9,1},... | collective-permute-start | bytes 122888 | tf_op jit(solution)/shard_map/ppermute | solution.py:712
  53.5 3.4 %collective-permute-start.23 = (bf16[80,256]{1,0:T(8,128)(2,1)S(1)}, bf16[80,256]{1,0:T(8,128)(2,1)S(1)}, u32[]{:S(2)}, u32[]{:S(2)}) collective-permute-start(bf16[80,256]{1,0:T(8,128)(2,1)S(1)} %add_convert_fusion.1.refs_7_.refs_5_), channel_id=1, source_target_pairs={{0,4},{1,5},{2,6},{3,7},{4,0},{5,1},{6,2},{7,3},{8,12},{9,13},{10,... | collective-permute-start | bytes 122888 | tf_op jit(solution)/shard_map/ppermute | solution.py:712
  56.4 1.2 collective-permute-start.27
  56.4 1.4 collective-permute-start.28
  56.9 1.2 collective-permute-start.29
  67.6 1.5 collective-permute-start.30
  69.2 7.0 %collective-permute-start.31 = (bf16[80,256]{1,0:T(8,128)(2,1)S(1)}, bf16[80,256]{1,0:T(8,128)(2,1)S(1)}, u32[]{:S(2)}, u32[]{:S(2)}) collective-permute-start(bf16[80,256]{1,0:T(8,128)(2,1)S(1)} %get-tuple-element.199), channel_id=1, source_target_pairs={{0,8},{1,9},{2,10},{3,11},{4,12},{5,13},{6,14},{7,15},{8,0},{9,1},... | collective-permute-start | bytes 122888 | tf_op jit(solution)/shard_map/ppermute | solution.py:712
  70.4 5.2 %collective-permute-start.33 = (bf16[80,256]{1,0:T(8,128)(2,1)S(1)}, bf16[80,256]{1,0:T(8,128)(2,1)S(1)}, u32[]{:S(2)}, u32[]{:S(2)}) collective-permute-start(bf16[80,256]{1,0:T(8,128)(2,1)S(1)} %get-tuple-element.197), channel_id=1, source_target_pairs={{0,24},{1,25},{2,26},{3,27},{4,28},{5,29},{6,30},{7,31},{8,16},{9,... | collective-permute-start | bytes 122888 | tf_op jit(solution)/shard_map/ppermute | solution.py:712
  72.2 4.0 %collective-permute-start.32 = (bf16[80,256]{1,0:T(8,128)(2,1)S(1)}, bf16[80,256]{1,0:T(8,128)(2,1)S(1)}, u32[]{:S(2)}, u32[]{:S(2)}) collective-permute-start(bf16[80,256]{1,0:T(8,128)(2,1)S(1)} %get-tuple-element.198), channel_id=1, source_target_pairs={{0,16},{1,17},{2,18},{3,19},{4,20},{5,21},{6,22},{7,23},{8,24},{9,... | collective-permute-start | bytes 122888 | tf_op jit(solution)/shard_map/ppermute | solution.py:712
  76.2 7.8 %collective-permute-start.36 = (bf16[80,256]{1,0:T(8,128)(2,1)S(1)}, bf16[80,256]{1,0:T(8,128)(2,1)S(1)}, u32[]{:S(2)}, u32[]{:S(2)}) collective-permute-start(bf16[80,256]{1,0:T(8,128)(2,1)S(1)} %fusion.4), channel_id=1, source_target_pairs={{0,3},{1,2},{2,1},{3,0},{4,7},{5,6},{6,5},{7,4},{8,11},{9,10},{10,... | collective-permute-start | bytes 122888 | tf_op jit(solution)/shard_map/ppermute | solution.py:712
  78.9 5.1 %collective-permute-start.35 = (bf16[80,256]{1,0:T(8,128)(2,1)S(1)}, bf16[80,256]{1,0:T(8,128)(2,1)S(1)}, u32[]{:S(2)}, u32[]{:S(2)}) collective-permute-start(bf16[80,256]{1,0:T(8,128)(2,1)S(1)} %fusion.4), channel_id=1, source_target_pairs={{0,2},{1,3},{2,0},{3,1},{4,6},{5,7},{6,4},{7,5},{8,10},{9,11},{10,... | collective-permute-start | bytes 122888 | tf_op jit(solution)/shard_map/ppermute | solution.py:712
  79.3 4.8 %collective-permute-start.34 = (bf16[80,256]{1,0:T(8,128)(2,1)S(1)}, bf16[80,256]{1,0:T(8,128)(2,1)S(1)}, u32[]{:S(2)}, u32[]{:S(2)}) collective-permute-start(bf16[80,256]{1,0:T(8,128)(2,1)S(1)} %fusion.4), channel_id=1, source_target_pairs={{0,1},{1,0},{2,3},{3,2},{4,5},{5,4},{6,7},{7,6},{8,9},{9,8},{10,11... | collective-permute-start | bytes 122888 | tf_op jit(solution)/shard_map/ppermute | solution.py:712
  84.1 5.4 %collective-permute-start.40 = (bf16[80,256]{1,0:T(8,128)(2,1)S(1)}, bf16[80,256]{1,0:T(8,128)(2,1)S(1)}, u32[]{:S(2)}, u32[]{:S(2)}) collective-permute-start(bf16[80,256]{1,0:T(8,128)(2,1)S(1)} %add_convert_fusion.refs_9_), channel_id=1, source_target_pairs={{0,24},{1,25},{2,26},{3,27},{4,28},{5,29},{6,30},{7,31},{8,16},{9,... | collective-permute-start | bytes 122888 | tf_op jit(solution)/shard_map/ppermute | solution.py:712
  85.7 4.0 %collective-permute-start.39 = (bf16[80,256]{1,0:T(8,128)(2,1)S(1)}, bf16[80,256]{1,0:T(8,128)(2,1)S(1)}, u32[]{:S(2)}, u32[]{:S(2)}) collective-permute-start(bf16[80,256]{1,0:T(8,128)(2,1)S(1)} %add_convert_fusion.refs_9_), channel_id=1, source_target_pairs={{0,16},{1,17},{2,18},{3,19},{4,20},{5,21},{6,22},{7,23},{8,24},{9,... | collective-permute-start | bytes 122888 | tf_op jit(solution)/shard_map/ppermute | solution.py:712
  86.8 4.0 %collective-permute-start.38 = (bf16[80,256]{1,0:T(8,128)(2,1)S(1)}, bf16[80,256]{1,0:T(8,128)(2,1)S(1)}, u32[]{:S(2)}, u32[]{:S(2)}) collective-permute-start(bf16[80,256]{1,0:T(8,128)(2,1)S(1)} %add_convert_fusion.refs_9_), channel_id=1, source_target_pairs={{0,8},{1,9},{2,10},{3,11},{4,12},{5,13},{6,14},{7,15},{8,0},{9,1},... | collective-permute-start | bytes 122888 | tf_op jit(solution)/shard_map/ppermute | solution.py:712
  87.7 3.6 %collective-permute-start.37 = (bf16[80,256]{1,0:T(8,128)(2,1)S(1)}, bf16[80,256]{1,0:T(8,128)(2,1)S(1)}, u32[]{:S(2)}, u32[]{:S(2)}) collective-permute-start(bf16[80,256]{1,0:T(8,128)(2,1)S(1)} %add_convert_fusion.refs_9_), channel_id=1, source_target_pairs={{0,4},{1,5},{2,6},{3,7},{4,0},{5,1},{6,2},{7,3},{8,12},{9,13},{10,... | collective-permute-start | bytes 122888 | tf_op jit(solution)/shard_map/ppermute | solution.py:712
  90.8 1.2 collective-permute-start.41
  90.8 1.4 collective-permute-start.42
  91.3 1.2 collective-permute-start.43
  100.1 3.1 %collective-permute-start.44 = (bf16[4,4,320,128]{3,2,1,0:T(8,128)(2,1)S(1)}, bf16[4,4,320,128]{3,2,1,0:T(8,128)(2,1)S(1)}, u32[]{:S(2)}, u32[]{:S(2)}) collective-permute-start(bf16[4,4,320,128]{3,2,1,0:T(8,128)(2,1)S(1)} %get-tuple-element.150), channel_id=1, source_target_pairs={{0,4},{1,5},{2,6},{3,7},{4,0},{5,1},{6,2},{7,3},{8,12},{9,13},{10,... | collective-permute-start | bytes 3932168 | tf_op jit(solution)/shard_map/ppermute | solution.py:712
  103.8 18.7 %collective-permute-start.45 = (bf16[4,320,128]{2,1,0:T(8,128)(2,1)S(1)}, bf16[4,320,128]{2,1,0:T(8,128)(2,1)S(1)}, u32[]{:S(2)}, u32[]{:S(2)}) collective-permute-start(bf16[4,320,128]{2,1,0:T(8,128)(2,1)S(1)} %get-tuple-element.193), channel_id=1, source_target_pairs={{0,8},{1,9},{2,10},{3,11},{4,12},{5,13},{6,14},{7,15},{8,0},{9,1},... | collective-permute-start | bytes 983048 | tf_op jit(solution)/shard_map/ppermute | solution.py:712
  104.7 16.4 %collective-permute-start.47 = (bf16[4,320,128]{2,1,0:T(8,128)(2,1)S(1)}, bf16[4,320,128]{2,1,0:T(8,128)(2,1)S(1)}, u32[]{:S(2)}, u32[]{:S(2)}) collective-permute-start(bf16[4,320,128]{2,1,0:T(8,128)(2,1)S(1)} %get-tuple-element.191), channel_id=1, source_target_pairs={{0,24},{1,25},{2,26},{3,27},{4,28},{5,29},{6,30},{7,31},{8,16},{9,... | collective-permute-start | bytes 983048 | tf_op jit(solution)/shard_map/ppermute | solution.py:712
  106.2 16.2 %collective-permute-start.46 = (bf16[4,320,128]{2,1,0:T(8,128)(2,1)S(1)}, bf16[4,320,128]{2,1,0:T(8,128)(2,1)S(1)}, u32[]{:S(2)}, u32[]{:S(2)}) collective-permute-start(bf16[4,320,128]{2,1,0:T(8,128)(2,1)S(1)} %get-tuple-element.192), channel_id=1, source_target_pairs={{0,16},{1,17},{2,18},{3,19},{4,20},{5,21},{6,22},{7,23},{8,24},{9,... | collective-permute-start | bytes 983048 | tf_op jit(solution)/shard_map/ppermute | solution.py:712
  122.5 24.4 %copy-start.4 = (f32[128,2048]{1,0:T(8,128)S(1)}, f32[128,2048]{1,0:T(8,128)}, u32[]{:S(2)}) copy-start(f32[128,2048]{1,0:T(8,128)} %refs_9_.1) | copy-start | bytes 3145732
  122.5 24.4 %copy-start.5 = (f32[128,2048]{1,0:T(8,128)S(1)}, f32[128,2048]{1,0:T(8,128)}, u32[]{:S(2)}) copy-start(f32[128,2048]{1,0:T(8,128)} %refs_10_.1) | copy-start | bytes 3145732
  122.5 24.4 %copy-start.9 = (f32[128,512]{1,0:T(8,128)S(1)}, f32[128,512]{1,0:T(8,128)}, u32[]{:S(2)}) copy-start(f32[128,512]{1,0:T(8,128)} %refs_12_.1) | copy-start | bytes 786436
  122.7 6.6 %collective-permute-start.50 = (bf16[320,128]{1,0:T(8,128)(2,1)S(1)}, bf16[320,128]{1,0:T(8,128)(2,1)S(1)}, u32[]{:S(2)}, u32[]{:S(2)}) collective-permute-start(bf16[320,128]{1,0:T(8,128)(2,1)S(1)} %get-tuple-element.194), channel_id=1, source_target_pairs={{0,3},{1,2},{2,1},{3,0},{4,7},{5,6},{6,5},{7,4},{8,11},{9,10},{10,... | collective-permute-start | bytes 245768 | tf_op jit(solution)/shard_map/ppermute | solution.py:712
  125.2 6.1 %collective-permute-start.49 = (bf16[320,128]{1,0:T(8,128)(2,1)S(1)}, bf16[320,128]{1,0:T(8,128)(2,1)S(1)}, u32[]{:S(2)}, u32[]{:S(2)}) collective-permute-start(bf16[320,128]{1,0:T(8,128)(2,1)S(1)} %get-tuple-element.195), channel_id=1, source_target_pairs={{0,2},{1,3},{2,0},{3,1},{4,6},{5,7},{6,4},{7,5},{8,10},{9,11},{10,... | collective-permute-start | bytes 245768 | tf_op jit(solution)/shard_map/ppermute | solution.py:712
  125.2 6.1 %collective-permute-start.48 = (bf16[320,128]{1,0:T(8,128)(2,1)S(1)}, bf16[320,128]{1,0:T(8,128)(2,1)S(1)}, u32[]{:S(2)}, u32[]{:S(2)}) collective-permute-start(bf16[320,128]{1,0:T(8,128)(2,1)S(1)} %get-tuple-element.196), channel_id=1, source_target_pairs={{0,1},{1,0},{2,3},{3,2},{4,5},{5,4},{6,7},{7,6},{8,9},{9,8},{10,11... | collective-permute-start | bytes 245768 | tf_op jit(solution)/shard_map/ppermute | solution.py:712
  131.3 5.4 %collective-permute-start.56 = (bf16[320,128]{1,0:T(8,128)(2,1)S(1)}, bf16[320,128]{1,0:T(8,128)(2,1)S(1)}, u32[]{:S(2)}, u32[]{:S(2)}) collective-permute-start(bf16[320,128]{1,0:T(8,128)(2,1)S(1)} %finish.1.refs_0_.refs_1_), channel_id=1, source_target_pairs={{0,24},{1,25},{2,26},{3,27},{4,28},{5,29},{6,30},{7,31},{8,16},{9,... | collective-permute-start | bytes 245768 | tf_op jit(solution)/shard_map/ppermute | solution.py:712
  132.8 4.8 %collective-permute-start.54 = (bf16[320,128]{1,0:T(8,128)(2,1)S(1)}, bf16[320,128]{1,0:T(8,128)(2,1)S(1)}, u32[]{:S(2)}, u32[]{:S(2)}) collective-permute-start(bf16[320,128]{1,0:T(8,128)(2,1)S(1)} %finish.1.refs_0_.refs_1_), channel_id=1, source_target_pairs={{0,16},{1,17},{2,18},{3,19},{4,20},{5,21},{6,22},{7,23},{8,24},{9,... | collective-permute-start | bytes 245768 | tf_op jit(solution)/shard_map/ppermute | solution.py:712
  133.8 4.4 %collective-permute-start.52 = (bf16[320,128]{1,0:T(8,128)(2,1)S(1)}, bf16[320,128]{1,0:T(8,128)(2,1)S(1)}, u32[]{:S(2)}, u32[]{:S(2)}) collective-permute-start(bf16[320,128]{1,0:T(8,128)(2,1)S(1)} %finish.1.refs_0_.refs_1_), channel_id=1, source_target_pairs={{0,8},{1,9},{2,10},{3,11},{4,12},{5,13},{6,14},{7,15},{8,0},{9,1},... | collective-permute-start | bytes 245768 | tf_op jit(solution)/shard_map/ppermute | solution.py:712
  134.9 3.3 %collective-permute-start.51 = (bf16[320,128]{1,0:T(8,128)(2,1)S(1)}, bf16[320,128]{1,0:T(8,128)(2,1)S(1)}, u32[]{:S(2)}, u32[]{:S(2)}) collective-permute-start(bf16[320,128]{1,0:T(8,128)(2,1)S(1)} %finish.1.refs_0_.refs_1_), channel_id=1, source_target_pairs={{0,4},{1,5},{2,6},{3,7},{4,0},{5,1},{6,2},{7,3},{8,12},{9,13},{10,... | collective-permute-start | bytes 245768 | tf_op jit(solution)/shard_map/ppermute | solution.py:712
  136.8 1.4 collective-permute-start.57
  137.6 1.3 collective-permute-start.55
  138.2 1.3 collective-permute-start.53
  139.7 5.4 %collective-permute-start.60 = (f32[8,128]{1,0:T(8,128)S(1)}, f32[8,128]{1,0:T(8,128)S(1)}, u32[]{:S(2)}, u32[]{:S(2)}) collective-permute-start(f32[8,128]{1,0:T(8,128)S(1)} %squares.1.refs_1_), channel_id=1, source_target_pairs={{0,3},{1,2},{2,1},{3,0},{4,7},{5,6},{6,5},{7,4},{8,11},{9,10},{10,... | collective-permute-start | bytes 12296 | tf_op jit(solution)/shard_map/ppermute | solution.py:712
  142.3 4.5 %collective-permute-start.59 = (f32[8,128]{1,0:T(8,128)S(1)}, f32[8,128]{1,0:T(8,128)S(1)}, u32[]{:S(2)}, u32[]{:S(2)}) collective-permute-start(f32[8,128]{1,0:T(8,128)S(1)} %squares.1.refs_1_), channel_id=1, source_target_pairs={{0,2},{1,3},{2,0},{3,1},{4,6},{5,7},{6,4},{7,5},{8,10},{9,11},{10,... | collective-permute-start | bytes 12296 | tf_op jit(solution)/shard_map/ppermute | solution.py:712
  142.3 4.5 %collective-permute-start.58 = (f32[8,128]{1,0:T(8,128)S(1)}, f32[8,128]{1,0:T(8,128)S(1)}, u32[]{:S(2)}, u32[]{:S(2)}) collective-permute-start(f32[8,128]{1,0:T(8,128)S(1)} %squares.1.refs_1_), channel_id=1, source_target_pairs={{0,1},{1,0},{2,3},{3,2},{4,5},{5,4},{6,7},{7,6},{8,9},{9,8},{10,11... | collective-permute-start | bytes 12296 | tf_op jit(solution)/shard_map/ppermute | solution.py:712
  (12 other events, 170.0 us)

commit v4 on v3

--- a/solution.py
+++ b/solution.py
@@ -175,7 +175,7 @@
                 send[slot] = block.astype(bf_type)
 
 
-def key_kernel(pieces, steps, step, place, x, ids, *refs):
+def key_kernel(pieces, step, place, x, ids, *refs):
     mine, other = refs[:pieces], refs[pieces : 2 * pieces]
     key_slope, key_out, value_out, keep, send, weights, masked, acc = refs[2 * pieces :]
     core, node, count = place[0], place[1], place[3]
@@ -183,14 +183,11 @@
     rows = x.shape[0]
     half = width // GROUPS
 
-    @pl.when(step == 0)
-    def _():
-        span = mine[0].shape[1]
-        for d in range(pieces):
-            cols = slice(d * span, (d + 1) * span)
-            weights[pl.ds(pl.multiple_of(core * width, 16), width), cols] = mine[d][0:width]
-            weights[pl.ds(pl.multiple_of((1 - core) * width, 16), width), cols] = other[d][0:width]
-        acc[...] = jnp.zeros_like(acc)
+    span = mine[0].shape[1]
+    for d in range(pieces):
+        cols = slice(d * span, (d + 1) * span)
+        weights[pl.ds(pl.multiple_of(core * width, 16), width), cols] = mine[d][...]
+        weights[pl.ds(pl.multiple_of((1 - core) * width, 16), width), cols] = other[d][...]
 
     table = members(ids)
     valid = valid_row(count, step * rows, rows)
@@ -205,15 +202,13 @@
         for c in range(CLUSTERS):
             masked[c * half : (c + 1) * half, :] = value * table[c : c + 1, :]
         masked[CLUSTERS * half :, :] = table
-        acc[g] += dot_nt(masked[...], keys)
-
-    @pl.when(step == steps - 1)
-    def _():
-        def extra(g, c):
-            row = acc[g, CLUSTERS * half + c : CLUSTERS * half + c + 1, :]
-            return jnp.concatenate([row, jnp.zeros((PAD - 1, half), fl_type)], axis=0)
-
-        put_chunks(acc, keep, send, node, extra)
+        acc[g] = dot_nt(masked[...], keys)
+
+    def extra(g, c):
+        row = acc[g, CLUSTERS * half + c : CLUSTERS * half + c + 1, :]
+        return jnp.concatenate([row, jnp.zeros((PAD - 1, half), fl_type)], axis=0)
+
+    put_chunks(acc, keep, send, node, extra)
 
 
 def weights_kernel(pieces, step, place, own, *refs):
@@ -510,6 +505,24 @@
     grad_out[...] += dot_nn(prod[...], g[...])
 
 
+def early_kernel(pieces, step, place, grad_query, grad_gate, grad_out, keep, send):
+    node, shard = place[1], place[2]
+    width = grad_out.shape[1]
+    span = width // pieces
+    tall = 2 * width // 8
+    lanes = width // 4
+    short = span // 2
+
+    def blocks(z, chunk):
+        source = grad_query if chunk < 4 else grad_gate
+        top = source[(chunk % 4) * tall : (chunk % 4 + 1) * tall, z * span : (z + 1) * span]
+        start = pl.multiple_of(lax.bitwise_xor(shard, z) * span + (chunk % 2) * short, 8)
+        bottom = grad_out[pl.ds(start, short), (chunk // 2) * lanes : (chunk // 2 + 1) * lanes]
+        return jnp.concatenate([top, fold(bottom, span)], axis=0)
+
+    write_pieces(pieces, node, shard, span, keep, send, blocks)
+
+
 def fold(block, span):
     return jnp.concatenate(
         [block[:, i * span : (i + 1) * span] for i in range(block.shape[1] // span)], axis=0
@@ -529,7 +542,7 @@
     result[...] = x[...].astype(fl_type) + dot_tn(prod[...], out_weight[...])
 
 
-def key_back_kernel(pieces, steps, step, place, ids, key_slope, key, value, x, grad_query, grad_gate, grad_out, *refs):
+def key_back_kernel(pieces, step, place, ids, key_slope, key, value, x, *refs):
     chunk_refs = refs[:CHUNKS]
     dkey_out, dvalue_out, norm_out, keep, send = refs[CHUNKS : CHUNKS + 5]
     stage, left_key, left_value, sums, stack, key_stack, acc = refs[CHUNKS + 5 :]
@@ -554,7 +567,6 @@
                 sums[c, gr * half : (gr + 1) * half, :] = jnp.broadcast_to(column[:, 0:1], (half, 128))
                 if c == 0:
                     norm_out[:, gr * half : (gr + 1) * half] = chunk[head : head + 8]
-        acc[...] = jnp.zeros_like(acc)
 
     table = members(ids)
     valid = valid_row(count, step * rows, rows)
@@ -562,35 +574,25 @@
         at = slice(p * 2 * head, (p + 1) * 2 * head)
         part = value[at, :]
         for c in range(CLUSTERS):
-            stack[p, c * 2 * head : (c + 1) * 2 * head, :] = part * table[c : c + 1, :]
-        dk = dot_nn(left_key[p], stack[p])
+            stack[p % 2, c * 2 * head : (c + 1) * 2 * head, :] = part * table[c : c + 1, :]
+        dk = dot_nn(left_key[p], stack[p % 2])
         for h in range(2):
             sub = slice((p * 2 + h) * head, (p * 2 + h + 1) * head)
             full = dk[h * head : (h + 1) * head] + pick_rows(sums, sub, ids, rows)
             dkey_out[sub, :] = (full * key_slope[sub, :]).astype(bf_type)
         part = key[at, :]
         for c in range(CLUSTERS):
-            key_stack[p, c * 2 * head : (c + 1) * 2 * head, :] = part * table[c : c + 1, :]
-        dvalue_out[at, :] = dot_nn(left_value[p], key_stack[p]).astype(bf_type)
-    acc[0:width] += dot_nn(dkey_out[...], x[...])
-    acc[width : 2 * width] += dot_nn(dvalue_out[...], x[...])
-
-    @pl.when(step == steps - 1)
-    def _():
-        tall = 2 * width // 8
-        lanes = width // 4
-        short = span // 2
-
-        def blocks(z, chunk):
-            cols = slice(z * span, (z + 1) * span)
-            top = acc[chunk * tall : (chunk + 1) * tall, cols]
-            source = grad_query if chunk < 4 else grad_gate
-            center = source[(chunk % 4) * tall : (chunk % 4 + 1) * tall, cols]
-            start = pl.multiple_of(lax.bitwise_xor(shard, z) * span + (chunk % 2) * short, 8)
-            bottom = grad_out[pl.ds(start, short), (chunk // 2) * lanes : (chunk // 2 + 1) * lanes]
-            return jnp.concatenate([top, center, fold(bottom, span)], axis=0)
-
-        write_pieces(pieces, node, shard, span, keep, send, blocks)
+            key_stack[p % 2, c * 2 * head : (c + 1) * 2 * head, :] = part * table[c : c + 1, :]
+        dvalue_out[at, :] = dot_nn(left_value[p], key_stack[p % 2]).astype(bf_type)
+    acc[0:width] = dot_nn(dkey_out[...], x[...])
+    acc[width : 2 * width] = dot_nn(dvalue_out[...], x[...])
+
+    tall = 2 * width // 8
+
+    def blocks(z, chunk):
+        return acc[chunk * tall : (chunk + 1) * tall, z * span : (z + 1) * span]
+
+    write_pieces(pieces, node, shard, span, keep, send, blocks)
 
 
 def input_kernel(step, place, dquery, dkey, dvalue, dgate, full_query, full_key, full_gate, g, result):
@@ -783,15 +785,6 @@
         "prep",
         vmem=60,
     )
-    mine, other = [message], [kv_half]
-    for z in range(1, shards):
-        mine.append(exchange(message, 0, z))
-    stack = jnp.stack([exchange(part, 0, z) for z in range(1, shards)])
-    stacks = [stack] + [None] * 7
-    for e in range(1, 4):
-        stacks[2 * e] = exchange(stack, 2 * e, 0)
-    for z in range(1, shards):
-        other.append(exchange(tie(mine[z], stack), 1, 0))
     x_turned = jnp.concatenate(
         [
             lax.dynamic_slice(x, (0, lax.bitwise_xor(shard, z) * span), (rows, span))
@@ -799,30 +792,40 @@
         ],
         axis=1,
     )
-
+    mine, other = [message], [kv_half]
+    for z in range(1, shards):
+        late = z == 2
+        mine.append(exchange(tie(message, x_turned) if late else message, 0, z))
+    stack = jnp.stack([exchange(part, 0, z) for z in range(1, shards)])
+    stacks = [stack] + [None] * 7
+    for e in range(1, 4):
+        stacks[2 * e] = exchange(stack, 2 * e, 0)
+    for z in range(1, shards):
+        other.append(exchange(tie(mine[z], stack), 1, 0))
     key_slope, key, value, keep, send = call(
-        functools.partial(key_kernel, shards, steps),
-        steps,
+        functools.partial(key_kernel, shards),
+        1,
         (place, x_turned, ids, *mine, *other),
         ["smem", "row", "lane"] + [None] * (2 * shards),
         [wide(fl_type), wide(bf_type), wide(bf_type), out(chunk_shape, fl_type), out(chunk_shape, bf_type)],
         ["lane", "lane", "lane", None, None],
         [
             vmem((2 * width, width), bf_type),
-            vmem((CLUSTERS * half + PAD, block), bf_type),
+            vmem((CLUSTERS * half + PAD, rows), bf_type),
             vmem((GROUPS, CLUSTERS * half + PAD, half), fl_type),
         ],
         1e3,
         "keys",
-        block,
+        rows,
+        vmem=26,
     )
 
-    def swap(pieces, peers, filler):
+    def swap(pieces, peers, filler, cast=True):
         got = [exchange(p, *at) for p, at in zip(pieces, peers)]
         if filler is not None:
             done = filler(pieces[0])
             got = list(tie(tuple(got), done))
-        return to_float(got)
+        return to_float(got) if cast else got
 
     plane = [(2 * e, 0) for e in range(1, 4)]
     along = [(0, z) for z in range(1, shards)]
@@ -961,6 +964,11 @@
         block,
     )
 
+    short = tall + (span // 2) * (width // 4 // span)
+    height = tall + short
+    early_shape = (4, shards, short, span)
+    late_shape = (4, shards, tall, span)
+
     def fill_gate_back(dep):
         made["gate_back"] = call(
             gate_back_kernel,
@@ -996,7 +1004,7 @@
     def fill_query_back(dep):
         made["dquery"] = call(
             query_back_kernel,
-            steps,
+            1,
             (tie(place, dep), ids, dnum, dden, query_slope, *chunks),
             ["smem", "lane", "lane", "lane", "lane"] + [None] * CHUNKS,
             [wide(bf_type)],
@@ -1005,11 +1013,12 @@
                 vmem((CHUNKS, head + PAD, half), bf_type),
                 vmem((PAIRS, 2 * head, CLUSTERS * 2 * head), bf_type),
                 vmem((CLUSTERS, width, 128), fl_type),
-                vmem((PAIRS, CLUSTERS * 2 * head, block), bf_type),
+                vmem((PAIRS, CLUSTERS * 2 * head, rows), bf_type),
             ],
             2 * work,
             "query_back",
-            block,
+            rows,
+            vmem=26,
         )[0]
         return made["dquery"]
 
@@ -1026,24 +1035,39 @@
             "grad_query",
             vmem=12,
         )[0]
-        return made["grad_query"]
+        made["early"] = call(
+            functools.partial(early_kernel, shards),
+            1,
+            (place, made["grad_query"], *made["gate_back"]),
+            ["smem"] + [None] * 3,
+            [out(early_shape, fl_type), out(early_shape, bf_type)],
+            [None] * 2,
+            [],
+            1e6,
+            "early",
+            vmem=8,
+        )
+        return made["early"][1]
 
     back_chunks = reduce_chunks(keep, send, (fill_gate_back, fill_query_back, fill_grad_query))
-    dquery, grad_query = made["dquery"], made["grad_query"]
-
-    height = 2 * tall + (span // 2) * (width // 4 // span)
-    piece_shape = (4, shards, height, span)
+    dquery = made["dquery"]
+
+    early_keep, early_send = made["early"]
+    early_send = tie(early_send, *back_chunks[2::2])
+    early_mine = early_keep + exchange(early_send, 1, 0).astype(fl_type)
+    early_pieces = tie(tuple(early_mine[e].astype(bf_type) for e in range(1, 4)))
+    early_got = [exchange(p, *at) for p, at in zip(early_pieces, plane)]
     dkey, dvalue, norm_grad, keep, send = call(
-        functools.partial(key_back_kernel, shards, steps),
-        steps,
-        (place, ids, key_slope, key, value, x_turned, grad_query, *made["gate_back"], *back_chunks),
-        ["smem", "lane", "lane", "lane", "lane", "row"] + [None] * (3 + CHUNKS),
+        functools.partial(key_back_kernel, shards),
+        1,
+        (place, ids, key_slope, key, value, x_turned, *back_chunks),
+        ["smem", "lane", "lane", "lane", "lane", "row"] + [None] * CHUNKS,
         [
             wide(bf_type),
             wide(bf_type),
             out((8, width), fl_type),
-            out(piece_shape, fl_type),
-            out(piece_shape, bf_type),
+            out(late_shape, fl_type),
+            out(late_shape, bf_type),
         ],
         ["lane", "lane", None, None, None],
         [
@@ -1051,13 +1075,14 @@
             vmem((PAIRS, 2 * head, CLUSTERS * 2 * head), bf_type),
             vmem((PAIRS, 2 * head, CLUSTERS * 2 * head), bf_type),
             vmem((CLUSTERS, width, 128), fl_type),
-            vmem((PAIRS, CLUSTERS * 2 * head, block), bf_type),
-            vmem((PAIRS, CLUSTERS * 2 * head, block), bf_type),
+            vmem((2, CLUSTERS * 2 * head, rows), bf_type),
+            vmem((2, CLUSTERS * 2 * head, rows), bf_type),
             vmem((2 * width, width), fl_type),
         ],
         6 * work,
         "key_back",
-        block,
+        rows,
+        vmem=26,
     )
 
     full_key = call(
@@ -1087,14 +1112,15 @@
             block,
             piped=True,
         )[0]
-        fill_output(dep)
-        return made["inputs"], made["output"]
-
+        return made["inputs"]
+
+    send = tie(send, *early_got)
     mine_sum = keep + exchange(send, 1, 0).astype(fl_type)
+    early_sum = tree_sum([early_mine[0], *to_float(early_got)])
     got = swap([mine_sum[e].astype(bf_type) for e in range(1, 4)], plane, fill_inputs)
-    mine_sum = tree_sum([mine_sum[0], *got])
-    got = [exchange(mine_sum[z].astype(bf_type), *along[z - 1]) for z in range(1, shards)]
-    owned_parts = [mine_sum[0], *got]
+    mine_sum = jnp.concatenate([tree_sum([mine_sum[0], *got]), early_sum], axis=1)
+    pieces = tie(tuple(mine_sum[z].astype(bf_type) for z in range(1, shards)))
+    owned_parts = [mine_sum[0], *swap(pieces, along, fill_output, cast=False)]
     if outer > 1:
         own = tree_sum(to_float(owned_parts)).astype(bf_type)
         got = [own] + [exchange(own, 8 * o, 0) for o in range(1, outer)]

time: 151 us -> 146 us (0.967)
  waiting for transfers between devices: 31.3 us -> 23.3 us
  starting transfers between devices: 57.6 us -> 60 us
    ppermute x61 -> x65, waiting for transfers between devices: 31.3 us -> 23.3 us  [exchange(): return lax.ppermute(value, AXES, pairs)]
    ppermute x61 -> x65, starting transfers between devices: 57.6 us -> 60 us  [exchange(): return lax.ppermute(value, AXES, pairs)]
    pallas_call x18 -> x19, Pallas kernels: 57 us -> 56.8 us  [call(): pl.pallas_call(body, grid=(steps,) if piped else (), in_specs=specs[:len(...]
  transfers between devices with their start and end apart: 61 -> 65, of which waited for: 30 -> 26; matrix products, arithmetic and copies ran while one was open for 1% -> 2% of each run, Pallas kernels for 22% -> 28%
where the time goes in v4:
time: 146 us
  starting transfers between devices  60 us (41%)
  Pallas kernels  56.8 us (39%)
  waiting for transfers between devices  23.3 us (16%)
  local copies, waits for them, and re-layouts  2.51 us (2%)
  between operations  2.04 us (1%)
    ppermute x65, starting transfers between devices, exchange(): return lax.ppermute(value, AXES, pairs)  60 us
    pallas_call x19, Pallas kernels, call(): pl.pallas_call(body, grid=(steps,) if piped else (), in_specs=specs[:len(...  56.8 us
    ppermute x65, waiting for transfers between devices, exchange(): return lax.ppermute(value, AXES, pairs)  23.3 us
  transfers between devices with their start and end apart: 65, of which 26 were waited for; matrix products, arithmetic and copies ran while one was open for 2% of the time, Pallas kernels for 28%

profile of v4, /device:TPU:0, one launch (start us, length us, event | category | flops | bytes accessed | tf_op | source)
XLA Modules:
  0.0 145.8 jit_solution(4739457253029918725)
XLA Ops:
  0.6 2.4 %prep.1 = (bf16[512,128]{1,0:T(8,128)(2,1)}, bf16[512,128]{1,0:T(8,128)(2,1)}, bf16[208,128]{1,0:T(8,128)(2,1)}, bf16[1664,128]{1,0:T(8,128)(2,1)}) custom-call(f32[128,2048]{1,0:T(8,128)} %refs_8_.3, f32[128,512]{1,0:T(8,128)} %refs_11_.1, f32[2,128]{1,0:T(2,128)} %refs_14_.1), custom_call_target="tpu_custom_call" | custom-call | flops 1000000 | bytes 2053120 | tf_op jit(solution)/shard_map/prep/pallas_call | solution.py:94
  3.1 5.1 %collective-permute-start.5 = (bf16[208,128]{1,0:T(8,128)(2,1)}, bf16[208,128]{1,0:T(8,128)(2,1)S(1)}, u32[]{:S(2)}, u32[]{:S(2)}) collective-permute-start(bf16[208,128]{1,0:T(8,128)(2,1)} %get-tuple-element.115), channel_id=1, source_target_pairs={{0,3},{1,2},{2,1},{3,0},{4,7},{5,6},{6,5},{7,4},{8,11},{9,10},{10,... | collective-permute-start | bytes 159752 | tf_op jit(solution)/shard_map/ppermute | solution.py:714
  8.2 0.6 collective-permute-start.3
  8.8 3.7 %collective-permute-start.2 = (bf16[512,128]{1,0:T(8,128)(2,1)}, bf16[512,128]{1,0:T(8,128)(2,1)S(1)}, u32[]{:S(2)}, u32[]{:S(2)}) collective-permute-start(bf16[512,128]{1,0:T(8,128)(2,1)} %get-tuple-element.113.refs_3_.refs_1_), channel_id=1, source_target_pairs={{0,3},{1,2},{2,1},{3,0},{4,7},{5,6},{6,5},{7,4},{8,11},{9,10},{10,... | collective-permute-start | bytes 393224 | tf_op jit(solution)/shard_map/ppermute | solution.py:714
  12.6 1.7 %constant_dynamic-slice_fusion.3 = (bf16[2048,128]{1,0:T(8,128)(2,1)S(1)}, bf16[2048,128]{1,0:T(8,128)(2,1)S(1)}, bf16[2048,128]{1,0:T(8,128)(2,1)S(1)}, bf16[2048,128]{1,0:T(8,128)(2,1)S(1)}) fusion(bf16[2048,512]{1,0:T(8,128)(2,1)} %refs_1_.5, s32[]{:T(128)S(6)} %select_n.12, s32[]{:T(128)S(6)} %select_n.14, s32[]{:T(128)S(6)} %select_n.13, s32[]{:T(128)S(6)} %select_n.15), kind=kLoop, calls=%fused_computation.46 | loop fusion | bytes 4194320 | tf_op jit(solution)/shard_map/dynamic_slice | solution.py:790
  15.2 0.6 collective-permute-start.1
  15.9 2.3 %collective-permute-done.2.refs_6_.refs_4_ = bf16[512,128]{1,0:T(8,128)(2,1)S(1)} collective-permute-done((bf16[512,128]{1,0:T(8,128)(2,1)}, bf16[512,128]{1,0:T(8,128)(2,1)S(1)}, u32[]{:S(2)}, u32[]{:S(2)}) %collective-permute-start.2) | collective-permute-done | bytes 131104 | tf_op jit(solution)/shard_map/ppermute | solution.py:714
  18.2 2.4 %collective-permute-start.11 = (bf16[3,208,128]{2,1,0:T(8,128)(2,1)S(1)}, bf16[3,208,128]{2,1,0:T(8,128)(2,1)S(1)}, u32[]{:S(2)}, u32[]{:S(2)}) collective-permute-start(bf16[3,208,128]{2,1,0:T(8,128)(2,1)S(1)} %pad_maximum_fusion.2.refs_2_), channel_id=1, source_target_pairs={{0,24},{1,25},{2,26},{3,27},{4,28},{5,29},{6,30},{7,31},{8,16},{9,... | collective-permute-start | bytes 479240 | tf_op jit(solution)/shard_map/ppermute | solution.py:714
  21.7 2.7 %collective-permute-done.1.refs_5_.refs_3_ = bf16[512,128]{1,0:T(8,128)(2,1)S(1)} collective-permute-done((bf16[512,128]{1,0:T(8,128)(2,1)S(1)}, bf16[512,128]{1,0:T(8,128)(2,1)S(1)}, u32[]{:S(2)}, u32[]{:S(2)}) %collective-permute-start.1) | collective-permute-done | bytes 131104 | tf_op jit(solution)/shard_map/ppermute | solution.py:714
  26.0 5.5 %keys.1 = (f32[512,2048]{1,0:T(8,128)S(1)}, bf16[512,2048]{1,0:T(8,128)(2,1)S(1)}, bf16[512,2048]{1,0:T(8,128)(2,1)S(1)}, f32[4,80,256]{2,1,0:T(8,128)S(1)}, bf16[4,80,256]{2,1,0:T(8,128)(2,1)S(1)}) custom-call(s32[4]{0:T(128)S(1)} %pad_add_fusion.refs_0_, bf16[2048,512]{1,0:T(8,128)(2,1)S(1)} %pad_maximum_fusion.refs_1_.refs_3_.refs_2_.refs_5_, ...), custom_call_target="tpu_custom_call" | custom-call | flops 1000 | bytes 12034064 | tf_op jit(solution)/shard_map/keys/pallas_call | solution.py:94
  33.0 2.5 %collective-permute-start.15 = (bf16[80,256]{1,0:T(8,128)(2,1)S(1)}, bf16[80,256]{1,0:T(8,128)(2,1)S(1)}, u32[]{:S(2)}, u32[]{:S(2)}) collective-permute-start(bf16[80,256]{1,0:T(8,128)(2,1)S(1)} %get-tuple-element.233), channel_id=1, source_target_pairs={{0,24},{1,25},{2,26},{3,27},{4,28},{5,29},{6,30},{7,31},{8,16},{9,... | collective-permute-start | bytes 122888 | tf_op jit(solution)/shard_map/ppermute | solution.py:714
  36.6 1.8 %weights.1 = (bf16[512,512]{1,0:T(8,128)(2,1)S(1)}, bf16[512,512]{1,0:T(8,128)(2,1)S(1)}, bf16[512,512]{1,0:T(8,128)(2,1)S(1)}, f32[512,128]{1,0:T(8,128)S(1)}, ...) custom-call(s32[4]{0:T(128)S(1)} %pad_add_fusion.refs_0_, ...), custom_call_target="tpu_custom_call" | custom-call | flops 1000000 | bytes 4849680 | tf_op jit(solution)/shard_map/weights/pallas_call | solution.py:94
  38.3 1.2 collective-permute-done.14
  40.0 2.7 %collective-permute-start.22 = (bf16[80,256]{1,0:T(8,128)(2,1)S(1)}, bf16[80,256]{1,0:T(8,128)(2,1)S(1)}, u32[]{:S(2)}, u32[]{:S(2)}) collective-permute-start(bf16[80,256]{1,0:T(8,128)(2,1)S(1)} %fusion.12), channel_id=1, source_target_pairs={{0,3},{1,2},{2,1},{3,0},{4,7},{5,6},{6,5},{7,4},{8,11},{9,10},{10,... | collective-permute-start | bytes 122888 | tf_op jit(solution)/shard_map/ppermute | solution.py:714
  42.7 0.9 collective-permute-start.21
  43.7 0.8 collective-permute-start.20
  44.5 1.9 %query.1 = (f32[512,2048]{1,0:T(8,128)S(1)}, bf16[512,2048]{1,0:T(8,128)(2,1)S(1)}) custom-call(s32[4]{0:T(128)S(1)} %pad_add_fusion.refs_0_, bf16[2048,512]{1,0:T(8,128)(2,1)S(1)} %pad_maximum_fusion.refs_1_.refs_3_.refs_2_.refs_5_, bf16[512,512]{1,0:T(8,128)(2,1)S(1)} %get-tuple-element.127.refs_2_), custom_call_target="tpu_custom_call" | custom-call | flops 1073741824 | bytes 8912912 | tf_op jit(solution)/shard_map/query/pallas_call | solution.py:94
  46.4 1.9 %gate.1.refs_3_ = f32[512,2048]{1,0:T(8,128)S(1)} custom-call(s32[4]{0:T(128)S(1)} %pad_add_fusion.refs_0_, bf16[2048,512]{1,0:T(8,128)(2,1)S(1)} %pad_maximum_fusion.refs_1_.refs_3_.refs_2_.refs_5_, bf16[512,512]{1,0:T(8,128)(2,1)S(1)} %get-tuple-element.133.refs_2_), custom_call_target="tpu_custom_call" | custom-call | flops 1073741824 | bytes 6815760 | tf_op jit(solution)/shard_map/gate/pallas_call | solution.py:94
  48.3 1.6 %collective-permute-start.26 = (bf16[80,256]{1,0:T(8,128)(2,1)S(1)}, bf16[80,256]{1,0:T(8,128)(2,1)S(1)}, u32[]{:S(2)}, u32[]{:S(2)}) collective-permute-start(bf16[80,256]{1,0:T(8,128)(2,1)S(1)} %add_convert_fusion.1.refs_7_.refs_5_), channel_id=1, source_target_pairs={{0,24},{1,25},{2,26},{3,27},{4,28},{5,29},{6,30},{7,31},{8,16},{9,... | collective-permute-start | bytes 122888 | tf_op jit(solution)/shard_map/ppermute | solution.py:714
  50.4 1.5 %collective-permute-start.24 = (bf16[80,256]{1,0:T(8,128)(2,1)S(1)}, bf16[80,256]{1,0:T(8,128)(2,1)S(1)}, u32[]{:S(2)}, u32[]{:S(2)}) collective-permute-start(bf16[80,256]{1,0:T(8,128)(2,1)S(1)} %add_convert_fusion.1.refs_7_.refs_5_), channel_id=1, source_target_pairs={{0,8},{1,9},{2,10},{3,11},{4,12},{5,13},{6,14},{7,15},{8,0},{9,1},... | collective-permute-start | bytes 122888 | tf_op jit(solution)/shard_map/ppermute | solution.py:714
  51.9 1.8 %grad_prod.1.refs_4_ = f32[512,2048]{1,0:T(8,128)S(1)} custom-call(s32[4]{0:T(128)S(1)} %pad_add_fusion.refs_0_, bf16[2048,512]{1,0:T(8,128)(2,1)S(1)} %copy-done, bf16[512,512]{1,0:T(8,128)(2,1)S(1)} %get-tuple-element.138.refs_2_.refs_3_), custom_call_target="tpu_custom_call" | custom-call | flops 1073741824 | bytes 6815760 | tf_op jit(solution)/shard_map/grad_prod/pallas_call | solution.py:94
  54.9 0.7 collective-permute-done.27.refs_10_.refs_8_
  56.1 9.5 %middle.1 = (bf16[512,2048]{1,0:T(8,128)(2,1)S(1)}, bf16[512,2048]{1,0:T(8,128)(2,1)S(1)}, bf16[512,2048]{1,0:T(8,128)(2,1)S(1)}, f32[16,2048]{1,0:T(8,128)S(1)}...) custom-call(s32[4]{0:T(128)S(1)} %pad_add_fusion.refs_0_, s32[1,2048]{1,0:T(1,128)S(1)} %bitcast.69, ...), custom_call_target="tpu_custom_call" | custom-call | flops 6442450944 | bytes 18259984 | tf_op jit(solution)/shard_map/middle/pallas_call | solution.py:94
  65.9 1.2 collective-permute-done.30
  67.2 1.6 %collective-permute-start.31 = (bf16[80,256]{1,0:T(8,128)(2,1)S(1)}, bf16[80,256]{1,0:T(8,128)(2,1)S(1)}, u32[]{:S(2)}, u32[]{:S(2)}) collective-permute-start(bf16[80,256]{1,0:T(8,128)(2,1)S(1)} %get-tuple-element.232), channel_id=1, source_target_pairs={{0,8},{1,9},{2,10},{3,11},{4,12},{5,13},{6,14},{7,15},{8,0},{9,1},... | collective-permute-start | bytes 122888 | tf_op jit(solution)/shard_map/ppermute | solution.py:714
  68.8 1.5 %collective-permute-start.33 = (bf16[80,256]{1,0:T(8,128)(2,1)S(1)}, bf16[80,256]{1,0:T(8,128)(2,1)S(1)}, u32[]{:S(2)}, u32[]{:S(2)}) collective-permute-start(bf16[80,256]{1,0:T(8,128)(2,1)S(1)} %get-tuple-element.230), channel_id=1, source_target_pairs={{0,24},{1,25},{2,26},{3,27},{4,28},{5,29},{6,30},{7,31},{8,16},{9,... | collective-permute-start | bytes 122888 | tf_op jit(solution)/shard_map/ppermute | solution.py:714
  70.8 2.9 %gate_back.1 = (f32[512,512]{1,0:T(8,128)S(1)}, f32[512,512]{1,0:T(8,128)S(1)}) custom-call(s32[4]{0:T(128)S(1)} %pad_add_fusion.refs_0_, bf16[512,2048]{1,0:T(8,128)(2,1)S(1)} %get-tuple-element.147.refs_1_.refs_4_, bf16[512,2048]{1,0:T(8,128)(2,1)S(1)} %get-tuple-element.148.refs_2_, bf16[2048,512]{1,0:T(8,128)(2,1)S(1)} %pad_maximum_fusion.refs_1_.refs_3_.refs_2_.refs_5_, ...), custom_call_target="tpu_custom_call" | custom-call | flops 2147483648 | bytes 10485776 | tf_op jit(solution)/shard_map/gate_back/pallas_call | solution.py:94
  74.3 2.7 %collective-permute-start.36 = (bf16[80,256]{1,0:T(8,128)(2,1)S(1)}, bf16[80,256]{1,0:T(8,128)(2,1)S(1)}, u32[]{:S(2)}, u32[]{:S(2)}) collective-permute-start(bf16[80,256]{1,0:T(8,128)(2,1)S(1)} %fusion.9), channel_id=1, source_target_pairs={{0,3},{1,2},{2,1},{3,0},{4,7},{5,6},{6,5},{7,4},{8,11},{9,10},{10,... | collective-permute-start | bytes 122888 | tf_op jit(solution)/shard_map/ppermute | solution.py:714
  77.0 1.7 %collective-permute-start.34 = (bf16[80,256]{1,0:T(8,128)(2,1)S(1)}, bf16[80,256]{1,0:T(8,128)(2,1)S(1)}, u32[]{:S(2)}, u32[]{:S(2)}) collective-permute-start(bf16[80,256]{1,0:T(8,128)(2,1)S(1)} %fusion.9), channel_id=1, source_target_pairs={{0,1},{1,0},{2,3},{3,2},{4,5},{5,4},{6,7},{7,6},{8,9},{9,8},{10,11... | collective-permute-start | bytes 122888 | tf_op jit(solution)/shard_map/ppermute | solution.py:714
  78.8 3.1 %query_back.1.refs_1_ = bf16[512,2048]{1,0:T(8,128)(2,1)S(1)} custom-call(s32[4]{0:T(128)S(1)} %pad_add_fusion.refs_0_, s32[1,2048]{1,0:T(1,128)S(1)} %bitcast.70, bf16[512,2048]{1,0:T(8,128)(2,1)S(1)} %get-tuple-element.154.refs_2_, f32[16,2048]{1,0:T(8,128)S(1)} %get-tuple-element.155.refs_3_, f32[512,2048]{1,0:T(8,128)S(1)} %get-tuple-element.156.refs_4_, ...), custom_call_target="tpu_custom_call" | custom-call | flops 2147483648 | bytes 8855568 | tf_op jit(solution)/shard_map/query_back/pallas_call | solution.py:94
  82.2 1.8 %collective-permute-start.40 = (bf16[80,256]{1,0:T(8,128)(2,1)S(1)}, bf16[80,256]{1,0:T(8,128)(2,1)S(1)}, u32[]{:S(2)}, u32[]{:S(2)}) collective-permute-start(bf16[80,256]{1,0:T(8,128)(2,1)S(1)} %add_convert_fusion.refs_6_), channel_id=1, source_target_pairs={{0,24},{1,25},{2,26},{3,27},{4,28},{5,29},{6,30},{7,31},{8,16},{9,... | collective-permute-start | bytes 122888 | tf_op jit(solution)/shard_map/ppermute | solution.py:714
  84.0 1.0 collective-permute-start.39
  85.0 0.8 collective-permute-start.38
  85.8 1.8 %grad_query.1.refs_1_ = f32[512,512]{1,0:T(8,128)S(1)} custom-call(s32[4]{0:T(128)S(1)} %pad_add_fusion.refs_0_, bf16[512,2048]{1,0:T(8,128)(2,1)S(1)} %query_back.1.refs_1_, bf16[2048,512]{1,0:T(8,128)(2,1)S(1)} %pad_maximum_fusion.refs_1_.refs_3_.refs_2_.refs_5_), custom_call_target="tpu_custom_call" | custom-call | flops 1073741824 | bytes 5242896 | tf_op jit(solution)/shard_map/grad_query/pallas_call | solution.py:94
  87.6 1.2 early.1
  90.0 1.3 collective-permute-done.44
  91.6 1.2 collective-permute-start.45
  92.9 1.0 collective-permute-start.46
  93.9 1.3 collective-permute-start.47
  95.2 6.7 %key_back.1 = (bf16[512,2048]{1,0:T(8,128)(2,1)S(1)}, bf16[512,2048]{1,0:T(8,128)(2,1)S(1)}, f32[8,512]{1,0:T(8,128)S(1)}, f32[4,4,128,128]{3,2,1,0:T(8,128)S(1)}, bf16[4,4,128,128]{3,2,1,0:T(8,128)(2,1)S(1)}) custom-call(s32[4]{0:T(128)S(1)} %pad_add_fusion.refs_0_, s32[1,2048]{1,0:T(1,128)S(1)} %bitcast.71, f32[512,2048]{1,0:T(8,128)S(1)} %get-tuple-element.119.refs_2_, ...), custom_call_target="tpu_custom_call" | custom-call | flops 6442450944 | bytes 16605200 | tf_op jit(solution)/shard_map/key_back/pallas_call | solution.py:94
  101.9 1.8 %collective-permute-done.46 = bf16[4,192,128]{2,1,0:T(8,128)(2,1)S(1)} collective-permute-done((bf16[4,192,128]{2,1,0:T(8,128)(2,1)S(1)}, bf16[4,192,128]{2,1,0:T(8,128)(2,1)S(1)}, u32[]{:S(2)}, u32[]{:S(2)}) %collective-permute-start.46) | collective-permute-done | bytes 196640 | tf_op jit(solution)/shard_map/ppermute | solution.py:714
  103.7 0.8 key_weights.1.refs_6_
  104.6 1.0 collective-permute-done.48
  105.9 0.9 collective-permute-start.49
  106.8 1.6 %collective-permute-start.51 = (bf16[4,128,128]{2,1,0:T(8,128)(2,1)S(1)}, bf16[4,128,128]{2,1,0:T(8,128)(2,1)S(1)}, u32[]{:S(2)}, u32[]{:S(2)}) collective-permute-start(bf16[4,128,128]{2,1,0:T(8,128)(2,1)S(1)} %get-tuple-element.224), channel_id=1, source_target_pairs={{0,24},{1,25},{2,26},{3,27},{4,28},{5,29},{6,30},{7,31},{8,16},{9,... | collective-permute-start | bytes 393224 | tf_op jit(solution)/shard_map/ppermute | solution.py:714
  108.4 1.0 collective-permute-start.50
  109.4 7.0 %inputs.1 = f32[2048,512]{1,0:T(8,128)} custom-call(s32[4]{0:T(128)S(1)} %pad_add_fusion.refs_0_, bf16[512,2048]{1,0:T(8,128)(2,1)S(1)} %query_back.1.refs_1_, bf16[512,2048]{1,0:T(8,128)(2,1)S(1)} %get-tuple-element.175.refs_2_, bf16[512,2048]{1,0:T(8,128)(2,1)S(1)} %get-tuple-element.176.refs_3_, bf16[512,2048]{1,0:T(8,128)(2,1)S(1)} %get-tuple-element.147.refs_1_.refs_4_, ...), custom_call_target="tpu_custom_call" | custom-call | flops 4294967296 | bytes 16777232 | tf_op jit(solution)/shard_map/inputs/pallas_call | solution.py:94
  116.6 0.9 collective-permute-start.52
  117.5 2.4 %collective-permute-start.53 = (bf16[320,128]{1,0:T(8,128)(2,1)S(1)}, bf16[320,128]{1,0:T(8,128)(2,1)S(1)}, u32[]{:S(2)}, u32[]{:S(2)}) collective-permute-start(bf16[320,128]{1,0:T(8,128)(2,1)S(1)} %get-tuple-element.184), channel_id=1, source_target_pairs={{0,2},{1,3},{2,0},{3,1},{4,6},{5,7},{6,4},{7,5},{8,10},{9,11},{10,... | collective-permute-start | bytes 245768 | tf_op jit(solution)/shard_map/ppermute | solution.py:714
  119.9 1.2 collective-permute-start.54
  121.1 3.5 %output.1 = f32[2048,512]{1,0:T(8,128)} custom-call(s32[4]{0:T(128)S(1)} %pad_add_fusion.refs_0_, bf16[2048,512]{1,0:T(8,128)(2,1)S(1)} %copy-done.1, bf16[512,2048]{1,0:T(8,128)(2,1)S(1)} %get-tuple-element.148.refs_2_, bf16[512,512]{1,0:T(8,128)(2,1)S(1)} %get-tuple-element.138.refs_2_.refs_3_), custom_call_target="tpu_custom_call" | custom-call | flops 1073741824 | bytes 8912912 | tf_op jit(solution)/shard_map/output/pallas_call | solution.py:94
  124.6 0.7 collective-permute-done.53.refs_2_
  125.3 1.0 collective-permute-done.54.refs_3_
  126.3 1.3 collective-permute-start.60
  127.6 1.1 collective-permute-start.58
  128.7 1.2 collective-permute-start.56
  129.9 1.9 %collective-permute-done.60.refs_6_.refs_7_ = bf16[320,128]{1,0:T(8,128)(2,1)S(1)} collective-permute-done((bf16[320,128]{1,0:T(8,128)(2,1)S(1)}, bf16[320,128]{1,0:T(8,128)(2,1)S(1)}, u32[]{:S(2)}, u32[]{:S(2)}) %collective-permute-start.60) | collective-permute-done | bytes 81952 | tf_op jit(solution)/shard_map/ppermute | solution.py:714
  131.8 0.8 collective-permute-done.58.refs_4_.refs_5_
  133.1 0.7 collective-permute-done.59.refs_5_.refs_6_
  134.6 2.6 %collective-permute-start.64 = (f32[8,128]{1,0:T(8,128)S(1)}, f32[8,128]{1,0:T(8,128)S(1)}, u32[]{:S(2)}, u32[]{:S(2)}) collective-permute-start(f32[8,128]{1,0:T(8,128)S(1)} %squares.1.refs_1_), channel_id=1, source_target_pairs={{0,3},{1,2},{2,1},{3,0},{4,7},{5,6},{6,5},{7,4},{8,11},{9,10},{10,... | collective-permute-start | bytes 12296 | tf_op jit(solution)/shard_map/ppermute | solution.py:714
  137.4 1.6 %collective-permute-start.62 = (f32[8,128]{1,0:T(8,128)S(1)}, f32[8,128]{1,0:T(8,128)S(1)}, u32[]{:S(2)}, u32[]{:S(2)}) collective-permute-start(f32[8,128]{1,0:T(8,128)S(1)} %squares.1.refs_1_), channel_id=1, source_target_pairs={{0,1},{1,0},{2,3},{3,2},{4,5},{5,4},{6,7},{7,6},{8,9},{9,8},{10,11... | collective-permute-start | bytes 12296 | tf_op jit(solution)/shard_map/ppermute | solution.py:714
  139.0 1.0 assemble.1
  140.0 1.7 %collective-permute-done.63.refs_3_ = f32[8,128]{1,0:T(8,128)S(1)} collective-permute-done((f32[8,128]{1,0:T(8,128)S(1)}, f32[8,128]{1,0:T(8,128)S(1)}, u32[]{:S(2)}, u32[]{:S(2)}) %collective-permute-start.63) | collective-permute-done | bytes 4128 | tf_op jit(solution)/shard_map/ppermute | solution.py:714
  141.8 3.8 %update.1 = (f32[1,1]{1,0:T(1,128)}, f32[128,2048]{1,0:T(8,128)}, f32[128,2048]{1,0:T(8,128)}, f32[128,2048]{1,0:T(8,128)}, bf16[128,2048]{1,0:T(8,128)(2,1)}, /...) custom-call(s32[4]{0:T(128)S(1)} %pad_add_fusion.refs_0_, ...), custom_call_target="tpu_custom_call" | custom-call | flops 1000000 | bytes 9870356 | tf_op jit(solution)/shard_map/update/pallas_call | solution.py:94
  (136 shorter events, 13.7 us)
Async XLA Ops:
  3.1 11.5 %collective-permute-start.5 = (bf16[208,128]{1,0:T(8,128)(2,1)}, bf16[208,128]{1,0:T(8,128)(2,1)S(1)}, u32[]{:S(2)}, u32[]{:S(2)}) collective-permute-start(bf16[208,128]{1,0:T(8,128)(2,1)} %get-tuple-element.115), channel_id=1, source_target_pairs={{0,3},{1,2},{2,1},{3,0},{4,7},{5,6},{6,5},{7,4},{8,11},{9,10},{10,... | collective-permute-start | bytes 159752 | tf_op jit(solution)/shard_map/ppermute | solution.py:714
  8.2 7.6 %collective-permute-start.4 = (bf16[208,128]{1,0:T(8,128)(2,1)}, bf16[208,128]{1,0:T(8,128)(2,1)S(1)}, u32[]{:S(2)}, u32[]{:S(2)}) collective-permute-start(bf16[208,128]{1,0:T(8,128)(2,1)} %get-tuple-element.115), channel_id=1, source_target_pairs={{0,2},{1,3},{2,0},{3,1},{4,6},{5,7},{6,4},{7,5},{8,10},{9,11},{10,... | collective-permute-start | bytes 159752 | tf_op jit(solution)/shard_map/ppermute | solution.py:714
  8.2 7.6 %collective-permute-start.3 = (bf16[208,128]{1,0:T(8,128)(2,1)}, bf16[208,128]{1,0:T(8,128)(2,1)S(1)}, u32[]{:S(2)}, u32[]{:S(2)}) collective-permute-start(bf16[208,128]{1,0:T(8,128)(2,1)} %get-tuple-element.115), channel_id=1, source_target_pairs={{0,1},{1,0},{2,3},{3,2},{4,5},{5,4},{6,7},{7,6},{8,9},{9,8},{10,11... | collective-permute-start | bytes 159752 | tf_op jit(solution)/shard_map/ppermute | solution.py:714
  8.8 9.3 %collective-permute-start.2 = (bf16[512,128]{1,0:T(8,128)(2,1)}, bf16[512,128]{1,0:T(8,128)(2,1)S(1)}, u32[]{:S(2)}, u32[]{:S(2)}) collective-permute-start(bf16[512,128]{1,0:T(8,128)(2,1)} %get-tuple-element.113.refs_3_.refs_1_), channel_id=1, source_target_pairs={{0,3},{1,2},{2,1},{3,0},{4,7},{5,6},{6,5},{7,4},{8,11},{9,10},{10,... | collective-permute-start | bytes 393224 | tf_op jit(solution)/shard_map/ppermute | solution.py:714
  12.6 8.6 %collective-permute-start = (bf16[512,128]{1,0:T(8,128)(2,1)}, bf16[512,128]{1,0:T(8,128)(2,1)S(1)}, u32[]{:S(2)}, u32[]{:S(2)}) collective-permute-start(bf16[512,128]{1,0:T(8,128)(2,1)} %get-tuple-element.113.refs_3_.refs_1_), channel_id=1, source_target_pairs={{0,1},{1,0},{2,3},{3,2},{4,5},{5,4},{6,7},{7,6},{8,9},{9,8},{10,11... | collective-permute-start | bytes 393224 | tf_op jit(solution)/shard_map/ppermute | solution.py:714
  15.2 9.2 %collective-permute-start.1 = (bf16[512,128]{1,0:T(8,128)(2,1)S(1)}, bf16[512,128]{1,0:T(8,128)(2,1)S(1)}, u32[]{:S(2)}, u32[]{:S(2)}) collective-permute-start(bf16[512,128]{1,0:T(8,128)(2,1)S(1)} %copy-done.6), channel_id=1, source_target_pairs={{0,2},{1,3},{2,0},{3,1},{4,6},{5,7},{6,4},{7,5},{8,10},{9,11},{10,... | collective-permute-start | bytes 393224 | tf_op jit(solution)/shard_map/ppermute | solution.py:714
  18.2 6.2 %collective-permute-start.8 = (bf16[512,128]{1,0:T(8,128)(2,1)S(1)}, bf16[512,128]{1,0:T(8,128)(2,1)S(1)}, u32[]{:S(2)}, u32[]{:S(2)}) collective-permute-start(bf16[512,128]{1,0:T(8,128)(2,1)S(1)} %collective-permute-done.2.refs_6_.refs_4_), channel_id=1, source_target_pairs={{0,4},{1,5},{2,6},{3,7},{4,0},{5,1},{6,2},{7,3},{8,12},{9,13},{10,... | collective-permute-start | bytes 393224 | tf_op jit(solution)/shard_map/ppermute | solution.py:714
  18.2 13.2 %collective-permute-start.11 = (bf16[3,208,128]{2,1,0:T(8,128)(2,1)S(1)}, bf16[3,208,128]{2,1,0:T(8,128)(2,1)S(1)}, u32[]{:S(2)}, u32[]{:S(2)}) collective-permute-start(bf16[3,208,128]{2,1,0:T(8,128)(2,1)S(1)} %pad_maximum_fusion.2.refs_2_), channel_id=1, source_target_pairs={{0,24},{1,25},{2,26},{3,27},{4,28},{5,29},{6,30},{7,31},{8,16},{9,... | collective-permute-start | bytes 479240 | tf_op jit(solution)/shard_map/ppermute | solution.py:714
  20.6 10.8 %collective-permute-start.10 = (bf16[3,208,128]{2,1,0:T(8,128)(2,1)S(1)}, bf16[3,208,128]{2,1,0:T(8,128)(2,1)}, u32[]{:S(2)}, u32[]{:S(2)}) collective-permute-start(bf16[3,208,128]{2,1,0:T(8,128)(2,1)S(1)} %pad_maximum_fusion.2.refs_2_), channel_id=1, source_target_pairs={{0,16},{1,17},{2,18},{3,19},{4,20},{5,21},{6,22},{7,23},{8,24},{9,... | collective-permute-start | bytes 479240 | tf_op jit(solution)/shard_map/ppermute | solution.py:714
  21.1 10.3 %collective-permute-start.9 = (bf16[3,208,128]{2,1,0:T(8,128)(2,1)S(1)}, bf16[3,208,128]{2,1,0:T(8,128)(2,1)}, u32[]{:S(2)}, u32[]{:S(2)}) collective-permute-start(bf16[3,208,128]{2,1,0:T(8,128)(2,1)S(1)} %pad_maximum_fusion.2.refs_2_), channel_id=1, source_target_pairs={{0,8},{1,9},{2,10},{3,11},{4,12},{5,13},{6,14},{7,15},{8,0},{9,1},... | collective-permute-start | bytes 479240 | tf_op jit(solution)/shard_map/ppermute | solution.py:714
  24.4 1.3 collective-permute-start.6
  24.4 1.5 %collective-permute-start.7 = (bf16[512,128]{1,0:T(8,128)(2,1)S(1)}, bf16[512,128]{1,0:T(8,128)(2,1)S(1)}, u32[]{:S(2)}, u32[]{:S(2)}) collective-permute-start(bf16[512,128]{1,0:T(8,128)(2,1)S(1)} %collective-permute-done.1.refs_5_.refs_3_), channel_id=1, source_target_pairs={{0,4},{1,5},{2,6},{3,7},{4,0},{5,1},{6,2},{7,3},{8,12},{9,13},{10,... | collective-permute-start | bytes 393224 | tf_op jit(solution)/shard_map/ppermute | solution.py:714
  31.5 1.5 %collective-permute-start.12 = (bf16[4,80,256]{2,1,0:T(8,128)(2,1)S(1)}, bf16[4,80,256]{2,1,0:T(8,128)(2,1)S(1)}, u32[]{:S(2)}, u32[]{:S(2)}) collective-permute-start(bf16[4,80,256]{2,1,0:T(8,128)(2,1)S(1)} %get-tuple-element.124), channel_id=1, source_target_pairs={{0,4},{1,5},{2,6},{3,7},{4,0},{5,1},{6,2},{7,3},{8,12},{9,13},{10,... | collective-permute-start | bytes 491528 | tf_op jit(solution)/shard_map/ppermute | solution.py:714
  31.8 3.6 %collective-permute-start.16 = (bf16[3,208,128]{2,1,0:T(8,128)(2,1)S(1)}, bf16[3,208,128]{2,1,0:T(8,128)(2,1)S(1)}, u32[]{:S(2)}, u32[]{:S(2)}) collective-permute-start(bf16[3,208,128]{2,1,0:T(8,128)(2,1)S(1)} %pad_maximum_fusion.2.refs_2_), channel_id=1, source_target_pairs={{0,4},{1,5},{2,6},{3,7},{4,0},{5,1},{6,2},{7,3},{8,12},{9,13},{10,... | collective-permute-start | bytes 479240 | tf_op jit(solution)/shard_map/ppermute | solution.py:714
  32.0 4.0 %collective-permute-start.19 = (bf16[3,208,128]{2,1,0:T(8,128)(2,1)S(1)}, bf16[3,208,128]{2,1,0:T(8,128)(2,1)S(1)}, u32[]{:S(2)}, u32[]{:S(2)}) collective-permute-start(bf16[3,208,128]{2,1,0:T(8,128)(2,1)S(1)} %collective-permute-done.11.refs_8_), channel_id=1, source_target_pairs={{0,4},{1,5},{2,6},{3,7},{4,0},{5,1},{6,2},{7,3},{8,12},{9,13},{10,... | collective-permute-start | bytes 479240 | tf_op jit(solution)/shard_map/ppermute | solution.py:714
  32.4 4.2 %collective-permute-start.18 = (bf16[3,208,128]{2,1,0:T(8,128)(2,1)}, bf16[3,208,128]{2,1,0:T(8,128)(2,1)S(1)}, u32[]{:S(2)}, u32[]{:S(2)}) collective-permute-start(bf16[3,208,128]{2,1,0:T(8,128)(2,1)} %collective-permute-done.10.refs_6_), channel_id=1, source_target_pairs={{0,4},{1,5},{2,6},{3,7},{4,0},{5,1},{6,2},{7,3},{8,12},{9,13},{10,... | collective-permute-start | bytes 479240 | tf_op jit(solution)/shard_map/ppermute | solution.py:714
  32.5 4.0 %collective-permute-start.17 = (bf16[3,208,128]{2,1,0:T(8,128)(2,1)}, bf16[3,208,128]{2,1,0:T(8,128)(2,1)S(1)}, u32[]{:S(2)}, u32[]{:S(2)}) collective-permute-start(bf16[3,208,128]{2,1,0:T(8,128)(2,1)} %collective-permute-done.9.refs_4_), channel_id=1, source_target_pairs={{0,4},{1,5},{2,6},{3,7},{4,0},{5,1},{6,2},{7,3},{8,12},{9,13},{10,... | collective-permute-start | bytes 479240 | tf_op jit(solution)/shard_map/ppermute | solution.py:714
  33.0 5.4 %collective-permute-start.15 = (bf16[80,256]{1,0:T(8,128)(2,1)S(1)}, bf16[80,256]{1,0:T(8,128)(2,1)S(1)}, u32[]{:S(2)}, u32[]{:S(2)}) collective-permute-start(bf16[80,256]{1,0:T(8,128)(2,1)S(1)} %get-tuple-element.233), channel_id=1, source_target_pairs={{0,24},{1,25},{2,26},{3,27},{4,28},{5,29},{6,30},{7,31},{8,16},{9,... | collective-permute-start | bytes 122888 | tf_op jit(solution)/shard_map/ppermute | solution.py:714
  35.5 4.0 %collective-permute-start.14 = (bf16[80,256]{1,0:T(8,128)(2,1)S(1)}, bf16[80,256]{1,0:T(8,128)(2,1)S(1)}, u32[]{:S(2)}, u32[]{:S(2)}) collective-permute-start(bf16[80,256]{1,0:T(8,128)(2,1)S(1)} %get-tuple-element.234), channel_id=1, source_target_pairs={{0,16},{1,17},{2,18},{3,19},{4,20},{5,21},{6,22},{7,23},{8,24},{9,... | collective-permute-start | bytes 122888 | tf_op jit(solution)/shard_map/ppermute | solution.py:714
  36.0 4.0 %collective-permute-start.13 = (bf16[80,256]{1,0:T(8,128)(2,1)S(1)}, bf16[80,256]{1,0:T(8,128)(2,1)S(1)}, u32[]{:S(2)}, u32[]{:S(2)}) collective-permute-start(bf16[80,256]{1,0:T(8,128)(2,1)S(1)} %get-tuple-element.235), channel_id=1, source_target_pairs={{0,8},{1,9},{2,10},{3,11},{4,12},{5,13},{6,14},{7,15},{8,0},{9,1},... | collective-permute-start | bytes 122888 | tf_op jit(solution)/shard_map/ppermute | solution.py:714
  40.0 8.2 %collective-permute-start.22 = (bf16[80,256]{1,0:T(8,128)(2,1)S(1)}, bf16[80,256]{1,0:T(8,128)(2,1)S(1)}, u32[]{:S(2)}, u32[]{:S(2)}) collective-permute-start(bf16[80,256]{1,0:T(8,128)(2,1)S(1)} %fusion.12), channel_id=1, source_target_pairs={{0,3},{1,2},{2,1},{3,0},{4,7},{5,6},{6,5},{7,4},{8,11},{9,10},{10,... | collective-permute-start | bytes 122888 | tf_op jit(solution)/shard_map/ppermute | solution.py:714
  42.7 5.5 %collective-permute-start.21 = (bf16[80,256]{1,0:T(8,128)(2,1)S(1)}, bf16[80,256]{1,0:T(8,128)(2,1)S(1)}, u32[]{:S(2)}, u32[]{:S(2)}) collective-permute-start(bf16[80,256]{1,0:T(8,128)(2,1)S(1)} %fusion.12), channel_id=1, source_target_pairs={{0,2},{1,3},{2,0},{3,1},{4,6},{5,7},{6,4},{7,5},{8,10},{9,11},{10,... | collective-permute-start | bytes 122888 | tf_op jit(solution)/shard_map/ppermute | solution.py:714
  43.7 4.6 %collective-permute-start.20 = (bf16[80,256]{1,0:T(8,128)(2,1)S(1)}, bf16[80,256]{1,0:T(8,128)(2,1)S(1)}, u32[]{:S(2)}, u32[]{:S(2)}) collective-permute-start(bf16[80,256]{1,0:T(8,128)(2,1)S(1)} %fusion.12), channel_id=1, source_target_pairs={{0,1},{1,0},{2,3},{3,2},{4,5},{5,4},{6,7},{7,6},{8,9},{9,8},{10,11... | collective-permute-start | bytes 122888 | tf_op jit(solution)/shard_map/ppermute | solution.py:714
  48.3 5.4 %collective-permute-start.26 = (bf16[80,256]{1,0:T(8,128)(2,1)S(1)}, bf16[80,256]{1,0:T(8,128)(2,1)S(1)}, u32[]{:S(2)}, u32[]{:S(2)}) collective-permute-start(bf16[80,256]{1,0:T(8,128)(2,1)S(1)} %add_convert_fusion.1.refs_7_.refs_5_), channel_id=1, source_target_pairs={{0,24},{1,25},{2,26},{3,27},{4,28},{5,29},{6,30},{7,31},{8,16},{9,... | collective-permute-start | bytes 122888 | tf_op jit(solution)/shard_map/ppermute | solution.py:714
  49.9 4.0 %collective-permute-start.25 = (bf16[80,256]{1,0:T(8,128)(2,1)S(1)}, bf16[80,256]{1,0:T(8,128)(2,1)S(1)}, u32[]{:S(2)}, u32[]{:S(2)}) collective-permute-start(bf16[80,256]{1,0:T(8,128)(2,1)S(1)} %add_convert_fusion.1.refs_7_.refs_5_), channel_id=1, source_target_pairs={{0,16},{1,17},{2,18},{3,19},{4,20},{5,21},{6,22},{7,23},{8,24},{9,... | collective-permute-start | bytes 122888 | tf_op jit(solution)/shard_map/ppermute | solution.py:714
  50.4 4.0 %collective-permute-start.24 = (bf16[80,256]{1,0:T(8,128)(2,1)S(1)}, bf16[80,256]{1,0:T(8,128)(2,1)S(1)}, u32[]{:S(2)}, u32[]{:S(2)}) collective-permute-start(bf16[80,256]{1,0:T(8,128)(2,1)S(1)} %add_convert_fusion.1.refs_7_.refs_5_), channel_id=1, source_target_pairs={{0,8},{1,9},{2,10},{3,11},{4,12},{5,13},{6,14},{7,15},{8,0},{9,1},... | collective-permute-start | bytes 122888 | tf_op jit(solution)/shard_map/ppermute | solution.py:714
  51.9 3.0 %collective-permute-start.23 = (bf16[80,256]{1,0:T(8,128)(2,1)S(1)}, bf16[80,256]{1,0:T(8,128)(2,1)S(1)}, u32[]{:S(2)}, u32[]{:S(2)}) collective-permute-start(bf16[80,256]{1,0:T(8,128)(2,1)S(1)} %add_convert_fusion.1.refs_7_.refs_5_), channel_id=1, source_target_pairs={{0,4},{1,5},{2,6},{3,7},{4,0},{5,1},{6,2},{7,3},{8,12},{9,13},{10,... | collective-permute-start | bytes 122888 | tf_op jit(solution)/shard_map/ppermute | solution.py:714
  54.4 1.4 collective-permute-start.28
  54.9 1.2 collective-permute-start.29
  65.7 1.5 %collective-permute-start.30 = (bf16[4,80,256]{2,1,0:T(8,128)(2,1)S(1)}, bf16[4,80,256]{2,1,0:T(8,128)(2,1)S(1)}, u32[]{:S(2)}, u32[]{:S(2)}) collective-permute-start(bf16[4,80,256]{2,1,0:T(8,128)(2,1)S(1)} %get-tuple-element.145), channel_id=1, source_target_pairs={{0,4},{1,5},{2,6},{3,7},{4,0},{5,1},{6,2},{7,3},{8,12},{9,13},{10,... | collective-permute-start | bytes 491528 | tf_op jit(solution)/shard_map/ppermute | solution.py:714
  67.2 7.1 %collective-permute-start.31 = (bf16[80,256]{1,0:T(8,128)(2,1)S(1)}, bf16[80,256]{1,0:T(8,128)(2,1)S(1)}, u32[]{:S(2)}, u32[]{:S(2)}) collective-permute-start(bf16[80,256]{1,0:T(8,128)(2,1)S(1)} %get-tuple-element.232), channel_id=1, source_target_pairs={{0,8},{1,9},{2,10},{3,11},{4,12},{5,13},{6,14},{7,15},{8,0},{9,1},... | collective-permute-start | bytes 122888 | tf_op jit(solution)/shard_map/ppermute | solution.py:714
  68.8 4.9 %collective-permute-start.33 = (bf16[80,256]{1,0:T(8,128)(2,1)S(1)}, bf16[80,256]{1,0:T(8,128)(2,1)S(1)}, u32[]{:S(2)}, u32[]{:S(2)}) collective-permute-start(bf16[80,256]{1,0:T(8,128)(2,1)S(1)} %get-tuple-element.230), channel_id=1, source_target_pairs={{0,24},{1,25},{2,26},{3,27},{4,28},{5,29},{6,30},{7,31},{8,16},{9,... | collective-permute-start | bytes 122888 | tf_op jit(solution)/shard_map/ppermute | solution.py:714
  70.3 4.0 %collective-permute-start.32 = (bf16[80,256]{1,0:T(8,128)(2,1)S(1)}, bf16[80,256]{1,0:T(8,128)(2,1)S(1)}, u32[]{:S(2)}, u32[]{:S(2)}) collective-permute-start(bf16[80,256]{1,0:T(8,128)(2,1)S(1)} %get-tuple-element.231), channel_id=1, source_target_pairs={{0,16},{1,17},{2,18},{3,19},{4,20},{5,21},{6,22},{7,23},{8,24},{9,... | collective-permute-start | bytes 122888 | tf_op jit(solution)/shard_map/ppermute | solution.py:714
  74.3 7.6 %collective-permute-start.36 = (bf16[80,256]{1,0:T(8,128)(2,1)S(1)}, bf16[80,256]{1,0:T(8,128)(2,1)S(1)}, u32[]{:S(2)}, u32[]{:S(2)}) collective-permute-start(bf16[80,256]{1,0:T(8,128)(2,1)S(1)} %fusion.9), channel_id=1, source_target_pairs={{0,3},{1,2},{2,1},{3,0},{4,7},{5,6},{6,5},{7,4},{8,11},{9,10},{10,... | collective-permute-start | bytes 122888 | tf_op jit(solution)/shard_map/ppermute | solution.py:714
  77.0 5.2 %collective-permute-start.35 = (bf16[80,256]{1,0:T(8,128)(2,1)S(1)}, bf16[80,256]{1,0:T(8,128)(2,1)S(1)}, u32[]{:S(2)}, u32[]{:S(2)}) collective-permute-start(bf16[80,256]{1,0:T(8,128)(2,1)S(1)} %fusion.9), channel_id=1, source_target_pairs={{0,2},{1,3},{2,0},{3,1},{4,6},{5,7},{6,4},{7,5},{8,10},{9,11},{10,... | collective-permute-start | bytes 122888 | tf_op jit(solution)/shard_map/ppermute | solution.py:714
  77.0 5.2 %collective-permute-start.34 = (bf16[80,256]{1,0:T(8,128)(2,1)S(1)}, bf16[80,256]{1,0:T(8,128)(2,1)S(1)}, u32[]{:S(2)}, u32[]{:S(2)}) collective-permute-start(bf16[80,256]{1,0:T(8,128)(2,1)S(1)} %fusion.9), channel_id=1, source_target_pairs={{0,1},{1,0},{2,3},{3,2},{4,5},{5,4},{6,7},{7,6},{8,9},{9,8},{10,11... | collective-permute-start | bytes 122888 | tf_op jit(solution)/shard_map/ppermute | solution.py:714
  82.2 6.6 %collective-permute-start.40 = (bf16[80,256]{1,0:T(8,128)(2,1)S(1)}, bf16[80,256]{1,0:T(8,128)(2,1)S(1)}, u32[]{:S(2)}, u32[]{:S(2)}) collective-permute-start(bf16[80,256]{1,0:T(8,128)(2,1)S(1)} %add_convert_fusion.refs_6_), channel_id=1, source_target_pairs={{0,24},{1,25},{2,26},{3,27},{4,28},{5,29},{6,30},{7,31},{8,16},{9,... | collective-permute-start | bytes 122888 | tf_op jit(solution)/shard_map/ppermute | solution.py:714
  84.0 4.8 %collective-permute-start.39 = (bf16[80,256]{1,0:T(8,128)(2,1)S(1)}, bf16[80,256]{1,0:T(8,128)(2,1)S(1)}, u32[]{:S(2)}, u32[]{:S(2)}) collective-permute-start(bf16[80,256]{1,0:T(8,128)(2,1)S(1)} %add_convert_fusion.refs_6_), channel_id=1, source_target_pairs={{0,16},{1,17},{2,18},{3,19},{4,20},{5,21},{6,22},{7,23},{8,24},{9,... | collective-permute-start | bytes 122888 | tf_op jit(solution)/shard_map/ppermute | solution.py:714
  85.0 4.0 %collective-permute-start.38 = (bf16[80,256]{1,0:T(8,128)(2,1)S(1)}, bf16[80,256]{1,0:T(8,128)(2,1)S(1)}, u32[]{:S(2)}, u32[]{:S(2)}) collective-permute-start(bf16[80,256]{1,0:T(8,128)(2,1)S(1)} %add_convert_fusion.refs_6_), channel_id=1, source_target_pairs={{0,8},{1,9},{2,10},{3,11},{4,12},{5,13},{6,14},{7,15},{8,0},{9,1},... | collective-permute-start | bytes 122888 | tf_op jit(solution)/shard_map/ppermute | solution.py:714
  89.0 2.3 %collective-permute-start.44 = (bf16[4,4,192,128]{3,2,1,0:T(8,128)(2,1)S(1)}, bf16[4,4,192,128]{3,2,1,0:T(8,128)(2,1)S(1)}, u32[]{:S(2)}, u32[]{:S(2)}) collective-permute-start(bf16[4,4,192,128]{3,2,1,0:T(8,128)(2,1)S(1)} %get-tuple-element.169), channel_id=1, source_target_pairs={{0,4},{1,5},{2,6},{3,7},{4,0},{5,1},{6,2},{7,3},{8,12},{9,13},{10,... | collective-permute-start | bytes 2359304 | tf_op jit(solution)/shard_map/ppermute | solution.py:714
  89.0 3.8 %collective-permute-start.37 = (bf16[80,256]{1,0:T(8,128)(2,1)S(1)}, bf16[80,256]{1,0:T(8,128)(2,1)S(1)}, u32[]{:S(2)}, u32[]{:S(2)}) collective-permute-start(bf16[80,256]{1,0:T(8,128)(2,1)S(1)} %add_convert_fusion.refs_6_), channel_id=1, source_target_pairs={{0,4},{1,5},{2,6},{3,7},{4,0},{5,1},{6,2},{7,3},{8,12},{9,13},{10,... | collective-permute-start | bytes 122888 | tf_op jit(solution)/shard_map/ppermute | solution.py:714
  89.5 4.4 %collective-permute-start.41 = (bf16[80,256]{1,0:T(8,128)(2,1)S(1)}, bf16[80,256]{1,0:T(8,128)(2,1)S(1)}, u32[]{:S(2)}, u32[]{:S(2)}) collective-permute-start(bf16[80,256]{1,0:T(8,128)(2,1)S(1)} %collective-permute-done.38.refs_8_), channel_id=1, source_target_pairs={{0,4},{1,5},{2,6},{3,7},{4,0},{5,1},{6,2},{7,3},{8,12},{9,13},{10,... | collective-permute-start | bytes 122888 | tf_op jit(solution)/shard_map/ppermute | solution.py:714
  89.5 5.7 %collective-permute-start.42 = (bf16[80,256]{1,0:T(8,128)(2,1)S(1)}, bf16[80,256]{1,0:T(8,128)(2,1)S(1)}, u32[]{:S(2)}, u32[]{:S(2)}) collective-permute-start(bf16[80,256]{1,0:T(8,128)(2,1)S(1)} %collective-permute-done.39.refs_10_), channel_id=1, source_target_pairs={{0,4},{1,5},{2,6},{3,7},{4,0},{5,1},{6,2},{7,3},{8,12},{9,13},{10,... | collective-permute-start | bytes 122888 | tf_op jit(solution)/shard_map/ppermute | solution.py:714
  90.0 5.2 %collective-permute-start.43 = (bf16[80,256]{1,0:T(8,128)(2,1)S(1)}, bf16[80,256]{1,0:T(8,128)(2,1)S(1)}, u32[]{:S(2)}, u32[]{:S(2)}) collective-permute-start(bf16[80,256]{1,0:T(8,128)(2,1)S(1)} %collective-permute-done.40.refs_12_), channel_id=1, source_target_pairs={{0,4},{1,5},{2,6},{3,7},{4,0},{5,1},{6,2},{7,3},{8,12},{9,13},{10,... | collective-permute-start | bytes 122888 | tf_op jit(solution)/shard_map/ppermute | solution.py:714
  91.6 10.3 %collective-permute-start.45 = (bf16[4,192,128]{2,1,0:T(8,128)(2,1)S(1)}, bf16[4,192,128]{2,1,0:T(8,128)(2,1)S(1)}, u32[]{:S(2)}, u32[]{:S(2)}) collective-permute-start(bf16[4,192,128]{2,1,0:T(8,128)(2,1)S(1)} %get-tuple-element.170), channel_id=1, source_target_pairs={{0,8},{1,9},{2,10},{3,11},{4,12},{5,13},{6,14},{7,15},{8,0},{9,1},... | collective-permute-start | bytes 589832 | tf_op jit(solution)/shard_map/ppermute | solution.py:714
  92.9 10.9 %collective-permute-start.46 = (bf16[4,192,128]{2,1,0:T(8,128)(2,1)S(1)}, bf16[4,192,128]{2,1,0:T(8,128)(2,1)S(1)}, u32[]{:S(2)}, u32[]{:S(2)}) collective-permute-start(bf16[4,192,128]{2,1,0:T(8,128)(2,1)S(1)} %get-tuple-element.171), channel_id=1, source_target_pairs={{0,16},{1,17},{2,18},{3,19},{4,20},{5,21},{6,22},{7,23},{8,24},{9,... | collective-permute-start | bytes 589832 | tf_op jit(solution)/shard_map/ppermute | solution.py:714
  93.9 9.8 %collective-permute-start.47 = (bf16[4,192,128]{2,1,0:T(8,128)(2,1)S(1)}, bf16[4,192,128]{2,1,0:T(8,128)(2,1)S(1)}, u32[]{:S(2)}, u32[]{:S(2)}) collective-permute-start(bf16[4,192,128]{2,1,0:T(8,128)(2,1)S(1)} %get-tuple-element.172), channel_id=1, source_target_pairs={{0,24},{1,25},{2,26},{3,27},{4,28},{5,29},{6,30},{7,31},{8,16},{9,... | collective-permute-start | bytes 589832 | tf_op jit(solution)/shard_map/ppermute | solution.py:714
  103.7 1.9 %collective-permute-start.48 = (bf16[4,4,128,128]{3,2,1,0:T(8,128)(2,1)S(1)}, bf16[4,4,128,128]{3,2,1,0:T(8,128)(2,1)S(1)}, u32[]{:S(2)}, u32[]{:S(2)}) collective-permute-start(bf16[4,4,128,128]{3,2,1,0:T(8,128)(2,1)S(1)} %get-tuple-element.173), channel_id=1, source_target_pairs={{0,4},{1,5},{2,6},{3,7},{4,0},{5,1},{6,2},{7,3},{8,12},{9,13},{10,... | collective-permute-start | bytes 1572872 | tf_op jit(solution)/shard_map/ppermute | solution.py:714
  105.9 10.5 %collective-permute-start.49 = (bf16[4,128,128]{2,1,0:T(8,128)(2,1)S(1)}, bf16[4,128,128]{2,1,0:T(8,128)(2,1)S(1)}, u32[]{:S(2)}, u32[]{:S(2)}) collective-permute-start(bf16[4,128,128]{2,1,0:T(8,128)(2,1)S(1)} %get-tuple-element.226), channel_id=1, source_target_pairs={{0,8},{1,9},{2,10},{3,11},{4,12},{5,13},{6,14},{7,15},{8,0},{9,1},... | collective-permute-start | bytes 393224 | tf_op jit(solution)/shard_map/ppermute | solution.py:714
  106.8 9.6 %collective-permute-start.51 = (bf16[4,128,128]{2,1,0:T(8,128)(2,1)S(1)}, bf16[4,128,128]{2,1,0:T(8,128)(2,1)S(1)}, u32[]{:S(2)}, u32[]{:S(2)}) collective-permute-start(bf16[4,128,128]{2,1,0:T(8,128)(2,1)S(1)} %get-tuple-element.224), channel_id=1, source_target_pairs={{0,24},{1,25},{2,26},{3,27},{4,28},{5,29},{6,30},{7,31},{8,16},{9,... | collective-permute-start | bytes 393224 | tf_op jit(solution)/shard_map/ppermute | solution.py:714
  108.4 8.0 %collective-permute-start.50 = (bf16[4,128,128]{2,1,0:T(8,128)(2,1)S(1)}, bf16[4,128,128]{2,1,0:T(8,128)(2,1)S(1)}, u32[]{:S(2)}, u32[]{:S(2)}) collective-permute-start(bf16[4,128,128]{2,1,0:T(8,128)(2,1)S(1)} %get-tuple-element.225), channel_id=1, source_target_pairs={{0,16},{1,17},{2,18},{3,19},{4,20},{5,21},{6,22},{7,23},{8,24},{9,... | collective-permute-start | bytes 393224 | tf_op jit(solution)/shard_map/ppermute | solution.py:714
  116.6 9.6 %collective-permute-start.52 = (bf16[320,128]{1,0:T(8,128)(2,1)S(1)}, bf16[320,128]{1,0:T(8,128)(2,1)S(1)}, u32[]{:S(2)}, u32[]{:S(2)}) collective-permute-start(bf16[320,128]{1,0:T(8,128)(2,1)S(1)} %get-tuple-element.182), channel_id=1, source_target_pairs={{0,1},{1,0},{2,3},{3,2},{4,5},{5,4},{6,7},{7,6},{8,9},{9,8},{10,11... | collective-permute-start | bytes 245768 | tf_op jit(solution)/shard_map/ppermute | solution.py:714
  117.5 7.8 %collective-permute-start.53 = (bf16[320,128]{1,0:T(8,128)(2,1)S(1)}, bf16[320,128]{1,0:T(8,128)(2,1)S(1)}, u32[]{:S(2)}, u32[]{:S(2)}) collective-permute-start(bf16[320,128]{1,0:T(8,128)(2,1)S(1)} %get-tuple-element.184), channel_id=1, source_target_pairs={{0,2},{1,3},{2,0},{3,1},{4,6},{5,7},{6,4},{7,5},{8,10},{9,11},{10,... | collective-permute-start | bytes 245768 | tf_op jit(solution)/shard_map/ppermute | solution.py:714
  119.9 6.3 %collective-permute-start.54 = (bf16[320,128]{1,0:T(8,128)(2,1)S(1)}, bf16[320,128]{1,0:T(8,128)(2,1)S(1)}, u32[]{:S(2)}, u32[]{:S(2)}) collective-permute-start(bf16[320,128]{1,0:T(8,128)(2,1)S(1)} %get-tuple-element.185), channel_id=1, source_target_pairs={{0,3},{1,2},{2,1},{3,0},{4,7},{5,6},{6,5},{7,4},{8,11},{9,10},{10,... | collective-permute-start | bytes 245768 | tf_op jit(solution)/shard_map/ppermute | solution.py:714
  126.3 5.5 %collective-permute-start.60 = (bf16[320,128]{1,0:T(8,128)(2,1)S(1)}, bf16[320,128]{1,0:T(8,128)(2,1)S(1)}, u32[]{:S(2)}, u32[]{:S(2)}) collective-permute-start(bf16[320,128]{1,0:T(8,128)(2,1)S(1)} %finish.1.refs_0_.refs_1_), channel_id=1, source_target_pairs={{0,24},{1,25},{2,26},{3,27},{4,28},{5,29},{6,30},{7,31},{8,16},{9,... | collective-permute-start | bytes 245768 | tf_op jit(solution)/shard_map/ppermute | solution.py:714
  127.6 5.0 %collective-permute-start.58 = (bf16[320,128]{1,0:T(8,128)(2,1)S(1)}, bf16[320,128]{1,0:T(8,128)(2,1)S(1)}, u32[]{:S(2)}, u32[]{:S(2)}) collective-permute-start(bf16[320,128]{1,0:T(8,128)(2,1)S(1)} %finish.1.refs_0_.refs_1_), channel_id=1, source_target_pairs={{0,16},{1,17},{2,18},{3,19},{4,20},{5,21},{6,22},{7,23},{8,24},{9,... | collective-permute-start | bytes 245768 | tf_op jit(solution)/shard_map/ppermute | solution.py:714
  128.7 4.4 %collective-permute-start.56 = (bf16[320,128]{1,0:T(8,128)(2,1)S(1)}, bf16[320,128]{1,0:T(8,128)(2,1)S(1)}, u32[]{:S(2)}, u32[]{:S(2)}) collective-permute-start(bf16[320,128]{1,0:T(8,128)(2,1)S(1)} %finish.1.refs_0_.refs_1_), channel_id=1, source_target_pairs={{0,8},{1,9},{2,10},{3,11},{4,12},{5,13},{6,14},{7,15},{8,0},{9,1},... | collective-permute-start | bytes 245768 | tf_op jit(solution)/shard_map/ppermute | solution.py:714
  129.9 3.3 %collective-permute-start.55 = (bf16[320,128]{1,0:T(8,128)(2,1)S(1)}, bf16[320,128]{1,0:T(8,128)(2,1)S(1)}, u32[]{:S(2)}, u32[]{:S(2)}) collective-permute-start(bf16[320,128]{1,0:T(8,128)(2,1)S(1)} %finish.1.refs_0_.refs_1_), channel_id=1, source_target_pairs={{0,4},{1,5},{2,6},{3,7},{4,0},{5,1},{6,2},{7,3},{8,12},{9,13},{10,... | collective-permute-start | bytes 245768 | tf_op jit(solution)/shard_map/ppermute | solution.py:714
  131.8 1.4 collective-permute-start.61
  132.6 1.3 collective-permute-start.59
  133.1 1.3 collective-permute-start.57
  134.6 5.4 %collective-permute-start.64 = (f32[8,128]{1,0:T(8,128)S(1)}, f32[8,128]{1,0:T(8,128)S(1)}, u32[]{:S(2)}, u32[]{:S(2)}) collective-permute-start(f32[8,128]{1,0:T(8,128)S(1)} %squares.1.refs_1_), channel_id=1, source_target_pairs={{0,3},{1,2},{2,1},{3,0},{4,7},{5,6},{6,5},{7,4},{8,11},{9,10},{10,... | collective-permute-start | bytes 12296 | tf_op jit(solution)/shard_map/ppermute | solution.py:714
  137.2 4.5 %collective-permute-start.63 = (f32[8,128]{1,0:T(8,128)S(1)}, f32[8,128]{1,0:T(8,128)S(1)}, u32[]{:S(2)}, u32[]{:S(2)}) collective-permute-start(f32[8,128]{1,0:T(8,128)S(1)} %squares.1.refs_1_), channel_id=1, source_target_pairs={{0,2},{1,3},{2,0},{3,1},{4,6},{5,7},{6,4},{7,5},{8,10},{9,11},{10,... | collective-permute-start | bytes 12296 | tf_op jit(solution)/shard_map/ppermute | solution.py:714
  137.4 4.3 %collective-permute-start.62 = (f32[8,128]{1,0:T(8,128)S(1)}, f32[8,128]{1,0:T(8,128)S(1)}, u32[]{:S(2)}, u32[]{:S(2)}) collective-permute-start(f32[8,128]{1,0:T(8,128)S(1)} %squares.1.refs_1_), channel_id=1, source_target_pairs={{0,1},{1,0},{2,3},{3,2},{4,5},{5,4},{6,7},{7,6},{8,9},{9,8},{10,11... | collective-permute-start | bytes 12296 | tf_op jit(solution)/shard_map/ppermute | solution.py:714
  (16 other events, 255.6 us)

commit v5 on v4

--- a/solution.py
+++ b/solution.py
@@ -505,20 +505,24 @@
     grad_out[...] += dot_nn(prod[...], g[...])
 
 
+def out_part(grad_out, shard, z, chunk, which, span):
+    lanes = grad_out.shape[1] // 4
+    quarter = span // 4
+    start = lax.bitwise_xor(shard, z) * span + (chunk % 2) * 2 * quarter + which * quarter
+    rows = grad_out[pl.ds(pl.multiple_of(start, 8), quarter), (chunk // 2) * lanes : (chunk // 2 + 1) * lanes]
+    return fold(rows, span)
+
+
 def early_kernel(pieces, step, place, grad_query, grad_gate, grad_out, keep, send):
     node, shard = place[1], place[2]
     width = grad_out.shape[1]
     span = width // pieces
     tall = 2 * width // 8
-    lanes = width // 4
-    short = span // 2
 
     def blocks(z, chunk):
         source = grad_query if chunk < 4 else grad_gate
         top = source[(chunk % 4) * tall : (chunk % 4 + 1) * tall, z * span : (z + 1) * span]
-        start = pl.multiple_of(lax.bitwise_xor(shard, z) * span + (chunk % 2) * short, 8)
-        bottom = grad_out[pl.ds(start, short), (chunk // 2) * lanes : (chunk // 2 + 1) * lanes]
-        return jnp.concatenate([top, fold(bottom, span)], axis=0)
+        return jnp.concatenate([top, out_part(grad_out, shard, z, chunk, 1, span)], axis=0)
 
     write_pieces(pieces, node, shard, span, keep, send, blocks)
 
@@ -542,7 +546,7 @@
     result[...] = x[...].astype(fl_type) + dot_tn(prod[...], out_weight[...])
 
 
-def key_back_kernel(pieces, step, place, ids, key_slope, key, value, x, *refs):
+def key_back_kernel(pieces, step, place, ids, key_slope, key, value, x, grad_out, *refs):
     chunk_refs = refs[:CHUNKS]
     dkey_out, dvalue_out, norm_out, keep, send = refs[CHUNKS : CHUNKS + 5]
     stage, left_key, left_value, sums, stack, key_stack, acc = refs[CHUNKS + 5 :]
@@ -590,19 +594,31 @@
     tall = 2 * width // 8
 
     def blocks(z, chunk):
-        return acc[chunk * tall : (chunk + 1) * tall, z * span : (z + 1) * span]
+        top = acc[chunk * tall : (chunk + 1) * tall, z * span : (z + 1) * span]
+        return jnp.concatenate([top, out_part(grad_out, shard, z, chunk, 0, span)], axis=0)
 
     write_pieces(pieces, node, shard, span, keep, send, blocks)
 
 
-def input_kernel(step, place, dquery, dkey, dvalue, dgate, full_query, full_key, full_gate, g, result):
-    width = g.shape[1]
+def input_kernel(steps, step, place, dquery, dkey, dvalue, dgate, full_query, full_key, full_gate, g, result, blocks, sems):
+    rows, width = g.shape
     total = g[...].astype(fl_type)
     total = total + dot_tn(dquery[...], full_query[...])
     total = total + dot_tn(dkey[...], full_key[0:width, :])
     total = total + dot_tn(dvalue[...], full_key[width:, :])
     total = total + dot_tn(dgate[...], full_gate[...])
-    result[...] = total
+    blocks[step] = total
+
+    def copy(i):
+        at = pl.ds(pl.multiple_of(i * rows, 8), rows)
+        return pltpu.make_async_copy(blocks.at[i], result.at[at, :], sems.at[i])
+
+    copy(step).start()
+
+    @pl.when(step == steps - 1)
+    def _():
+        for i in range(steps):
+            copy(i).wait()
 
 
 def finish_kernel(step, *refs):
@@ -631,14 +647,18 @@
     for d in range(CHUNKS):
         chunk = lax.bitwise_xor(node, d)
         stage[chunk] = parts[d][...].astype(fl_type)
+    rows = rows // 2
+    late = tall + rows * folds
     for chunk in range(CHUNKS):
         query_at = (0 if chunk < 4 else 3 * width) + (chunk % 4) * tall
         grad_proj[:, width + chunk * tall : width + (chunk + 1) * tall] = stage[chunk, 0:tall].T
-        grad_proj[:, query_at : query_at + tall] = stage[chunk, tall : 2 * tall].T
-        for i in range(folds):
-            at = slice((chunk // 2) * lanes + i * span, (chunk // 2) * lanes + (i + 1) * span)
-            block = stage[chunk, 2 * tall + i * rows : 2 * tall + (i + 1) * rows]
-            grad_out[(chunk % 2) * rows : (chunk % 2 + 1) * rows, at] = block
+        grad_proj[:, query_at : query_at + tall] = stage[chunk, late : late + tall].T
+        for which in range(2):
+            for i in range(folds):
+                at = slice((chunk // 2) * lanes + i * span, (chunk // 2) * lanes + (i + 1) * span)
+                start = which * late + tall + i * rows
+                row = (chunk % 2 * 2 + which) * rows
+                grad_out[row : row + rows, at] = stage[chunk, start : start + rows]
 
 
 def adam(master_w, moment_old, square_old, clipped, decay_coef, step_rate):
@@ -964,10 +984,9 @@
         block,
     )
 
-    short = tall + (span // 2) * (width // 4 // span)
-    height = tall + short
-    early_shape = (4, shards, short, span)
-    late_shape = (4, shards, tall, span)
+    short = tall + (span // 4) * (width // 4 // span)
+    height = 2 * short
+    early_shape = late_shape = (4, shards, short, span)
 
     def fill_gate_back(dep):
         made["gate_back"] = call(
@@ -1060,8 +1079,8 @@
     dkey, dvalue, norm_grad, keep, send = call(
         functools.partial(key_back_kernel, shards),
         1,
-        (place, ids, key_slope, key, value, x_turned, *back_chunks),
-        ["smem", "lane", "lane", "lane", "lane", "row"] + [None] * CHUNKS,
+        (place, ids, key_slope, key, value, x_turned, made["gate_back"][1], *back_chunks),
+        ["smem", "lane", "lane", "lane", "lane", "row", None] + [None] * CHUNKS,
         [
             wide(bf_type),
             wide(bf_type),
@@ -1100,17 +1119,16 @@
 
     def fill_inputs(dep):
         made["inputs"] = call(
-            input_kernel,
-            steps,
+            functools.partial(input_kernel, 2),
+            2,
             (tie(place, dep), dquery, dkey, dvalue, dgate, full_query, full_key, full_gate, g),
             ["smem"] + ["lane"] * 4 + [None] * 3 + ["row"],
             [out((rows, width), fl_type)],
-            ["row"],
-            [],
+            ["hbm"],
+            [vmem((2, rows // 2, width), fl_type), pltpu.SemaphoreType.DMA((2,))],
             4 * work,
             "inputs",
-            block,
-            piped=True,
+            rows // 2,
         )[0]
         return made["inputs"]
 

time: 146 us -> 145 us (level)
  transfers between devices with their start and end apart: 65 -> 65, of which waited for: 26 -> 27; matrix products, arithmetic and copies ran while one was open for 2% -> 2% of each run, Pallas kernels for 28% -> 28%
where the time goes in v5:
time: 145 us
  starting transfers between devices  60 us (41%)
  Pallas kernels  56.8 us (39%)
  waiting for transfers between devices  22.2 us (15%)
  local copies, waits for them, and re-layouts  2.52 us (2%)
  between operations  2.07 us (1%)
    ppermute x65, starting transfers between devices, exchange(): return lax.ppermute(value, AXES, pairs)  60 us
    pallas_call x19, Pallas kernels, call(): pl.pallas_call(body, grid=(steps,) if piped else (), in_specs=specs[:len(...  56.8 us
    ppermute x65, waiting for transfers between devices, exchange(): return lax.ppermute(value, AXES, pairs)  22.2 us
  transfers between devices with their start and end apart: 65, of which 27 were waited for; matrix products, arithmetic and copies ran while one was open for 2% of the time, Pallas kernels for 28%

profile of v5, /device:TPU:0, one launch (start us, length us, event | category | flops | bytes accessed | tf_op | source)
XLA Modules:
  0.0 144.8 jit_solution(13172439251535310694)
XLA Ops:
  0.6 2.4 %prep.1 = (bf16[512,128]{1,0:T(8,128)(2,1)}, bf16[512,128]{1,0:T(8,128)(2,1)}, bf16[208,128]{1,0:T(8,128)(2,1)}, bf16[1664,128]{1,0:T(8,128)(2,1)}) custom-call(f32[128,2048]{1,0:T(8,128)} %refs_8_.3, f32[128,512]{1,0:T(8,128)} %refs_11_.1, f32[2,128]{1,0:T(2,128)} %refs_14_.1), custom_call_target="tpu_custom_call" | custom-call | flops 1000000 | bytes 2053120 | tf_op jit(solution)/shard_map/prep/pallas_call | solution.py:94
  3.1 5.1 %collective-permute-start.5 = (bf16[208,128]{1,0:T(8,128)(2,1)}, bf16[208,128]{1,0:T(8,128)(2,1)S(1)}, u32[]{:S(2)}, u32[]{:S(2)}) collective-permute-start(bf16[208,128]{1,0:T(8,128)(2,1)} %get-tuple-element.115), channel_id=1, source_target_pairs={{0,3},{1,2},{2,1},{3,0},{4,7},{5,6},{6,5},{7,4},{8,11},{9,10},{10,... | collective-permute-start | bytes 159752 | tf_op jit(solution)/shard_map/ppermute | solution.py:734
  8.2 0.6 collective-permute-start.3
  8.8 3.7 %collective-permute-start.2 = (bf16[512,128]{1,0:T(8,128)(2,1)}, bf16[512,128]{1,0:T(8,128)(2,1)S(1)}, u32[]{:S(2)}, u32[]{:S(2)}) collective-permute-start(bf16[512,128]{1,0:T(8,128)(2,1)} %get-tuple-element.113.refs_3_.refs_1_), channel_id=1, source_target_pairs={{0,3},{1,2},{2,1},{3,0},{4,7},{5,6},{6,5},{7,4},{8,11},{9,10},{10,... | collective-permute-start | bytes 393224 | tf_op jit(solution)/shard_map/ppermute | solution.py:734
  12.6 1.7 %constant_dynamic-slice_fusion.3 = (bf16[2048,128]{1,0:T(8,128)(2,1)S(1)}, bf16[2048,128]{1,0:T(8,128)(2,1)S(1)}, bf16[2048,128]{1,0:T(8,128)(2,1)S(1)}, bf16[2048,128]{1,0:T(8,128)(2,1)S(1)}) fusion(bf16[2048,512]{1,0:T(8,128)(2,1)} %refs_1_.5, s32[]{:T(128)S(6)} %select_n.12, s32[]{:T(128)S(6)} %select_n.14, s32[]{:T(128)S(6)} %select_n.13, s32[]{:T(128)S(6)} %select_n.15), kind=kLoop, calls=%fused_computation.46 | loop fusion | bytes 4194320 | tf_op jit(solution)/shard_map/dynamic_slice | solution.py:810
  14.6 0.6 copy-done.6
  15.2 0.6 collective-permute-start.1
  15.9 2.3 %collective-permute-done.2.refs_6_.refs_4_ = bf16[512,128]{1,0:T(8,128)(2,1)S(1)} collective-permute-done((bf16[512,128]{1,0:T(8,128)(2,1)}, bf16[512,128]{1,0:T(8,128)(2,1)S(1)}, u32[]{:S(2)}, u32[]{:S(2)}) %collective-permute-start.2) | collective-permute-done | bytes 131104 | tf_op jit(solution)/shard_map/ppermute | solution.py:734
  18.2 2.4 %collective-permute-start.11 = (bf16[3,208,128]{2,1,0:T(8,128)(2,1)S(1)}, bf16[3,208,128]{2,1,0:T(8,128)(2,1)S(1)}, u32[]{:S(2)}, u32[]{:S(2)}) collective-permute-start(bf16[3,208,128]{2,1,0:T(8,128)(2,1)S(1)} %pad_maximum_fusion.2.refs_2_), channel_id=1, source_target_pairs={{0,24},{1,25},{2,26},{3,27},{4,28},{5,29},{6,30},{7,31},{8,16},{9,... | collective-permute-start | bytes 479240 | tf_op jit(solution)/shard_map/ppermute | solution.py:734
  21.7 2.7 %collective-permute-done.1.refs_5_.refs_3_ = bf16[512,128]{1,0:T(8,128)(2,1)S(1)} collective-permute-done((bf16[512,128]{1,0:T(8,128)(2,1)S(1)}, bf16[512,128]{1,0:T(8,128)(2,1)S(1)}, u32[]{:S(2)}, u32[]{:S(2)}) %collective-permute-start.1) | collective-permute-done | bytes 131104 | tf_op jit(solution)/shard_map/ppermute | solution.py:734
  26.0 5.5 %keys.1 = (f32[512,2048]{1,0:T(8,128)S(1)}, bf16[512,2048]{1,0:T(8,128)(2,1)S(1)}, bf16[512,2048]{1,0:T(8,128)(2,1)S(1)}, f32[4,80,256]{2,1,0:T(8,128)S(1)}, bf16[4,80,256]{2,1,0:T(8,128)(2,1)S(1)}) custom-call(s32[4]{0:T(128)S(1)} %pad_add_fusion.refs_0_, bf16[2048,512]{1,0:T(8,128)(2,1)S(1)} %pad_maximum_fusion.refs_1_.refs_3_.refs_2_.refs_5_, ...), custom_call_target="tpu_custom_call" | custom-call | flops 1000 | bytes 12034064 | tf_op jit(solution)/shard_map/keys/pallas_call | solution.py:94
  33.0 2.5 %collective-permute-start.15 = (bf16[80,256]{1,0:T(8,128)(2,1)S(1)}, bf16[80,256]{1,0:T(8,128)(2,1)S(1)}, u32[]{:S(2)}, u32[]{:S(2)}) collective-permute-start(bf16[80,256]{1,0:T(8,128)(2,1)S(1)} %get-tuple-element.233), channel_id=1, source_target_pairs={{0,24},{1,25},{2,26},{3,27},{4,28},{5,29},{6,30},{7,31},{8,16},{9,... | collective-permute-start | bytes 122888 | tf_op jit(solution)/shard_map/ppermute | solution.py:734
  36.6 1.8 %weights.1 = (bf16[512,512]{1,0:T(8,128)(2,1)S(1)}, bf16[512,512]{1,0:T(8,128)(2,1)S(1)}, bf16[512,512]{1,0:T(8,128)(2,1)S(1)}, f32[512,128]{1,0:T(8,128)S(1)}, ...) custom-call(s32[4]{0:T(128)S(1)} %pad_add_fusion.refs_0_, ...), custom_call_target="tpu_custom_call" | custom-call | flops 1000000 | bytes 4849680 | tf_op jit(solution)/shard_map/weights/pallas_call | solution.py:94
  38.4 1.2 collective-permute-done.14
  40.0 2.7 %collective-permute-start.22 = (bf16[80,256]{1,0:T(8,128)(2,1)S(1)}, bf16[80,256]{1,0:T(8,128)(2,1)S(1)}, u32[]{:S(2)}, u32[]{:S(2)}) collective-permute-start(bf16[80,256]{1,0:T(8,128)(2,1)S(1)} %fusion.12), channel_id=1, source_target_pairs={{0,3},{1,2},{2,1},{3,0},{4,7},{5,6},{6,5},{7,4},{8,11},{9,10},{10,... | collective-permute-start | bytes 122888 | tf_op jit(solution)/shard_map/ppermute | solution.py:734
  42.7 0.9 collective-permute-start.21
  43.7 0.8 collective-permute-start.20
  44.5 1.9 %query.1 = (f32[512,2048]{1,0:T(8,128)S(1)}, bf16[512,2048]{1,0:T(8,128)(2,1)S(1)}) custom-call(s32[4]{0:T(128)S(1)} %pad_add_fusion.refs_0_, bf16[2048,512]{1,0:T(8,128)(2,1)S(1)} %pad_maximum_fusion.refs_1_.refs_3_.refs_2_.refs_5_, bf16[512,512]{1,0:T(8,128)(2,1)S(1)} %get-tuple-element.127.refs_2_), custom_call_target="tpu_custom_call" | custom-call | flops 1073741824 | bytes 8912912 | tf_op jit(solution)/shard_map/query/pallas_call | solution.py:94
  46.4 1.9 %gate.1.refs_3_ = f32[512,2048]{1,0:T(8,128)S(1)} custom-call(s32[4]{0:T(128)S(1)} %pad_add_fusion.refs_0_, bf16[2048,512]{1,0:T(8,128)(2,1)S(1)} %pad_maximum_fusion.refs_1_.refs_3_.refs_2_.refs_5_, bf16[512,512]{1,0:T(8,128)(2,1)S(1)} %get-tuple-element.133.refs_2_), custom_call_target="tpu_custom_call" | custom-call | flops 1073741824 | bytes 6815760 | tf_op jit(solution)/shard_map/gate/pallas_call | solution.py:94
  48.4 1.6 %collective-permute-start.26 = (bf16[80,256]{1,0:T(8,128)(2,1)S(1)}, bf16[80,256]{1,0:T(8,128)(2,1)S(1)}, u32[]{:S(2)}, u32[]{:S(2)}) collective-permute-start(bf16[80,256]{1,0:T(8,128)(2,1)S(1)} %add_convert_fusion.1.refs_7_.refs_5_), channel_id=1, source_target_pairs={{0,24},{1,25},{2,26},{3,27},{4,28},{5,29},{6,30},{7,31},{8,16},{9,... | collective-permute-start | bytes 122888 | tf_op jit(solution)/shard_map/ppermute | solution.py:734
  50.4 1.5 %collective-permute-start.24 = (bf16[80,256]{1,0:T(8,128)(2,1)S(1)}, bf16[80,256]{1,0:T(8,128)(2,1)S(1)}, u32[]{:S(2)}, u32[]{:S(2)}) collective-permute-start(bf16[80,256]{1,0:T(8,128)(2,1)S(1)} %add_convert_fusion.1.refs_7_.refs_5_), channel_id=1, source_target_pairs={{0,8},{1,9},{2,10},{3,11},{4,12},{5,13},{6,14},{7,15},{8,0},{9,1},... | collective-permute-start | bytes 122888 | tf_op jit(solution)/shard_map/ppermute | solution.py:734
  51.9 1.8 %grad_prod.1.refs_4_ = f32[512,2048]{1,0:T(8,128)S(1)} custom-call(s32[4]{0:T(128)S(1)} %pad_add_fusion.refs_0_, bf16[2048,512]{1,0:T(8,128)(2,1)S(1)} %copy-done, bf16[512,512]{1,0:T(8,128)(2,1)S(1)} %get-tuple-element.138.refs_2_.refs_3_), custom_call_target="tpu_custom_call" | custom-call | flops 1073741824 | bytes 6815760 | tf_op jit(solution)/shard_map/grad_prod/pallas_call | solution.py:94
  55.0 0.7 collective-permute-done.27.refs_10_.refs_8_
  56.2 9.6 %middle.1 = (bf16[512,2048]{1,0:T(8,128)(2,1)S(1)}, bf16[512,2048]{1,0:T(8,128)(2,1)S(1)}, bf16[512,2048]{1,0:T(8,128)(2,1)S(1)}, f32[16,2048]{1,0:T(8,128)S(1)}...) custom-call(s32[4]{0:T(128)S(1)} %pad_add_fusion.refs_0_, s32[1,2048]{1,0:T(1,128)S(1)} %bitcast.69, ...), custom_call_target="tpu_custom_call" | custom-call | flops 6442450944 | bytes 18259984 | tf_op jit(solution)/shard_map/middle/pallas_call | solution.py:94
  66.0 1.2 collective-permute-done.30
  67.3 1.6 %collective-permute-start.31 = (bf16[80,256]{1,0:T(8,128)(2,1)S(1)}, bf16[80,256]{1,0:T(8,128)(2,1)S(1)}, u32[]{:S(2)}, u32[]{:S(2)}) collective-permute-start(bf16[80,256]{1,0:T(8,128)(2,1)S(1)} %get-tuple-element.232), channel_id=1, source_target_pairs={{0,8},{1,9},{2,10},{3,11},{4,12},{5,13},{6,14},{7,15},{8,0},{9,1},... | collective-permute-start | bytes 122888 | tf_op jit(solution)/shard_map/ppermute | solution.py:734
  68.8 1.5 %collective-permute-start.33 = (bf16[80,256]{1,0:T(8,128)(2,1)S(1)}, bf16[80,256]{1,0:T(8,128)(2,1)S(1)}, u32[]{:S(2)}, u32[]{:S(2)}) collective-permute-start(bf16[80,256]{1,0:T(8,128)(2,1)S(1)} %get-tuple-element.230), channel_id=1, source_target_pairs={{0,24},{1,25},{2,26},{3,27},{4,28},{5,29},{6,30},{7,31},{8,16},{9,... | collective-permute-start | bytes 122888 | tf_op jit(solution)/shard_map/ppermute | solution.py:734
  70.8 2.9 %gate_back.1 = (f32[512,512]{1,0:T(8,128)S(1)}, f32[512,512]{1,0:T(8,128)S(1)}) custom-call(s32[4]{0:T(128)S(1)} %pad_add_fusion.refs_0_, bf16[512,2048]{1,0:T(8,128)(2,1)S(1)} %get-tuple-element.147.refs_1_.refs_4_, bf16[512,2048]{1,0:T(8,128)(2,1)S(1)} %get-tuple-element.148.refs_2_, bf16[2048,512]{1,0:T(8,128)(2,1)S(1)} %pad_maximum_fusion.refs_1_.refs_3_.refs_2_.refs_5_, ...), custom_call_target="tpu_custom_call" | custom-call | flops 2147483648 | bytes 10485776 | tf_op jit(solution)/shard_map/gate_back/pallas_call | solution.py:94
  74.4 2.7 %collective-permute-start.36 = (bf16[80,256]{1,0:T(8,128)(2,1)S(1)}, bf16[80,256]{1,0:T(8,128)(2,1)S(1)}, u32[]{:S(2)}, u32[]{:S(2)}) collective-permute-start(bf16[80,256]{1,0:T(8,128)(2,1)S(1)} %fusion.9), channel_id=1, source_target_pairs={{0,3},{1,2},{2,1},{3,0},{4,7},{5,6},{6,5},{7,4},{8,11},{9,10},{10,... | collective-permute-start | bytes 122888 | tf_op jit(solution)/shard_map/ppermute | solution.py:734
  77.1 1.8 %collective-permute-start.34 = (bf16[80,256]{1,0:T(8,128)(2,1)S(1)}, bf16[80,256]{1,0:T(8,128)(2,1)S(1)}, u32[]{:S(2)}, u32[]{:S(2)}) collective-permute-start(bf16[80,256]{1,0:T(8,128)(2,1)S(1)} %fusion.9), channel_id=1, source_target_pairs={{0,1},{1,0},{2,3},{3,2},{4,5},{5,4},{6,7},{7,6},{8,9},{9,8},{10,11... | collective-permute-start | bytes 122888 | tf_op jit(solution)/shard_map/ppermute | solution.py:734
  78.8 3.1 %query_back.1.refs_1_ = bf16[512,2048]{1,0:T(8,128)(2,1)S(1)} custom-call(s32[4]{0:T(128)S(1)} %pad_add_fusion.refs_0_, s32[1,2048]{1,0:T(1,128)S(1)} %bitcast.70, bf16[512,2048]{1,0:T(8,128)(2,1)S(1)} %get-tuple-element.155.refs_2_, f32[16,2048]{1,0:T(8,128)S(1)} %get-tuple-element.156.refs_3_, f32[512,2048]{1,0:T(8,128)S(1)} %get-tuple-element.157.refs_4_, ...), custom_call_target="tpu_custom_call" | custom-call | flops 2147483648 | bytes 8855568 | tf_op jit(solution)/shard_map/query_back/pallas_call | solution.py:94
  82.3 1.8 %collective-permute-start.40 = (bf16[80,256]{1,0:T(8,128)(2,1)S(1)}, bf16[80,256]{1,0:T(8,128)(2,1)S(1)}, u32[]{:S(2)}, u32[]{:S(2)}) collective-permute-start(bf16[80,256]{1,0:T(8,128)(2,1)S(1)} %add_convert_fusion.refs_7_), channel_id=1, source_target_pairs={{0,24},{1,25},{2,26},{3,27},{4,28},{5,29},{6,30},{7,31},{8,16},{9,... | collective-permute-start | bytes 122888 | tf_op jit(solution)/shard_map/ppermute | solution.py:734
  84.0 1.0 collective-permute-start.39
  85.0 0.8 collective-permute-start.38
  85.8 1.8 %grad_query.1.refs_1_ = f32[512,512]{1,0:T(8,128)S(1)} custom-call(s32[4]{0:T(128)S(1)} %pad_add_fusion.refs_0_, bf16[512,2048]{1,0:T(8,128)(2,1)S(1)} %query_back.1.refs_1_, bf16[2048,512]{1,0:T(8,128)(2,1)S(1)} %pad_maximum_fusion.refs_1_.refs_3_.refs_2_.refs_5_), custom_call_target="tpu_custom_call" | custom-call | flops 1073741824 | bytes 5242896 | tf_op jit(solution)/shard_map/grad_query/pallas_call | solution.py:94
  87.6 1.2 early.1
  90.1 1.1 collective-permute-done.44
  91.4 1.2 collective-permute-start.45
  92.6 1.0 collective-permute-start.46
  93.6 1.3 collective-permute-start.47
  95.0 7.1 %key_back.1 = (bf16[512,2048]{1,0:T(8,128)(2,1)S(1)}, bf16[512,2048]{1,0:T(8,128)(2,1)S(1)}, f32[8,512]{1,0:T(8,128)S(1)}, f32[4,4,160,128]{3,2,1,0:T(8,128)S(1)}, bf16[4,4,160,128]{3,2,1,0:T(8,128)(2,1)S(1)}) custom-call(s32[4]{0:T(128)S(1)} %pad_add_fusion.refs_0_, s32[1,2048]{1,0:T(1,128)S(1)} %bitcast.71, f32[512,2048]{1,0:T(8,128)S(1)} %copy-done.16, ...), custom_call_target="tpu_custom_call" | custom-call | flops 6442450944 | bytes 18046992 | tf_op jit(solution)/shard_map/key_back/pallas_call | solution.py:94
  102.2 0.8 key_weights.1.refs_6_
  103.0 1.3 collective-permute-done.48
  104.6 1.2 collective-permute-start.49
  105.8 1.4 collective-permute-start.51
  107.1 1.0 collective-permute-start.50
  108.1 6.6 %inputs.1 = f32[2048,512]{1,0:T(8,128)} custom-call(s32[4]{0:T(128)S(1)} %pad_add_fusion.refs_0_, bf16[512,2048]{1,0:T(8,128)(2,1)S(1)} %query_back.1.refs_1_, bf16[512,2048]{1,0:T(8,128)(2,1)S(1)} %get-tuple-element.175.refs_2_, bf16[512,2048]{1,0:T(8,128)(2,1)S(1)} %get-tuple-element.176.refs_3_, bf16[512,2048]{1,0:T(8,128)(2,1)S(1)} %get-tuple-element.147.refs_1_.refs_4_, ...), custom_call_target="tpu_custom_call" | custom-call | flops 4294967296 | bytes 16777232 | tf_op jit(solution)/shard_map/inputs/pallas_call | solution.py:94
  115.0 1.4 collective-permute-done.50
  116.7 0.8 collective-permute-start.52
  117.4 2.4 %collective-permute-start.53 = (bf16[320,128]{1,0:T(8,128)(2,1)S(1)}, bf16[320,128]{1,0:T(8,128)(2,1)S(1)}, u32[]{:S(2)}, u32[]{:S(2)}) collective-permute-start(bf16[320,128]{1,0:T(8,128)(2,1)S(1)} %get-tuple-element.184), channel_id=1, source_target_pairs={{0,2},{1,3},{2,0},{3,1},{4,6},{5,7},{6,4},{7,5},{8,10},{9,11},{10,... | collective-permute-start | bytes 245768 | tf_op jit(solution)/shard_map/ppermute | solution.py:734
  119.8 1.3 collective-permute-start.54
  121.1 3.5 %output.1 = f32[2048,512]{1,0:T(8,128)} custom-call(s32[4]{0:T(128)S(1)} %pad_add_fusion.refs_0_, bf16[2048,512]{1,0:T(8,128)(2,1)S(1)} %copy-done.1, bf16[512,2048]{1,0:T(8,128)(2,1)S(1)} %get-tuple-element.148.refs_2_, bf16[512,512]{1,0:T(8,128)(2,1)S(1)} %get-tuple-element.138.refs_2_.refs_3_), custom_call_target="tpu_custom_call" | custom-call | flops 1073741824 | bytes 8912912 | tf_op jit(solution)/shard_map/output/pallas_call | solution.py:94
  124.6 1.5 %collective-permute-done.54.refs_3_ = bf16[320,128]{1,0:T(8,128)(2,1)S(1)} collective-permute-done((bf16[320,128]{1,0:T(8,128)(2,1)S(1)}, bf16[320,128]{1,0:T(8,128)(2,1)S(1)}, u32[]{:S(2)}, u32[]{:S(2)}) %collective-permute-start.54) | collective-permute-done | bytes 81952 | tf_op jit(solution)/shard_map/ppermute | solution.py:734
  126.1 1.7 %collective-permute-start.60 = (bf16[320,128]{1,0:T(8,128)(2,1)S(1)}, bf16[320,128]{1,0:T(8,128)(2,1)S(1)}, u32[]{:S(2)}, u32[]{:S(2)}) collective-permute-start(bf16[320,128]{1,0:T(8,128)(2,1)S(1)} %finish.1.refs_0_.refs_1_), channel_id=1, source_target_pairs={{0,24},{1,25},{2,26},{3,27},{4,28},{5,29},{6,30},{7,31},{8,16},{9,... | collective-permute-start | bytes 245768 | tf_op jit(solution)/shard_map/ppermute | solution.py:734
  127.9 0.9 collective-permute-start.58
  128.8 0.9 collective-permute-start.56
  129.7 1.9 %collective-permute-done.60.refs_6_.refs_7_ = bf16[320,128]{1,0:T(8,128)(2,1)S(1)} collective-permute-done((bf16[320,128]{1,0:T(8,128)(2,1)S(1)}, bf16[320,128]{1,0:T(8,128)(2,1)S(1)}, u32[]{:S(2)}, u32[]{:S(2)}) %collective-permute-start.60) | collective-permute-done | bytes 81952 | tf_op jit(solution)/shard_map/ppermute | solution.py:734
  131.5 0.9 collective-permute-done.58.refs_4_.refs_5_
  132.4 0.8 collective-permute-done.56.refs_2_.refs_3_
  133.7 0.8 collective-permute-done.57.refs_3_.refs_4_
  134.7 1.3 collective-permute-start.64
  136.0 3.1 %collective-permute-start.62 = (f32[8,128]{1,0:T(8,128)S(1)}, f32[8,128]{1,0:T(8,128)S(1)}, u32[]{:S(2)}, u32[]{:S(2)}) collective-permute-start(f32[8,128]{1,0:T(8,128)S(1)} %squares.1.refs_1_), channel_id=1, source_target_pairs={{0,1},{1,0},{2,3},{3,2},{4,5},{5,4},{6,7},{7,6},{8,9},{9,8},{10,11... | collective-permute-start | bytes 12296 | tf_op jit(solution)/shard_map/ppermute | solution.py:734
  139.1 1.0 assemble.1
  140.8 3.8 %update.1 = (f32[1,1]{1,0:T(1,128)}, f32[128,2048]{1,0:T(8,128)}, f32[128,2048]{1,0:T(8,128)}, f32[128,2048]{1,0:T(8,128)}, bf16[128,2048]{1,0:T(8,128)(2,1)}, /...) custom-call(s32[4]{0:T(128)S(1)} %pad_add_fusion.refs_0_, ...), custom_call_target="tpu_custom_call" | custom-call | flops 1000000 | bytes 9870356 | tf_op jit(solution)/shard_map/update/pallas_call | solution.py:94
  (139 shorter events, 13.0 us)
Async XLA Ops:
  3.1 11.5 %collective-permute-start.5 = (bf16[208,128]{1,0:T(8,128)(2,1)}, bf16[208,128]{1,0:T(8,128)(2,1)S(1)}, u32[]{:S(2)}, u32[]{:S(2)}) collective-permute-start(bf16[208,128]{1,0:T(8,128)(2,1)} %get-tuple-element.115), channel_id=1, source_target_pairs={{0,3},{1,2},{2,1},{3,0},{4,7},{5,6},{6,5},{7,4},{8,11},{9,10},{10,... | collective-permute-start | bytes 159752 | tf_op jit(solution)/shard_map/ppermute | solution.py:734
  8.2 7.6 %collective-permute-start.4 = (bf16[208,128]{1,0:T(8,128)(2,1)}, bf16[208,128]{1,0:T(8,128)(2,1)S(1)}, u32[]{:S(2)}, u32[]{:S(2)}) collective-permute-start(bf16[208,128]{1,0:T(8,128)(2,1)} %get-tuple-element.115), channel_id=1, source_target_pairs={{0,2},{1,3},{2,0},{3,1},{4,6},{5,7},{6,4},{7,5},{8,10},{9,11},{10,... | collective-permute-start | bytes 159752 | tf_op jit(solution)/shard_map/ppermute | solution.py:734
  8.2 7.6 %collective-permute-start.3 = (bf16[208,128]{1,0:T(8,128)(2,1)}, bf16[208,128]{1,0:T(8,128)(2,1)S(1)}, u32[]{:S(2)}, u32[]{:S(2)}) collective-permute-start(bf16[208,128]{1,0:T(8,128)(2,1)} %get-tuple-element.115), channel_id=1, source_target_pairs={{0,1},{1,0},{2,3},{3,2},{4,5},{5,4},{6,7},{7,6},{8,9},{9,8},{10,11... | collective-permute-start | bytes 159752 | tf_op jit(solution)/shard_map/ppermute | solution.py:734
  8.8 9.3 %collective-permute-start.2 = (bf16[512,128]{1,0:T(8,128)(2,1)}, bf16[512,128]{1,0:T(8,128)(2,1)S(1)}, u32[]{:S(2)}, u32[]{:S(2)}) collective-permute-start(bf16[512,128]{1,0:T(8,128)(2,1)} %get-tuple-element.113.refs_3_.refs_1_), channel_id=1, source_target_pairs={{0,3},{1,2},{2,1},{3,0},{4,7},{5,6},{6,5},{7,4},{8,11},{9,10},{10,... | collective-permute-start | bytes 393224 | tf_op jit(solution)/shard_map/ppermute | solution.py:734
  12.6 8.6 %collective-permute-start = (bf16[512,128]{1,0:T(8,128)(2,1)}, bf16[512,128]{1,0:T(8,128)(2,1)S(1)}, u32[]{:S(2)}, u32[]{:S(2)}) collective-permute-start(bf16[512,128]{1,0:T(8,128)(2,1)} %get-tuple-element.113.refs_3_.refs_1_), channel_id=1, source_target_pairs={{0,1},{1,0},{2,3},{3,2},{4,5},{5,4},{6,7},{7,6},{8,9},{9,8},{10,11... | collective-permute-start | bytes 393224 | tf_op jit(solution)/shard_map/ppermute | solution.py:734
  15.2 9.2 %collective-permute-start.1 = (bf16[512,128]{1,0:T(8,128)(2,1)S(1)}, bf16[512,128]{1,0:T(8,128)(2,1)S(1)}, u32[]{:S(2)}, u32[]{:S(2)}) collective-permute-start(bf16[512,128]{1,0:T(8,128)(2,1)S(1)} %copy-done.6), channel_id=1, source_target_pairs={{0,2},{1,3},{2,0},{3,1},{4,6},{5,7},{6,4},{7,5},{8,10},{9,11},{10,... | collective-permute-start | bytes 393224 | tf_op jit(solution)/shard_map/ppermute | solution.py:734
  18.2 6.2 %collective-permute-start.8 = (bf16[512,128]{1,0:T(8,128)(2,1)S(1)}, bf16[512,128]{1,0:T(8,128)(2,1)S(1)}, u32[]{:S(2)}, u32[]{:S(2)}) collective-permute-start(bf16[512,128]{1,0:T(8,128)(2,1)S(1)} %collective-permute-done.2.refs_6_.refs_4_), channel_id=1, source_target_pairs={{0,4},{1,5},{2,6},{3,7},{4,0},{5,1},{6,2},{7,3},{8,12},{9,13},{10,... | collective-permute-start | bytes 393224 | tf_op jit(solution)/shard_map/ppermute | solution.py:734
  18.2 13.3 %collective-permute-start.11 = (bf16[3,208,128]{2,1,0:T(8,128)(2,1)S(1)}, bf16[3,208,128]{2,1,0:T(8,128)(2,1)S(1)}, u32[]{:S(2)}, u32[]{:S(2)}) collective-permute-start(bf16[3,208,128]{2,1,0:T(8,128)(2,1)S(1)} %pad_maximum_fusion.2.refs_2_), channel_id=1, source_target_pairs={{0,24},{1,25},{2,26},{3,27},{4,28},{5,29},{6,30},{7,31},{8,16},{9,... | collective-permute-start | bytes 479240 | tf_op jit(solution)/shard_map/ppermute | solution.py:734
  20.6 10.8 %collective-permute-start.10 = (bf16[3,208,128]{2,1,0:T(8,128)(2,1)S(1)}, bf16[3,208,128]{2,1,0:T(8,128)(2,1)}, u32[]{:S(2)}, u32[]{:S(2)}) collective-permute-start(bf16[3,208,128]{2,1,0:T(8,128)(2,1)S(1)} %pad_maximum_fusion.2.refs_2_), channel_id=1, source_target_pairs={{0,16},{1,17},{2,18},{3,19},{4,20},{5,21},{6,22},{7,23},{8,24},{9,... | collective-permute-start | bytes 479240 | tf_op jit(solution)/shard_map/ppermute | solution.py:734
  21.1 10.3 %collective-permute-start.9 = (bf16[3,208,128]{2,1,0:T(8,128)(2,1)S(1)}, bf16[3,208,128]{2,1,0:T(8,128)(2,1)}, u32[]{:S(2)}, u32[]{:S(2)}) collective-permute-start(bf16[3,208,128]{2,1,0:T(8,128)(2,1)S(1)} %pad_maximum_fusion.2.refs_2_), channel_id=1, source_target_pairs={{0,8},{1,9},{2,10},{3,11},{4,12},{5,13},{6,14},{7,15},{8,0},{9,1},... | collective-permute-start | bytes 479240 | tf_op jit(solution)/shard_map/ppermute | solution.py:734
  24.4 1.3 collective-permute-start.6
  24.4 1.5 %collective-permute-start.7 = (bf16[512,128]{1,0:T(8,128)(2,1)S(1)}, bf16[512,128]{1,0:T(8,128)(2,1)S(1)}, u32[]{:S(2)}, u32[]{:S(2)}) collective-permute-start(bf16[512,128]{1,0:T(8,128)(2,1)S(1)} %collective-permute-done.1.refs_5_.refs_3_), channel_id=1, source_target_pairs={{0,4},{1,5},{2,6},{3,7},{4,0},{5,1},{6,2},{7,3},{8,12},{9,13},{10,... | collective-permute-start | bytes 393224 | tf_op jit(solution)/shard_map/ppermute | solution.py:734
  31.5 1.5 %collective-permute-start.12 = (bf16[4,80,256]{2,1,0:T(8,128)(2,1)S(1)}, bf16[4,80,256]{2,1,0:T(8,128)(2,1)S(1)}, u32[]{:S(2)}, u32[]{:S(2)}) collective-permute-start(bf16[4,80,256]{2,1,0:T(8,128)(2,1)S(1)} %get-tuple-element.124), channel_id=1, source_target_pairs={{0,4},{1,5},{2,6},{3,7},{4,0},{5,1},{6,2},{7,3},{8,12},{9,13},{10,... | collective-permute-start | bytes 491528 | tf_op jit(solution)/shard_map/ppermute | solution.py:734
  31.9 3.6 %collective-permute-start.16 = (bf16[3,208,128]{2,1,0:T(8,128)(2,1)S(1)}, bf16[3,208,128]{2,1,0:T(8,128)(2,1)S(1)}, u32[]{:S(2)}, u32[]{:S(2)}) collective-permute-start(bf16[3,208,128]{2,1,0:T(8,128)(2,1)S(1)} %pad_maximum_fusion.2.refs_2_), channel_id=1, source_target_pairs={{0,4},{1,5},{2,6},{3,7},{4,0},{5,1},{6,2},{7,3},{8,12},{9,13},{10,... | collective-permute-start | bytes 479240 | tf_op jit(solution)/shard_map/ppermute | solution.py:734
  32.0 4.0 %collective-permute-start.19 = (bf16[3,208,128]{2,1,0:T(8,128)(2,1)S(1)}, bf16[3,208,128]{2,1,0:T(8,128)(2,1)S(1)}, u32[]{:S(2)}, u32[]{:S(2)}) collective-permute-start(bf16[3,208,128]{2,1,0:T(8,128)(2,1)S(1)} %collective-permute-done.11.refs_8_), channel_id=1, source_target_pairs={{0,4},{1,5},{2,6},{3,7},{4,0},{5,1},{6,2},{7,3},{8,12},{9,13},{10,... | collective-permute-start | bytes 479240 | tf_op jit(solution)/shard_map/ppermute | solution.py:734
  32.4 4.2 %collective-permute-start.18 = (bf16[3,208,128]{2,1,0:T(8,128)(2,1)}, bf16[3,208,128]{2,1,0:T(8,128)(2,1)S(1)}, u32[]{:S(2)}, u32[]{:S(2)}) collective-permute-start(bf16[3,208,128]{2,1,0:T(8,128)(2,1)} %collective-permute-done.10.refs_6_), channel_id=1, source_target_pairs={{0,4},{1,5},{2,6},{3,7},{4,0},{5,1},{6,2},{7,3},{8,12},{9,13},{10,... | collective-permute-start | bytes 479240 | tf_op jit(solution)/shard_map/ppermute | solution.py:734
  32.6 4.0 %collective-permute-start.17 = (bf16[3,208,128]{2,1,0:T(8,128)(2,1)}, bf16[3,208,128]{2,1,0:T(8,128)(2,1)S(1)}, u32[]{:S(2)}, u32[]{:S(2)}) collective-permute-start(bf16[3,208,128]{2,1,0:T(8,128)(2,1)} %collective-permute-done.9.refs_4_), channel_id=1, source_target_pairs={{0,4},{1,5},{2,6},{3,7},{4,0},{5,1},{6,2},{7,3},{8,12},{9,13},{10,... | collective-permute-start | bytes 479240 | tf_op jit(solution)/shard_map/ppermute | solution.py:734
  33.0 5.4 %collective-permute-start.15 = (bf16[80,256]{1,0:T(8,128)(2,1)S(1)}, bf16[80,256]{1,0:T(8,128)(2,1)S(1)}, u32[]{:S(2)}, u32[]{:S(2)}) collective-permute-start(bf16[80,256]{1,0:T(8,128)(2,1)S(1)} %get-tuple-element.233), channel_id=1, source_target_pairs={{0,24},{1,25},{2,26},{3,27},{4,28},{5,29},{6,30},{7,31},{8,16},{9,... | collective-permute-start | bytes 122888 | tf_op jit(solution)/shard_map/ppermute | solution.py:734
  35.5 4.0 %collective-permute-start.14 = (bf16[80,256]{1,0:T(8,128)(2,1)S(1)}, bf16[80,256]{1,0:T(8,128)(2,1)S(1)}, u32[]{:S(2)}, u32[]{:S(2)}) collective-permute-start(bf16[80,256]{1,0:T(8,128)(2,1)S(1)} %get-tuple-element.234), channel_id=1, source_target_pairs={{0,16},{1,17},{2,18},{3,19},{4,20},{5,21},{6,22},{7,23},{8,24},{9,... | collective-permute-start | bytes 122888 | tf_op jit(solution)/shard_map/ppermute | solution.py:734
  36.0 4.0 %collective-permute-start.13 = (bf16[80,256]{1,0:T(8,128)(2,1)S(1)}, bf16[80,256]{1,0:T(8,128)(2,1)S(1)}, u32[]{:S(2)}, u32[]{:S(2)}) collective-permute-start(bf16[80,256]{1,0:T(8,128)(2,1)S(1)} %get-tuple-element.235), channel_id=1, source_target_pairs={{0,8},{1,9},{2,10},{3,11},{4,12},{5,13},{6,14},{7,15},{8,0},{9,1},... | collective-permute-start | bytes 122888 | tf_op jit(solution)/shard_map/ppermute | solution.py:734
  40.0 8.3 %collective-permute-start.22 = (bf16[80,256]{1,0:T(8,128)(2,1)S(1)}, bf16[80,256]{1,0:T(8,128)(2,1)S(1)}, u32[]{:S(2)}, u32[]{:S(2)}) collective-permute-start(bf16[80,256]{1,0:T(8,128)(2,1)S(1)} %fusion.12), channel_id=1, source_target_pairs={{0,3},{1,2},{2,1},{3,0},{4,7},{5,6},{6,5},{7,4},{8,11},{9,10},{10,... | collective-permute-start | bytes 122888 | tf_op jit(solution)/shard_map/ppermute | solution.py:734
  42.7 5.6 %collective-permute-start.21 = (bf16[80,256]{1,0:T(8,128)(2,1)S(1)}, bf16[80,256]{1,0:T(8,128)(2,1)S(1)}, u32[]{:S(2)}, u32[]{:S(2)}) collective-permute-start(bf16[80,256]{1,0:T(8,128)(2,1)S(1)} %fusion.12), channel_id=1, source_target_pairs={{0,2},{1,3},{2,0},{3,1},{4,6},{5,7},{6,4},{7,5},{8,10},{9,11},{10,... | collective-permute-start | bytes 122888 | tf_op jit(solution)/shard_map/ppermute | solution.py:734
  43.7 4.7 %collective-permute-start.20 = (bf16[80,256]{1,0:T(8,128)(2,1)S(1)}, bf16[80,256]{1,0:T(8,128)(2,1)S(1)}, u32[]{:S(2)}, u32[]{:S(2)}) collective-permute-start(bf16[80,256]{1,0:T(8,128)(2,1)S(1)} %fusion.12), channel_id=1, source_target_pairs={{0,1},{1,0},{2,3},{3,2},{4,5},{5,4},{6,7},{7,6},{8,9},{9,8},{10,11... | collective-permute-start | bytes 122888 | tf_op jit(solution)/shard_map/ppermute | solution.py:734
  48.4 5.4 %collective-permute-start.26 = (bf16[80,256]{1,0:T(8,128)(2,1)S(1)}, bf16[80,256]{1,0:T(8,128)(2,1)S(1)}, u32[]{:S(2)}, u32[]{:S(2)}) collective-permute-start(bf16[80,256]{1,0:T(8,128)(2,1)S(1)} %add_convert_fusion.1.refs_7_.refs_5_), channel_id=1, source_target_pairs={{0,24},{1,25},{2,26},{3,27},{4,28},{5,29},{6,30},{7,31},{8,16},{9,... | collective-permute-start | bytes 122888 | tf_op jit(solution)/shard_map/ppermute | solution.py:734
  49.9 4.0 %collective-permute-start.25 = (bf16[80,256]{1,0:T(8,128)(2,1)S(1)}, bf16[80,256]{1,0:T(8,128)(2,1)S(1)}, u32[]{:S(2)}, u32[]{:S(2)}) collective-permute-start(bf16[80,256]{1,0:T(8,128)(2,1)S(1)} %add_convert_fusion.1.refs_7_.refs_5_), channel_id=1, source_target_pairs={{0,16},{1,17},{2,18},{3,19},{4,20},{5,21},{6,22},{7,23},{8,24},{9,... | collective-permute-start | bytes 122888 | tf_op jit(solution)/shard_map/ppermute | solution.py:734
  50.4 4.0 %collective-permute-start.24 = (bf16[80,256]{1,0:T(8,128)(2,1)S(1)}, bf16[80,256]{1,0:T(8,128)(2,1)S(1)}, u32[]{:S(2)}, u32[]{:S(2)}) collective-permute-start(bf16[80,256]{1,0:T(8,128)(2,1)S(1)} %add_convert_fusion.1.refs_7_.refs_5_), channel_id=1, source_target_pairs={{0,8},{1,9},{2,10},{3,11},{4,12},{5,13},{6,14},{7,15},{8,0},{9,1},... | collective-permute-start | bytes 122888 | tf_op jit(solution)/shard_map/ppermute | solution.py:734
  51.9 3.0 %collective-permute-start.23 = (bf16[80,256]{1,0:T(8,128)(2,1)S(1)}, bf16[80,256]{1,0:T(8,128)(2,1)S(1)}, u32[]{:S(2)}, u32[]{:S(2)}) collective-permute-start(bf16[80,256]{1,0:T(8,128)(2,1)S(1)} %add_convert_fusion.1.refs_7_.refs_5_), channel_id=1, source_target_pairs={{0,4},{1,5},{2,6},{3,7},{4,0},{5,1},{6,2},{7,3},{8,12},{9,13},{10,... | collective-permute-start | bytes 122888 | tf_op jit(solution)/shard_map/ppermute | solution.py:734
  54.4 1.4 collective-permute-start.28
  54.9 1.2 collective-permute-start.29
  65.7 1.5 %collective-permute-start.30 = (bf16[4,80,256]{2,1,0:T(8,128)(2,1)S(1)}, bf16[4,80,256]{2,1,0:T(8,128)(2,1)S(1)}, u32[]{:S(2)}, u32[]{:S(2)}) collective-permute-start(bf16[4,80,256]{2,1,0:T(8,128)(2,1)S(1)} %get-tuple-element.145), channel_id=1, source_target_pairs={{0,4},{1,5},{2,6},{3,7},{4,0},{5,1},{6,2},{7,3},{8,12},{9,13},{10,... | collective-permute-start | bytes 491528 | tf_op jit(solution)/shard_map/ppermute | solution.py:734
  67.3 7.1 %collective-permute-start.31 = (bf16[80,256]{1,0:T(8,128)(2,1)S(1)}, bf16[80,256]{1,0:T(8,128)(2,1)S(1)}, u32[]{:S(2)}, u32[]{:S(2)}) collective-permute-start(bf16[80,256]{1,0:T(8,128)(2,1)S(1)} %get-tuple-element.232), channel_id=1, source_target_pairs={{0,8},{1,9},{2,10},{3,11},{4,12},{5,13},{6,14},{7,15},{8,0},{9,1},... | collective-permute-start | bytes 122888 | tf_op jit(solution)/shard_map/ppermute | solution.py:734
  68.8 4.9 %collective-permute-start.33 = (bf16[80,256]{1,0:T(8,128)(2,1)S(1)}, bf16[80,256]{1,0:T(8,128)(2,1)S(1)}, u32[]{:S(2)}, u32[]{:S(2)}) collective-permute-start(bf16[80,256]{1,0:T(8,128)(2,1)S(1)} %get-tuple-element.230), channel_id=1, source_target_pairs={{0,24},{1,25},{2,26},{3,27},{4,28},{5,29},{6,30},{7,31},{8,16},{9,... | collective-permute-start | bytes 122888 | tf_op jit(solution)/shard_map/ppermute | solution.py:734
  70.3 4.0 %collective-permute-start.32 = (bf16[80,256]{1,0:T(8,128)(2,1)S(1)}, bf16[80,256]{1,0:T(8,128)(2,1)S(1)}, u32[]{:S(2)}, u32[]{:S(2)}) collective-permute-start(bf16[80,256]{1,0:T(8,128)(2,1)S(1)} %get-tuple-element.231), channel_id=1, source_target_pairs={{0,16},{1,17},{2,18},{3,19},{4,20},{5,21},{6,22},{7,23},{8,24},{9,... | collective-permute-start | bytes 122888 | tf_op jit(solution)/shard_map/ppermute | solution.py:734
  74.4 7.6 %collective-permute-start.36 = (bf16[80,256]{1,0:T(8,128)(2,1)S(1)}, bf16[80,256]{1,0:T(8,128)(2,1)S(1)}, u32[]{:S(2)}, u32[]{:S(2)}) collective-permute-start(bf16[80,256]{1,0:T(8,128)(2,1)S(1)} %fusion.9), channel_id=1, source_target_pairs={{0,3},{1,2},{2,1},{3,0},{4,7},{5,6},{6,5},{7,4},{8,11},{9,10},{10,... | collective-permute-start | bytes 122888 | tf_op jit(solution)/shard_map/ppermute | solution.py:734
  77.0 5.2 %collective-permute-start.35 = (bf16[80,256]{1,0:T(8,128)(2,1)S(1)}, bf16[80,256]{1,0:T(8,128)(2,1)S(1)}, u32[]{:S(2)}, u32[]{:S(2)}) collective-permute-start(bf16[80,256]{1,0:T(8,128)(2,1)S(1)} %fusion.9), channel_id=1, source_target_pairs={{0,2},{1,3},{2,0},{3,1},{4,6},{5,7},{6,4},{7,5},{8,10},{9,11},{10,... | collective-permute-start | bytes 122888 | tf_op jit(solution)/shard_map/ppermute | solution.py:734
  77.1 5.2 %collective-permute-start.34 = (bf16[80,256]{1,0:T(8,128)(2,1)S(1)}, bf16[80,256]{1,0:T(8,128)(2,1)S(1)}, u32[]{:S(2)}, u32[]{:S(2)}) collective-permute-start(bf16[80,256]{1,0:T(8,128)(2,1)S(1)} %fusion.9), channel_id=1, source_target_pairs={{0,1},{1,0},{2,3},{3,2},{4,5},{5,4},{6,7},{7,6},{8,9},{9,8},{10,11... | collective-permute-start | bytes 122888 | tf_op jit(solution)/shard_map/ppermute | solution.py:734
  82.3 6.6 %collective-permute-start.40 = (bf16[80,256]{1,0:T(8,128)(2,1)S(1)}, bf16[80,256]{1,0:T(8,128)(2,1)S(1)}, u32[]{:S(2)}, u32[]{:S(2)}) collective-permute-start(bf16[80,256]{1,0:T(8,128)(2,1)S(1)} %add_convert_fusion.refs_7_), channel_id=1, source_target_pairs={{0,24},{1,25},{2,26},{3,27},{4,28},{5,29},{6,30},{7,31},{8,16},{9,... | collective-permute-start | bytes 122888 | tf_op jit(solution)/shard_map/ppermute | solution.py:734
  84.0 4.8 %collective-permute-start.39 = (bf16[80,256]{1,0:T(8,128)(2,1)S(1)}, bf16[80,256]{1,0:T(8,128)(2,1)S(1)}, u32[]{:S(2)}, u32[]{:S(2)}) collective-permute-start(bf16[80,256]{1,0:T(8,128)(2,1)S(1)} %add_convert_fusion.refs_7_), channel_id=1, source_target_pairs={{0,16},{1,17},{2,18},{3,19},{4,20},{5,21},{6,22},{7,23},{8,24},{9,... | collective-permute-start | bytes 122888 | tf_op jit(solution)/shard_map/ppermute | solution.py:734
  85.0 4.0 %collective-permute-start.38 = (bf16[80,256]{1,0:T(8,128)(2,1)S(1)}, bf16[80,256]{1,0:T(8,128)(2,1)S(1)}, u32[]{:S(2)}, u32[]{:S(2)}) collective-permute-start(bf16[80,256]{1,0:T(8,128)(2,1)S(1)} %add_convert_fusion.refs_7_), channel_id=1, source_target_pairs={{0,8},{1,9},{2,10},{3,11},{4,12},{5,13},{6,14},{7,15},{8,0},{9,1},... | collective-permute-start | bytes 122888 | tf_op jit(solution)/shard_map/ppermute | solution.py:734
  89.0 2.1 %collective-permute-start.44 = (bf16[4,4,160,128]{3,2,1,0:T(8,128)(2,1)S(1)}, bf16[4,4,160,128]{3,2,1,0:T(8,128)(2,1)S(1)}, u32[]{:S(2)}, u32[]{:S(2)}) collective-permute-start(bf16[4,4,160,128]{3,2,1,0:T(8,128)(2,1)S(1)} %get-tuple-element.169), channel_id=1, source_target_pairs={{0,4},{1,5},{2,6},{3,7},{4,0},{5,1},{6,2},{7,3},{8,12},{9,13},{10,... | collective-permute-start | bytes 1966088 | tf_op jit(solution)/shard_map/ppermute | solution.py:734
  89.0 3.6 %collective-permute-start.37 = (bf16[80,256]{1,0:T(8,128)(2,1)S(1)}, bf16[80,256]{1,0:T(8,128)(2,1)S(1)}, u32[]{:S(2)}, u32[]{:S(2)}) collective-permute-start(bf16[80,256]{1,0:T(8,128)(2,1)S(1)} %add_convert_fusion.refs_7_), channel_id=1, source_target_pairs={{0,4},{1,5},{2,6},{3,7},{4,0},{5,1},{6,2},{7,3},{8,12},{9,13},{10,... | collective-permute-start | bytes 122888 | tf_op jit(solution)/shard_map/ppermute | solution.py:734
  89.5 4.1 %collective-permute-start.41 = (bf16[80,256]{1,0:T(8,128)(2,1)S(1)}, bf16[80,256]{1,0:T(8,128)(2,1)S(1)}, u32[]{:S(2)}, u32[]{:S(2)}) collective-permute-start(bf16[80,256]{1,0:T(8,128)(2,1)S(1)} %collective-permute-done.38.refs_9_), channel_id=1, source_target_pairs={{0,4},{1,5},{2,6},{3,7},{4,0},{5,1},{6,2},{7,3},{8,12},{9,13},{10,... | collective-permute-start | bytes 122888 | tf_op jit(solution)/shard_map/ppermute | solution.py:734
  89.5 5.4 %collective-permute-start.42 = (bf16[80,256]{1,0:T(8,128)(2,1)S(1)}, bf16[80,256]{1,0:T(8,128)(2,1)S(1)}, u32[]{:S(2)}, u32[]{:S(2)}) collective-permute-start(bf16[80,256]{1,0:T(8,128)(2,1)S(1)} %collective-permute-done.39.refs_11_), channel_id=1, source_target_pairs={{0,4},{1,5},{2,6},{3,7},{4,0},{5,1},{6,2},{7,3},{8,12},{9,13},{10,... | collective-permute-start | bytes 122888 | tf_op jit(solution)/shard_map/ppermute | solution.py:734
  90.1 4.9 %collective-permute-start.43 = (bf16[80,256]{1,0:T(8,128)(2,1)S(1)}, bf16[80,256]{1,0:T(8,128)(2,1)S(1)}, u32[]{:S(2)}, u32[]{:S(2)}) collective-permute-start(bf16[80,256]{1,0:T(8,128)(2,1)S(1)} %collective-permute-done.40.refs_13_), channel_id=1, source_target_pairs={{0,4},{1,5},{2,6},{3,7},{4,0},{5,1},{6,2},{7,3},{8,12},{9,13},{10,... | collective-permute-start | bytes 122888 | tf_op jit(solution)/shard_map/ppermute | solution.py:734
  91.4 10.7 %collective-permute-start.45 = (bf16[4,160,128]{2,1,0:T(8,128)(2,1)S(1)}, bf16[4,160,128]{2,1,0:T(8,128)(2,1)S(1)}, u32[]{:S(2)}, u32[]{:S(2)}) collective-permute-start(bf16[4,160,128]{2,1,0:T(8,128)(2,1)S(1)} %get-tuple-element.170), channel_id=1, source_target_pairs={{0,8},{1,9},{2,10},{3,11},{4,12},{5,13},{6,14},{7,15},{8,0},{9,1},... | collective-permute-start | bytes 491528 | tf_op jit(solution)/shard_map/ppermute | solution.py:734
  92.6 9.5 %collective-permute-start.46 = (bf16[4,160,128]{2,1,0:T(8,128)(2,1)S(1)}, bf16[4,160,128]{2,1,0:T(8,128)(2,1)S(1)}, u32[]{:S(2)}, u32[]{:S(2)}) collective-permute-start(bf16[4,160,128]{2,1,0:T(8,128)(2,1)S(1)} %get-tuple-element.171), channel_id=1, source_target_pairs={{0,16},{1,17},{2,18},{3,19},{4,20},{5,21},{6,22},{7,23},{8,24},{9,... | collective-permute-start | bytes 491528 | tf_op jit(solution)/shard_map/ppermute | solution.py:734
  93.6 8.5 %collective-permute-start.47 = (bf16[4,160,128]{2,1,0:T(8,128)(2,1)S(1)}, bf16[4,160,128]{2,1,0:T(8,128)(2,1)S(1)}, u32[]{:S(2)}, u32[]{:S(2)}) collective-permute-start(bf16[4,160,128]{2,1,0:T(8,128)(2,1)S(1)} %get-tuple-element.172), channel_id=1, source_target_pairs={{0,24},{1,25},{2,26},{3,27},{4,28},{5,29},{6,30},{7,31},{8,16},{9,... | collective-permute-start | bytes 491528 | tf_op jit(solution)/shard_map/ppermute | solution.py:734
  102.1 2.2 %collective-permute-start.48 = (bf16[4,4,160,128]{3,2,1,0:T(8,128)(2,1)S(1)}, bf16[4,4,160,128]{3,2,1,0:T(8,128)(2,1)S(1)}, u32[]{:S(2)}, u32[]{:S(2)}) collective-permute-start(bf16[4,4,160,128]{3,2,1,0:T(8,128)(2,1)S(1)} %get-tuple-element.173), channel_id=1, source_target_pairs={{0,4},{1,5},{2,6},{3,7},{4,0},{5,1},{6,2},{7,3},{8,12},{9,13},{10,... | collective-permute-start | bytes 1966088 | tf_op jit(solution)/shard_map/ppermute | solution.py:734
  104.6 11.8 %collective-permute-start.49 = (bf16[4,160,128]{2,1,0:T(8,128)(2,1)S(1)}, bf16[4,160,128]{2,1,0:T(8,128)(2,1)S(1)}, u32[]{:S(2)}, u32[]{:S(2)}) collective-permute-start(bf16[4,160,128]{2,1,0:T(8,128)(2,1)S(1)} %get-tuple-element.223), channel_id=1, source_target_pairs={{0,8},{1,9},{2,10},{3,11},{4,12},{5,13},{6,14},{7,15},{8,0},{9,1},... | collective-permute-start | bytes 491528 | tf_op jit(solution)/shard_map/ppermute | solution.py:734
  105.8 9.2 %collective-permute-start.51 = (bf16[4,160,128]{2,1,0:T(8,128)(2,1)S(1)}, bf16[4,160,128]{2,1,0:T(8,128)(2,1)S(1)}, u32[]{:S(2)}, u32[]{:S(2)}) collective-permute-start(bf16[4,160,128]{2,1,0:T(8,128)(2,1)S(1)} %get-tuple-element.221), channel_id=1, source_target_pairs={{0,24},{1,25},{2,26},{3,27},{4,28},{5,29},{6,30},{7,31},{8,16},{9,... | collective-permute-start | bytes 491528 | tf_op jit(solution)/shard_map/ppermute | solution.py:734
  107.1 9.2 %collective-permute-start.50 = (bf16[4,160,128]{2,1,0:T(8,128)(2,1)S(1)}, bf16[4,160,128]{2,1,0:T(8,128)(2,1)S(1)}, u32[]{:S(2)}, u32[]{:S(2)}) collective-permute-start(bf16[4,160,128]{2,1,0:T(8,128)(2,1)S(1)} %get-tuple-element.222), channel_id=1, source_target_pairs={{0,16},{1,17},{2,18},{3,19},{4,20},{5,21},{6,22},{7,23},{8,24},{9,... | collective-permute-start | bytes 491528 | tf_op jit(solution)/shard_map/ppermute | solution.py:734
  116.7 9.4 %collective-permute-start.52 = (bf16[320,128]{1,0:T(8,128)(2,1)S(1)}, bf16[320,128]{1,0:T(8,128)(2,1)S(1)}, u32[]{:S(2)}, u32[]{:S(2)}) collective-permute-start(bf16[320,128]{1,0:T(8,128)(2,1)S(1)} %get-tuple-element.182), channel_id=1, source_target_pairs={{0,1},{1,0},{2,3},{3,2},{4,5},{5,4},{6,7},{7,6},{8,9},{9,8},{10,11... | collective-permute-start | bytes 245768 | tf_op jit(solution)/shard_map/ppermute | solution.py:734
  117.4 7.2 %collective-permute-start.53 = (bf16[320,128]{1,0:T(8,128)(2,1)S(1)}, bf16[320,128]{1,0:T(8,128)(2,1)S(1)}, u32[]{:S(2)}, u32[]{:S(2)}) collective-permute-start(bf16[320,128]{1,0:T(8,128)(2,1)S(1)} %get-tuple-element.184), channel_id=1, source_target_pairs={{0,2},{1,3},{2,0},{3,1},{4,6},{5,7},{6,4},{7,5},{8,10},{9,11},{10,... | collective-permute-start | bytes 245768 | tf_op jit(solution)/shard_map/ppermute | solution.py:734
  119.8 6.3 %collective-permute-start.54 = (bf16[320,128]{1,0:T(8,128)(2,1)S(1)}, bf16[320,128]{1,0:T(8,128)(2,1)S(1)}, u32[]{:S(2)}, u32[]{:S(2)}) collective-permute-start(bf16[320,128]{1,0:T(8,128)(2,1)S(1)} %get-tuple-element.185), channel_id=1, source_target_pairs={{0,3},{1,2},{2,1},{3,0},{4,7},{5,6},{6,5},{7,4},{8,11},{9,10},{10,... | collective-permute-start | bytes 245768 | tf_op jit(solution)/shard_map/ppermute | solution.py:734
  126.1 5.4 %collective-permute-start.60 = (bf16[320,128]{1,0:T(8,128)(2,1)S(1)}, bf16[320,128]{1,0:T(8,128)(2,1)S(1)}, u32[]{:S(2)}, u32[]{:S(2)}) collective-permute-start(bf16[320,128]{1,0:T(8,128)(2,1)S(1)} %finish.1.refs_0_.refs_1_), channel_id=1, source_target_pairs={{0,24},{1,25},{2,26},{3,27},{4,28},{5,29},{6,30},{7,31},{8,16},{9,... | collective-permute-start | bytes 245768 | tf_op jit(solution)/shard_map/ppermute | solution.py:734
  127.9 4.5 %collective-permute-start.58 = (bf16[320,128]{1,0:T(8,128)(2,1)S(1)}, bf16[320,128]{1,0:T(8,128)(2,1)S(1)}, u32[]{:S(2)}, u32[]{:S(2)}) collective-permute-start(bf16[320,128]{1,0:T(8,128)(2,1)S(1)} %finish.1.refs_0_.refs_1_), channel_id=1, source_target_pairs={{0,16},{1,17},{2,18},{3,19},{4,20},{5,21},{6,22},{7,23},{8,24},{9,... | collective-permute-start | bytes 245768 | tf_op jit(solution)/shard_map/ppermute | solution.py:734
  128.8 4.4 %collective-permute-start.56 = (bf16[320,128]{1,0:T(8,128)(2,1)S(1)}, bf16[320,128]{1,0:T(8,128)(2,1)S(1)}, u32[]{:S(2)}, u32[]{:S(2)}) collective-permute-start(bf16[320,128]{1,0:T(8,128)(2,1)S(1)} %finish.1.refs_0_.refs_1_), channel_id=1, source_target_pairs={{0,8},{1,9},{2,10},{3,11},{4,12},{5,13},{6,14},{7,15},{8,0},{9,1},... | collective-permute-start | bytes 245768 | tf_op jit(solution)/shard_map/ppermute | solution.py:734
  129.7 3.6 %collective-permute-start.55 = (bf16[320,128]{1,0:T(8,128)(2,1)S(1)}, bf16[320,128]{1,0:T(8,128)(2,1)S(1)}, u32[]{:S(2)}, u32[]{:S(2)}) collective-permute-start(bf16[320,128]{1,0:T(8,128)(2,1)S(1)} %finish.1.refs_0_.refs_1_), channel_id=1, source_target_pairs={{0,4},{1,5},{2,6},{3,7},{4,0},{5,1},{6,2},{7,3},{8,12},{9,13},{10,... | collective-permute-start | bytes 245768 | tf_op jit(solution)/shard_map/ppermute | solution.py:734
  131.5 1.7 %collective-permute-start.61 = (bf16[320,128]{1,0:T(8,128)(2,1)S(1)}, bf16[320,128]{1,0:T(8,128)(2,1)S(1)}, u32[]{:S(2)}, u32[]{:S(2)}) collective-permute-start(bf16[320,128]{1,0:T(8,128)(2,1)S(1)} %collective-permute-done.60.refs_6_.refs_7_), channel_id=1, source_target_pairs={{0,4},{1,5},{2,6},{3,7},{4,0},{5,1},{6,2},{7,3},{8,12},{9,13},{10,... | collective-permute-start | bytes 245768 | tf_op jit(solution)/shard_map/ppermute | solution.py:734
  132.4 1.3 collective-permute-start.59
  133.2 1.3 collective-permute-start.57
  134.7 5.4 %collective-permute-start.64 = (f32[8,128]{1,0:T(8,128)S(1)}, f32[8,128]{1,0:T(8,128)S(1)}, u32[]{:S(2)}, u32[]{:S(2)}) collective-permute-start(f32[8,128]{1,0:T(8,128)S(1)} %squares.1.refs_1_), channel_id=1, source_target_pairs={{0,3},{1,2},{2,1},{3,0},{4,7},{5,6},{6,5},{7,4},{8,11},{9,10},{10,... | collective-permute-start | bytes 12296 | tf_op jit(solution)/shard_map/ppermute | solution.py:734
  136.0 4.5 %collective-permute-start.63 = (f32[8,128]{1,0:T(8,128)S(1)}, f32[8,128]{1,0:T(8,128)S(1)}, u32[]{:S(2)}, u32[]{:S(2)}) collective-permute-start(f32[8,128]{1,0:T(8,128)S(1)} %squares.1.refs_1_), channel_id=1, source_target_pairs={{0,2},{1,3},{2,0},{3,1},{4,6},{5,7},{6,4},{7,5},{8,10},{9,11},{10,... | collective-permute-start | bytes 12296 | tf_op jit(solution)/shard_map/ppermute | solution.py:734
  136.0 4.7 %collective-permute-start.62 = (f32[8,128]{1,0:T(8,128)S(1)}, f32[8,128]{1,0:T(8,128)S(1)}, u32[]{:S(2)}, u32[]{:S(2)}) collective-permute-start(f32[8,128]{1,0:T(8,128)S(1)} %squares.1.refs_1_), channel_id=1, source_target_pairs={{0,1},{1,0},{2,3},{3,2},{4,5},{5,4},{6,7},{7,6},{8,9},{9,8},{10,11... | collective-permute-start | bytes 12296 | tf_op jit(solution)/shard_map/ppermute | solution.py:734
  (18 other events, 265.1 us)

commit v6 on v5

--- a/solution.py
+++ b/solution.py
@@ -814,14 +814,14 @@
     )
     mine, other = [message], [kv_half]
     for z in range(1, shards):
-        late = z == 2
+        late = z == 3
         mine.append(exchange(tie(message, x_turned) if late else message, 0, z))
     stack = jnp.stack([exchange(part, 0, z) for z in range(1, shards)])
     stacks = [stack] + [None] * 7
     for e in range(1, 4):
         stacks[2 * e] = exchange(stack, 2 * e, 0)
     for z in range(1, shards):
-        other.append(exchange(tie(mine[z], stack), 1, 0))
+        other.append(exchange(mine[z], 1, 0))
     key_slope, key, value, keep, send = call(
         functools.partial(key_kernel, shards),
         1,
@@ -1135,7 +1135,8 @@
     send = tie(send, *early_got)
     mine_sum = keep + exchange(send, 1, 0).astype(fl_type)
     early_sum = tree_sum([early_mine[0], *to_float(early_got)])
-    got = swap([mine_sum[e].astype(bf_type) for e in range(1, 4)], plane, fill_inputs)
+    pieces = tie(tuple(mine_sum[e].astype(bf_type) for e in range(1, 4)))
+    got = swap(pieces, plane, fill_inputs)
     mine_sum = jnp.concatenate([tree_sum([mine_sum[0], *got]), early_sum], axis=1)
     pieces = tie(tuple(mine_sum[z].astype(bf_type) for z in range(1, shards)))
     owned_parts = [mine_sum[0], *swap(pieces, along, fill_output, cast=False)]

time: 145 us -> 144 us (level)
  no operation moved by 1% of the time
where the time goes in v6:
time: 144 us
  starting transfers between devices  59.7 us (41%)
  Pallas kernels  56.8 us (39%)
  waiting for transfers between devices  21.8 us (15%)
  local copies, waits for them, and re-layouts  2.52 us (2%)
  between operations  2.08 us (1%)
    ppermute x65, starting transfers between devices, exchange(): return lax.ppermute(value, AXES, pairs)  59.7 us
    pallas_call x19, Pallas kernels, call(): pl.pallas_call(body, grid=(steps,) if piped else (), in_specs=specs[:len(...  56.8 us
    ppermute x65, waiting for transfers between devices, exchange(): return lax.ppermute(value, AXES, pairs)  21.8 us
  transfers between devices with their start and end apart: 65, of which 27 were waited for; matrix products, arithmetic and copies ran while one was open for 2% of the time, Pallas kernels for 28%

profile of v6, /device:TPU:0, one launch (start us, length us, event | category | flops | bytes accessed | tf_op | source)
XLA Modules:
  0.0 144.2 jit_solution(4673450464106994476)
XLA Ops:
  0.6 2.4 %prep.1 = (bf16[512,128]{1,0:T(8,128)(2,1)}, bf16[512,128]{1,0:T(8,128)(2,1)}, bf16[208,128]{1,0:T(8,128)(2,1)}, bf16[1664,128]{1,0:T(8,128)(2,1)}) custom-call(f32[128,2048]{1,0:T(8,128)} %refs_8_.3, f32[128,512]{1,0:T(8,128)} %refs_11_.1, f32[2,128]{1,0:T(2,128)} %refs_14_.1), custom_call_target="tpu_custom_call" | custom-call | flops 1000000 | bytes 2053120 | tf_op jit(solution)/shard_map/prep/pallas_call | solution.py:94
  3.1 5.1 %collective-permute-start.8 = (bf16[208,128]{1,0:T(8,128)(2,1)}, bf16[208,128]{1,0:T(8,128)(2,1)S(1)}, u32[]{:S(2)}, u32[]{:S(2)}) collective-permute-start(bf16[208,128]{1,0:T(8,128)(2,1)} %get-tuple-element.120), channel_id=1, source_target_pairs={{0,3},{1,2},{2,1},{3,0},{4,7},{5,6},{6,5},{7,4},{8,11},{9,10},{10,... | collective-permute-start | bytes 159752 | tf_op jit(solution)/shard_map/ppermute | solution.py:734
  8.2 0.6 collective-permute-start.6
  8.8 2.3 %collective-permute-start.1 = (bf16[512,128]{1,0:T(8,128)(2,1)}, bf16[512,128]{1,0:T(8,128)(2,1)S(1)}, u32[]{:S(2)}, u32[]{:S(2)}) collective-permute-start(bf16[512,128]{1,0:T(8,128)(2,1)} %get-tuple-element.113.refs_3_.refs_1_), channel_id=1, source_target_pairs={{0,2},{1,3},{2,0},{3,1},{4,6},{5,7},{6,4},{7,5},{8,10},{9,11},{10,... | collective-permute-start | bytes 393224 | tf_op jit(solution)/shard_map/ppermute | solution.py:734
  11.1 2.0 %collective-permute-start = (bf16[512,128]{1,0:T(8,128)(2,1)}, bf16[512,128]{1,0:T(8,128)(2,1)S(1)}, u32[]{:S(2)}, u32[]{:S(2)}) collective-permute-start(bf16[512,128]{1,0:T(8,128)(2,1)} %get-tuple-element.113.refs_3_.refs_1_), channel_id=1, source_target_pairs={{0,1},{1,0},{2,3},{3,2},{4,5},{5,4},{6,7},{7,6},{8,9},{9,8},{10,11... | collective-permute-start | bytes 393224 | tf_op jit(solution)/shard_map/ppermute | solution.py:734
  13.1 1.7 %constant_dynamic-slice_fusion.3 = (bf16[2048,128]{1,0:T(8,128)(2,1)S(1)}, bf16[2048,128]{1,0:T(8,128)(2,1)S(1)}, bf16[2048,128]{1,0:T(8,128)(2,1)S(1)}, bf16[2048,128]{1,0:T(8,128)(2,1)S(1)}) fusion(bf16[2048,512]{1,0:T(8,128)(2,1)} %refs_1_.5, s32[]{:T(128)S(6)} %select_n.12, s32[]{:T(128)S(6)} %select_n.14, s32[]{:T(128)S(6)} %select_n.13, s32[]{:T(128)S(6)} %select_n.15), kind=kLoop, calls=%fused_computation.46 | loop fusion | bytes 4194320 | tf_op jit(solution)/shard_map/dynamic_slice | solution.py:810
  15.8 5.2 %collective-permute-done.1.refs_5_.refs_3_ = bf16[512,128]{1,0:T(8,128)(2,1)S(1)} collective-permute-done((bf16[512,128]{1,0:T(8,128)(2,1)}, bf16[512,128]{1,0:T(8,128)(2,1)S(1)}, u32[]{:S(2)}, u32[]{:S(2)}) %collective-permute-start.1) | collective-permute-done | bytes 131104 | tf_op jit(solution)/shard_map/ppermute | solution.py:734
  21.1 2.5 %collective-permute-start.11 = (bf16[3,208,128]{2,1,0:T(8,128)(2,1)S(1)}, bf16[3,208,128]{2,1,0:T(8,128)(2,1)S(1)}, u32[]{:S(2)}, u32[]{:S(2)}) collective-permute-start(bf16[3,208,128]{2,1,0:T(8,128)(2,1)S(1)} %pad_maximum_fusion.2.refs_2_), channel_id=1, source_target_pairs={{0,24},{1,25},{2,26},{3,27},{4,28},{5,29},{6,30},{7,31},{8,16},{9,... | collective-permute-start | bytes 479240 | tf_op jit(solution)/shard_map/ppermute | solution.py:734
  26.2 5.5 %keys.1 = (f32[512,2048]{1,0:T(8,128)S(1)}, bf16[512,2048]{1,0:T(8,128)(2,1)S(1)}, bf16[512,2048]{1,0:T(8,128)(2,1)S(1)}, f32[4,80,256]{2,1,0:T(8,128)S(1)}, bf16[4,80,256]{2,1,0:T(8,128)(2,1)S(1)}) custom-call(s32[4]{0:T(128)S(1)} %pad_add_fusion.refs_0_, bf16[2048,512]{1,0:T(8,128)(2,1)S(1)} %pad_maximum_fusion.refs_1_.refs_3_.refs_2_.refs_5_, ...), custom_call_target="tpu_custom_call" | custom-call | flops 1000 | bytes 12034064 | tf_op jit(solution)/shard_map/keys/pallas_call | solution.py:94
  33.7 2.1 %collective-permute-start.15 = (bf16[80,256]{1,0:T(8,128)(2,1)S(1)}, bf16[80,256]{1,0:T(8,128)(2,1)S(1)}, u32[]{:S(2)}, u32[]{:S(2)}) collective-permute-start(bf16[80,256]{1,0:T(8,128)(2,1)S(1)} %get-tuple-element.233), channel_id=1, source_target_pairs={{0,24},{1,25},{2,26},{3,27},{4,28},{5,29},{6,30},{7,31},{8,16},{9,... | collective-permute-start | bytes 122888 | tf_op jit(solution)/shard_map/ppermute | solution.py:734
  35.8 0.9 collective-permute-start.14
  37.3 1.8 %weights.1 = (bf16[512,512]{1,0:T(8,128)(2,1)S(1)}, bf16[512,512]{1,0:T(8,128)(2,1)S(1)}, bf16[512,512]{1,0:T(8,128)(2,1)S(1)}, f32[512,128]{1,0:T(8,128)S(1)}, ...) custom-call(s32[4]{0:T(128)S(1)} %pad_add_fusion.refs_0_, ...), custom_call_target="tpu_custom_call" | custom-call | flops 1000000 | bytes 4849680 | tf_op jit(solution)/shard_map/weights/pallas_call | solution.py:94
  39.1 0.7 collective-permute-done.14
  39.8 0.9 collective-permute-done.13
  40.8 1.8 %collective-permute-start.22 = (bf16[80,256]{1,0:T(8,128)(2,1)S(1)}, bf16[80,256]{1,0:T(8,128)(2,1)S(1)}, u32[]{:S(2)}, u32[]{:S(2)}) collective-permute-start(bf16[80,256]{1,0:T(8,128)(2,1)S(1)} %fusion.12), channel_id=1, source_target_pairs={{0,3},{1,2},{2,1},{3,0},{4,7},{5,6},{6,5},{7,4},{8,11},{9,10},{10,... | collective-permute-start | bytes 122888 | tf_op jit(solution)/shard_map/ppermute | solution.py:734
  42.5 2.7 %collective-permute-start.20 = (bf16[80,256]{1,0:T(8,128)(2,1)S(1)}, bf16[80,256]{1,0:T(8,128)(2,1)S(1)}, u32[]{:S(2)}, u32[]{:S(2)}) collective-permute-start(bf16[80,256]{1,0:T(8,128)(2,1)S(1)} %fusion.12), channel_id=1, source_target_pairs={{0,1},{1,0},{2,3},{3,2},{4,5},{5,4},{6,7},{7,6},{8,9},{9,8},{10,11... | collective-permute-start | bytes 122888 | tf_op jit(solution)/shard_map/ppermute | solution.py:734
  45.2 1.9 %query.1 = (f32[512,2048]{1,0:T(8,128)S(1)}, bf16[512,2048]{1,0:T(8,128)(2,1)S(1)}) custom-call(s32[4]{0:T(128)S(1)} %pad_add_fusion.refs_0_, bf16[2048,512]{1,0:T(8,128)(2,1)S(1)} %pad_maximum_fusion.refs_1_.refs_3_.refs_2_.refs_5_, bf16[512,512]{1,0:T(8,128)(2,1)S(1)} %get-tuple-element.124.refs_2_), custom_call_target="tpu_custom_call" | custom-call | flops 1073741824 | bytes 8912912 | tf_op jit(solution)/shard_map/query/pallas_call | solution.py:94
  47.1 1.9 %gate.1.refs_3_ = f32[512,2048]{1,0:T(8,128)S(1)} custom-call(s32[4]{0:T(128)S(1)} %pad_add_fusion.refs_0_, bf16[2048,512]{1,0:T(8,128)(2,1)S(1)} %pad_maximum_fusion.refs_1_.refs_3_.refs_2_.refs_5_, bf16[512,512]{1,0:T(8,128)(2,1)S(1)} %get-tuple-element.130.refs_2_), custom_call_target="tpu_custom_call" | custom-call | flops 1073741824 | bytes 6815760 | tf_op jit(solution)/shard_map/gate/pallas_call | solution.py:94
  49.1 1.5 %collective-permute-start.26 = (bf16[80,256]{1,0:T(8,128)(2,1)S(1)}, bf16[80,256]{1,0:T(8,128)(2,1)S(1)}, u32[]{:S(2)}, u32[]{:S(2)}) collective-permute-start(bf16[80,256]{1,0:T(8,128)(2,1)S(1)} %add_convert_fusion.1.refs_7_.refs_5_), channel_id=1, source_target_pairs={{0,24},{1,25},{2,26},{3,27},{4,28},{5,29},{6,30},{7,31},{8,16},{9,... | collective-permute-start | bytes 122888 | tf_op jit(solution)/shard_map/ppermute | solution.py:734
  51.1 1.5 %collective-permute-start.24 = (bf16[80,256]{1,0:T(8,128)(2,1)S(1)}, bf16[80,256]{1,0:T(8,128)(2,1)S(1)}, u32[]{:S(2)}, u32[]{:S(2)}) collective-permute-start(bf16[80,256]{1,0:T(8,128)(2,1)S(1)} %add_convert_fusion.1.refs_7_.refs_5_), channel_id=1, source_target_pairs={{0,8},{1,9},{2,10},{3,11},{4,12},{5,13},{6,14},{7,15},{8,0},{9,1},... | collective-permute-start | bytes 122888 | tf_op jit(solution)/shard_map/ppermute | solution.py:734
  52.6 1.8 %grad_prod.1.refs_4_ = f32[512,2048]{1,0:T(8,128)S(1)} custom-call(s32[4]{0:T(128)S(1)} %pad_add_fusion.refs_0_, bf16[2048,512]{1,0:T(8,128)(2,1)S(1)} %copy-done, bf16[512,512]{1,0:T(8,128)(2,1)S(1)} %get-tuple-element.135.refs_2_.refs_3_), custom_call_target="tpu_custom_call" | custom-call | flops 1073741824 | bytes 6815760 | tf_op jit(solution)/shard_map/grad_prod/pallas_call | solution.py:94
  55.7 0.7 collective-permute-done.27.refs_10_.refs_8_
  56.9 9.6 %middle.1 = (bf16[512,2048]{1,0:T(8,128)(2,1)S(1)}, bf16[512,2048]{1,0:T(8,128)(2,1)S(1)}, bf16[512,2048]{1,0:T(8,128)(2,1)S(1)}, f32[16,2048]{1,0:T(8,128)S(1)}...) custom-call(s32[4]{0:T(128)S(1)} %pad_add_fusion.refs_0_, s32[1,2048]{1,0:T(1,128)S(1)} %bitcast.69, ...), custom_call_target="tpu_custom_call" | custom-call | flops 6442450944 | bytes 18259984 | tf_op jit(solution)/shard_map/middle/pallas_call | solution.py:94
  66.7 1.2 collective-permute-done.30
  68.0 1.6 %collective-permute-start.31 = (bf16[80,256]{1,0:T(8,128)(2,1)S(1)}, bf16[80,256]{1,0:T(8,128)(2,1)S(1)}, u32[]{:S(2)}, u32[]{:S(2)}) collective-permute-start(bf16[80,256]{1,0:T(8,128)(2,1)S(1)} %get-tuple-element.232), channel_id=1, source_target_pairs={{0,8},{1,9},{2,10},{3,11},{4,12},{5,13},{6,14},{7,15},{8,0},{9,1},... | collective-permute-start | bytes 122888 | tf_op jit(solution)/shard_map/ppermute | solution.py:734
  69.5 1.4 collective-permute-start.33
  71.5 2.9 %gate_back.1 = (f32[512,512]{1,0:T(8,128)S(1)}, f32[512,512]{1,0:T(8,128)S(1)}) custom-call(s32[4]{0:T(128)S(1)} %pad_add_fusion.refs_0_, bf16[512,2048]{1,0:T(8,128)(2,1)S(1)} %get-tuple-element.144.refs_1_.refs_4_, bf16[512,2048]{1,0:T(8,128)(2,1)S(1)} %get-tuple-element.145.refs_2_, bf16[2048,512]{1,0:T(8,128)(2,1)S(1)} %pad_maximum_fusion.refs_1_.refs_3_.refs_2_.refs_5_, ...), custom_call_target="tpu_custom_call" | custom-call | flops 2147483648 | bytes 10485776 | tf_op jit(solution)/shard_map/gate_back/pallas_call | solution.py:94
  74.9 1.8 %collective-permute-start.36 = (bf16[80,256]{1,0:T(8,128)(2,1)S(1)}, bf16[80,256]{1,0:T(8,128)(2,1)S(1)}, u32[]{:S(2)}, u32[]{:S(2)}) collective-permute-start(bf16[80,256]{1,0:T(8,128)(2,1)S(1)} %fusion.9), channel_id=1, source_target_pairs={{0,3},{1,2},{2,1},{3,0},{4,7},{5,6},{6,5},{7,4},{8,11},{9,10},{10,... | collective-permute-start | bytes 122888 | tf_op jit(solution)/shard_map/ppermute | solution.py:734
  76.8 2.6 %collective-permute-start.34 = (bf16[80,256]{1,0:T(8,128)(2,1)S(1)}, bf16[80,256]{1,0:T(8,128)(2,1)S(1)}, u32[]{:S(2)}, u32[]{:S(2)}) collective-permute-start(bf16[80,256]{1,0:T(8,128)(2,1)S(1)} %fusion.9), channel_id=1, source_target_pairs={{0,1},{1,0},{2,3},{3,2},{4,5},{5,4},{6,7},{7,6},{8,9},{9,8},{10,11... | collective-permute-start | bytes 122888 | tf_op jit(solution)/shard_map/ppermute | solution.py:734
  79.4 3.1 %query_back.1.refs_1_ = bf16[512,2048]{1,0:T(8,128)(2,1)S(1)} custom-call(s32[4]{0:T(128)S(1)} %pad_add_fusion.refs_0_, s32[1,2048]{1,0:T(1,128)S(1)} %bitcast.70, bf16[512,2048]{1,0:T(8,128)(2,1)S(1)} %get-tuple-element.152.refs_2_, f32[16,2048]{1,0:T(8,128)S(1)} %get-tuple-element.153.refs_3_, f32[512,2048]{1,0:T(8,128)S(1)} %get-tuple-element.154.refs_4_, ...), custom_call_target="tpu_custom_call" | custom-call | flops 2147483648 | bytes 8855568 | tf_op jit(solution)/shard_map/query_back/pallas_call | solution.py:94
  82.6 1.6 %collective-permute-start.40 = (bf16[80,256]{1,0:T(8,128)(2,1)S(1)}, bf16[80,256]{1,0:T(8,128)(2,1)S(1)}, u32[]{:S(2)}, u32[]{:S(2)}) collective-permute-start(bf16[80,256]{1,0:T(8,128)(2,1)S(1)} %add_convert_fusion.refs_7_), channel_id=1, source_target_pairs={{0,24},{1,25},{2,26},{3,27},{4,28},{5,29},{6,30},{7,31},{8,16},{9,... | collective-permute-start | bytes 122888 | tf_op jit(solution)/shard_map/ppermute | solution.py:734
  84.2 1.1 collective-permute-start.39
  85.3 0.9 collective-permute-start.38
  86.2 1.8 %grad_query.1.refs_1_ = f32[512,512]{1,0:T(8,128)S(1)} custom-call(s32[4]{0:T(128)S(1)} %pad_add_fusion.refs_0_, bf16[512,2048]{1,0:T(8,128)(2,1)S(1)} %query_back.1.refs_1_, bf16[2048,512]{1,0:T(8,128)(2,1)S(1)} %pad_maximum_fusion.refs_1_.refs_3_.refs_2_.refs_5_), custom_call_target="tpu_custom_call" | custom-call | flops 1073741824 | bytes 5242896 | tf_op jit(solution)/shard_map/grad_query/pallas_call | solution.py:94
  88.0 1.2 early.1
  90.4 1.0 collective-permute-done.44
  91.7 1.2 collective-permute-start.45
  92.9 0.9 collective-permute-start.46
  93.8 1.4 collective-permute-start.47
  95.3 7.1 %key_back.1 = (bf16[512,2048]{1,0:T(8,128)(2,1)S(1)}, bf16[512,2048]{1,0:T(8,128)(2,1)S(1)}, f32[8,512]{1,0:T(8,128)S(1)}, f32[4,4,160,128]{3,2,1,0:T(8,128)S(1)}, bf16[4,4,160,128]{3,2,1,0:T(8,128)(2,1)S(1)}) custom-call(s32[4]{0:T(128)S(1)} %pad_add_fusion.refs_0_, s32[1,2048]{1,0:T(1,128)S(1)} %bitcast.71, f32[512,2048]{1,0:T(8,128)S(1)} %copy-done.16, ...), custom_call_target="tpu_custom_call" | custom-call | flops 6442450944 | bytes 18046992 | tf_op jit(solution)/shard_map/key_back/pallas_call | solution.py:94
  102.5 0.8 key_weights.1.refs_6_
  103.3 1.3 collective-permute-done.48
  104.8 1.2 collective-permute-start.49
  106.0 0.9 collective-permute-start.50
  107.0 1.4 collective-permute-start.51
  108.4 6.6 %inputs.1 = f32[2048,512]{1,0:T(8,128)} custom-call(s32[4]{0:T(128)S(1)} %pad_add_fusion.refs_0_, bf16[512,2048]{1,0:T(8,128)(2,1)S(1)} %query_back.1.refs_1_, bf16[512,2048]{1,0:T(8,128)(2,1)S(1)} %get-tuple-element.175.refs_2_, bf16[512,2048]{1,0:T(8,128)(2,1)S(1)} %get-tuple-element.176.refs_3_, bf16[512,2048]{1,0:T(8,128)(2,1)S(1)} %get-tuple-element.144.refs_1_.refs_4_, ...), custom_call_target="tpu_custom_call" | custom-call | flops 4294967296 | bytes 16777232 | tf_op jit(solution)/shard_map/inputs/pallas_call | solution.py:94
  115.9 0.9 collective-permute-start.52
  116.7 1.5 %collective-permute-start.53 = (bf16[320,128]{1,0:T(8,128)(2,1)S(1)}, bf16[320,128]{1,0:T(8,128)(2,1)S(1)}, u32[]{:S(2)}, u32[]{:S(2)}) collective-permute-start(bf16[320,128]{1,0:T(8,128)(2,1)S(1)} %get-tuple-element.184), channel_id=1, source_target_pairs={{0,2},{1,3},{2,0},{3,1},{4,6},{5,7},{6,4},{7,5},{8,10},{9,11},{10,... | collective-permute-start | bytes 245768 | tf_op jit(solution)/shard_map/ppermute | solution.py:734
  118.2 2.1 %collective-permute-start.54 = (bf16[320,128]{1,0:T(8,128)(2,1)S(1)}, bf16[320,128]{1,0:T(8,128)(2,1)S(1)}, u32[]{:S(2)}, u32[]{:S(2)}) collective-permute-start(bf16[320,128]{1,0:T(8,128)(2,1)S(1)} %get-tuple-element.185), channel_id=1, source_target_pairs={{0,3},{1,2},{2,1},{3,0},{4,7},{5,6},{6,5},{7,4},{8,11},{9,10},{10,... | collective-permute-start | bytes 245768 | tf_op jit(solution)/shard_map/ppermute | solution.py:734
  120.3 3.5 %output.1 = f32[2048,512]{1,0:T(8,128)} custom-call(s32[4]{0:T(128)S(1)} %pad_add_fusion.refs_0_, bf16[2048,512]{1,0:T(8,128)(2,1)S(1)} %copy-done.1, bf16[512,2048]{1,0:T(8,128)(2,1)S(1)} %get-tuple-element.145.refs_2_, bf16[512,512]{1,0:T(8,128)(2,1)S(1)} %get-tuple-element.135.refs_2_.refs_3_), custom_call_target="tpu_custom_call" | custom-call | flops 1073741824 | bytes 8912912 | tf_op jit(solution)/shard_map/output/pallas_call | solution.py:94
  123.8 1.2 collective-permute-done.53.refs_2_
  125.1 1.7 %collective-permute-start.60 = (bf16[320,128]{1,0:T(8,128)(2,1)S(1)}, bf16[320,128]{1,0:T(8,128)(2,1)S(1)}, u32[]{:S(2)}, u32[]{:S(2)}) collective-permute-start(bf16[320,128]{1,0:T(8,128)(2,1)S(1)} %finish.1.refs_0_.refs_1_), channel_id=1, source_target_pairs={{0,24},{1,25},{2,26},{3,27},{4,28},{5,29},{6,30},{7,31},{8,16},{9,... | collective-permute-start | bytes 245768 | tf_op jit(solution)/shard_map/ppermute | solution.py:734
  126.7 0.9 collective-permute-start.58
  127.7 1.0 collective-permute-start.56
  128.6 1.9 %collective-permute-done.60.refs_6_.refs_7_ = bf16[320,128]{1,0:T(8,128)(2,1)S(1)} collective-permute-done((bf16[320,128]{1,0:T(8,128)(2,1)S(1)}, bf16[320,128]{1,0:T(8,128)(2,1)S(1)}, u32[]{:S(2)}, u32[]{:S(2)}) %collective-permute-start.60) | collective-permute-done | bytes 81952 | tf_op jit(solution)/shard_map/ppermute | solution.py:734
  130.5 0.9 collective-permute-done.58.refs_4_.refs_5_
  131.4 0.7 collective-permute-done.56.refs_2_.refs_3_
  132.6 0.7 collective-permute-done.57.refs_3_.refs_4_
  133.6 1.7 %collective-permute-start.64 = (f32[8,128]{1,0:T(8,128)S(1)}, f32[8,128]{1,0:T(8,128)S(1)}, u32[]{:S(2)}, u32[]{:S(2)}) collective-permute-start(f32[8,128]{1,0:T(8,128)S(1)} %squares.1.refs_1_), channel_id=1, source_target_pairs={{0,3},{1,2},{2,1},{3,0},{4,7},{5,6},{6,5},{7,4},{8,11},{9,10},{10,... | collective-permute-start | bytes 12296 | tf_op jit(solution)/shard_map/ppermute | solution.py:734
  135.3 1.2 collective-permute-start.63
  136.5 1.5 %collective-permute-start.62 = (f32[8,128]{1,0:T(8,128)S(1)}, f32[8,128]{1,0:T(8,128)S(1)}, u32[]{:S(2)}, u32[]{:S(2)}) collective-permute-start(f32[8,128]{1,0:T(8,128)S(1)} %squares.1.refs_1_), channel_id=1, source_target_pairs={{0,1},{1,0},{2,3},{3,2},{4,5},{5,4},{6,7},{7,6},{8,9},{9,8},{10,11... | collective-permute-start | bytes 12296 | tf_op jit(solution)/shard_map/ppermute | solution.py:734
  138.0 1.0 assemble.1
  139.0 0.8 collective-permute-done.63.refs_3_
  140.2 3.8 %update.1 = (f32[1,1]{1,0:T(1,128)}, f32[128,2048]{1,0:T(8,128)}, f32[128,2048]{1,0:T(8,128)}, f32[128,2048]{1,0:T(8,128)}, bf16[128,2048]{1,0:T(8,128)(2,1)}, /...) custom-call(s32[4]{0:T(128)S(1)} %pad_add_fusion.refs_0_, ...), custom_call_target="tpu_custom_call" | custom-call | flops 1000000 | bytes 9870356 | tf_op jit(solution)/shard_map/update/pallas_call | solution.py:94
  (139 shorter events, 13.0 us)
Async XLA Ops:
  3.1 12.1 %collective-permute-start.8 = (bf16[208,128]{1,0:T(8,128)(2,1)}, bf16[208,128]{1,0:T(8,128)(2,1)S(1)}, u32[]{:S(2)}, u32[]{:S(2)}) collective-permute-start(bf16[208,128]{1,0:T(8,128)(2,1)} %get-tuple-element.120), channel_id=1, source_target_pairs={{0,3},{1,2},{2,1},{3,0},{4,7},{5,6},{6,5},{7,4},{8,11},{9,10},{10,... | collective-permute-start | bytes 159752 | tf_op jit(solution)/shard_map/ppermute | solution.py:734
  8.2 12.9 %collective-permute-start.7 = (bf16[208,128]{1,0:T(8,128)(2,1)}, bf16[208,128]{1,0:T(8,128)(2,1)S(1)}, u32[]{:S(2)}, u32[]{:S(2)}) collective-permute-start(bf16[208,128]{1,0:T(8,128)(2,1)} %get-tuple-element.120), channel_id=1, source_target_pairs={{0,2},{1,3},{2,0},{3,1},{4,6},{5,7},{6,4},{7,5},{8,10},{9,11},{10,... | collective-permute-start | bytes 159752 | tf_op jit(solution)/shard_map/ppermute | solution.py:734
  8.2 12.9 %collective-permute-start.6 = (bf16[208,128]{1,0:T(8,128)(2,1)}, bf16[208,128]{1,0:T(8,128)(2,1)S(1)}, u32[]{:S(2)}, u32[]{:S(2)}) collective-permute-start(bf16[208,128]{1,0:T(8,128)(2,1)} %get-tuple-element.120), channel_id=1, source_target_pairs={{0,1},{1,0},{2,3},{3,2},{4,5},{5,4},{6,7},{7,6},{8,9},{9,8},{10,11... | collective-permute-start | bytes 159752 | tf_op jit(solution)/shard_map/ppermute | solution.py:734
  8.8 12.2 %collective-permute-start.1 = (bf16[512,128]{1,0:T(8,128)(2,1)}, bf16[512,128]{1,0:T(8,128)(2,1)S(1)}, u32[]{:S(2)}, u32[]{:S(2)}) collective-permute-start(bf16[512,128]{1,0:T(8,128)(2,1)} %get-tuple-element.113.refs_3_.refs_1_), channel_id=1, source_target_pairs={{0,2},{1,3},{2,0},{3,1},{4,6},{5,7},{6,4},{7,5},{8,10},{9,11},{10,... | collective-permute-start | bytes 393224 | tf_op jit(solution)/shard_map/ppermute | solution.py:734
  11.1 13.0 %collective-permute-start = (bf16[512,128]{1,0:T(8,128)(2,1)}, bf16[512,128]{1,0:T(8,128)(2,1)S(1)}, u32[]{:S(2)}, u32[]{:S(2)}) collective-permute-start(bf16[512,128]{1,0:T(8,128)(2,1)} %get-tuple-element.113.refs_3_.refs_1_), channel_id=1, source_target_pairs={{0,1},{1,0},{2,3},{3,2},{4,5},{5,4},{6,7},{7,6},{8,9},{9,8},{10,11... | collective-permute-start | bytes 393224 | tf_op jit(solution)/shard_map/ppermute | solution.py:734
  15.8 8.9 %collective-permute-start.2 = (bf16[512,128]{1,0:T(8,128)(2,1)S(1)}, bf16[512,128]{1,0:T(8,128)(2,1)S(1)}, u32[]{:S(2)}, u32[]{:S(2)}) collective-permute-start(bf16[512,128]{1,0:T(8,128)(2,1)S(1)} %copy-done.6), channel_id=1, source_target_pairs={{0,3},{1,2},{2,1},{3,0},{4,7},{5,6},{6,5},{7,4},{8,11},{9,10},{10,... | collective-permute-start | bytes 393224 | tf_op jit(solution)/shard_map/ppermute | solution.py:734
  21.1 3.6 %collective-permute-start.4 = (bf16[512,128]{1,0:T(8,128)(2,1)S(1)}, bf16[512,128]{1,0:T(8,128)(2,1)S(1)}, u32[]{:S(2)}, u32[]{:S(2)}) collective-permute-start(bf16[512,128]{1,0:T(8,128)(2,1)S(1)} %collective-permute-done.1.refs_5_.refs_3_), channel_id=1, source_target_pairs={{0,4},{1,5},{2,6},{3,7},{4,0},{5,1},{6,2},{7,3},{8,12},{9,13},{10,... | collective-permute-start | bytes 393224 | tf_op jit(solution)/shard_map/ppermute | solution.py:734
  21.1 10.6 %collective-permute-start.11 = (bf16[3,208,128]{2,1,0:T(8,128)(2,1)S(1)}, bf16[3,208,128]{2,1,0:T(8,128)(2,1)S(1)}, u32[]{:S(2)}, u32[]{:S(2)}) collective-permute-start(bf16[3,208,128]{2,1,0:T(8,128)(2,1)S(1)} %pad_maximum_fusion.2.refs_2_), channel_id=1, source_target_pairs={{0,24},{1,25},{2,26},{3,27},{4,28},{5,29},{6,30},{7,31},{8,16},{9,... | collective-permute-start | bytes 479240 | tf_op jit(solution)/shard_map/ppermute | solution.py:734
  23.6 8.5 %collective-permute-start.10 = (bf16[3,208,128]{2,1,0:T(8,128)(2,1)S(1)}, bf16[3,208,128]{2,1,0:T(8,128)(2,1)}, u32[]{:S(2)}, u32[]{:S(2)}) collective-permute-start(bf16[3,208,128]{2,1,0:T(8,128)(2,1)S(1)} %pad_maximum_fusion.2.refs_2_), channel_id=1, source_target_pairs={{0,16},{1,17},{2,18},{3,19},{4,20},{5,21},{6,22},{7,23},{8,24},{9,... | collective-permute-start | bytes 479240 | tf_op jit(solution)/shard_map/ppermute | solution.py:734
  24.1 8.1 %collective-permute-start.9 = (bf16[3,208,128]{2,1,0:T(8,128)(2,1)S(1)}, bf16[3,208,128]{2,1,0:T(8,128)(2,1)}, u32[]{:S(2)}, u32[]{:S(2)}) collective-permute-start(bf16[3,208,128]{2,1,0:T(8,128)(2,1)S(1)} %pad_maximum_fusion.2.refs_2_), channel_id=1, source_target_pairs={{0,8},{1,9},{2,10},{3,11},{4,12},{5,13},{6,14},{7,15},{8,0},{9,1},... | collective-permute-start | bytes 479240 | tf_op jit(solution)/shard_map/ppermute | solution.py:734
  24.7 1.3 collective-permute-start.3
  24.7 1.5 %collective-permute-start.5 = (bf16[512,128]{1,0:T(8,128)(2,1)S(1)}, bf16[512,128]{1,0:T(8,128)(2,1)S(1)}, u32[]{:S(2)}, u32[]{:S(2)}) collective-permute-start(bf16[512,128]{1,0:T(8,128)(2,1)S(1)} %collective-permute-done.2.refs_6_.refs_4_), channel_id=1, source_target_pairs={{0,4},{1,5},{2,6},{3,7},{4,0},{5,1},{6,2},{7,3},{8,12},{9,13},{10,... | collective-permute-start | bytes 393224 | tf_op jit(solution)/shard_map/ppermute | solution.py:734
  32.2 1.4 collective-permute-start.12
  32.2 3.5 %collective-permute-start.16 = (bf16[3,208,128]{2,1,0:T(8,128)(2,1)S(1)}, bf16[3,208,128]{2,1,0:T(8,128)(2,1)S(1)}, u32[]{:S(2)}, u32[]{:S(2)}) collective-permute-start(bf16[3,208,128]{2,1,0:T(8,128)(2,1)S(1)} %pad_maximum_fusion.2.refs_2_), channel_id=1, source_target_pairs={{0,4},{1,5},{2,6},{3,7},{4,0},{5,1},{6,2},{7,3},{8,12},{9,13},{10,... | collective-permute-start | bytes 479240 | tf_op jit(solution)/shard_map/ppermute | solution.py:734
  32.7 4.0 %collective-permute-start.19 = (bf16[3,208,128]{2,1,0:T(8,128)(2,1)S(1)}, bf16[3,208,128]{2,1,0:T(8,128)(2,1)S(1)}, u32[]{:S(2)}, u32[]{:S(2)}) collective-permute-start(bf16[3,208,128]{2,1,0:T(8,128)(2,1)S(1)} %collective-permute-done.11.refs_8_), channel_id=1, source_target_pairs={{0,4},{1,5},{2,6},{3,7},{4,0},{5,1},{6,2},{7,3},{8,12},{9,13},{10,... | collective-permute-start | bytes 479240 | tf_op jit(solution)/shard_map/ppermute | solution.py:734
  32.7 4.5 %collective-permute-start.18 = (bf16[3,208,128]{2,1,0:T(8,128)(2,1)}, bf16[3,208,128]{2,1,0:T(8,128)(2,1)S(1)}, u32[]{:S(2)}, u32[]{:S(2)}) collective-permute-start(bf16[3,208,128]{2,1,0:T(8,128)(2,1)} %collective-permute-done.10.refs_6_), channel_id=1, source_target_pairs={{0,4},{1,5},{2,6},{3,7},{4,0},{5,1},{6,2},{7,3},{8,12},{9,13},{10,... | collective-permute-start | bytes 479240 | tf_op jit(solution)/shard_map/ppermute | solution.py:734
  33.3 4.0 %collective-permute-start.17 = (bf16[3,208,128]{2,1,0:T(8,128)(2,1)}, bf16[3,208,128]{2,1,0:T(8,128)(2,1)S(1)}, u32[]{:S(2)}, u32[]{:S(2)}) collective-permute-start(bf16[3,208,128]{2,1,0:T(8,128)(2,1)} %collective-permute-done.9.refs_4_), channel_id=1, source_target_pairs={{0,4},{1,5},{2,6},{3,7},{4,0},{5,1},{6,2},{7,3},{8,12},{9,13},{10,... | collective-permute-start | bytes 479240 | tf_op jit(solution)/shard_map/ppermute | solution.py:734
  33.7 5.4 %collective-permute-start.15 = (bf16[80,256]{1,0:T(8,128)(2,1)S(1)}, bf16[80,256]{1,0:T(8,128)(2,1)S(1)}, u32[]{:S(2)}, u32[]{:S(2)}) collective-permute-start(bf16[80,256]{1,0:T(8,128)(2,1)S(1)} %get-tuple-element.233), channel_id=1, source_target_pairs={{0,24},{1,25},{2,26},{3,27},{4,28},{5,29},{6,30},{7,31},{8,16},{9,... | collective-permute-start | bytes 122888 | tf_op jit(solution)/shard_map/ppermute | solution.py:734
  35.8 4.0 %collective-permute-start.14 = (bf16[80,256]{1,0:T(8,128)(2,1)S(1)}, bf16[80,256]{1,0:T(8,128)(2,1)S(1)}, u32[]{:S(2)}, u32[]{:S(2)}) collective-permute-start(bf16[80,256]{1,0:T(8,128)(2,1)S(1)} %get-tuple-element.234), channel_id=1, source_target_pairs={{0,16},{1,17},{2,18},{3,19},{4,20},{5,21},{6,22},{7,23},{8,24},{9,... | collective-permute-start | bytes 122888 | tf_op jit(solution)/shard_map/ppermute | solution.py:734
  36.7 4.0 %collective-permute-start.13 = (bf16[80,256]{1,0:T(8,128)(2,1)S(1)}, bf16[80,256]{1,0:T(8,128)(2,1)S(1)}, u32[]{:S(2)}, u32[]{:S(2)}) collective-permute-start(bf16[80,256]{1,0:T(8,128)(2,1)S(1)} %get-tuple-element.235), channel_id=1, source_target_pairs={{0,8},{1,9},{2,10},{3,11},{4,12},{5,13},{6,14},{7,15},{8,0},{9,1},... | collective-permute-start | bytes 122888 | tf_op jit(solution)/shard_map/ppermute | solution.py:734
  40.8 8.3 %collective-permute-start.22 = (bf16[80,256]{1,0:T(8,128)(2,1)S(1)}, bf16[80,256]{1,0:T(8,128)(2,1)S(1)}, u32[]{:S(2)}, u32[]{:S(2)}) collective-permute-start(bf16[80,256]{1,0:T(8,128)(2,1)S(1)} %fusion.12), channel_id=1, source_target_pairs={{0,3},{1,2},{2,1},{3,0},{4,7},{5,6},{6,5},{7,4},{8,11},{9,10},{10,... | collective-permute-start | bytes 122888 | tf_op jit(solution)/shard_map/ppermute | solution.py:734
  42.5 6.5 %collective-permute-start.21 = (bf16[80,256]{1,0:T(8,128)(2,1)S(1)}, bf16[80,256]{1,0:T(8,128)(2,1)S(1)}, u32[]{:S(2)}, u32[]{:S(2)}) collective-permute-start(bf16[80,256]{1,0:T(8,128)(2,1)S(1)} %fusion.12), channel_id=1, source_target_pairs={{0,2},{1,3},{2,0},{3,1},{4,6},{5,7},{6,4},{7,5},{8,10},{9,11},{10,... | collective-permute-start | bytes 122888 | tf_op jit(solution)/shard_map/ppermute | solution.py:734
  42.5 6.5 %collective-permute-start.20 = (bf16[80,256]{1,0:T(8,128)(2,1)S(1)}, bf16[80,256]{1,0:T(8,128)(2,1)S(1)}, u32[]{:S(2)}, u32[]{:S(2)}) collective-permute-start(bf16[80,256]{1,0:T(8,128)(2,1)S(1)} %fusion.12), channel_id=1, source_target_pairs={{0,1},{1,0},{2,3},{3,2},{4,5},{5,4},{6,7},{7,6},{8,9},{9,8},{10,11... | collective-permute-start | bytes 122888 | tf_op jit(solution)/shard_map/ppermute | solution.py:734
  49.1 5.4 %collective-permute-start.26 = (bf16[80,256]{1,0:T(8,128)(2,1)S(1)}, bf16[80,256]{1,0:T(8,128)(2,1)S(1)}, u32[]{:S(2)}, u32[]{:S(2)}) collective-permute-start(bf16[80,256]{1,0:T(8,128)(2,1)S(1)} %add_convert_fusion.1.refs_7_.refs_5_), channel_id=1, source_target_pairs={{0,24},{1,25},{2,26},{3,27},{4,28},{5,29},{6,30},{7,31},{8,16},{9,... | collective-permute-start | bytes 122888 | tf_op jit(solution)/shard_map/ppermute | solution.py:734
  50.5 4.0 %collective-permute-start.25 = (bf16[80,256]{1,0:T(8,128)(2,1)S(1)}, bf16[80,256]{1,0:T(8,128)(2,1)S(1)}, u32[]{:S(2)}, u32[]{:S(2)}) collective-permute-start(bf16[80,256]{1,0:T(8,128)(2,1)S(1)} %add_convert_fusion.1.refs_7_.refs_5_), channel_id=1, source_target_pairs={{0,16},{1,17},{2,18},{3,19},{4,20},{5,21},{6,22},{7,23},{8,24},{9,... | collective-permute-start | bytes 122888 | tf_op jit(solution)/shard_map/ppermute | solution.py:734
  51.1 4.0 %collective-permute-start.24 = (bf16[80,256]{1,0:T(8,128)(2,1)S(1)}, bf16[80,256]{1,0:T(8,128)(2,1)S(1)}, u32[]{:S(2)}, u32[]{:S(2)}) collective-permute-start(bf16[80,256]{1,0:T(8,128)(2,1)S(1)} %add_convert_fusion.1.refs_7_.refs_5_), channel_id=1, source_target_pairs={{0,8},{1,9},{2,10},{3,11},{4,12},{5,13},{6,14},{7,15},{8,0},{9,1},... | collective-permute-start | bytes 122888 | tf_op jit(solution)/shard_map/ppermute | solution.py:734
  52.6 3.0 %collective-permute-start.23 = (bf16[80,256]{1,0:T(8,128)(2,1)S(1)}, bf16[80,256]{1,0:T(8,128)(2,1)S(1)}, u32[]{:S(2)}, u32[]{:S(2)}) collective-permute-start(bf16[80,256]{1,0:T(8,128)(2,1)S(1)} %add_convert_fusion.1.refs_7_.refs_5_), channel_id=1, source_target_pairs={{0,4},{1,5},{2,6},{3,7},{4,0},{5,1},{6,2},{7,3},{8,12},{9,13},{10,... | collective-permute-start | bytes 122888 | tf_op jit(solution)/shard_map/ppermute | solution.py:734
  55.1 1.2 collective-permute-start.27
  55.1 1.4 collective-permute-start.28
  66.4 1.5 %collective-permute-start.30 = (bf16[4,80,256]{2,1,0:T(8,128)(2,1)S(1)}, bf16[4,80,256]{2,1,0:T(8,128)(2,1)S(1)}, u32[]{:S(2)}, u32[]{:S(2)}) collective-permute-start(bf16[4,80,256]{2,1,0:T(8,128)(2,1)S(1)} %get-tuple-element.142), channel_id=1, source_target_pairs={{0,4},{1,5},{2,6},{3,7},{4,0},{5,1},{6,2},{7,3},{8,12},{9,13},{10,... | collective-permute-start | bytes 491528 | tf_op jit(solution)/shard_map/ppermute | solution.py:734
  68.0 7.0 %collective-permute-start.31 = (bf16[80,256]{1,0:T(8,128)(2,1)S(1)}, bf16[80,256]{1,0:T(8,128)(2,1)S(1)}, u32[]{:S(2)}, u32[]{:S(2)}) collective-permute-start(bf16[80,256]{1,0:T(8,128)(2,1)S(1)} %get-tuple-element.232), channel_id=1, source_target_pairs={{0,8},{1,9},{2,10},{3,11},{4,12},{5,13},{6,14},{7,15},{8,0},{9,1},... | collective-permute-start | bytes 122888 | tf_op jit(solution)/shard_map/ppermute | solution.py:734
  69.5 4.9 %collective-permute-start.33 = (bf16[80,256]{1,0:T(8,128)(2,1)S(1)}, bf16[80,256]{1,0:T(8,128)(2,1)S(1)}, u32[]{:S(2)}, u32[]{:S(2)}) collective-permute-start(bf16[80,256]{1,0:T(8,128)(2,1)S(1)} %get-tuple-element.230), channel_id=1, source_target_pairs={{0,24},{1,25},{2,26},{3,27},{4,28},{5,29},{6,30},{7,31},{8,16},{9,... | collective-permute-start | bytes 122888 | tf_op jit(solution)/shard_map/ppermute | solution.py:734
  70.9 4.0 %collective-permute-start.32 = (bf16[80,256]{1,0:T(8,128)(2,1)S(1)}, bf16[80,256]{1,0:T(8,128)(2,1)S(1)}, u32[]{:S(2)}, u32[]{:S(2)}) collective-permute-start(bf16[80,256]{1,0:T(8,128)(2,1)S(1)} %get-tuple-element.231), channel_id=1, source_target_pairs={{0,16},{1,17},{2,18},{3,19},{4,20},{5,21},{6,22},{7,23},{8,24},{9,... | collective-permute-start | bytes 122888 | tf_op jit(solution)/shard_map/ppermute | solution.py:734
  74.9 7.6 %collective-permute-start.36 = (bf16[80,256]{1,0:T(8,128)(2,1)S(1)}, bf16[80,256]{1,0:T(8,128)(2,1)S(1)}, u32[]{:S(2)}, u32[]{:S(2)}) collective-permute-start(bf16[80,256]{1,0:T(8,128)(2,1)S(1)} %fusion.9), channel_id=1, source_target_pairs={{0,3},{1,2},{2,1},{3,0},{4,7},{5,6},{6,5},{7,4},{8,11},{9,10},{10,... | collective-permute-start | bytes 122888 | tf_op jit(solution)/shard_map/ppermute | solution.py:734
  76.8 5.8 %collective-permute-start.35 = (bf16[80,256]{1,0:T(8,128)(2,1)S(1)}, bf16[80,256]{1,0:T(8,128)(2,1)S(1)}, u32[]{:S(2)}, u32[]{:S(2)}) collective-permute-start(bf16[80,256]{1,0:T(8,128)(2,1)S(1)} %fusion.9), channel_id=1, source_target_pairs={{0,2},{1,3},{2,0},{3,1},{4,6},{5,7},{6,4},{7,5},{8,10},{9,11},{10,... | collective-permute-start | bytes 122888 | tf_op jit(solution)/shard_map/ppermute | solution.py:734
  76.8 5.8 %collective-permute-start.34 = (bf16[80,256]{1,0:T(8,128)(2,1)S(1)}, bf16[80,256]{1,0:T(8,128)(2,1)S(1)}, u32[]{:S(2)}, u32[]{:S(2)}) collective-permute-start(bf16[80,256]{1,0:T(8,128)(2,1)S(1)} %fusion.9), channel_id=1, source_target_pairs={{0,1},{1,0},{2,3},{3,2},{4,5},{5,4},{6,7},{7,6},{8,9},{9,8},{10,11... | collective-permute-start | bytes 122888 | tf_op jit(solution)/shard_map/ppermute | solution.py:734
  82.6 6.6 %collective-permute-start.40 = (bf16[80,256]{1,0:T(8,128)(2,1)S(1)}, bf16[80,256]{1,0:T(8,128)(2,1)S(1)}, u32[]{:S(2)}, u32[]{:S(2)}) collective-permute-start(bf16[80,256]{1,0:T(8,128)(2,1)S(1)} %add_convert_fusion.refs_7_), channel_id=1, source_target_pairs={{0,24},{1,25},{2,26},{3,27},{4,28},{5,29},{6,30},{7,31},{8,16},{9,... | collective-permute-start | bytes 122888 | tf_op jit(solution)/shard_map/ppermute | solution.py:734
  84.2 5.0 %collective-permute-start.39 = (bf16[80,256]{1,0:T(8,128)(2,1)S(1)}, bf16[80,256]{1,0:T(8,128)(2,1)S(1)}, u32[]{:S(2)}, u32[]{:S(2)}) collective-permute-start(bf16[80,256]{1,0:T(8,128)(2,1)S(1)} %add_convert_fusion.refs_7_), channel_id=1, source_target_pairs={{0,16},{1,17},{2,18},{3,19},{4,20},{5,21},{6,22},{7,23},{8,24},{9,... | collective-permute-start | bytes 122888 | tf_op jit(solution)/shard_map/ppermute | solution.py:734
  85.3 4.0 %collective-permute-start.38 = (bf16[80,256]{1,0:T(8,128)(2,1)S(1)}, bf16[80,256]{1,0:T(8,128)(2,1)S(1)}, u32[]{:S(2)}, u32[]{:S(2)}) collective-permute-start(bf16[80,256]{1,0:T(8,128)(2,1)S(1)} %add_convert_fusion.refs_7_), channel_id=1, source_target_pairs={{0,8},{1,9},{2,10},{3,11},{4,12},{5,13},{6,14},{7,15},{8,0},{9,1},... | collective-permute-start | bytes 122888 | tf_op jit(solution)/shard_map/ppermute | solution.py:734
  89.3 2.1 %collective-permute-start.44 = (bf16[4,4,160,128]{3,2,1,0:T(8,128)(2,1)S(1)}, bf16[4,4,160,128]{3,2,1,0:T(8,128)(2,1)S(1)}, u32[]{:S(2)}, u32[]{:S(2)}) collective-permute-start(bf16[4,4,160,128]{3,2,1,0:T(8,128)(2,1)S(1)} %get-tuple-element.166), channel_id=1, source_target_pairs={{0,4},{1,5},{2,6},{3,7},{4,0},{5,1},{6,2},{7,3},{8,12},{9,13},{10,... | collective-permute-start | bytes 1966088 | tf_op jit(solution)/shard_map/ppermute | solution.py:734
  89.3 3.6 %collective-permute-start.37 = (bf16[80,256]{1,0:T(8,128)(2,1)S(1)}, bf16[80,256]{1,0:T(8,128)(2,1)S(1)}, u32[]{:S(2)}, u32[]{:S(2)}) collective-permute-start(bf16[80,256]{1,0:T(8,128)(2,1)S(1)} %add_convert_fusion.refs_7_), channel_id=1, source_target_pairs={{0,4},{1,5},{2,6},{3,7},{4,0},{5,1},{6,2},{7,3},{8,12},{9,13},{10,... | collective-permute-start | bytes 122888 | tf_op jit(solution)/shard_map/ppermute | solution.py:734
  89.8 4.0 %collective-permute-start.41 = (bf16[80,256]{1,0:T(8,128)(2,1)S(1)}, bf16[80,256]{1,0:T(8,128)(2,1)S(1)}, u32[]{:S(2)}, u32[]{:S(2)}) collective-permute-start(bf16[80,256]{1,0:T(8,128)(2,1)S(1)} %collective-permute-done.38.refs_9_), channel_id=1, source_target_pairs={{0,4},{1,5},{2,6},{3,7},{4,0},{5,1},{6,2},{7,3},{8,12},{9,13},{10,... | collective-permute-start | bytes 122888 | tf_op jit(solution)/shard_map/ppermute | solution.py:734
  89.9 5.4 %collective-permute-start.42 = (bf16[80,256]{1,0:T(8,128)(2,1)S(1)}, bf16[80,256]{1,0:T(8,128)(2,1)S(1)}, u32[]{:S(2)}, u32[]{:S(2)}) collective-permute-start(bf16[80,256]{1,0:T(8,128)(2,1)S(1)} %collective-permute-done.39.refs_11_), channel_id=1, source_target_pairs={{0,4},{1,5},{2,6},{3,7},{4,0},{5,1},{6,2},{7,3},{8,12},{9,13},{10,... | collective-permute-start | bytes 122888 | tf_op jit(solution)/shard_map/ppermute | solution.py:734
  90.3 4.9 %collective-permute-start.43 = (bf16[80,256]{1,0:T(8,128)(2,1)S(1)}, bf16[80,256]{1,0:T(8,128)(2,1)S(1)}, u32[]{:S(2)}, u32[]{:S(2)}) collective-permute-start(bf16[80,256]{1,0:T(8,128)(2,1)S(1)} %collective-permute-done.40.refs_13_), channel_id=1, source_target_pairs={{0,4},{1,5},{2,6},{3,7},{4,0},{5,1},{6,2},{7,3},{8,12},{9,13},{10,... | collective-permute-start | bytes 122888 | tf_op jit(solution)/shard_map/ppermute | solution.py:734
  91.7 10.7 %collective-permute-start.45 = (bf16[4,160,128]{2,1,0:T(8,128)(2,1)S(1)}, bf16[4,160,128]{2,1,0:T(8,128)(2,1)S(1)}, u32[]{:S(2)}, u32[]{:S(2)}) collective-permute-start(bf16[4,160,128]{2,1,0:T(8,128)(2,1)S(1)} %get-tuple-element.167), channel_id=1, source_target_pairs={{0,8},{1,9},{2,10},{3,11},{4,12},{5,13},{6,14},{7,15},{8,0},{9,1},... | collective-permute-start | bytes 491528 | tf_op jit(solution)/shard_map/ppermute | solution.py:734
  92.9 9.5 %collective-permute-start.46 = (bf16[4,160,128]{2,1,0:T(8,128)(2,1)S(1)}, bf16[4,160,128]{2,1,0:T(8,128)(2,1)S(1)}, u32[]{:S(2)}, u32[]{:S(2)}) collective-permute-start(bf16[4,160,128]{2,1,0:T(8,128)(2,1)S(1)} %get-tuple-element.168), channel_id=1, source_target_pairs={{0,16},{1,17},{2,18},{3,19},{4,20},{5,21},{6,22},{7,23},{8,24},{9,... | collective-permute-start | bytes 491528 | tf_op jit(solution)/shard_map/ppermute | solution.py:734
  93.8 8.6 %collective-permute-start.47 = (bf16[4,160,128]{2,1,0:T(8,128)(2,1)S(1)}, bf16[4,160,128]{2,1,0:T(8,128)(2,1)S(1)}, u32[]{:S(2)}, u32[]{:S(2)}) collective-permute-start(bf16[4,160,128]{2,1,0:T(8,128)(2,1)S(1)} %get-tuple-element.169), channel_id=1, source_target_pairs={{0,24},{1,25},{2,26},{3,27},{4,28},{5,29},{6,30},{7,31},{8,16},{9,... | collective-permute-start | bytes 491528 | tf_op jit(solution)/shard_map/ppermute | solution.py:734
  102.4 2.2 %collective-permute-start.48 = (bf16[4,4,160,128]{3,2,1,0:T(8,128)(2,1)S(1)}, bf16[4,4,160,128]{3,2,1,0:T(8,128)(2,1)S(1)}, u32[]{:S(2)}, u32[]{:S(2)}) collective-permute-start(bf16[4,4,160,128]{3,2,1,0:T(8,128)(2,1)S(1)} %get-tuple-element.170), channel_id=1, source_target_pairs={{0,4},{1,5},{2,6},{3,7},{4,0},{5,1},{6,2},{7,3},{8,12},{9,13},{10,... | collective-permute-start | bytes 1966088 | tf_op jit(solution)/shard_map/ppermute | solution.py:734
  104.8 10.7 %collective-permute-start.49 = (bf16[4,160,128]{2,1,0:T(8,128)(2,1)S(1)}, bf16[4,160,128]{2,1,0:T(8,128)(2,1)S(1)}, u32[]{:S(2)}, u32[]{:S(2)}) collective-permute-start(bf16[4,160,128]{2,1,0:T(8,128)(2,1)S(1)} %get-tuple-element.171), channel_id=1, source_target_pairs={{0,8},{1,9},{2,10},{3,11},{4,12},{5,13},{6,14},{7,15},{8,0},{9,1},... | collective-permute-start | bytes 491528 | tf_op jit(solution)/shard_map/ppermute | solution.py:734
  106.0 9.5 %collective-permute-start.50 = (bf16[4,160,128]{2,1,0:T(8,128)(2,1)S(1)}, bf16[4,160,128]{2,1,0:T(8,128)(2,1)S(1)}, u32[]{:S(2)}, u32[]{:S(2)}) collective-permute-start(bf16[4,160,128]{2,1,0:T(8,128)(2,1)S(1)} %get-tuple-element.172), channel_id=1, source_target_pairs={{0,16},{1,17},{2,18},{3,19},{4,20},{5,21},{6,22},{7,23},{8,24},{9,... | collective-permute-start | bytes 491528 | tf_op jit(solution)/shard_map/ppermute | solution.py:734
  107.0 8.5 %collective-permute-start.51 = (bf16[4,160,128]{2,1,0:T(8,128)(2,1)S(1)}, bf16[4,160,128]{2,1,0:T(8,128)(2,1)S(1)}, u32[]{:S(2)}, u32[]{:S(2)}) collective-permute-start(bf16[4,160,128]{2,1,0:T(8,128)(2,1)S(1)} %get-tuple-element.173), channel_id=1, source_target_pairs={{0,24},{1,25},{2,26},{3,27},{4,28},{5,29},{6,30},{7,31},{8,16},{9,... | collective-permute-start | bytes 491528 | tf_op jit(solution)/shard_map/ppermute | solution.py:734
  115.9 9.2 %collective-permute-start.52 = (bf16[320,128]{1,0:T(8,128)(2,1)S(1)}, bf16[320,128]{1,0:T(8,128)(2,1)S(1)}, u32[]{:S(2)}, u32[]{:S(2)}) collective-permute-start(bf16[320,128]{1,0:T(8,128)(2,1)S(1)} %get-tuple-element.182), channel_id=1, source_target_pairs={{0,1},{1,0},{2,3},{3,2},{4,5},{5,4},{6,7},{7,6},{8,9},{9,8},{10,11... | collective-permute-start | bytes 245768 | tf_op jit(solution)/shard_map/ppermute | solution.py:734
  116.7 8.3 %collective-permute-start.53 = (bf16[320,128]{1,0:T(8,128)(2,1)S(1)}, bf16[320,128]{1,0:T(8,128)(2,1)S(1)}, u32[]{:S(2)}, u32[]{:S(2)}) collective-permute-start(bf16[320,128]{1,0:T(8,128)(2,1)S(1)} %get-tuple-element.184), channel_id=1, source_target_pairs={{0,2},{1,3},{2,0},{3,1},{4,6},{5,7},{6,4},{7,5},{8,10},{9,11},{10,... | collective-permute-start | bytes 245768 | tf_op jit(solution)/shard_map/ppermute | solution.py:734
  118.2 6.8 %collective-permute-start.54 = (bf16[320,128]{1,0:T(8,128)(2,1)S(1)}, bf16[320,128]{1,0:T(8,128)(2,1)S(1)}, u32[]{:S(2)}, u32[]{:S(2)}) collective-permute-start(bf16[320,128]{1,0:T(8,128)(2,1)S(1)} %get-tuple-element.185), channel_id=1, source_target_pairs={{0,3},{1,2},{2,1},{3,0},{4,7},{5,6},{6,5},{7,4},{8,11},{9,10},{10,... | collective-permute-start | bytes 245768 | tf_op jit(solution)/shard_map/ppermute | solution.py:734
  125.1 5.4 %collective-permute-start.60 = (bf16[320,128]{1,0:T(8,128)(2,1)S(1)}, bf16[320,128]{1,0:T(8,128)(2,1)S(1)}, u32[]{:S(2)}, u32[]{:S(2)}) collective-permute-start(bf16[320,128]{1,0:T(8,128)(2,1)S(1)} %finish.1.refs_0_.refs_1_), channel_id=1, source_target_pairs={{0,24},{1,25},{2,26},{3,27},{4,28},{5,29},{6,30},{7,31},{8,16},{9,... | collective-permute-start | bytes 245768 | tf_op jit(solution)/shard_map/ppermute | solution.py:734
  126.7 4.6 %collective-permute-start.58 = (bf16[320,128]{1,0:T(8,128)(2,1)S(1)}, bf16[320,128]{1,0:T(8,128)(2,1)S(1)}, u32[]{:S(2)}, u32[]{:S(2)}) collective-permute-start(bf16[320,128]{1,0:T(8,128)(2,1)S(1)} %finish.1.refs_0_.refs_1_), channel_id=1, source_target_pairs={{0,16},{1,17},{2,18},{3,19},{4,20},{5,21},{6,22},{7,23},{8,24},{9,... | collective-permute-start | bytes 245768 | tf_op jit(solution)/shard_map/ppermute | solution.py:734
  127.7 4.4 %collective-permute-start.56 = (bf16[320,128]{1,0:T(8,128)(2,1)S(1)}, bf16[320,128]{1,0:T(8,128)(2,1)S(1)}, u32[]{:S(2)}, u32[]{:S(2)}) collective-permute-start(bf16[320,128]{1,0:T(8,128)(2,1)S(1)} %finish.1.refs_0_.refs_1_), channel_id=1, source_target_pairs={{0,8},{1,9},{2,10},{3,11},{4,12},{5,13},{6,14},{7,15},{8,0},{9,1},... | collective-permute-start | bytes 245768 | tf_op jit(solution)/shard_map/ppermute | solution.py:734
  128.6 3.5 %collective-permute-start.55 = (bf16[320,128]{1,0:T(8,128)(2,1)S(1)}, bf16[320,128]{1,0:T(8,128)(2,1)S(1)}, u32[]{:S(2)}, u32[]{:S(2)}) collective-permute-start(bf16[320,128]{1,0:T(8,128)(2,1)S(1)} %finish.1.refs_0_.refs_1_), channel_id=1, source_target_pairs={{0,4},{1,5},{2,6},{3,7},{4,0},{5,1},{6,2},{7,3},{8,12},{9,13},{10,... | collective-permute-start | bytes 245768 | tf_op jit(solution)/shard_map/ppermute | solution.py:734
  130.5 1.6 %collective-permute-start.61 = (bf16[320,128]{1,0:T(8,128)(2,1)S(1)}, bf16[320,128]{1,0:T(8,128)(2,1)S(1)}, u32[]{:S(2)}, u32[]{:S(2)}) collective-permute-start(bf16[320,128]{1,0:T(8,128)(2,1)S(1)} %collective-permute-done.60.refs_6_.refs_7_), channel_id=1, source_target_pairs={{0,4},{1,5},{2,6},{3,7},{4,0},{5,1},{6,2},{7,3},{8,12},{9,13},{10,... | collective-permute-start | bytes 245768 | tf_op jit(solution)/shard_map/ppermute | solution.py:734
  131.4 1.3 collective-permute-start.59
  132.1 1.3 collective-permute-start.57
  133.6 5.4 %collective-permute-start.64 = (f32[8,128]{1,0:T(8,128)S(1)}, f32[8,128]{1,0:T(8,128)S(1)}, u32[]{:S(2)}, u32[]{:S(2)}) collective-permute-start(f32[8,128]{1,0:T(8,128)S(1)} %squares.1.refs_1_), channel_id=1, source_target_pairs={{0,3},{1,2},{2,1},{3,0},{4,7},{5,6},{6,5},{7,4},{8,11},{9,10},{10,... | collective-permute-start | bytes 12296 | tf_op jit(solution)/shard_map/ppermute | solution.py:734
  135.3 4.5 %collective-permute-start.63 = (f32[8,128]{1,0:T(8,128)S(1)}, f32[8,128]{1,0:T(8,128)S(1)}, u32[]{:S(2)}, u32[]{:S(2)}) collective-permute-start(f32[8,128]{1,0:T(8,128)S(1)} %squares.1.refs_1_), channel_id=1, source_target_pairs={{0,2},{1,3},{2,0},{3,1},{4,6},{5,7},{6,4},{7,5},{8,10},{9,11},{10,... | collective-permute-start | bytes 12296 | tf_op jit(solution)/shard_map/ppermute | solution.py:734
  136.5 3.6 %collective-permute-start.62 = (f32[8,128]{1,0:T(8,128)S(1)}, f32[8,128]{1,0:T(8,128)S(1)}, u32[]{:S(2)}, u32[]{:S(2)}) collective-permute-start(f32[8,128]{1,0:T(8,128)S(1)} %squares.1.refs_1_), channel_id=1, source_target_pairs={{0,1},{1,0},{2,3},{3,2},{4,5},{5,4},{6,7},{7,6},{8,9},{9,8},{10,11... | collective-permute-start | bytes 12296 | tf_op jit(solution)/shard_map/ppermute | solution.py:734
  (18 other events, 267.3 us)

commit v7 on v6

--- a/solution.py
+++ b/solution.py
@@ -894,7 +894,7 @@
             1e6,
             "weights",
         )
-        return made["weights"][0]
+        return fill_query(dep)
 
     def fill_query(dep):
         made["query"] = call(
@@ -910,7 +910,7 @@
             rows,
             vmem=16,
         )
-        return made["query"][1], fill_gate(dep)
+        return made["query"][1]
 
     def fill_gate(dep):
         gate_weight = made["weights"][1]
@@ -949,7 +949,7 @@
     send = tie(send, *stacks[2::2])
     for e in range(4):
         stacks[2 * e + 1] = exchange(stacks[2 * e], 1, 0)
-    chunks = reduce_chunks(keep, send, (fill_weights, fill_query, fill_grad_prod))
+    chunks = reduce_chunks(keep, send, (fill_weights, fill_gate, fill_grad_prod))
     out_weight, gain, shift, full_query, full_gate = made["weights"][2:]
     query_slope, query = made["query"]
 

time: 144 us -> 144 us (level)
  transfers between devices with their start and end apart: 65 -> 65, of which waited for: 27 -> 25; matrix products, arithmetic and copies ran while one was open for 2% -> 2% of each run, Pallas kernels for 28% -> 28%
where the time goes in v7:
time: 144 us
  starting transfers between devices  59.8 us (42%)
  Pallas kernels  56.8 us (39%)
  waiting for transfers between devices  21.2 us (15%)
  local copies, waits for them, and re-layouts  2.52 us (2%)
  between operations  2.1 us (1%)
    ppermute x65, starting transfers between devices, exchange(): return lax.ppermute(value, AXES, pairs)  59.8 us
    pallas_call x19, Pallas kernels, call(): pl.pallas_call(body, grid=(steps,) if piped else (), in_specs=specs[:len(...  56.8 us
    ppermute x65, waiting for transfers between devices, exchange(): return lax.ppermute(value, AXES, pairs)  21.2 us
  transfers between devices with their start and end apart: 65, of which 25 were waited for; matrix products, arithmetic and copies ran while one was open for 2% of the time, Pallas kernels for 28%

profile of v7, /device:TPU:0, one launch (start us, length us, event | category | flops | bytes accessed | tf_op | source)
XLA Modules:
  0.0 143.7 jit_solution(5502860563022711957)
XLA Ops:
  0.6 2.4 %prep.1 = (bf16[512,128]{1,0:T(8,128)(2,1)}, bf16[512,128]{1,0:T(8,128)(2,1)}, bf16[208,128]{1,0:T(8,128)(2,1)}, bf16[1664,128]{1,0:T(8,128)(2,1)}) custom-call(f32[128,2048]{1,0:T(8,128)} %refs_8_.3, f32[128,512]{1,0:T(8,128)} %refs_11_.1, f32[2,128]{1,0:T(2,128)} %refs_14_.1), custom_call_target="tpu_custom_call" | custom-call | flops 1000000 | bytes 2053120 | tf_op jit(solution)/shard_map/prep/pallas_call | solution.py:94
  3.1 5.1 %collective-permute-start.8 = (bf16[208,128]{1,0:T(8,128)(2,1)}, bf16[208,128]{1,0:T(8,128)(2,1)S(1)}, u32[]{:S(2)}, u32[]{:S(2)}) collective-permute-start(bf16[208,128]{1,0:T(8,128)(2,1)} %get-tuple-element.120), channel_id=1, source_target_pairs={{0,3},{1,2},{2,1},{3,0},{4,7},{5,6},{6,5},{7,4},{8,11},{9,10},{10,... | collective-permute-start | bytes 159752 | tf_op jit(solution)/shard_map/ppermute | solution.py:734
  8.2 0.6 collective-permute-start.6
  8.8 2.3 %collective-permute-start.1 = (bf16[512,128]{1,0:T(8,128)(2,1)}, bf16[512,128]{1,0:T(8,128)(2,1)S(1)}, u32[]{:S(2)}, u32[]{:S(2)}) collective-permute-start(bf16[512,128]{1,0:T(8,128)(2,1)} %get-tuple-element.113.refs_3_.refs_1_), channel_id=1, source_target_pairs={{0,2},{1,3},{2,0},{3,1},{4,6},{5,7},{6,4},{7,5},{8,10},{9,11},{10,... | collective-permute-start | bytes 393224 | tf_op jit(solution)/shard_map/ppermute | solution.py:734
  11.1 2.0 %collective-permute-start = (bf16[512,128]{1,0:T(8,128)(2,1)}, bf16[512,128]{1,0:T(8,128)(2,1)S(1)}, u32[]{:S(2)}, u32[]{:S(2)}) collective-permute-start(bf16[512,128]{1,0:T(8,128)(2,1)} %get-tuple-element.113.refs_3_.refs_1_), channel_id=1, source_target_pairs={{0,1},{1,0},{2,3},{3,2},{4,5},{5,4},{6,7},{7,6},{8,9},{9,8},{10,11... | collective-permute-start | bytes 393224 | tf_op jit(solution)/shard_map/ppermute | solution.py:734
  13.1 1.7 %constant_dynamic-slice_fusion.3 = (bf16[2048,128]{1,0:T(8,128)(2,1)S(1)}, bf16[2048,128]{1,0:T(8,128)(2,1)S(1)}, bf16[2048,128]{1,0:T(8,128)(2,1)S(1)}, bf16[2048,128]{1,0:T(8,128)(2,1)S(1)}) fusion(bf16[2048,512]{1,0:T(8,128)(2,1)} %refs_1_.5, s32[]{:T(128)S(6)} %select_n.12, s32[]{:T(128)S(6)} %select_n.14, s32[]{:T(128)S(6)} %select_n.13, s32[]{:T(128)S(6)} %select_n.15), kind=kLoop, calls=%fused_computation.46 | loop fusion | bytes 4194320 | tf_op jit(solution)/shard_map/dynamic_slice | solution.py:810
  15.8 5.2 %collective-permute-done.1.refs_5_.refs_3_ = bf16[512,128]{1,0:T(8,128)(2,1)S(1)} collective-permute-done((bf16[512,128]{1,0:T(8,128)(2,1)}, bf16[512,128]{1,0:T(8,128)(2,1)S(1)}, u32[]{:S(2)}, u32[]{:S(2)}) %collective-permute-start.1) | collective-permute-done | bytes 131104 | tf_op jit(solution)/shard_map/ppermute | solution.py:734
  21.1 2.5 %collective-permute-start.11 = (bf16[3,208,128]{2,1,0:T(8,128)(2,1)S(1)}, bf16[3,208,128]{2,1,0:T(8,128)(2,1)S(1)}, u32[]{:S(2)}, u32[]{:S(2)}) collective-permute-start(bf16[3,208,128]{2,1,0:T(8,128)(2,1)S(1)} %pad_maximum_fusion.2.refs_2_), channel_id=1, source_target_pairs={{0,24},{1,25},{2,26},{3,27},{4,28},{5,29},{6,30},{7,31},{8,16},{9,... | collective-permute-start | bytes 479240 | tf_op jit(solution)/shard_map/ppermute | solution.py:734
  26.2 5.5 %keys.1 = (f32[512,2048]{1,0:T(8,128)S(1)}, bf16[512,2048]{1,0:T(8,128)(2,1)S(1)}, bf16[512,2048]{1,0:T(8,128)(2,1)S(1)}, f32[4,80,256]{2,1,0:T(8,128)S(1)}, bf16[4,80,256]{2,1,0:T(8,128)(2,1)S(1)}) custom-call(s32[4]{0:T(128)S(1)} %pad_add_fusion.refs_0_, bf16[2048,512]{1,0:T(8,128)(2,1)S(1)} %pad_maximum_fusion.refs_1_.refs_3_.refs_2_.refs_5_, ...), custom_call_target="tpu_custom_call" | custom-call | flops 1000 | bytes 12034064 | tf_op jit(solution)/shard_map/keys/pallas_call | solution.py:94
  33.7 1.6 %collective-permute-start.17 = (bf16[80,256]{1,0:T(8,128)(2,1)S(1)}, bf16[80,256]{1,0:T(8,128)(2,1)S(1)}, u32[]{:S(2)}, u32[]{:S(2)}) collective-permute-start(bf16[80,256]{1,0:T(8,128)(2,1)S(1)} %get-tuple-element.235), channel_id=1, source_target_pairs={{0,8},{1,9},{2,10},{3,11},{4,12},{5,13},{6,14},{7,15},{8,0},{9,1},... | collective-permute-start | bytes 122888 | tf_op jit(solution)/shard_map/ppermute | solution.py:734
  35.3 1.4 collective-permute-start.19
  37.3 1.8 %weights.1 = (bf16[512,512]{1,0:T(8,128)(2,1)S(1)}, bf16[512,512]{1,0:T(8,128)(2,1)S(1)}, bf16[512,512]{1,0:T(8,128)(2,1)S(1)}, f32[512,128]{1,0:T(8,128)S(1)}, ...) custom-call(s32[4]{0:T(128)S(1)} %pad_add_fusion.refs_0_, ...), custom_call_target="tpu_custom_call" | custom-call | flops 1000000 | bytes 4849680 | tf_op jit(solution)/shard_map/weights/pallas_call | solution.py:94
  39.0 1.9 %query.1 = (f32[512,2048]{1,0:T(8,128)S(1)}, bf16[512,2048]{1,0:T(8,128)(2,1)S(1)}) custom-call(s32[4]{0:T(128)S(1)} %pad_add_fusion.refs_0_, bf16[2048,512]{1,0:T(8,128)(2,1)S(1)} %pad_maximum_fusion.refs_1_.refs_3_.refs_2_.refs_5_, bf16[512,512]{1,0:T(8,128)(2,1)S(1)} %get-tuple-element.124.refs_2_), custom_call_target="tpu_custom_call" | custom-call | flops 1073741824 | bytes 8912912 | tf_op jit(solution)/shard_map/query/pallas_call | solution.py:94
  41.0 1.8 %collective-permute-start.22 = (bf16[80,256]{1,0:T(8,128)(2,1)S(1)}, bf16[80,256]{1,0:T(8,128)(2,1)S(1)}, u32[]{:S(2)}, u32[]{:S(2)}) collective-permute-start(bf16[80,256]{1,0:T(8,128)(2,1)S(1)} %fusion.12), channel_id=1, source_target_pairs={{0,3},{1,2},{2,1},{3,0},{4,7},{5,6},{6,5},{7,4},{8,11},{9,10},{10,... | collective-permute-start | bytes 122888 | tf_op jit(solution)/shard_map/ppermute | solution.py:734
  42.8 2.7 %collective-permute-start.20 = (bf16[80,256]{1,0:T(8,128)(2,1)S(1)}, bf16[80,256]{1,0:T(8,128)(2,1)S(1)}, u32[]{:S(2)}, u32[]{:S(2)}) collective-permute-start(bf16[80,256]{1,0:T(8,128)(2,1)S(1)} %fusion.12), channel_id=1, source_target_pairs={{0,1},{1,0},{2,3},{3,2},{4,5},{5,4},{6,7},{7,6},{8,9},{9,8},{10,11... | collective-permute-start | bytes 122888 | tf_op jit(solution)/shard_map/ppermute | solution.py:734
  45.5 1.9 %gate.1.refs_3_ = f32[512,2048]{1,0:T(8,128)S(1)} custom-call(s32[4]{0:T(128)S(1)} %pad_add_fusion.refs_0_, bf16[2048,512]{1,0:T(8,128)(2,1)S(1)} %pad_maximum_fusion.refs_1_.refs_3_.refs_2_.refs_5_, bf16[512,512]{1,0:T(8,128)(2,1)S(1)} %get-tuple-element.130.refs_2_), custom_call_target="tpu_custom_call" | custom-call | flops 1073741824 | bytes 6815760 | tf_op jit(solution)/shard_map/gate/pallas_call | solution.py:94
  47.4 0.8 collective-permute-done.21
  48.2 2.0 %collective-permute-start.26 = (bf16[80,256]{1,0:T(8,128)(2,1)S(1)}, bf16[80,256]{1,0:T(8,128)(2,1)S(1)}, u32[]{:S(2)}, u32[]{:S(2)}) collective-permute-start(bf16[80,256]{1,0:T(8,128)(2,1)S(1)} %add_convert_fusion.1.refs_7_.refs_5_), channel_id=1, source_target_pairs={{0,24},{1,25},{2,26},{3,27},{4,28},{5,29},{6,30},{7,31},{8,16},{9,... | collective-permute-start | bytes 122888 | tf_op jit(solution)/shard_map/ppermute | solution.py:734
  50.2 1.0 collective-permute-start.25
  51.8 1.8 %grad_prod.1.refs_4_ = f32[512,2048]{1,0:T(8,128)S(1)} custom-call(s32[4]{0:T(128)S(1)} %pad_add_fusion.refs_0_, bf16[2048,512]{1,0:T(8,128)(2,1)S(1)} %copy-done, bf16[512,512]{1,0:T(8,128)(2,1)S(1)} %get-tuple-element.135.refs_2_.refs_3_), custom_call_target="tpu_custom_call" | custom-call | flops 1073741824 | bytes 6815760 | tf_op jit(solution)/shard_map/grad_prod/pallas_call | solution.py:94
  54.2 1.0 collective-permute-done.24.refs_9_.refs_7_
  55.7 0.7 collective-permute-done.27.refs_10_.refs_8_
  57.0 9.6 %middle.1 = (bf16[512,2048]{1,0:T(8,128)(2,1)S(1)}, bf16[512,2048]{1,0:T(8,128)(2,1)S(1)}, bf16[512,2048]{1,0:T(8,128)(2,1)S(1)}, f32[16,2048]{1,0:T(8,128)S(1)}...) custom-call(s32[4]{0:T(128)S(1)} %pad_add_fusion.refs_0_, s32[1,2048]{1,0:T(1,128)S(1)} %bitcast.69, ...), custom_call_target="tpu_custom_call" | custom-call | flops 6442450944 | bytes 18259984 | tf_op jit(solution)/shard_map/middle/pallas_call | solution.py:94
  66.8 1.2 collective-permute-done.30
  68.7 1.9 %collective-permute-start.33 = (bf16[80,256]{1,0:T(8,128)(2,1)S(1)}, bf16[80,256]{1,0:T(8,128)(2,1)S(1)}, u32[]{:S(2)}, u32[]{:S(2)}) collective-permute-start(bf16[80,256]{1,0:T(8,128)(2,1)S(1)} %get-tuple-element.230), channel_id=1, source_target_pairs={{0,24},{1,25},{2,26},{3,27},{4,28},{5,29},{6,30},{7,31},{8,16},{9,... | collective-permute-start | bytes 122888 | tf_op jit(solution)/shard_map/ppermute | solution.py:734
  70.6 1.0 collective-permute-start.32
  71.6 2.9 %gate_back.1 = (f32[512,512]{1,0:T(8,128)S(1)}, f32[512,512]{1,0:T(8,128)S(1)}) custom-call(s32[4]{0:T(128)S(1)} %pad_add_fusion.refs_0_, bf16[512,2048]{1,0:T(8,128)(2,1)S(1)} %get-tuple-element.144.refs_1_.refs_4_, bf16[512,2048]{1,0:T(8,128)(2,1)S(1)} %get-tuple-element.145.refs_2_, bf16[2048,512]{1,0:T(8,128)(2,1)S(1)} %pad_maximum_fusion.refs_1_.refs_3_.refs_2_.refs_5_, ...), custom_call_target="tpu_custom_call" | custom-call | flops 2147483648 | bytes 10485776 | tf_op jit(solution)/shard_map/gate_back/pallas_call | solution.py:94
  74.6 2.0 %collective-permute-start.36 = (bf16[80,256]{1,0:T(8,128)(2,1)S(1)}, bf16[80,256]{1,0:T(8,128)(2,1)S(1)}, u32[]{:S(2)}, u32[]{:S(2)}) collective-permute-start(bf16[80,256]{1,0:T(8,128)(2,1)S(1)} %fusion.9), channel_id=1, source_target_pairs={{0,3},{1,2},{2,1},{3,0},{4,7},{5,6},{6,5},{7,4},{8,11},{9,10},{10,... | collective-permute-start | bytes 122888 | tf_op jit(solution)/shard_map/ppermute | solution.py:734
  76.6 0.9 collective-permute-start.35
  77.6 1.5 %collective-permute-start.34 = (bf16[80,256]{1,0:T(8,128)(2,1)S(1)}, bf16[80,256]{1,0:T(8,128)(2,1)S(1)}, u32[]{:S(2)}, u32[]{:S(2)}) collective-permute-start(bf16[80,256]{1,0:T(8,128)(2,1)S(1)} %fusion.9), channel_id=1, source_target_pairs={{0,1},{1,0},{2,3},{3,2},{4,5},{5,4},{6,7},{7,6},{8,9},{9,8},{10,11... | collective-permute-start | bytes 122888 | tf_op jit(solution)/shard_map/ppermute | solution.py:734
  79.1 3.1 %query_back.1.refs_1_ = bf16[512,2048]{1,0:T(8,128)(2,1)S(1)} custom-call(s32[4]{0:T(128)S(1)} %pad_add_fusion.refs_0_, s32[1,2048]{1,0:T(1,128)S(1)} %bitcast.70, bf16[512,2048]{1,0:T(8,128)(2,1)S(1)} %get-tuple-element.152.refs_2_, f32[16,2048]{1,0:T(8,128)S(1)} %get-tuple-element.153.refs_3_, f32[512,2048]{1,0:T(8,128)S(1)} %get-tuple-element.154.refs_4_, ...), custom_call_target="tpu_custom_call" | custom-call | flops 2147483648 | bytes 8855568 | tf_op jit(solution)/shard_map/query_back/pallas_call | solution.py:94
  82.3 1.4 collective-permute-start.40
  83.7 1.1 collective-permute-start.39
  84.8 1.1 collective-permute-start.38
  85.8 1.8 %grad_query.1.refs_1_ = f32[512,512]{1,0:T(8,128)S(1)} custom-call(s32[4]{0:T(128)S(1)} %pad_add_fusion.refs_0_, bf16[512,2048]{1,0:T(8,128)(2,1)S(1)} %query_back.1.refs_1_, bf16[2048,512]{1,0:T(8,128)(2,1)S(1)} %pad_maximum_fusion.refs_1_.refs_3_.refs_2_.refs_5_), custom_call_target="tpu_custom_call" | custom-call | flops 1073741824 | bytes 5242896 | tf_op jit(solution)/shard_map/grad_query/pallas_call | solution.py:94
  87.6 1.2 early.1
  90.0 1.0 collective-permute-done.44
  91.3 1.0 collective-permute-start.45
  92.3 1.0 collective-permute-start.46
  93.3 1.5 %collective-permute-start.47 = (bf16[4,160,128]{2,1,0:T(8,128)(2,1)S(1)}, bf16[4,160,128]{2,1,0:T(8,128)(2,1)S(1)}, u32[]{:S(2)}, u32[]{:S(2)}) collective-permute-start(bf16[4,160,128]{2,1,0:T(8,128)(2,1)S(1)} %get-tuple-element.169), channel_id=1, source_target_pairs={{0,24},{1,25},{2,26},{3,27},{4,28},{5,29},{6,30},{7,31},{8,16},{9,... | collective-permute-start | bytes 491528 | tf_op jit(solution)/shard_map/ppermute | solution.py:734
  94.9 7.1 %key_back.1 = (bf16[512,2048]{1,0:T(8,128)(2,1)S(1)}, bf16[512,2048]{1,0:T(8,128)(2,1)S(1)}, f32[8,512]{1,0:T(8,128)S(1)}, f32[4,4,160,128]{3,2,1,0:T(8,128)S(1)}, bf16[4,4,160,128]{3,2,1,0:T(8,128)(2,1)S(1)}) custom-call(s32[4]{0:T(128)S(1)} %pad_add_fusion.refs_0_, s32[1,2048]{1,0:T(1,128)S(1)} %bitcast.71, f32[512,2048]{1,0:T(8,128)S(1)} %copy-done.16, ...), custom_call_target="tpu_custom_call" | custom-call | flops 6442450944 | bytes 18046992 | tf_op jit(solution)/shard_map/key_back/pallas_call | solution.py:94
  102.1 0.8 key_weights.1.refs_6_
  102.9 1.3 collective-permute-done.48
  104.5 1.0 collective-permute-start.49
  105.5 1.0 collective-permute-start.50
  106.5 1.6 %collective-permute-start.51 = (bf16[4,160,128]{2,1,0:T(8,128)(2,1)S(1)}, bf16[4,160,128]{2,1,0:T(8,128)(2,1)S(1)}, u32[]{:S(2)}, u32[]{:S(2)}) collective-permute-start(bf16[4,160,128]{2,1,0:T(8,128)(2,1)S(1)} %get-tuple-element.173), channel_id=1, source_target_pairs={{0,24},{1,25},{2,26},{3,27},{4,28},{5,29},{6,30},{7,31},{8,16},{9,... | collective-permute-start | bytes 491528 | tf_op jit(solution)/shard_map/ppermute | solution.py:734
  108.0 6.6 %inputs.1 = f32[2048,512]{1,0:T(8,128)} custom-call(s32[4]{0:T(128)S(1)} %pad_add_fusion.refs_0_, bf16[512,2048]{1,0:T(8,128)(2,1)S(1)} %query_back.1.refs_1_, bf16[512,2048]{1,0:T(8,128)(2,1)S(1)} %get-tuple-element.175.refs_2_, bf16[512,2048]{1,0:T(8,128)(2,1)S(1)} %get-tuple-element.176.refs_3_, bf16[512,2048]{1,0:T(8,128)(2,1)S(1)} %get-tuple-element.144.refs_1_.refs_4_, ...), custom_call_target="tpu_custom_call" | custom-call | flops 4294967296 | bytes 16777232 | tf_op jit(solution)/shard_map/inputs/pallas_call | solution.py:94
  115.3 0.9 collective-permute-start.52
  116.2 1.6 %collective-permute-start.53 = (bf16[320,128]{1,0:T(8,128)(2,1)S(1)}, bf16[320,128]{1,0:T(8,128)(2,1)S(1)}, u32[]{:S(2)}, u32[]{:S(2)}) collective-permute-start(bf16[320,128]{1,0:T(8,128)(2,1)S(1)} %get-tuple-element.184), channel_id=1, source_target_pairs={{0,2},{1,3},{2,0},{3,1},{4,6},{5,7},{6,4},{7,5},{8,10},{9,11},{10,... | collective-permute-start | bytes 245768 | tf_op jit(solution)/shard_map/ppermute | solution.py:734
  117.8 1.9 %collective-permute-start.54 = (bf16[320,128]{1,0:T(8,128)(2,1)S(1)}, bf16[320,128]{1,0:T(8,128)(2,1)S(1)}, u32[]{:S(2)}, u32[]{:S(2)}) collective-permute-start(bf16[320,128]{1,0:T(8,128)(2,1)S(1)} %get-tuple-element.185), channel_id=1, source_target_pairs={{0,3},{1,2},{2,1},{3,0},{4,7},{5,6},{6,5},{7,4},{8,11},{9,10},{10,... | collective-permute-start | bytes 245768 | tf_op jit(solution)/shard_map/ppermute | solution.py:734
  119.8 3.5 %output.1 = f32[2048,512]{1,0:T(8,128)} custom-call(s32[4]{0:T(128)S(1)} %pad_add_fusion.refs_0_, bf16[2048,512]{1,0:T(8,128)(2,1)S(1)} %copy-done.1, bf16[512,2048]{1,0:T(8,128)(2,1)S(1)} %get-tuple-element.145.refs_2_, bf16[512,512]{1,0:T(8,128)(2,1)S(1)} %get-tuple-element.135.refs_2_.refs_3_), custom_call_target="tpu_custom_call" | custom-call | flops 1073741824 | bytes 8912912 | tf_op jit(solution)/shard_map/output/pallas_call | solution.py:94
  123.3 1.4 collective-permute-done.53.refs_2_
  124.7 1.5 %collective-permute-start.60 = (bf16[320,128]{1,0:T(8,128)(2,1)S(1)}, bf16[320,128]{1,0:T(8,128)(2,1)S(1)}, u32[]{:S(2)}, u32[]{:S(2)}) collective-permute-start(bf16[320,128]{1,0:T(8,128)(2,1)S(1)} %finish.1.refs_0_.refs_1_), channel_id=1, source_target_pairs={{0,24},{1,25},{2,26},{3,27},{4,28},{5,29},{6,30},{7,31},{8,16},{9,... | collective-permute-start | bytes 245768 | tf_op jit(solution)/shard_map/ppermute | solution.py:734
  126.2 0.9 collective-permute-start.58
  127.1 1.1 collective-permute-start.56
  128.3 1.9 %collective-permute-done.60.refs_6_.refs_7_ = bf16[320,128]{1,0:T(8,128)(2,1)S(1)} collective-permute-done((bf16[320,128]{1,0:T(8,128)(2,1)S(1)}, bf16[320,128]{1,0:T(8,128)(2,1)S(1)}, u32[]{:S(2)}, u32[]{:S(2)}) %collective-permute-start.60) | collective-permute-done | bytes 81952 | tf_op jit(solution)/shard_map/ppermute | solution.py:734
  130.2 0.8 collective-permute-done.58.refs_4_.refs_5_
  131.6 0.7 collective-permute-done.59.refs_5_.refs_6_
  133.1 1.9 %collective-permute-start.64 = (f32[8,128]{1,0:T(8,128)S(1)}, f32[8,128]{1,0:T(8,128)S(1)}, u32[]{:S(2)}, u32[]{:S(2)}) collective-permute-start(f32[8,128]{1,0:T(8,128)S(1)} %squares.1.refs_1_), channel_id=1, source_target_pairs={{0,3},{1,2},{2,1},{3,0},{4,7},{5,6},{6,5},{7,4},{8,11},{9,10},{10,... | collective-permute-start | bytes 12296 | tf_op jit(solution)/shard_map/ppermute | solution.py:734
  134.9 1.0 collective-permute-start.63
  136.0 1.5 %collective-permute-start.62 = (f32[8,128]{1,0:T(8,128)S(1)}, f32[8,128]{1,0:T(8,128)S(1)}, u32[]{:S(2)}, u32[]{:S(2)}) collective-permute-start(f32[8,128]{1,0:T(8,128)S(1)} %squares.1.refs_1_), channel_id=1, source_target_pairs={{0,1},{1,0},{2,3},{3,2},{4,5},{5,4},{6,7},{7,6},{8,9},{9,8},{10,11... | collective-permute-start | bytes 12296 | tf_op jit(solution)/shard_map/ppermute | solution.py:734
  137.5 1.0 assemble.1
  138.5 1.0 collective-permute-done.63.refs_3_
  139.7 3.8 %update.1 = (f32[1,1]{1,0:T(1,128)}, f32[128,2048]{1,0:T(8,128)}, f32[128,2048]{1,0:T(8,128)}, f32[128,2048]{1,0:T(8,128)}, bf16[128,2048]{1,0:T(8,128)(2,1)}, /...) custom-call(s32[4]{0:T(128)S(1)} %pad_add_fusion.refs_0_, ...), custom_call_target="tpu_custom_call" | custom-call | flops 1000000 | bytes 9870356 | tf_op jit(solution)/shard_map/update/pallas_call | solution.py:94
  (139 shorter events, 12.8 us)
Async XLA Ops:
  3.1 12.1 %collective-permute-start.8 = (bf16[208,128]{1,0:T(8,128)(2,1)}, bf16[208,128]{1,0:T(8,128)(2,1)S(1)}, u32[]{:S(2)}, u32[]{:S(2)}) collective-permute-start(bf16[208,128]{1,0:T(8,128)(2,1)} %get-tuple-element.120), channel_id=1, source_target_pairs={{0,3},{1,2},{2,1},{3,0},{4,7},{5,6},{6,5},{7,4},{8,11},{9,10},{10,... | collective-permute-start | bytes 159752 | tf_op jit(solution)/shard_map/ppermute | solution.py:734
  8.2 12.9 %collective-permute-start.7 = (bf16[208,128]{1,0:T(8,128)(2,1)}, bf16[208,128]{1,0:T(8,128)(2,1)S(1)}, u32[]{:S(2)}, u32[]{:S(2)}) collective-permute-start(bf16[208,128]{1,0:T(8,128)(2,1)} %get-tuple-element.120), channel_id=1, source_target_pairs={{0,2},{1,3},{2,0},{3,1},{4,6},{5,7},{6,4},{7,5},{8,10},{9,11},{10,... | collective-permute-start | bytes 159752 | tf_op jit(solution)/shard_map/ppermute | solution.py:734
  8.2 12.9 %collective-permute-start.6 = (bf16[208,128]{1,0:T(8,128)(2,1)}, bf16[208,128]{1,0:T(8,128)(2,1)S(1)}, u32[]{:S(2)}, u32[]{:S(2)}) collective-permute-start(bf16[208,128]{1,0:T(8,128)(2,1)} %get-tuple-element.120), channel_id=1, source_target_pairs={{0,1},{1,0},{2,3},{3,2},{4,5},{5,4},{6,7},{7,6},{8,9},{9,8},{10,11... | collective-permute-start | bytes 159752 | tf_op jit(solution)/shard_map/ppermute | solution.py:734
  8.8 12.2 %collective-permute-start.1 = (bf16[512,128]{1,0:T(8,128)(2,1)}, bf16[512,128]{1,0:T(8,128)(2,1)S(1)}, u32[]{:S(2)}, u32[]{:S(2)}) collective-permute-start(bf16[512,128]{1,0:T(8,128)(2,1)} %get-tuple-element.113.refs_3_.refs_1_), channel_id=1, source_target_pairs={{0,2},{1,3},{2,0},{3,1},{4,6},{5,7},{6,4},{7,5},{8,10},{9,11},{10,... | collective-permute-start | bytes 393224 | tf_op jit(solution)/shard_map/ppermute | solution.py:734
  11.1 13.0 %collective-permute-start = (bf16[512,128]{1,0:T(8,128)(2,1)}, bf16[512,128]{1,0:T(8,128)(2,1)S(1)}, u32[]{:S(2)}, u32[]{:S(2)}) collective-permute-start(bf16[512,128]{1,0:T(8,128)(2,1)} %get-tuple-element.113.refs_3_.refs_1_), channel_id=1, source_target_pairs={{0,1},{1,0},{2,3},{3,2},{4,5},{5,4},{6,7},{7,6},{8,9},{9,8},{10,11... | collective-permute-start | bytes 393224 | tf_op jit(solution)/shard_map/ppermute | solution.py:734
  15.8 8.9 %collective-permute-start.2 = (bf16[512,128]{1,0:T(8,128)(2,1)S(1)}, bf16[512,128]{1,0:T(8,128)(2,1)S(1)}, u32[]{:S(2)}, u32[]{:S(2)}) collective-permute-start(bf16[512,128]{1,0:T(8,128)(2,1)S(1)} %copy-done.6), channel_id=1, source_target_pairs={{0,3},{1,2},{2,1},{3,0},{4,7},{5,6},{6,5},{7,4},{8,11},{9,10},{10,... | collective-permute-start | bytes 393224 | tf_op jit(solution)/shard_map/ppermute | solution.py:734
  21.1 3.6 %collective-permute-start.4 = (bf16[512,128]{1,0:T(8,128)(2,1)S(1)}, bf16[512,128]{1,0:T(8,128)(2,1)S(1)}, u32[]{:S(2)}, u32[]{:S(2)}) collective-permute-start(bf16[512,128]{1,0:T(8,128)(2,1)S(1)} %collective-permute-done.1.refs_5_.refs_3_), channel_id=1, source_target_pairs={{0,4},{1,5},{2,6},{3,7},{4,0},{5,1},{6,2},{7,3},{8,12},{9,13},{10,... | collective-permute-start | bytes 393224 | tf_op jit(solution)/shard_map/ppermute | solution.py:734
  21.1 10.6 %collective-permute-start.11 = (bf16[3,208,128]{2,1,0:T(8,128)(2,1)S(1)}, bf16[3,208,128]{2,1,0:T(8,128)(2,1)S(1)}, u32[]{:S(2)}, u32[]{:S(2)}) collective-permute-start(bf16[3,208,128]{2,1,0:T(8,128)(2,1)S(1)} %pad_maximum_fusion.2.refs_2_), channel_id=1, source_target_pairs={{0,24},{1,25},{2,26},{3,27},{4,28},{5,29},{6,30},{7,31},{8,16},{9,... | collective-permute-start | bytes 479240 | tf_op jit(solution)/shard_map/ppermute | solution.py:734
  23.6 8.5 %collective-permute-start.10 = (bf16[3,208,128]{2,1,0:T(8,128)(2,1)S(1)}, bf16[3,208,128]{2,1,0:T(8,128)(2,1)}, u32[]{:S(2)}, u32[]{:S(2)}) collective-permute-start(bf16[3,208,128]{2,1,0:T(8,128)(2,1)S(1)} %pad_maximum_fusion.2.refs_2_), channel_id=1, source_target_pairs={{0,16},{1,17},{2,18},{3,19},{4,20},{5,21},{6,22},{7,23},{8,24},{9,... | collective-permute-start | bytes 479240 | tf_op jit(solution)/shard_map/ppermute | solution.py:734
  24.1 8.1 %collective-permute-start.9 = (bf16[3,208,128]{2,1,0:T(8,128)(2,1)S(1)}, bf16[3,208,128]{2,1,0:T(8,128)(2,1)}, u32[]{:S(2)}, u32[]{:S(2)}) collective-permute-start(bf16[3,208,128]{2,1,0:T(8,128)(2,1)S(1)} %pad_maximum_fusion.2.refs_2_), channel_id=1, source_target_pairs={{0,8},{1,9},{2,10},{3,11},{4,12},{5,13},{6,14},{7,15},{8,0},{9,1},... | collective-permute-start | bytes 479240 | tf_op jit(solution)/shard_map/ppermute | solution.py:734
  24.7 1.3 collective-permute-start.3
  24.7 1.5 %collective-permute-start.5 = (bf16[512,128]{1,0:T(8,128)(2,1)S(1)}, bf16[512,128]{1,0:T(8,128)(2,1)S(1)}, u32[]{:S(2)}, u32[]{:S(2)}) collective-permute-start(bf16[512,128]{1,0:T(8,128)(2,1)S(1)} %collective-permute-done.2.refs_6_.refs_4_), channel_id=1, source_target_pairs={{0,4},{1,5},{2,6},{3,7},{4,0},{5,1},{6,2},{7,3},{8,12},{9,13},{10,... | collective-permute-start | bytes 393224 | tf_op jit(solution)/shard_map/ppermute | solution.py:734
  32.2 1.4 collective-permute-start.12
  32.2 3.0 %collective-permute-start.13 = (bf16[3,208,128]{2,1,0:T(8,128)(2,1)S(1)}, bf16[3,208,128]{2,1,0:T(8,128)(2,1)S(1)}, u32[]{:S(2)}, u32[]{:S(2)}) collective-permute-start(bf16[3,208,128]{2,1,0:T(8,128)(2,1)S(1)} %pad_maximum_fusion.2.refs_2_), channel_id=1, source_target_pairs={{0,4},{1,5},{2,6},{3,7},{4,0},{5,1},{6,2},{7,3},{8,12},{9,13},{10,... | collective-permute-start | bytes 479240 | tf_op jit(solution)/shard_map/ppermute | solution.py:734
  32.7 3.9 %collective-permute-start.16 = (bf16[3,208,128]{2,1,0:T(8,128)(2,1)S(1)}, bf16[3,208,128]{2,1,0:T(8,128)(2,1)S(1)}, u32[]{:S(2)}, u32[]{:S(2)}) collective-permute-start(bf16[3,208,128]{2,1,0:T(8,128)(2,1)S(1)} %collective-permute-done.11.refs_8_), channel_id=1, source_target_pairs={{0,4},{1,5},{2,6},{3,7},{4,0},{5,1},{6,2},{7,3},{8,12},{9,13},{10,... | collective-permute-start | bytes 479240 | tf_op jit(solution)/shard_map/ppermute | solution.py:734
  32.7 4.5 %collective-permute-start.15 = (bf16[3,208,128]{2,1,0:T(8,128)(2,1)}, bf16[3,208,128]{2,1,0:T(8,128)(2,1)S(1)}, u32[]{:S(2)}, u32[]{:S(2)}) collective-permute-start(bf16[3,208,128]{2,1,0:T(8,128)(2,1)} %collective-permute-done.10.refs_6_), channel_id=1, source_target_pairs={{0,4},{1,5},{2,6},{3,7},{4,0},{5,1},{6,2},{7,3},{8,12},{9,13},{10,... | collective-permute-start | bytes 479240 | tf_op jit(solution)/shard_map/ppermute | solution.py:734
  33.3 4.0 %collective-permute-start.14 = (bf16[3,208,128]{2,1,0:T(8,128)(2,1)}, bf16[3,208,128]{2,1,0:T(8,128)(2,1)S(1)}, u32[]{:S(2)}, u32[]{:S(2)}) collective-permute-start(bf16[3,208,128]{2,1,0:T(8,128)(2,1)} %collective-permute-done.9.refs_4_), channel_id=1, source_target_pairs={{0,4},{1,5},{2,6},{3,7},{4,0},{5,1},{6,2},{7,3},{8,12},{9,13},{10,... | collective-permute-start | bytes 479240 | tf_op jit(solution)/shard_map/ppermute | solution.py:734
  33.7 7.3 %collective-permute-start.17 = (bf16[80,256]{1,0:T(8,128)(2,1)S(1)}, bf16[80,256]{1,0:T(8,128)(2,1)S(1)}, u32[]{:S(2)}, u32[]{:S(2)}) collective-permute-start(bf16[80,256]{1,0:T(8,128)(2,1)S(1)} %get-tuple-element.235), channel_id=1, source_target_pairs={{0,8},{1,9},{2,10},{3,11},{4,12},{5,13},{6,14},{7,15},{8,0},{9,1},... | collective-permute-start | bytes 122888 | tf_op jit(solution)/shard_map/ppermute | solution.py:734
  35.3 5.7 %collective-permute-start.19 = (bf16[80,256]{1,0:T(8,128)(2,1)S(1)}, bf16[80,256]{1,0:T(8,128)(2,1)S(1)}, u32[]{:S(2)}, u32[]{:S(2)}) collective-permute-start(bf16[80,256]{1,0:T(8,128)(2,1)S(1)} %get-tuple-element.233), channel_id=1, source_target_pairs={{0,24},{1,25},{2,26},{3,27},{4,28},{5,29},{6,30},{7,31},{8,16},{9,... | collective-permute-start | bytes 122888 | tf_op jit(solution)/shard_map/ppermute | solution.py:734
  36.7 4.3 %collective-permute-start.18 = (bf16[80,256]{1,0:T(8,128)(2,1)S(1)}, bf16[80,256]{1,0:T(8,128)(2,1)S(1)}, u32[]{:S(2)}, u32[]{:S(2)}) collective-permute-start(bf16[80,256]{1,0:T(8,128)(2,1)S(1)} %get-tuple-element.234), channel_id=1, source_target_pairs={{0,16},{1,17},{2,18},{3,19},{4,20},{5,21},{6,22},{7,23},{8,24},{9,... | collective-permute-start | bytes 122888 | tf_op jit(solution)/shard_map/ppermute | solution.py:734
  41.0 6.3 %collective-permute-start.22 = (bf16[80,256]{1,0:T(8,128)(2,1)S(1)}, bf16[80,256]{1,0:T(8,128)(2,1)S(1)}, u32[]{:S(2)}, u32[]{:S(2)}) collective-permute-start(bf16[80,256]{1,0:T(8,128)(2,1)S(1)} %fusion.12), channel_id=1, source_target_pairs={{0,3},{1,2},{2,1},{3,0},{4,7},{5,6},{6,5},{7,4},{8,11},{9,10},{10,... | collective-permute-start | bytes 122888 | tf_op jit(solution)/shard_map/ppermute | solution.py:734
  42.8 5.3 %collective-permute-start.21 = (bf16[80,256]{1,0:T(8,128)(2,1)S(1)}, bf16[80,256]{1,0:T(8,128)(2,1)S(1)}, u32[]{:S(2)}, u32[]{:S(2)}) collective-permute-start(bf16[80,256]{1,0:T(8,128)(2,1)S(1)} %fusion.12), channel_id=1, source_target_pairs={{0,2},{1,3},{2,0},{3,1},{4,6},{5,7},{6,4},{7,5},{8,10},{9,11},{10,... | collective-permute-start | bytes 122888 | tf_op jit(solution)/shard_map/ppermute | solution.py:734
  42.8 5.3 %collective-permute-start.20 = (bf16[80,256]{1,0:T(8,128)(2,1)S(1)}, bf16[80,256]{1,0:T(8,128)(2,1)S(1)}, u32[]{:S(2)}, u32[]{:S(2)}) collective-permute-start(bf16[80,256]{1,0:T(8,128)(2,1)S(1)} %fusion.12), channel_id=1, source_target_pairs={{0,1},{1,0},{2,3},{3,2},{4,5},{5,4},{6,7},{7,6},{8,9},{9,8},{10,11... | collective-permute-start | bytes 122888 | tf_op jit(solution)/shard_map/ppermute | solution.py:734
  48.2 5.4 %collective-permute-start.26 = (bf16[80,256]{1,0:T(8,128)(2,1)S(1)}, bf16[80,256]{1,0:T(8,128)(2,1)S(1)}, u32[]{:S(2)}, u32[]{:S(2)}) collective-permute-start(bf16[80,256]{1,0:T(8,128)(2,1)S(1)} %add_convert_fusion.1.refs_7_.refs_5_), channel_id=1, source_target_pairs={{0,24},{1,25},{2,26},{3,27},{4,28},{5,29},{6,30},{7,31},{8,16},{9,... | collective-permute-start | bytes 122888 | tf_op jit(solution)/shard_map/ppermute | solution.py:734
  50.2 4.0 %collective-permute-start.25 = (bf16[80,256]{1,0:T(8,128)(2,1)S(1)}, bf16[80,256]{1,0:T(8,128)(2,1)S(1)}, u32[]{:S(2)}, u32[]{:S(2)}) collective-permute-start(bf16[80,256]{1,0:T(8,128)(2,1)S(1)} %add_convert_fusion.1.refs_7_.refs_5_), channel_id=1, source_target_pairs={{0,16},{1,17},{2,18},{3,19},{4,20},{5,21},{6,22},{7,23},{8,24},{9,... | collective-permute-start | bytes 122888 | tf_op jit(solution)/shard_map/ppermute | solution.py:734
  51.2 4.0 %collective-permute-start.24 = (bf16[80,256]{1,0:T(8,128)(2,1)S(1)}, bf16[80,256]{1,0:T(8,128)(2,1)S(1)}, u32[]{:S(2)}, u32[]{:S(2)}) collective-permute-start(bf16[80,256]{1,0:T(8,128)(2,1)S(1)} %add_convert_fusion.1.refs_7_.refs_5_), channel_id=1, source_target_pairs={{0,8},{1,9},{2,10},{3,11},{4,12},{5,13},{6,14},{7,15},{8,0},{9,1},... | collective-permute-start | bytes 122888 | tf_op jit(solution)/shard_map/ppermute | solution.py:734
  51.7 4.0 %collective-permute-start.23 = (bf16[80,256]{1,0:T(8,128)(2,1)S(1)}, bf16[80,256]{1,0:T(8,128)(2,1)S(1)}, u32[]{:S(2)}, u32[]{:S(2)}) collective-permute-start(bf16[80,256]{1,0:T(8,128)(2,1)S(1)} %add_convert_fusion.1.refs_7_.refs_5_), channel_id=1, source_target_pairs={{0,4},{1,5},{2,6},{3,7},{4,0},{5,1},{6,2},{7,3},{8,12},{9,13},{10,... | collective-permute-start | bytes 122888 | tf_op jit(solution)/shard_map/ppermute | solution.py:734
  55.2 1.4 collective-permute-start.28
  55.7 1.2 collective-permute-start.29
  66.5 1.5 %collective-permute-start.30 = (bf16[4,80,256]{2,1,0:T(8,128)(2,1)S(1)}, bf16[4,80,256]{2,1,0:T(8,128)(2,1)S(1)}, u32[]{:S(2)}, u32[]{:S(2)}) collective-permute-start(bf16[4,80,256]{2,1,0:T(8,128)(2,1)S(1)} %get-tuple-element.142), channel_id=1, source_target_pairs={{0,4},{1,5},{2,6},{3,7},{4,0},{5,1},{6,2},{7,3},{8,12},{9,13},{10,... | collective-permute-start | bytes 491528 | tf_op jit(solution)/shard_map/ppermute | solution.py:734
  68.0 6.5 %collective-permute-start.31 = (bf16[80,256]{1,0:T(8,128)(2,1)S(1)}, bf16[80,256]{1,0:T(8,128)(2,1)S(1)}, u32[]{:S(2)}, u32[]{:S(2)}) collective-permute-start(bf16[80,256]{1,0:T(8,128)(2,1)S(1)} %get-tuple-element.232), channel_id=1, source_target_pairs={{0,8},{1,9},{2,10},{3,11},{4,12},{5,13},{6,14},{7,15},{8,0},{9,1},... | collective-permute-start | bytes 122888 | tf_op jit(solution)/shard_map/ppermute | solution.py:734
  68.7 5.8 %collective-permute-start.33 = (bf16[80,256]{1,0:T(8,128)(2,1)S(1)}, bf16[80,256]{1,0:T(8,128)(2,1)S(1)}, u32[]{:S(2)}, u32[]{:S(2)}) collective-permute-start(bf16[80,256]{1,0:T(8,128)(2,1)S(1)} %get-tuple-element.230), channel_id=1, source_target_pairs={{0,24},{1,25},{2,26},{3,27},{4,28},{5,29},{6,30},{7,31},{8,16},{9,... | collective-permute-start | bytes 122888 | tf_op jit(solution)/shard_map/ppermute | solution.py:734
  70.6 4.0 %collective-permute-start.32 = (bf16[80,256]{1,0:T(8,128)(2,1)S(1)}, bf16[80,256]{1,0:T(8,128)(2,1)S(1)}, u32[]{:S(2)}, u32[]{:S(2)}) collective-permute-start(bf16[80,256]{1,0:T(8,128)(2,1)S(1)} %get-tuple-element.231), channel_id=1, source_target_pairs={{0,16},{1,17},{2,18},{3,19},{4,20},{5,21},{6,22},{7,23},{8,24},{9,... | collective-permute-start | bytes 122888 | tf_op jit(solution)/shard_map/ppermute | solution.py:734
  74.6 7.6 %collective-permute-start.36 = (bf16[80,256]{1,0:T(8,128)(2,1)S(1)}, bf16[80,256]{1,0:T(8,128)(2,1)S(1)}, u32[]{:S(2)}, u32[]{:S(2)}) collective-permute-start(bf16[80,256]{1,0:T(8,128)(2,1)S(1)} %fusion.9), channel_id=1, source_target_pairs={{0,3},{1,2},{2,1},{3,0},{4,7},{5,6},{6,5},{7,4},{8,11},{9,10},{10,... | collective-permute-start | bytes 122888 | tf_op jit(solution)/shard_map/ppermute | solution.py:734
  76.6 5.6 %collective-permute-start.35 = (bf16[80,256]{1,0:T(8,128)(2,1)S(1)}, bf16[80,256]{1,0:T(8,128)(2,1)S(1)}, u32[]{:S(2)}, u32[]{:S(2)}) collective-permute-start(bf16[80,256]{1,0:T(8,128)(2,1)S(1)} %fusion.9), channel_id=1, source_target_pairs={{0,2},{1,3},{2,0},{3,1},{4,6},{5,7},{6,4},{7,5},{8,10},{9,11},{10,... | collective-permute-start | bytes 122888 | tf_op jit(solution)/shard_map/ppermute | solution.py:734
  77.6 4.7 %collective-permute-start.34 = (bf16[80,256]{1,0:T(8,128)(2,1)S(1)}, bf16[80,256]{1,0:T(8,128)(2,1)S(1)}, u32[]{:S(2)}, u32[]{:S(2)}) collective-permute-start(bf16[80,256]{1,0:T(8,128)(2,1)S(1)} %fusion.9), channel_id=1, source_target_pairs={{0,1},{1,0},{2,3},{3,2},{4,5},{5,4},{6,7},{7,6},{8,9},{9,8},{10,11... | collective-permute-start | bytes 122888 | tf_op jit(solution)/shard_map/ppermute | solution.py:734
  82.3 6.6 %collective-permute-start.40 = (bf16[80,256]{1,0:T(8,128)(2,1)S(1)}, bf16[80,256]{1,0:T(8,128)(2,1)S(1)}, u32[]{:S(2)}, u32[]{:S(2)}) collective-permute-start(bf16[80,256]{1,0:T(8,128)(2,1)S(1)} %add_convert_fusion.refs_7_), channel_id=1, source_target_pairs={{0,24},{1,25},{2,26},{3,27},{4,28},{5,29},{6,30},{7,31},{8,16},{9,... | collective-permute-start | bytes 122888 | tf_op jit(solution)/shard_map/ppermute | solution.py:734
  83.7 5.2 %collective-permute-start.39 = (bf16[80,256]{1,0:T(8,128)(2,1)S(1)}, bf16[80,256]{1,0:T(8,128)(2,1)S(1)}, u32[]{:S(2)}, u32[]{:S(2)}) collective-permute-start(bf16[80,256]{1,0:T(8,128)(2,1)S(1)} %add_convert_fusion.refs_7_), channel_id=1, source_target_pairs={{0,16},{1,17},{2,18},{3,19},{4,20},{5,21},{6,22},{7,23},{8,24},{9,... | collective-permute-start | bytes 122888 | tf_op jit(solution)/shard_map/ppermute | solution.py:734
  84.8 4.1 %collective-permute-start.38 = (bf16[80,256]{1,0:T(8,128)(2,1)S(1)}, bf16[80,256]{1,0:T(8,128)(2,1)S(1)}, u32[]{:S(2)}, u32[]{:S(2)}) collective-permute-start(bf16[80,256]{1,0:T(8,128)(2,1)S(1)} %add_convert_fusion.refs_7_), channel_id=1, source_target_pairs={{0,8},{1,9},{2,10},{3,11},{4,12},{5,13},{6,14},{7,15},{8,0},{9,1},... | collective-permute-start | bytes 122888 | tf_op jit(solution)/shard_map/ppermute | solution.py:734
  88.9 2.2 %collective-permute-start.44 = (bf16[4,4,160,128]{3,2,1,0:T(8,128)(2,1)S(1)}, bf16[4,4,160,128]{3,2,1,0:T(8,128)(2,1)S(1)}, u32[]{:S(2)}, u32[]{:S(2)}) collective-permute-start(bf16[4,4,160,128]{3,2,1,0:T(8,128)(2,1)S(1)} %get-tuple-element.166), channel_id=1, source_target_pairs={{0,4},{1,5},{2,6},{3,7},{4,0},{5,1},{6,2},{7,3},{8,12},{9,13},{10,... | collective-permute-start | bytes 1966088 | tf_op jit(solution)/shard_map/ppermute | solution.py:734
  88.9 3.4 %collective-permute-start.37 = (bf16[80,256]{1,0:T(8,128)(2,1)S(1)}, bf16[80,256]{1,0:T(8,128)(2,1)S(1)}, u32[]{:S(2)}, u32[]{:S(2)}) collective-permute-start(bf16[80,256]{1,0:T(8,128)(2,1)S(1)} %add_convert_fusion.refs_7_), channel_id=1, source_target_pairs={{0,4},{1,5},{2,6},{3,7},{4,0},{5,1},{6,2},{7,3},{8,12},{9,13},{10,... | collective-permute-start | bytes 122888 | tf_op jit(solution)/shard_map/ppermute | solution.py:734
  89.4 3.9 %collective-permute-start.41 = (bf16[80,256]{1,0:T(8,128)(2,1)S(1)}, bf16[80,256]{1,0:T(8,128)(2,1)S(1)}, u32[]{:S(2)}, u32[]{:S(2)}) collective-permute-start(bf16[80,256]{1,0:T(8,128)(2,1)S(1)} %collective-permute-done.38.refs_9_), channel_id=1, source_target_pairs={{0,4},{1,5},{2,6},{3,7},{4,0},{5,1},{6,2},{7,3},{8,12},{9,13},{10,... | collective-permute-start | bytes 122888 | tf_op jit(solution)/shard_map/ppermute | solution.py:734
  89.5 5.4 %collective-permute-start.42 = (bf16[80,256]{1,0:T(8,128)(2,1)S(1)}, bf16[80,256]{1,0:T(8,128)(2,1)S(1)}, u32[]{:S(2)}, u32[]{:S(2)}) collective-permute-start(bf16[80,256]{1,0:T(8,128)(2,1)S(1)} %collective-permute-done.39.refs_11_), channel_id=1, source_target_pairs={{0,4},{1,5},{2,6},{3,7},{4,0},{5,1},{6,2},{7,3},{8,12},{9,13},{10,... | collective-permute-start | bytes 122888 | tf_op jit(solution)/shard_map/ppermute | solution.py:734
  90.0 4.9 %collective-permute-start.43 = (bf16[80,256]{1,0:T(8,128)(2,1)S(1)}, bf16[80,256]{1,0:T(8,128)(2,1)S(1)}, u32[]{:S(2)}, u32[]{:S(2)}) collective-permute-start(bf16[80,256]{1,0:T(8,128)(2,1)S(1)} %collective-permute-done.40.refs_13_), channel_id=1, source_target_pairs={{0,4},{1,5},{2,6},{3,7},{4,0},{5,1},{6,2},{7,3},{8,12},{9,13},{10,... | collective-permute-start | bytes 122888 | tf_op jit(solution)/shard_map/ppermute | solution.py:734
  91.3 10.7 %collective-permute-start.45 = (bf16[4,160,128]{2,1,0:T(8,128)(2,1)S(1)}, bf16[4,160,128]{2,1,0:T(8,128)(2,1)S(1)}, u32[]{:S(2)}, u32[]{:S(2)}) collective-permute-start(bf16[4,160,128]{2,1,0:T(8,128)(2,1)S(1)} %get-tuple-element.167), channel_id=1, source_target_pairs={{0,8},{1,9},{2,10},{3,11},{4,12},{5,13},{6,14},{7,15},{8,0},{9,1},... | collective-permute-start | bytes 491528 | tf_op jit(solution)/shard_map/ppermute | solution.py:734
  92.3 9.7 %collective-permute-start.46 = (bf16[4,160,128]{2,1,0:T(8,128)(2,1)S(1)}, bf16[4,160,128]{2,1,0:T(8,128)(2,1)S(1)}, u32[]{:S(2)}, u32[]{:S(2)}) collective-permute-start(bf16[4,160,128]{2,1,0:T(8,128)(2,1)S(1)} %get-tuple-element.168), channel_id=1, source_target_pairs={{0,16},{1,17},{2,18},{3,19},{4,20},{5,21},{6,22},{7,23},{8,24},{9,... | collective-permute-start | bytes 491528 | tf_op jit(solution)/shard_map/ppermute | solution.py:734
  93.3 8.7 %collective-permute-start.47 = (bf16[4,160,128]{2,1,0:T(8,128)(2,1)S(1)}, bf16[4,160,128]{2,1,0:T(8,128)(2,1)S(1)}, u32[]{:S(2)}, u32[]{:S(2)}) collective-permute-start(bf16[4,160,128]{2,1,0:T(8,128)(2,1)S(1)} %get-tuple-element.169), channel_id=1, source_target_pairs={{0,24},{1,25},{2,26},{3,27},{4,28},{5,29},{6,30},{7,31},{8,16},{9,... | collective-permute-start | bytes 491528 | tf_op jit(solution)/shard_map/ppermute | solution.py:734
  102.0 2.2 %collective-permute-start.48 = (bf16[4,4,160,128]{3,2,1,0:T(8,128)(2,1)S(1)}, bf16[4,4,160,128]{3,2,1,0:T(8,128)(2,1)S(1)}, u32[]{:S(2)}, u32[]{:S(2)}) collective-permute-start(bf16[4,4,160,128]{3,2,1,0:T(8,128)(2,1)S(1)} %get-tuple-element.170), channel_id=1, source_target_pairs={{0,4},{1,5},{2,6},{3,7},{4,0},{5,1},{6,2},{7,3},{8,12},{9,13},{10,... | collective-permute-start | bytes 1966088 | tf_op jit(solution)/shard_map/ppermute | solution.py:734
  104.5 10.5 %collective-permute-start.49 = (bf16[4,160,128]{2,1,0:T(8,128)(2,1)S(1)}, bf16[4,160,128]{2,1,0:T(8,128)(2,1)S(1)}, u32[]{:S(2)}, u32[]{:S(2)}) collective-permute-start(bf16[4,160,128]{2,1,0:T(8,128)(2,1)S(1)} %get-tuple-element.171), channel_id=1, source_target_pairs={{0,8},{1,9},{2,10},{3,11},{4,12},{5,13},{6,14},{7,15},{8,0},{9,1},... | collective-permute-start | bytes 491528 | tf_op jit(solution)/shard_map/ppermute | solution.py:734
  105.5 9.5 %collective-permute-start.50 = (bf16[4,160,128]{2,1,0:T(8,128)(2,1)S(1)}, bf16[4,160,128]{2,1,0:T(8,128)(2,1)S(1)}, u32[]{:S(2)}, u32[]{:S(2)}) collective-permute-start(bf16[4,160,128]{2,1,0:T(8,128)(2,1)S(1)} %get-tuple-element.172), channel_id=1, source_target_pairs={{0,16},{1,17},{2,18},{3,19},{4,20},{5,21},{6,22},{7,23},{8,24},{9,... | collective-permute-start | bytes 491528 | tf_op jit(solution)/shard_map/ppermute | solution.py:734
  106.5 8.5 %collective-permute-start.51 = (bf16[4,160,128]{2,1,0:T(8,128)(2,1)S(1)}, bf16[4,160,128]{2,1,0:T(8,128)(2,1)S(1)}, u32[]{:S(2)}, u32[]{:S(2)}) collective-permute-start(bf16[4,160,128]{2,1,0:T(8,128)(2,1)S(1)} %get-tuple-element.173), channel_id=1, source_target_pairs={{0,24},{1,25},{2,26},{3,27},{4,28},{5,29},{6,30},{7,31},{8,16},{9,... | collective-permute-start | bytes 491528 | tf_op jit(solution)/shard_map/ppermute | solution.py:734
  115.3 9.4 %collective-permute-start.52 = (bf16[320,128]{1,0:T(8,128)(2,1)S(1)}, bf16[320,128]{1,0:T(8,128)(2,1)S(1)}, u32[]{:S(2)}, u32[]{:S(2)}) collective-permute-start(bf16[320,128]{1,0:T(8,128)(2,1)S(1)} %get-tuple-element.182), channel_id=1, source_target_pairs={{0,1},{1,0},{2,3},{3,2},{4,5},{5,4},{6,7},{7,6},{8,9},{9,8},{10,11... | collective-permute-start | bytes 245768 | tf_op jit(solution)/shard_map/ppermute | solution.py:734
  116.2 8.5 %collective-permute-start.53 = (bf16[320,128]{1,0:T(8,128)(2,1)S(1)}, bf16[320,128]{1,0:T(8,128)(2,1)S(1)}, u32[]{:S(2)}, u32[]{:S(2)}) collective-permute-start(bf16[320,128]{1,0:T(8,128)(2,1)S(1)} %get-tuple-element.184), channel_id=1, source_target_pairs={{0,2},{1,3},{2,0},{3,1},{4,6},{5,7},{6,4},{7,5},{8,10},{9,11},{10,... | collective-permute-start | bytes 245768 | tf_op jit(solution)/shard_map/ppermute | solution.py:734
  117.8 6.9 %collective-permute-start.54 = (bf16[320,128]{1,0:T(8,128)(2,1)S(1)}, bf16[320,128]{1,0:T(8,128)(2,1)S(1)}, u32[]{:S(2)}, u32[]{:S(2)}) collective-permute-start(bf16[320,128]{1,0:T(8,128)(2,1)S(1)} %get-tuple-element.185), channel_id=1, source_target_pairs={{0,3},{1,2},{2,1},{3,0},{4,7},{5,6},{6,5},{7,4},{8,11},{9,10},{10,... | collective-permute-start | bytes 245768 | tf_op jit(solution)/shard_map/ppermute | solution.py:734
  124.7 5.4 %collective-permute-start.60 = (bf16[320,128]{1,0:T(8,128)(2,1)S(1)}, bf16[320,128]{1,0:T(8,128)(2,1)S(1)}, u32[]{:S(2)}, u32[]{:S(2)}) collective-permute-start(bf16[320,128]{1,0:T(8,128)(2,1)S(1)} %finish.1.refs_0_.refs_1_), channel_id=1, source_target_pairs={{0,24},{1,25},{2,26},{3,27},{4,28},{5,29},{6,30},{7,31},{8,16},{9,... | collective-permute-start | bytes 245768 | tf_op jit(solution)/shard_map/ppermute | solution.py:734
  126.2 4.8 %collective-permute-start.58 = (bf16[320,128]{1,0:T(8,128)(2,1)S(1)}, bf16[320,128]{1,0:T(8,128)(2,1)S(1)}, u32[]{:S(2)}, u32[]{:S(2)}) collective-permute-start(bf16[320,128]{1,0:T(8,128)(2,1)S(1)} %finish.1.refs_0_.refs_1_), channel_id=1, source_target_pairs={{0,16},{1,17},{2,18},{3,19},{4,20},{5,21},{6,22},{7,23},{8,24},{9,... | collective-permute-start | bytes 245768 | tf_op jit(solution)/shard_map/ppermute | solution.py:734
  127.1 4.4 %collective-permute-start.56 = (bf16[320,128]{1,0:T(8,128)(2,1)S(1)}, bf16[320,128]{1,0:T(8,128)(2,1)S(1)}, u32[]{:S(2)}, u32[]{:S(2)}) collective-permute-start(bf16[320,128]{1,0:T(8,128)(2,1)S(1)} %finish.1.refs_0_.refs_1_), channel_id=1, source_target_pairs={{0,8},{1,9},{2,10},{3,11},{4,12},{5,13},{6,14},{7,15},{8,0},{9,1},... | collective-permute-start | bytes 245768 | tf_op jit(solution)/shard_map/ppermute | solution.py:734
  128.3 3.3 %collective-permute-start.55 = (bf16[320,128]{1,0:T(8,128)(2,1)S(1)}, bf16[320,128]{1,0:T(8,128)(2,1)S(1)}, u32[]{:S(2)}, u32[]{:S(2)}) collective-permute-start(bf16[320,128]{1,0:T(8,128)(2,1)S(1)} %finish.1.refs_0_.refs_1_), channel_id=1, source_target_pairs={{0,4},{1,5},{2,6},{3,7},{4,0},{5,1},{6,2},{7,3},{8,12},{9,13},{10,... | collective-permute-start | bytes 245768 | tf_op jit(solution)/shard_map/ppermute | solution.py:734
  130.2 1.4 collective-permute-start.61
  131.0 1.3 collective-permute-start.59
  131.6 1.3 collective-permute-start.57
  133.1 5.4 %collective-permute-start.64 = (f32[8,128]{1,0:T(8,128)S(1)}, f32[8,128]{1,0:T(8,128)S(1)}, u32[]{:S(2)}, u32[]{:S(2)}) collective-permute-start(f32[8,128]{1,0:T(8,128)S(1)} %squares.1.refs_1_), channel_id=1, source_target_pairs={{0,3},{1,2},{2,1},{3,0},{4,7},{5,6},{6,5},{7,4},{8,11},{9,10},{10,... | collective-permute-start | bytes 12296 | tf_op jit(solution)/shard_map/ppermute | solution.py:734
  134.9 4.5 %collective-permute-start.63 = (f32[8,128]{1,0:T(8,128)S(1)}, f32[8,128]{1,0:T(8,128)S(1)}, u32[]{:S(2)}, u32[]{:S(2)}) collective-permute-start(f32[8,128]{1,0:T(8,128)S(1)} %squares.1.refs_1_), channel_id=1, source_target_pairs={{0,2},{1,3},{2,0},{3,1},{4,6},{5,7},{6,4},{7,5},{8,10},{9,11},{10,... | collective-permute-start | bytes 12296 | tf_op jit(solution)/shard_map/ppermute | solution.py:734
  136.0 3.6 %collective-permute-start.62 = (f32[8,128]{1,0:T(8,128)S(1)}, f32[8,128]{1,0:T(8,128)S(1)}, u32[]{:S(2)}, u32[]{:S(2)}) collective-permute-start(f32[8,128]{1,0:T(8,128)S(1)} %squares.1.refs_1_), channel_id=1, source_target_pairs={{0,1},{1,0},{2,3},{3,2},{4,5},{5,4},{6,7},{7,6},{8,9},{9,8},{10,11... | collective-permute-start | bytes 12296 | tf_op jit(solution)/shard_map/ppermute | solution.py:734
  (18 other events, 262.2 us)
